TPU v7x, 128 devices: a whole 4x4x4 slice. The times are simulated.
128 devices in a mesh: seq: 32 (over x, y_lo, z), head: 4 (over y_hi, core).
Axes of the slice: x: 4, y: 4 (y_hi: 2, y_lo: 2; y = y_hi * 2 + y_lo), z: 4, core: 2. Of those that a mesh axis runs over, the one named last changes fastest.
Arguments:
- queries: bfloat16 [16384, 1536], P('seq', 'head'), may hold values from -6 to 6
- keys: bfloat16 [16384, 1536], P('seq', 'head'), may hold values from -6 to 6
- values: bfloat16 [16384, 1536], P('seq', 'head'), may hold values from -6 to 6
- upstream_out: bfloat16 [16384, 1536], P('seq'), may hold values from -192 to 192
- out_weight: bfloat16 [1536, 1536], P('head'), may hold values from -0.15625 to 0.15625
- qkv_weight: bfloat16 [3, 1536, 1536], P(None, None, 'head'), may hold values from -0.15625 to 0.15625
- rand_links: int32 [128, 3], replicated, may hold values from 0 to 127, as said below
- global_links: int32 [2], replicated, may hold values from 0 to 127, as said below
Outputs:
- grad_input: bfloat16 [1536, 16384], P('head', 'seq')
Inputs may be any that keep to these rules, and one draw needn't show every extreme that they name: `rand_links`: counting each of the 2 global blocks once, the 14 blocks named by a run of 4 consecutive query blocks starting at a multiple of 4 fall at most 2 times into any run of 4 consecutive key blocks starting at a multiple of 4, and exactly 2 times into some such run. `global_links`: the 2 blocks differ; the last block of the sequence is always one of them.
All inputs are finite; a program needn't handle non-finite values.
Results may differ from a plain program's by a relative error of at most 0.02.
Values may be sent and summed in bfloat16 or wider, within the bound.
No kernel may reach another device: no remote copies, remote signals or barrier semaphores. Data moves between devices by JAX's collectives and lax.ppermute only.
A program may use at most 192 MiB of HBM per device.

v0:
```python
import math

import jax
import jax.numpy as jnp
from jax import lax
from jax.sharding import PartitionSpec as P

HD = 128
BLK = 128
R = 3
G = 2
BLK_DEV = 4


def with_halo(block, sides, width):
    for axis, dim in sides:
        count = lax.axis_size(axis)
        forward = [(i, i + 1) for i in range(count - 1)]
        forward.append((count - 1, 0))
        backward = [(target, source) for source, target in forward]
        low = lax.ppermute(
            lax.slice_in_dim(block, block.shape[dim] - width, None, axis=dim), axis, forward
        )
        high = lax.ppermute(lax.slice_in_dim(block, 0, width, axis=dim), axis, backward)
        block = jnp.concatenate([low, block, high], axis=dim)
    return block


def score_parts(queries, keys, values, upstream, scale):
    scores = (
        jnp.einsum("bqhd,bkhd->bhqk", queries, keys, preferred_element_type=jnp.float32) * scale
    )
    slope = jnp.einsum("bqhd,bkhd->bhqk", upstream, values, preferred_element_type=jnp.float32)
    return (scores, slope)


def grads_from(probs, slope, weighted, queries, upstream, scale):
    coeff = (probs * (slope - weighted)).astype(jnp.bfloat16)
    probs_low = probs.astype(jnp.bfloat16)
    key_part = (
        jnp.einsum("bhqk,bqhd->bkhd", coeff, queries, preferred_element_type=jnp.float32) * scale
    )
    value_part = jnp.einsum(
        "bhqk,bqhd->bkhd", probs_low, upstream, preferred_element_type=jnp.float32
    )
    return (coeff, key_part, value_part)


def block_step(inputs, scale):
    queries, upstream, keys, values = inputs
    scores, slope = score_parts(queries, keys, values, upstream, scale)
    peak = jnp.max(scores, axis=-1, keepdims=True)
    log_total = peak + jnp.log(jnp.sum(jnp.exp(scores - peak), axis=-1, keepdims=True))
    probs = jnp.exp(scores - log_total)
    weighted = jnp.sum(probs * slope, axis=-1, keepdims=True)
    coeff, key_part, value_part = grads_from(probs, slope, weighted, queries, upstream, scale)
    query_part = (
        jnp.einsum("bhqk,bkhd->bqhd", coeff, keys, preferred_element_type=jnp.float32) * scale
    )
    return (
        query_part.astype(jnp.bfloat16),
        key_part,
        value_part,
        log_total[..., 0],
        weighted[..., 0],
    )


def body(queries, keys, values, upstream_out, out_weight, qkv_weight, rand_links, global_links):
    scale = HD ** (-0.5)
    tok_rows, feat = queries.shape
    heads_here = feat // HD
    groups = lax.axis_size("seq")
    me = lax.axis_index("seq")
    nkey = 3 + R + G
    req = BLK_DEV * R + G
    cap = max(2, (req + groups - 1) // groups)
    grad_ctx = lax.dot_general(
        upstream_out, out_weight, (((1,), (1,)), ((), ())), preferred_element_type=jnp.float32
    ).astype(jnp.bfloat16)
    pair = jnp.stack((keys, values), axis=1)
    padded = with_halo(pair, (("seq", 0),), BLK)
    pblocks = padded.reshape(BLK_DEV + 2, BLK, 2, feat)
    window = jnp.stack(
        [pblocks[0:BLK_DEV], pblocks[1 : BLK_DEV + 1], pblocks[2 : BLK_DEV + 2]], axis=1
    )
    links = jnp.concatenate(
        [
            rand_links.reshape(groups, BLK_DEV * R),
            jnp.broadcast_to(global_links[None, :], (groups, G)),
        ],
        axis=1,
    )
    owner = links // BLK_DEV
    local = links % BLK_DEV
    earlier = jnp.arange(req, dtype=jnp.int32)[None, :] < jnp.arange(req, dtype=jnp.int32)[:, None]
    same_owner = owner[:, :, None] == owner[:, None, :]
    rank = jnp.sum((same_owner & earlier[None]).astype(jnp.int32), axis=2)
    slot = owner * cap + rank
    my_slot = lax.dynamic_index_in_dim(slot, me, 0, keepdims=False)
    mine = (owner == me)[:, :, None] & (
        rank[:, :, None] == jnp.arange(cap, dtype=jnp.int32)[None, None, :]
    )
    slot_local = jnp.sum(jnp.where(mine, local[:, :, None], 0), axis=1)
    slot_used = jnp.any(mine, axis=1)
    kv_blocks = pair.reshape(BLK_DEV, BLK, 2, feat)
    outgoing = jnp.take(kv_blocks, slot_local.reshape(-1), axis=0).reshape(
        groups, cap, BLK, 2, feat
    )
    incoming = lax.all_to_all(outgoing, "seq", split_axis=0, concat_axis=0, tiled=True)
    fetched = jnp.take(incoming.reshape(groups * cap, BLK, 2, feat), my_slot, axis=0)
    rand_kv = fetched[: BLK_DEV * R].reshape(BLK_DEV, R, BLK, 2, feat)
    glob_kv = jnp.broadcast_to(fetched[BLK_DEV * R :][None], (BLK_DEV, G, BLK, 2, feat))
    all_kv = jnp.concatenate([window, rand_kv, glob_kv], axis=1)
    sub = math.gcd(BLK_DEV, 4)
    steps = BLK_DEV // sub
    span = nkey * BLK
    q_steps = queries.reshape(steps, sub, BLK, heads_here, HD)
    d_steps = grad_ctx.reshape(steps, sub, BLK, heads_here, HD)
    k_steps = all_kv[:, :, :, 0].reshape(steps, sub, span, heads_here, HD)
    v_steps = all_kv[:, :, :, 1].reshape(steps, sub, span, heads_here, HD)
    query_part, key_part, value_part, log_total, weighted = lax.map(
        lambda inputs: block_step(inputs, scale), (q_steps, d_steps, k_steps, v_steps)
    )
    grad_q = query_part.reshape(tok_rows, feat)
    kv_grad = jnp.stack(
        (key_part.reshape(BLK_DEV, nkey, BLK, feat), value_part.reshape(BLK_DEV, nkey, BLK, feat)),
        axis=3,
    )
    acc = jnp.pad(kv_grad[:, 0], ((0, 2), (0, 0), (0, 0), (0, 0)))
    acc = acc + jnp.pad(kv_grad[:, 1], ((1, 1), (0, 0), (0, 0), (0, 0)))
    acc = acc + jnp.pad(kv_grad[:, 2], ((2, 0), (0, 0), (0, 0), (0, 0)))
    rims = jnp.concatenate([acc[0], acc[BLK_DEV + 1]], axis=0)
    back = with_halo(rims.astype(jnp.bfloat16), (("seq", 0),), BLK).astype(rims.dtype)
    local_grad = acc[1 : BLK_DEV + 1]
    local_grad = local_grad.at[0].add(back[:BLK]).at[BLK_DEV - 1].add(back[3 * BLK :])
    selector = (
        (
            (slot_local[:, :, None] == jnp.arange(BLK_DEV, dtype=jnp.int32)[None, None, :])
            & slot_used[:, :, None]
        )
        .astype(jnp.bfloat16)
        .reshape(groups * cap, BLK_DEV)
    )
    glob_grad = jnp.sum(kv_grad[:, 3 + R :], axis=0).astype(jnp.bfloat16)
    rand_grad = kv_grad[:, 3 : 3 + R].reshape(BLK_DEV * R, BLK, 2, feat).astype(jnp.bfloat16)
    link_grad = jnp.concatenate([rand_grad, glob_grad], axis=0)
    buffer = jnp.zeros((groups * cap, BLK, 2, feat), jnp.bfloat16).at[my_slot].set(link_grad)
    returned = lax.all_to_all(
        buffer.reshape(groups, cap, BLK, 2, feat), "seq", split_axis=0, concat_axis=0, tiled=True
    )
    added = lax.dot_general(
        selector,
        returned.reshape(groups * cap, BLK * 2 * feat),
        (((0,), (0,)), ((), ())),
        preferred_element_type=jnp.float32,
    )
    local_grad = local_grad + added.reshape(BLK_DEV, BLK, 2, feat)
    key_value_grad = local_grad.astype(jnp.bfloat16).reshape(tok_rows, 2, feat)
    stacked = jnp.stack((grad_q, key_value_grad[:, 0], key_value_grad[:, 1]), axis=0)
    return lax.psum_scatter(
        lax.dot_general(
            qkv_weight, stacked, (((0, 2), (0, 2)), ((), ())), preferred_element_type=jnp.float32
        ).astype(jnp.bfloat16),
        "head",
        scatter_dimension=0,
        tiled=True,
    )


def solution(mesh):
    in_specs = (
        P("seq", "head"),
        P("seq", "head"),
        P("seq", "head"),
        P("seq", None),
        P("head", None),
        P(None, None, "head"),
        P(),
        P(),
    )
    out_specs = P("head", "seq")
    return jax.shard_map(body, mesh=mesh, in_specs=in_specs, out_specs=out_specs, check_vma=False)
```

profile of v0, /device:TPU:1, one launch (start us, length us, event | category | flops | bytes accessed | tf_op | source)
XLA Modules:
  0.0 730.1 jit_solution(10036309039206196364)
XLA Ops:
  17.0 2.1 pad_maximum_fusion.6
  19.1 8.4 %gather_fusion = bf16[64,128,2,384]{3,1,2,0:T(8,128)(2,1)} fusion(bf16[4,128,2,384]{3,1,0,2:T(8,128)(2,1)} %pad_maximum_fusion.6, s32[1024]{0:T(1024)} %pad_clamp_fusion.1), kind=kCustom, calls=%fused_computation | custom fusion | bytes 25166080 | tf_op jit(solution)/shard_map/jit(_take)/gather | solution.py:107
  27.6 10.8 %broadcast_select_fusion = bf16[32,2,128,2,384]{4,2,3,1,0:T(8,128)(2,1)} fusion(bf16[32,2,128,2,384]{4,2,3,1,0:T(8,128)(2,1)} %bitcast.113, pred[32,2]{1,0:T(8,128)(4,1)} %copy.179), kind=kLoop, calls=%fused_computation.13 | loop fusion | flops 6291456 | bytes 25165888 | tf_op jit(solution)/shard_map/jit(_take)/select_n | solution.py:107
  38.4 9.8 %all-to-all-start = ((bf16[32,2,128,2,384]{4,2,3,1,0:T(8,128)(2,1)}), bf16[32,2,128,2,384]{4,2,3,1,0:T(8,128)(2,1)}, u32[]{:S(2)}, u32[]{:S(2)}) async-start(bf16[32,2,128,2,384]{4,2,3,1,0:T(8,128)(2,1)} %broadcast_select_fusion), calls=%async_computation | async-start | bytes 25165824 | tf_op jit(solution)/shard_map/all_to_all | solution.py:110
  50.0 5.5 collective-permute-start.1
  55.5 3.5 convolution_convert_fusion
  59.0 2.5 reshape.485
  61.5 2.0 copy.197
  63.5 2.0 reshape.482
  67.6 144.3 %collective-permute-done.1 = bf16[128,2,384]{2,0,1:T(8,128)(2,1)} collective-permute-done((bf16[128,2,384]{2,0,1:T(8,128)(2,1)}, bf16[128,2,384]{2,0,1:T(8,128)(2,1)}, u32[]{:S(2)}, u32[]{:S(2)}) %collective-permute-start.1) | collective-permute-done | bytes 196640 | tf_op jit(solution)/shard_map/ppermute | solution.py:24
  211.9 10.1 %collective-permute-done = bf16[128,2,384]{2,0,1:T(8,128)(2,1)} collective-permute-done((bf16[128,2,384]{2,0,1:T(8,128)(2,1)}, bf16[128,2,384]{2,0,1:T(8,128)(2,1)}, u32[]{:S(2)}, u32[]{:S(2)}) %collective-permute-start) | collective-permute-done | bytes 196640 | tf_op jit(solution)/shard_map/ppermute | solution.py:21
  226.5 9.1 %all-to-all-done = bf16[32,2,128,2,384]{4,2,3,1,0:T(8,128)(2,1)} async-done(((bf16[32,2,128,2,384]{4,2,3,1,0:T(8,128)(2,1)}), bf16[32,2,128,2,384]{4,2,3,1,0:T(8,128)(2,1)}, u32[]{:S(2)}, u32[]{:S(2)}) %all-to-all-start) | async-done | bytes 12582944 | tf_op jit(solution)/shard_map/all_to_all | solution.py:110
  235.6 7.3 gather_fusion.1
  242.9 2.2 broadcast_select_fusion.1
  248.3 6.6 fusion.53
  254.9 9.0 %reshape.478 = bf16[4,1024,3,128]{3,2,1,0:T(4,128)(2,1)} reshape(bf16[4,8,128,1,384]{4,2,3,1,0:T(8,128)(2,1)} %get-tuple-element.60) | data formatting | bytes 6291456 | tf_op jit(solution)/shard_map/while/body/jit(dynamic_index_in_dim)/squeeze | solution.py:122
  263.9 5.0 copy.183
  268.9 5.8 squeeze.43
  274.7 3.3 bitcast_reduce_fusion
  282.5 4.1 multiply_reduce_fusion
  286.6 4.1 copy.231
  290.8 10.4 %copy.200 = f32[4,8,128,1,384]{4,3,2,0,1:T(1,128)} copy(f32[4,8,128,1,384]{2,1,4,0,3:T(8,128)} %bitcast.114) | data formatting | bytes 12582912 | tf_op jit(solution)/shard_map/stack;reshape | solution.py:126
  301.2 6.1 multiply_convert_fusion
  309.0 3.6 multiply_bitcast_fusion
  312.7 6.6 copy.196
  319.2 7.0 copy.230
  326.2 10.3 %copy.199 = f32[4,8,128,1,384]{4,3,2,0,1:T(1,128)} copy(f32[4,8,128,1,384]{2,1,4,0,3:T(8,128)} %bitcast.116) | data formatting | bytes 12582912 | tf_op jit(solution)/shard_map/stack;reshape | solution.py:126
  336.5 5.2 fusion.10
  341.7 5.8 fusion.6
  349.9 6.6 broadcast_in_dim.83
  356.5 10.1 %scatter_fusion = bf16[64,128,2,384]{3,1,2,0:T(8,128)(2,1)} fusion(bf16[64,128,2,384]{3,1,2,0:T(8,128)(2,1)} %broadcast_in_dim.83, s32[14]{0:T(128)} %copy-done.17, bf16[14,128,2,384]{3,1,2,0:T(8,128)(2,1)} %pad_maximum_fusion.1), kind=kCustom, calls=%fused_computation.2 | custom fusion | bytes 8257592 | tf_op jit(solution)/shard_map/scatter | solution.py:148
  366.6 23.6 %copy.207 = bf16[32,2,128,2,384]{4,3,2,1,0:T(2,128)(2,1)} copy(bf16[32,2,128,2,384]{4,2,3,1,0:T(8,128)(2,1)} %bitcast.111) | data formatting | bytes 25165824 | tf_op jit(solution)/shard_map/reshape | solution.py:150
  390.2 27.0 %all-to-all-start.1 = ((bf16[32,2,128,2,384]{4,3,2,1,0:T(2,128)(2,1)}), bf16[32,2,128,2,384]{4,3,2,1,0:T(2,128)(2,1)}, u32[]{:S(2)}, u32[]{:S(2)}) async-start(bf16[32,2,128,2,384]{4,3,2,1,0:T(2,128)(2,1)} %copy.207), calls=%async_computation.1 | async-start | bytes 25165824 | tf_op jit(solution)/shard_map/all_to_all | solution.py:149
  418.9 5.8 fusion.22
  424.7 2.7 fusion.52
  429.6 4.5 collective-permute-start.3
  435.8 2.1 copy.221
  437.9 2.0 reshape.479
  439.9 1.9 slice.162
  441.9 134.4 %collective-permute-done.2 = bf16[128,2,384]{2,1,0:T(2,128)(2,1)} collective-permute-done((bf16[128,2,384]{2,1,0:T(2,128)(2,1)}, bf16[128,2,384]{2,1,0:T(2,128)(2,1)}, u32[]{:S(2)}, u32[]{:S(2)}) %collective-permute-start.2) | collective-permute-done | bytes 196640 | tf_op jit(solution)/shard_map/ppermute | solution.py:21
  577.7 2.2 copy.202
  582.3 8.9 %scatter-add.9 = f32[4,128,2,384]{3,0,2,1:T(4,128)} dynamic-update-slice(f32[4,128,2,384]{3,0,2,1:T(4,128)} %copy.202, f32[1,128,2,384]{3,0,2,1:T(1,128)} %copy_add_fusion, s32[]{:T(128)} %constant.142.clone.1, s32[]{:T(128)} %constant.141.clone.1, s32[]{:T(128)} %constant.141.clone.1, s32[]{:T(128)} %constant.141.clone.1) | dynamic-update-slice | bytes 786436 | tf_op jit(solution)/shard_map/scatter-add | solution.py:136
  592.7 14.8 %reshape.450 = bf16[64,98304]{1,0:T(8,128)(2,1)} reshape(bf16[32,2,128,2,384]{4,3,2,1,0:T(2,128)(2,1)} %all-to-all-done.1) | data formatting | bytes 25165824 | tf_op jit(solution)/shard_map/reshape | solution.py:154
  607.5 15.8 %dot_general.40 = bf16[128,2,384,64]{2,1,0,3:T(2,128)(2,1)} reshape(bf16[98304,64]{0,1:T(8,128)(2,1)} %bitcast.112) | data formatting | bytes 25165824 | tf_op jit(solution)/shard_map/dot_general | solution.py:152
  623.3 14.1 %add_convert_fusion = bf16[4,128,2,384]{3,0,2,1:T(4,128)(2,1)S(1)} fusion(f32[4,128,2,384]{3,0,2,1:T(4,128)} %scatter-add.9, bf16[128,2,384,64]{2,1,0,3:T(2,128)(2,1)} %dot_general.40, s32[64]{0:T(128)S(1)} %copy-done.18, pred[64]{0:T(512)(128)(4,1)S(1)} %and.96), kind=kOutput, calls=%fused_computation.42 | convolution fusion | flops 51118592 | bytes 14942528 | tf_op jit(solution)/shard_map/dot_general | solution.py:152
  638.4 3.4 fusion.16
  641.8 2.6 copy.222
  644.4 78.4 %reduce-scatter.4.cloned.1.call-done = bf16[384,512]{1,0:T(8,128)(2,1)} async-done(((bf16[1536,512]{1,0:T(8,128)(2,1)}), bf16[384,512]{1,0:T(8,128)(2,1)}) %reduce-scatter.4.cloned.1.call-update) | async-done | bytes 393232 | tf_op jit(solution)/shard_map/reduce_scatter | solution.py:161
  (90 shorter events, 42.7 us)
Async XLA Ops:
  6.5 631.1 %copy-start = (bf16[3,1536,384]{2,1,0:T(8,128)(2,1)S(1)}, bf16[3,1536,384]{2,1,0:T(8,128)(2,1)}, u32[]{:S(2)}) copy-start(bf16[3,1536,384]{2,1,0:T(8,128)(2,1)} %param.17) | copy-start | bytes 10616836
  11.3 0.6 copy-start.13
  11.3 0.6 copy-start.15
  11.5 0.6 copy-start.12
  12.1 0.6 copy-start.16
  38.4 197.2 %all-to-all-start = ((bf16[32,2,128,2,384]{4,2,3,1,0:T(8,128)(2,1)}), bf16[32,2,128,2,384]{4,2,3,1,0:T(8,128)(2,1)}, u32[]{:S(2)}, u32[]{:S(2)}) async-start(bf16[32,2,128,2,384]{4,2,3,1,0:T(8,128)(2,1)} %broadcast_select_fusion), calls=%async_computation | async-start | bytes 25165824 | tf_op jit(solution)/shard_map/all_to_all | solution.py:110
  50.0 161.9 %collective-permute-start.1 = (bf16[128,2,384]{2,0,1:T(8,128)(2,1)}, bf16[128,2,384]{2,0,1:T(8,128)(2,1)}, u32[]{:S(2)}, u32[]{:S(2)}) collective-permute-start(bf16[128,2,384]{2,0,1:T(8,128)(2,1)} %get-tuple-element.68), channel_id=1, source_target_pairs={{4,0},{8,4},{12,8},{16,12},{20,16},{24,20},{28,24},{32,28},{36,32}... | collective-permute-start | bytes 589832 | tf_op jit(solution)/shard_map/ppermute | solution.py:24
  55.5 166.6 %collective-permute-start = (bf16[128,2,384]{2,0,1:T(8,128)(2,1)}, bf16[128,2,384]{2,0,1:T(8,128)(2,1)}, u32[]{:S(2)}, u32[]{:S(2)}) collective-permute-start(bf16[128,2,384]{2,0,1:T(8,128)(2,1)} %get-tuple-element.69), channel_id=1, source_target_pairs={{0,4},{4,8},{8,12},{12,16},{16,20},{20,24},{24,28},{28,32},{32,36}... | collective-permute-start | bytes 589832 | tf_op jit(solution)/shard_map/ppermute | solution.py:21
  65.5 159.1 %copy-start.7 = (bf16[512,384]{1,0:T(8,128)(2,1)S(1)}, bf16[512,384]{1,0:T(8,128)(2,1)}, u32[]{:S(2)}) copy-start(bf16[512,384]{1,0:T(8,128)(2,1)} %param.14) | copy-start | bytes 1179652
  65.5 159.1 %copy-start.8 = (bf16[512,384]{1,0:T(8,128)(2,1)S(1)}, bf16[512,384]{1,0:T(8,128)(2,1)}, u32[]{:S(2)}) copy-start(bf16[512,384]{1,0:T(8,128)(2,1)} %param.13) | copy-start | bytes 1179652
  66.5 145.5 %copy-start.17 = (s32[14]{0:T(128)}, s32[14]{0:T(128)S(1)}, u32[]{:S(2)}) copy-start(s32[14]{0:T(128)S(1)} %fusion.49) | copy-start | bytes 172
  278.0 2.7 copy-start.1
  278.0 1.3 copy-start.10
  279.3 1.5 copy-start.14
  279.3 3.2 copy-start.6
  301.2 7.8 %copy-start.9 = (bf16[4,128,3,128]{3,2,1,0:T(4,128)(2,1)S(1)}, bf16[4,128,3,128]{3,2,1,0:T(4,128)(2,1)}, u32[]{:S(2)}) copy-start(bf16[4,128,3,128]{3,2,1,0:T(4,128)(2,1)} %reshape.482) | copy-start | bytes 1179652
  307.3 1.7 copy-start.3
  336.5 5.2 copy-start.2
  390.2 202.5 %all-to-all-start.1 = ((bf16[32,2,128,2,384]{4,3,2,1,0:T(2,128)(2,1)}), bf16[32,2,128,2,384]{4,3,2,1,0:T(2,128)(2,1)}, u32[]{:S(2)}, u32[]{:S(2)}) async-start(bf16[32,2,128,2,384]{4,3,2,1,0:T(2,128)(2,1)} %copy.207), calls=%async_computation.1 | async-start | bytes 25165824 | tf_op jit(solution)/shard_map/all_to_all | solution.py:149
  417.2 305.6 %reduce-scatter.4.cloned.1.call-start = ((), (), s32[]{:S(2)}) async-start(), calls=%async_computation.3 | async-start | bytes 1966080 | tf_op jit(solution)/shard_map/reduce_scatter | solution.py:161
  424.7 9.4 %copy-start.4 = (bf16[4,3,128,1024]{2,3,1,0:T(8,128)(2,1)S(1)}, bf16[4,3,128,1024]{2,3,1,0:T(8,128)(2,1)}, u32[]{:S(2)}) copy-start(bf16[4,3,128,1024]{2,3,1,0:T(8,128)(2,1)} %copy-done.3) | copy-start | bytes 9437188
  424.7 9.4 %copy-start.5 = (bf16[4,1024,3,128]{1,3,2,0:T(8,128)(2,1)S(1)}, bf16[4,1024,3,128]{1,3,2,0:T(8,128)(2,1)}, u32[]{:S(2)}) copy-start(bf16[4,1024,3,128]{1,3,2,0:T(8,128)(2,1)} %squeeze.43) | copy-start | bytes 9437188
  428.4 147.8 %collective-permute-start.2 = (bf16[128,2,384]{2,1,0:T(2,128)(2,1)}, bf16[128,2,384]{2,1,0:T(2,128)(2,1)}, u32[]{:S(2)}, u32[]{:S(2)}) collective-permute-start(bf16[128,2,384]{2,1,0:T(2,128)(2,1)} %get-tuple-element.62), channel_id=1, source_target_pairs={{0,4},{4,8},{8,12},{12,16},{16,20},{20,24},{24,28},{28,32},{32,36}... | collective-permute-start | bytes 589832 | tf_op jit(solution)/shard_map/ppermute | solution.py:21
  429.6 146.7 %collective-permute-start.3 = (bf16[128,2,384]{2,1,0:T(2,128)(2,1)}, bf16[128,2,384]{2,1,0:T(2,128)(2,1)}, u32[]{:S(2)}, u32[]{:S(2)}) collective-permute-start(bf16[128,2,384]{2,1,0:T(2,128)(2,1)} %get-tuple-element.63), channel_id=1, source_target_pairs={{4,0},{8,4},{12,8},{16,12},{20,16},{24,20},{28,24},{32,28},{36,32}... | collective-permute-start | bytes 589832 | tf_op jit(solution)/shard_map/ppermute | solution.py:24
  607.5 15.8 %copy-start.18 = (s32[64]{0:T(128)S(1)}, s32[64]{0:T(128)}, u32[]{:S(2)}) copy-start(s32[64]{0:T(128)} %reshape.448) | copy-start | bytes 772
  637.4 1.0 copy-start.11
Sparse Core Ops, SparseCore 0:
  644.5 78.2 reduce-scatter.3
where the time goes:
time: 737 us; the launch traced here: 730 us
  waiting for transfers between devices  378 us (51%)
  local copies, waits for them, and re-layouts  199 us (27%)
  other arithmetic  56.5 us (8%)
  starting transfers between devices  48 us (7%)
  matrix products  34.9 us (5%)
  between operations  14.1 us (2%)
    ppermute x2, waiting for transfers between devices, with_halo(): lax.ppermute(lax.slice_in_dim(block, block.shape[dim] - width, None, axis...  144 us
    ppermute x2, waiting for transfers between devices, with_halo(): lax.ppermute(lax.slice_in_dim(block, 0, width, axis=dim), axis, backward)  144 us
    reduce_scatter x1, waiting for transfers between devices, body(): lax.psum_scatter(lax.dot_general(qkv_weight, stacked, (((0, 2), (0, 2)),...  78.4 us
    all_to_all x1, starting transfers between devices, body(): lax.all_to_all(buffer.reshape(groups, cap, BLK, 2, feat), 'seq', split_ax...  27 us
    unnamed x45, local copies, waits for them, and re-layouts  24.8 us
    reshape x1, local copies, waits for them, and re-layouts, body(): buffer.reshape(groups, cap, BLK, 2, feat)  23.6 us
    squeeze x5, local copies, waits for them, and re-layouts, body(): lax.map(lambda inputs: block_step(inputs, scale), (q_steps, d_steps, k_st...  21.3 us
    another operation x2, local copies, waits for them, and re-layouts, body(): jnp.stack((key_part.reshape(BLK_DEV, nkey, BLK, feat), value_part.reshape...  20.7 us
  transfers between devices with their start and end apart: 7, of which 6 were waited for; matrix products, arithmetic and copies ran while one was open for 7% of the time, Pallas kernels for 0%

commit v1 on v0

v1 whole, which is shorter than its diff:
```python
import functools

import jax
import jax.numpy as jnp
from jax import lax
from jax.experimental import pallas as pl
from jax.experimental.pallas import tpu as pltpu
from jax.sharding import PartitionSpec as P

HD = 128
BLK = 128
R = 3
G = 2
BLK_DEV = 4
NKEY = 3 + R + G
AXES = ("seq", "head")
LINE = 4
NQ = LINE * BLK_DEV
ROWS = NQ * BLK
NSHARD = 8
HALF = ROWS // 2
F32 = jnp.float32
BF16 = jnp.bfloat16


def moved(dev, ring, pair, line):
    h, s = dev % 4, dev // 4
    x, y, z = s // 8, (s // 4) % 2, s % 4
    if h % 2 == 0:
        x, z = (x + ring) % 4, (z + line) % 4
    else:
        z, x = (z + ring) % 4, (x + line) % 4
    y = (y + pair) % 2
    return ((x * 2 + y) * 4 + z) * 4 + h


def line_pos(dev):
    h, s = dev % 4, dev // 4
    return s % 4 if h % 2 == 0 else s // 8


DEVS = range(128)
DEAL = {
    k: [(d, moved(d, 0, 0, k)) for d in DEVS if line_pos(moved(d, 0, 0, k)) < 3] for k in (1, 2, 3)
}
BACK = {k: [(t, d) for d, t in DEAL[k]] for k in (1, 2, 3)}
RING = {k: [(d, moved(d, k, 0, 0)) for d in DEVS if line_pos(d) < 3] for k in (1, -1)}
PAIR = [(d, moved(d, 0, 1, 0)) for d in DEVS if line_pos(d) < 3]
CORE = [(d, d ^ 1) for d in DEVS]
FAR = [(d, d ^ 2) for d in DEVS]


def send(x, perm):
    return lax.ppermute(x, AXES, perm)


def attend_kernel(table, qd_ref, *refs):
    kv_refs = refs[:NSHARD]
    gq_ref = refs[NSHARD]
    out_refs = refs[NSHARD + 1 : 2 * NSHARD + 1]
    kv, acc, kv_now, sems = refs[2 * NSHARD + 1 :]
    scale = HD ** (-0.5)
    copies = [
        pltpu.make_async_copy(kv_refs[n], kv.at[pl.ds(n * ROWS, ROWS)], sems.at[n])
        for n in range(NSHARD)
    ]
    for c in copies:
        c.start()

    def zero(n, carry):
        acc[pl.ds(n * BLK, BLK), :] = jnp.zeros((BLK, 2 * HD), F32)
        return carry

    lax.fori_loop(0, NSHARD * NQ, zero, 0)
    for c in copies:
        c.wait()

    def step(n, carry):
        rows = pl.ds(pl.multiple_of(n * BLK, BLK), BLK)
        q = qd_ref[rows, :HD]
        d = qd_ref[rows, HD:]
        for j in range(NKEY):
            at = pl.multiple_of(table[n, j] * BLK, BLK)
            kv_now[j * BLK : (j + 1) * BLK, :] = kv[pl.ds(at, BLK), :]
        k = kv_now[:, :HD]
        v = kv_now[:, HD:]
        nt = (((1,), (1,)), ((), ()))
        scores = lax.dot_general(k, q, nt, preferred_element_type=F32)
        slope = lax.dot_general(v, d, nt, preferred_element_type=F32)
        peak = jnp.max(scores, axis=0, keepdims=True)
        e = jnp.exp((scores - peak) * scale)
        inv = 1.0 / jnp.sum(e, axis=0, keepdims=True)
        weighted = jnp.sum(e * slope, axis=0, keepdims=True) * inv
        probs = e * inv
        coeff = (probs * (slope - weighted)).astype(BF16)
        low = probs.astype(BF16)
        gq = lax.dot_general(coeff, k, (((0,), (0,)), ((), ())), preferred_element_type=F32)
        gq_ref[rows, :] = (gq * scale).astype(BF16)
        nn = (((1,), (0,)), ((), ()))
        gk = lax.dot_general(coeff, q, nn, preferred_element_type=F32)
        gv = lax.dot_general(low, d, nn, preferred_element_type=F32)
        for j in range(NKEY):
            at = pl.multiple_of(table[n, j] * BLK, BLK)
            part = slice(j * BLK, (j + 1) * BLK)
            acc[pl.ds(at, BLK), :HD] += gk[part]
            acc[pl.ds(at, BLK), HD:] += gv[part]
        return carry

    lax.fori_loop(0, NQ, step, 0)

    for m in range(NSHARD):

        def put(n, carry, m=m):
            rows = pl.ds(pl.multiple_of(n * BLK, BLK), BLK)
            src = pl.ds(pl.multiple_of(m * ROWS + n * BLK, BLK), BLK)
            out_refs[m][rows, :HD] = (acc[src, :HD] * scale).astype(BF16)
            out_refs[m][rows, HD:] = acc[src, HD:].astype(BF16)
            return carry

        lax.fori_loop(0, NQ, put, 0)


def attend(table, qd, shards):
    shard = jax.ShapeDtypeStruct((ROWS, 2 * HD), BF16)
    vmem = pl.BlockSpec(memory_space=pltpu.VMEM)
    out = pl.pallas_call(
        attend_kernel,
        name="attend",
        out_shape=(jax.ShapeDtypeStruct((ROWS, HD), BF16),) + (shard,) * NSHARD,
        grid_spec=pltpu.PrefetchScalarGridSpec(
            num_scalar_prefetch=1,
            grid=(),
            in_specs=[vmem] + [pl.BlockSpec(memory_space=pl.ANY)] * NSHARD,
            out_specs=(vmem,) * (NSHARD + 1),
            scratch_shapes=[
                pltpu.VMEM((NSHARD * ROWS, 2 * HD), BF16),
                pltpu.VMEM((NSHARD * ROWS, 2 * HD), F32),
                pltpu.VMEM((NKEY * BLK, 2 * HD), BF16),
                pltpu.SemaphoreType.DMA((NSHARD,)),
            ],
        ),
        compiler_params=pltpu.CompilerParams(vmem_limit_bytes=56 << 20),
    )(table, qd, *shards)
    return out[0], out[1:]


def add(*terms):
    return functools.reduce(lambda a, b: a + b, [t.astype(F32) for t in terms]).astype(BF16)


def ring_gather(shard):
    one = send(shard, RING[1])
    three = send(shard, RING[-1])
    two = jnp.concatenate([send(one[:HALF], RING[1]), send(three[HALF:], RING[-1])], axis=0)
    return [shard, one, two, three]


def ring_reduce(parts):
    zero, one, two, three = parts
    down = send(two[:HALF], RING[1])
    up = send(two[HALF:], RING[-1])
    three = jnp.concatenate([add(three[:HALF], down), three[HALF:]], axis=0)
    one = jnp.concatenate([one[:HALF], add(one[HALF:], up)], axis=0)
    return add(zero, send(three, RING[1]), send(one, RING[-1]))


def deal(pair, pos):
    heads = pair.reshape(2, BLK_DEV * BLK, 3, HD).transpose(2, 1, 0, 3)
    heads = heads.reshape(3, BLK_DEV * BLK, 2 * HD)

    def head(k):
        return lax.dynamic_index_in_dim(heads, jnp.minimum((pos + k) % 4, 2), 0, keepdims=False)

    return jnp.concatenate([head(0)] + [send(head(k), DEAL[k]) for k in (1, 2, 3)], axis=0)


def give_back(grads, pos, width):
    grads = grads.reshape(LINE, BLK_DEV * BLK, width)
    got = jnp.stack([grads[0]] + [send(grads[k], BACK[k]) for k in (1, 2, 3)], axis=0)
    return jnp.stack(
        [lax.dynamic_index_in_dim(got, (p - pos) % 4, 0, keepdims=False) for p in range(3)], axis=0
    )


def body(queries, keys, values, upstream_out, out_weight, qkv_weight, rand_links, global_links):
    s = lax.axis_index("seq")
    h = lax.axis_index("head")
    x, y, z = s // 8, (s // 4) % 2, s % 4
    core = h % 2
    ring = jnp.where(core == 0, x, z)
    pos = jnp.where(core == 0, z, x)

    n = jnp.arange(NQ, dtype=jnp.int32)
    line = (pos - n // BLK_DEV) % 4
    seq = jnp.where(core == 0, (x * 2 + y) * 4 + line, (line * 2 + y) * 4 + z)
    block = seq * BLK_DEV + n % BLK_DEV
    total = rand_links.shape[0]
    mine = block[:, None, None] == jnp.arange(total, dtype=jnp.int32)[None, :, None]
    rand = jnp.sum(jnp.where(mine, rand_links[None], 0), axis=1)
    window = (block[:, None] + jnp.arange(-1, 2, dtype=jnp.int32)[None]) % total
    glob = jnp.broadcast_to(global_links[None], (NQ, G))
    key = jnp.concatenate([window, rand, glob], axis=1)
    ks = key // BLK_DEV
    kx, ky, kz = ks // 8, (ks // 4) % 2, ks % 4
    k_ring = jnp.where(core == 0, kx, kz)
    k_pos = jnp.where(core == 0, kz, kx)
    shard_of = jnp.where(ky == y, 0, 4) + (ring - k_ring) % 4
    table = shard_of * NQ + ((pos - k_pos) % 4) * BLK_DEV + key % BLK_DEV

    own = deal(jnp.stack([keys, values], axis=0), pos)
    other = send(own, PAIR)
    shards = ring_gather(own) + ring_gather(other)
    grad_ctx = lax.dot_general(
        upstream_out, out_weight, (((1,), (1,)), ((), ())), preferred_element_type=F32
    ).astype(BF16)
    qd = deal(jnp.stack([queries, grad_ctx], axis=0), pos)
    grad_q, parts = attend(table, qd, shards)

    other_sum = ring_reduce(parts[4:])
    own_sum = ring_reduce(parts[:4])
    grad_kv = add(own_sum, send(other_sum, PAIR))
    q_back = give_back(grad_q, pos, HD)
    kv_back = give_back(grad_kv, pos, 2 * HD)
    stacked = jnp.stack([q_back, kv_back[:, :, :HD], kv_back[:, :, HD:]], axis=0)
    weight = qkv_weight.reshape(3, qkv_weight.shape[1], 3, HD)
    share = lax.dot_general(
        weight, stacked, (((0, 2, 3), (0, 1, 3)), ((), ())), preferred_element_type=F32
    ).astype(BF16)
    share = share.reshape(2, 2, share.shape[0] // 4, share.shape[1])
    mine_of = lax.dynamic_index_in_dim(share, core, 1, keepdims=False)
    theirs = lax.dynamic_index_in_dim(share, 1 - core, 1, keepdims=False)
    both = add(mine_of, send(theirs, CORE))
    far = h // 2
    keep = lax.dynamic_index_in_dim(both, far, 0, keepdims=False)
    give = lax.dynamic_index_in_dim(both, 1 - far, 0, keepdims=False)
    return add(keep, send(give, FAR))


def solution(mesh):
    in_specs = (
        P("seq", "head"),
        P("seq", "head"),
        P("seq", "head"),
        P("seq", None),
        P("head", None),
        P(None, None, "head"),
        P(),
        P(),
    )
    out_specs = P("head", "seq")
    return jax.shard_map(body, mesh=mesh, in_specs=in_specs, out_specs=out_specs, check_vma=False)
```

time: 737 us -> 242 us (0.33)
  waiting for transfers between devices: 378 us -> 47.8 us
  local copies, waits for them, and re-layouts: 199 us -> 35 us
  starting transfers between devices: 48 us -> 110 us
  other arithmetic: 56.5 us -> 15.6 us
  matrix products: 34.9 us -> 4.26 us
  Pallas kernels: 0 us -> 26.1 us
  between operations: 14.1 us -> 1 us
    ppermute x4 -> x32, waiting for transfers between devices: 289 us -> 47.8 us  [send(): return lax.ppermute(x, AXES, perm)]
    ppermute x4 -> x32, starting transfers between devices: 11.2 us -> 110 us  [send(): return lax.ppermute(x, AXES, perm)]
    reduce_scatter x1 -> x0, waiting for transfers between devices: 78.4 us -> none  [body(): lax.psum_scatter(lax.dot_general(qkv_weight, stacked, (((0, 2), (0, 2)),...]
    reshape x6 -> x1, local copies, waits for them, and re-layouts: 42 us -> 0.4 us  [body(): share = share.reshape(2, 2, share.shape[0] // 4, share.shape[1])]
    all_to_all x2 -> x0, starting transfers between devices: 36.8 us -> none  [the longest x1 27 us: body(): lax.all_to_all(buffer.reshape(groups, cap, BLK, 2, feat), 'seq', split_ax...]
    dot_general x7 -> x1, matrix products: 31.4 us -> 2.19 us  [body(): lax.dot_general(weight, stacked, (((0, 2, 3), (0, 1, 3)), ((), ())), pref...]
    pallas_call x0 -> x1, Pallas kernels: none -> 26.1 us  [attend(): pl.pallas_call(attend_kernel, name='attend', out_shape=(jax.ShapeDtypeStr...]
    another operation x6 -> x1, local copies, waits for them, and re-layouts: 25 us -> 0.14 us  [body(): jnp.stack([q_back, kv_back[:, :, :HD], kv_back[:, :, HD:]], axis=0)]
  transfers between devices with their start and end apart: 7 -> 32, of which waited for: 6 -> 10; matrix products, arithmetic and copies ran while one was open for 7% -> 12% of each run, Pallas kernels for 0% -> 0%
where the time goes in v1:
time: 242 us; the launch traced here: 240 us
  starting transfers between devices  110 us (45%)
  waiting for transfers between devices  47.8 us (20%)
  local copies, waits for them, and re-layouts  35 us (14%)
  Pallas kernels  26.1 us (11%)
  other arithmetic  15.6 us (6%)
  matrix products  4.26 us (2%)
    ppermute x32, starting transfers between devices, send(): return lax.ppermute(x, AXES, perm)  110 us
    ppermute x32, waiting for transfers between devices, send(): return lax.ppermute(x, AXES, perm)  47.8 us
    pallas_call x1, Pallas kernels, attend(): pl.pallas_call(attend_kernel, name='attend', out_shape=(jax.ShapeDtypeStr...  26.1 us
    unnamed x37, local copies, waits for them, and re-layouts  13.9 us
    convert_element_type x8, other arithmetic, add(): functools.reduce(lambda a, b: a + b, [t.astype(F32) for t in terms])  6.35 us
  transfers between devices with their start and end apart: 32, of which 10 were waited for; matrix products, arithmetic and copies ran while one was open for 12% of the time, Pallas kernels for 0%

profile of v1, /device:TPU:1, one launch (start us, length us, event | category | flops | bytes accessed | tf_op | source)
XLA Modules:
  0.0 239.8 jit_solution(14059628808198032560)
XLA Ops:
  2.9 2.1 convolution_convert_fusion
  7.2 3.9 %collective-permute-start.3 = (bf16[512,256]{1,0:T(8,128)(2,1)S(1)}, bf16[512,256]{1,0:T(8,128)(2,1)S(1)}, u32[]{:S(2)}, u32[]{:S(2)}) collective-permute-start(bf16[512,256]{1,0:T(8,128)(2,1)S(1)} %bitcast.71), channel_id=1, source_target_pairs={{0,4},{1,33},{2,6},{3,35},{4,8},{5,37},{6,10},{7,39},{9,41},{11,43... | collective-permute-start | bytes 786440 | tf_op jit(solution)/shard_map/ppermute | solution.py:54
  11.3 2.8 %collective-permute-start.4 = (bf16[512,256]{1,0:T(8,128)(2,1)S(1)}, bf16[512,256]{1,0:T(8,128)(2,1)S(1)}, u32[]{:S(2)}, u32[]{:S(2)}) collective-permute-start(bf16[512,256]{1,0:T(8,128)(2,1)S(1)} %bitcast.72), channel_id=1, source_target_pairs={{0,8},{1,65},{2,10},{3,67},{5,69},{7,71},{8,0},{9,73},{10,2},{11,7... | collective-permute-start | bytes 786440 | tf_op jit(solution)/shard_map/ppermute | solution.py:54
  15.8 4.4 %collective-permute-done.4 = bf16[512,256]{1,0:T(8,128)(2,1)S(1)} collective-permute-done((bf16[512,256]{1,0:T(8,128)(2,1)S(1)}, bf16[512,256]{1,0:T(8,128)(2,1)S(1)}, u32[]{:S(2)}, u32[]{:S(2)}) %collective-permute-start.4) | collective-permute-done | bytes 262176 | tf_op jit(solution)/shard_map/ppermute | solution.py:54
  21.8 3.3 %collective-permute-start.10 = (bf16[2048,256]{1,0:T(8,128)(2,1)S(1)}, bf16[2048,256]{1,0:T(8,128)(2,1)}, u32[]{:S(2)}, u32[]{:S(2)}) collective-permute-start(bf16[2048,256]{1,0:T(8,128)(2,1)S(1)} %pad_maximum_fusion.1.refs_0_), channel_id=1, source_target_pairs={{0,16},{1,17},{2,18},{3,19},{4,20},{5,21},{6,22},{7,23},{8,24},{9,... | collective-permute-start | bytes 3145736 | tf_op jit(solution)/shard_map/ppermute | solution.py:54
  25.1 3.5 %collective-permute-start.6 = (bf16[2048,256]{1,0:T(8,128)(2,1)S(1)}, bf16[2048,256]{1,0:T(8,128)(2,1)S(1)}, u32[]{:S(2)}, u32[]{:S(2)}) collective-permute-start(bf16[2048,256]{1,0:T(8,128)(2,1)S(1)} %pad_maximum_fusion.1.refs_0_), channel_id=1, source_target_pairs={{0,32},{1,5},{2,34},{3,7},{4,36},{5,9},{6,38},{7,11},{8,40},{9,13}... | collective-permute-start | bytes 3145736 | tf_op jit(solution)/shard_map/ppermute | solution.py:54
  28.7 3.7 %collective-permute-start.8 = (bf16[2048,256]{1,0:T(8,128)(2,1)S(1)}, bf16[2048,256]{1,0:T(8,128)(2,1)}, u32[]{:S(2)}, u32[]{:S(2)}) collective-permute-start(bf16[2048,256]{1,0:T(8,128)(2,1)S(1)} %pad_maximum_fusion.1.refs_0_), channel_id=1, source_target_pairs={{0,96},{1,13},{2,98},{3,15},{4,100},{5,1},{6,102},{7,3},{8,104},{9... | collective-permute-start | bytes 3145736 | tf_op jit(solution)/shard_map/ppermute | solution.py:54
  32.4 13.5 %collective-permute-done.10.refs_4_ = bf16[2048,256]{1,0:T(8,128)(2,1)} collective-permute-done((bf16[2048,256]{1,0:T(8,128)(2,1)S(1)}, bf16[2048,256]{1,0:T(8,128)(2,1)}, u32[]{:S(2)}, u32[]{:S(2)}) %collective-permute-start.10) | collective-permute-done | bytes 1048608 | tf_op jit(solution)/shard_map/ppermute | solution.py:54
  45.9 2.6 %collective-permute-start.11 = (bf16[2048,256]{1,0:T(8,128)(2,1)}, bf16[2048,256]{1,0:T(8,128)(2,1)}, u32[]{:S(2)}, u32[]{:S(2)}) collective-permute-start(bf16[2048,256]{1,0:T(8,128)(2,1)} %collective-permute-done.10.refs_4_), channel_id=1, source_target_pairs={{0,32},{1,5},{2,34},{3,7},{4,36},{5,9},{6,38},{7,11},{8,40},{9,13}... | collective-permute-start | bytes 3145736 | tf_op jit(solution)/shard_map/ppermute | solution.py:54
  48.5 3.9 %collective-permute-start.13 = (bf16[2048,256]{1,0:T(8,128)(2,1)}, bf16[2048,256]{1,0:T(8,128)(2,1)}, u32[]{:S(2)}, u32[]{:S(2)}) collective-permute-start(bf16[2048,256]{1,0:T(8,128)(2,1)} %collective-permute-done.10.refs_4_), channel_id=1, source_target_pairs={{0,96},{1,13},{2,98},{3,15},{4,100},{5,1},{6,102},{7,3},{8,104},{9... | collective-permute-start | bytes 3145736 | tf_op jit(solution)/shard_map/ppermute | solution.py:54
  52.5 5.8 %collective-permute-start = (bf16[512,256]{1,0:T(8,128)(2,1)S(1)}, bf16[512,256]{1,0:T(8,128)(2,1)}, u32[]{:S(2)}, u32[]{:S(2)}) collective-permute-start(bf16[512,256]{1,0:T(8,128)(2,1)S(1)} %bitcast.68), channel_id=1, source_target_pairs={{0,4},{1,33},{2,6},{3,35},{4,8},{5,37},{6,10},{7,39},{9,41},{11,43... | collective-permute-start | bytes 786440 | tf_op jit(solution)/shard_map/ppermute | solution.py:54
  59.5 1.9 collective-permute-start.1
  62.8 1.9 slice.119
  64.7 2.9 %collective-permute-start.7 = (bf16[1024,256]{1,0:T(8,128)(2,1)S(1)}, bf16[1024,256]{1,0:T(8,128)(2,1)}, u32[]{:S(2)}, u32[]{:S(2)}) collective-permute-start(bf16[1024,256]{1,0:T(8,128)(2,1)S(1)} %slice.118), channel_id=1, source_target_pairs={{0,32},{1,5},{2,34},{3,7},{4,36},{5,9},{6,38},{7,11},{8,40},{9,13}... | collective-permute-start | bytes 1572872 | tf_op jit(solution)/shard_map/ppermute | solution.py:54
  67.6 3.6 %collective-permute-start.9 = (bf16[1024,256]{1,0:T(8,128)(2,1)}, bf16[1024,256]{1,0:T(8,128)(2,1)}, u32[]{:S(2)}, u32[]{:S(2)}) collective-permute-start(bf16[1024,256]{1,0:T(8,128)(2,1)} %slice.119), channel_id=1, source_target_pairs={{0,96},{1,13},{2,98},{3,15},{4,100},{5,1},{6,102},{7,3},{8,104},{9... | collective-permute-start | bytes 1572872 | tf_op jit(solution)/shard_map/ppermute | solution.py:54
  71.5 1.9 slice.120
  73.4 1.9 slice.121
  75.3 1.9 collective-permute-start.12
  77.3 4.6 %collective-permute-start.14 = (bf16[1024,256]{1,0:T(8,128)(2,1)}, bf16[1024,256]{1,0:T(8,128)(2,1)S(1)}, u32[]{:S(2)}, u32[]{:S(2)}) collective-permute-start(bf16[1024,256]{1,0:T(8,128)(2,1)} %slice.121), channel_id=1, source_target_pairs={{0,96},{1,13},{2,98},{3,15},{4,100},{5,1},{6,102},{7,3},{8,104},{9... | collective-permute-start | bytes 1572872 | tf_op jit(solution)/shard_map/ppermute | solution.py:54
  82.7 2.2 pad_maximum_fusion.qd_ref
  84.9 2.2 pad_maximum_fusion.2.refs_2_
  89.3 26.1 %attend.1 = (bf16[2048,128]{1,0:T(8,128)(2,1)}, bf16[2048,256]{1,0:T(8,128)(2,1)}, bf16[2048,256]{1,0:T(8,128)(2,1)}, bf16[2048,256]{1,0:T(8,128)(2,1)}, bf16[20...) custom-call(s32[16,8]{1,0:T(8,128)} %fusion.16.table, ...), custom_call_target="tpu_custom_call" | custom-call | tf_op jit(solution)/shard_map/attend/pallas_call | solution.py:126
  116.8 2.8 %collective-permute-start.22 = (bf16[1024,256]{1,0:T(8,128)(2,1)S(1)}, bf16[1024,256]{1,0:T(8,128)(2,1)S(1)}, u32[]{:S(2)}, u32[]{:S(2)}) collective-permute-start(bf16[1024,256]{1,0:T(8,128)(2,1)S(1)} %get-tuple-element.34), channel_id=1, source_target_pairs={{0,32},{1,5},{2,34},{3,7},{4,36},{5,9},{6,38},{7,11},{8,40},{9,13}... | collective-permute-start | bytes 1572872 | tf_op jit(solution)/shard_map/ppermute | solution.py:54
  119.6 4.1 %collective-permute-start.24 = (bf16[1024,256]{1,0:T(8,128)(2,1)S(1)}, bf16[1024,256]{1,0:T(8,128)(2,1)S(1)}, u32[]{:S(2)}, u32[]{:S(2)}) collective-permute-start(bf16[1024,256]{1,0:T(8,128)(2,1)S(1)} %get-tuple-element.35), channel_id=1, source_target_pairs={{0,96},{1,13},{2,98},{3,15},{4,100},{5,1},{6,102},{7,3},{8,104},{9... | collective-permute-start | bytes 1572872 | tf_op jit(solution)/shard_map/ppermute | solution.py:54
  123.9 1.9 collective-permute-start.18
  125.9 2.5 %collective-permute-done.22 = bf16[1024,256]{1,0:T(8,128)(2,1)S(1)} collective-permute-done((bf16[1024,256]{1,0:T(8,128)(2,1)S(1)}, bf16[1024,256]{1,0:T(8,128)(2,1)S(1)}, u32[]{:S(2)}, u32[]{:S(2)}) %collective-permute-start.22) | collective-permute-done | bytes 524320 | tf_op jit(solution)/shard_map/ppermute | solution.py:54
  128.7 2.1 collective-permute-start.23
  131.0 4.6 %collective-permute-start.25 = (bf16[2048,256]{1,0:T(8,128)(2,1)S(1)}, bf16[2048,256]{1,0:T(8,128)(2,1)S(1)}, u32[]{:S(2)}, u32[]{:S(2)}) collective-permute-start(bf16[2048,256]{1,0:T(8,128)(2,1)S(1)} %pad_maximum_fusion.7), channel_id=1, source_target_pairs={{0,96},{1,13},{2,98},{3,15},{4,100},{5,1},{6,102},{7,3},{8,104},{9... | collective-permute-start | bytes 3145736 | tf_op jit(solution)/shard_map/ppermute | solution.py:54
  135.5 2.2 collective-permute-start.20
  139.0 3.3 %collective-permute-start.19 = (bf16[2048,256]{1,0:T(8,128)(2,1)}, bf16[2048,256]{1,0:T(8,128)(2,1)}, u32[]{:S(2)}, u32[]{:S(2)}) collective-permute-start(bf16[2048,256]{1,0:T(8,128)(2,1)} %pad_maximum_fusion.4), channel_id=1, source_target_pairs={{0,32},{1,5},{2,34},{3,7},{4,36},{5,9},{6,38},{7,11},{8,40},{9,13}... | collective-permute-start | bytes 3145736 | tf_op jit(solution)/shard_map/ppermute | solution.py:54
  142.2 10.6 %collective-permute-done.20 = bf16[1024,256]{1,0:T(8,128)(2,1)S(1)} collective-permute-done((bf16[1024,256]{1,0:T(8,128)(2,1)S(1)}, bf16[1024,256]{1,0:T(8,128)(2,1)S(1)}, u32[]{:S(2)}, u32[]{:S(2)}) %collective-permute-start.20) | collective-permute-done | bytes 524320 | tf_op jit(solution)/shard_map/ppermute | solution.py:54
  154.1 5.0 %collective-permute-start.21 = (bf16[2048,256]{1,0:T(8,128)(2,1)}, bf16[2048,256]{1,0:T(8,128)(2,1)S(1)}, u32[]{:S(2)}, u32[]{:S(2)}) collective-permute-start(bf16[2048,256]{1,0:T(8,128)(2,1)} %pad_maximum_fusion.5), channel_id=1, source_target_pairs={{0,96},{1,13},{2,98},{3,15},{4,100},{5,1},{6,102},{7,3},{8,104},{9... | collective-permute-start | bytes 3145736 | tf_op jit(solution)/shard_map/ppermute | solution.py:54
  160.5 3.2 %collective-permute-start.26 = (bf16[2048,256]{1,0:T(8,128)(2,1)}, bf16[2048,256]{1,0:T(8,128)(2,1)}, u32[]{:S(2)}, u32[]{:S(2)}) collective-permute-start(bf16[2048,256]{1,0:T(8,128)(2,1)} %add_convert_fusion.1), channel_id=1, source_target_pairs={{0,16},{1,17},{2,18},{3,19},{4,20},{5,21},{6,22},{7,23},{8,24},{9,... | collective-permute-start | bytes 3145736 | tf_op jit(solution)/shard_map/ppermute | solution.py:54
  163.7 6.2 %copy.56 = bf16[3,1536,384]{1,2,0:T(8,128)(2,1)} copy(bf16[3,1536,384]{2,1,0:T(8,128)(2,1)} %param.13) | data formatting | bytes 7077888 | tf_op args[5]
  170.0 1.9 collective-permute-start.15
  171.9 10.6 %collective-permute-start.16 = (bf16[512,128]{1,0:T(8,128)(2,1)S(1)}, bf16[512,128]{1,0:T(8,128)(2,1)S(1)}, u32[]{:S(2)}, u32[]{:S(2)}) collective-permute-start(bf16[512,128]{1,0:T(8,128)(2,1)S(1)} %get-tuple-element.51), channel_id=1, source_target_pairs={{8,0},{65,1},{10,2},{67,3},{69,5},{71,7},{0,8},{73,9},{2,10},{75,1... | collective-permute-start | bytes 393224 | tf_op jit(solution)/shard_map/ppermute | solution.py:54
  183.9 2.1 add_convert_fusion
  186.1 1.9 collective-permute-start.27
  188.0 9.7 %collective-permute-start.28 = (bf16[512,256]{1,0:T(8,128)(2,1)S(1)}, bf16[512,256]{1,0:T(8,128)(2,1)S(1)}, u32[]{:S(2)}, u32[]{:S(2)}) collective-permute-start(bf16[512,256]{1,0:T(8,128)(2,1)S(1)} %get-tuple-element.30), channel_id=1, source_target_pairs={{8,0},{65,1},{10,2},{67,3},{69,5},{71,7},{0,8},{73,9},{2,10},{75,1... | collective-permute-start | bytes 786440 | tf_op jit(solution)/shard_map/ppermute | solution.py:54
  199.4 2.0 collective-permute-done.28
  201.5 2.4 %collective-permute-done.29 = bf16[512,256]{1,0:T(8,128)(2,1)S(1)} collective-permute-done((bf16[512,256]{1,0:T(8,128)(2,1)S(1)}, bf16[512,256]{1,0:T(8,128)(2,1)S(1)}, u32[]{:S(2)}, u32[]{:S(2)}) %collective-permute-start.29) | collective-permute-done | bytes 262176 | tf_op jit(solution)/shard_map/ppermute | solution.py:54
  206.0 2.2 fusion.1
  208.6 4.4 %constant_dynamic-slice_fusion.1 = (bf16[2,1,384,512]{2,1,0,3:T(2,128)(2,1)S(1)}, bf16[2,1,384,512]{2,1,0,3:T(2,128)(2,1)}) fusion(bf16[2,2,384,512]{2,1,0,3:T(2,128)(2,1)S(1)} %reshape.155, s32[]{:T(128)S(6)} %select_n.272, s32[]{:T(128)S(6)} %select_n.273), kind=kLoop, calls=%fused_computation.86 | loop fusion | bytes 3145736 | tf_op jit(solution)/shard_map/jit(dynamic_index_in_dim)/dynamic_slice | solution.py:230
  213.0 4.6 %copy.59 = bf16[2,1,384,512]{3,2,0,1:T(8,128)(2,1)} copy(bf16[2,1,384,512]{2,1,0,3:T(2,128)(2,1)} %get-tuple-element.24) | data formatting | bytes 1572864 | tf_op jit(solution)/shard_map/jit(dynamic_index_in_dim)/dynamic_slice | solution.py:231
  217.7 4.1 %collective-permute-start.30 = (bf16[2,384,512]{2,1,0:T(8,128)(2,1)}, bf16[2,384,512]{2,1,0:T(8,128)(2,1)}, u32[]{:S(2)}, u32[]{:S(2)}) collective-permute-start(bf16[2,384,512]{2,1,0:T(8,128)(2,1)} %bitcast.32), channel_id=1, source_target_pairs={{0,1},{1,0},{2,3},{3,2},{4,5},{5,4},{6,7},{7,6},{8,9},{9,8},{10,11... | collective-permute-start | bytes 2359304 | tf_op jit(solution)/shard_map/ppermute | solution.py:54
  221.7 3.2 %copy.62 = bf16[2,1,384,512]{3,2,0,1:T(8,128)(2,1)} copy(bf16[2,1,384,512]{2,1,0,3:T(2,128)(2,1)S(1)} %get-tuple-element.23) | data formatting | bytes 1572864
  226.6 2.7 %collective-permute-start.31 = (bf16[384,512]{1,0:T(8,128)(2,1)S(1)}, bf16[384,512]{1,0:T(8,128)(2,1)S(1)}, u32[]{:S(2)}, u32[]{:S(2)}) collective-permute-start(bf16[384,512]{1,0:T(8,128)(2,1)S(1)} %dynamic-slice_bitcast_fusion), channel_id=1, source_target_pairs={{0,2},{1,3},{2,0},{3,1},{4,6},{5,7},{6,4},{7,5},{8,10},{9,11},{10,... | collective-permute-start | bytes 1179656 | tf_op jit(solution)/shard_map/ppermute | solution.py:54
  229.3 9.6 %collective-permute-done.31 = bf16[384,512]{1,0:T(8,128)(2,1)S(1)} collective-permute-done((bf16[384,512]{1,0:T(8,128)(2,1)S(1)}, bf16[384,512]{1,0:T(8,128)(2,1)S(1)}, u32[]{:S(2)}, u32[]{:S(2)}) %collective-permute-start.31) | collective-permute-done | bytes 393248 | tf_op jit(solution)/shard_map/ppermute | solution.py:54
  (116 shorter events, 28.1 us)
Async XLA Ops:
  0.0 2.9 %copy-start = (bf16[512,1536]{1,0:T(8,128)(2,1)S(1)}, bf16[512,1536]{1,0:T(8,128)(2,1)}, u32[]{:S(2)}) copy-start(bf16[512,1536]{1,0:T(8,128)(2,1)} %param.11) | copy-start | bytes 4718596
  1.3 1.4 copy-start.13
  7.2 8.6 %collective-permute-start.3 = (bf16[512,256]{1,0:T(8,128)(2,1)S(1)}, bf16[512,256]{1,0:T(8,128)(2,1)S(1)}, u32[]{:S(2)}, u32[]{:S(2)}) collective-permute-start(bf16[512,256]{1,0:T(8,128)(2,1)S(1)} %bitcast.71), channel_id=1, source_target_pairs={{0,4},{1,33},{2,6},{3,35},{4,8},{5,37},{6,10},{7,39},{9,41},{11,43... | collective-permute-start | bytes 786440 | tf_op jit(solution)/shard_map/ppermute | solution.py:54
  11.3 8.9 %collective-permute-start.4 = (bf16[512,256]{1,0:T(8,128)(2,1)S(1)}, bf16[512,256]{1,0:T(8,128)(2,1)S(1)}, u32[]{:S(2)}, u32[]{:S(2)}) collective-permute-start(bf16[512,256]{1,0:T(8,128)(2,1)S(1)} %bitcast.72), channel_id=1, source_target_pairs={{0,8},{1,65},{2,10},{3,67},{5,69},{7,71},{8,0},{9,73},{10,2},{11,7... | collective-permute-start | bytes 786440 | tf_op jit(solution)/shard_map/ppermute | solution.py:54
  14.2 7.4 %collective-permute-start.5 = (bf16[512,256]{1,0:T(8,128)(2,1)S(1)}, bf16[512,256]{1,0:T(8,128)(2,1)S(1)}, u32[]{:S(2)}, u32[]{:S(2)}) collective-permute-start(bf16[512,256]{1,0:T(8,128)(2,1)S(1)} %bitcast.73), channel_id=1, source_target_pairs={{4,0},{6,2},{8,4},{10,6},{12,8},{14,10},{20,16},{22,18},{24,20},{2... | collective-permute-start | bytes 786440 | tf_op jit(solution)/shard_map/ppermute | solution.py:54
  21.7 51.7 %copy-start.2 = (bf16[2048,256]{1,0:T(8,128)(2,1)}, bf16[2048,256]{1,0:T(8,128)(2,1)S(1)}, u32[]{:S(2)}) copy-start(bf16[2048,256]{1,0:T(8,128)(2,1)S(1)} %pad_maximum_fusion.1.refs_0_) | copy-start | bytes 3145732
  21.7 49.5 %copy-start.14 = (s32[128,3]{0,1:T(4,128)S(1)}, s32[128,3]{0,1:T(4,128)}, u32[]{:S(2)}) copy-start(s32[128,3]{0,1:T(4,128)} %param.14) | copy-start | bytes 4612
  21.7 49.7 %copy-start.15 = (s32[2]{0:T(128)S(1)}, s32[2]{0:T(128)}, u32[]{:S(2)}) copy-start(s32[2]{0:T(128)} %param.15) | copy-start | bytes 28
  21.8 24.1 %collective-permute-start.10 = (bf16[2048,256]{1,0:T(8,128)(2,1)S(1)}, bf16[2048,256]{1,0:T(8,128)(2,1)}, u32[]{:S(2)}, u32[]{:S(2)}) collective-permute-start(bf16[2048,256]{1,0:T(8,128)(2,1)S(1)} %pad_maximum_fusion.1.refs_0_), channel_id=1, source_target_pairs={{0,16},{1,17},{2,18},{3,19},{4,20},{5,21},{6,22},{7,23},{8,24},{9,... | collective-permute-start | bytes 3145736 | tf_op jit(solution)/shard_map/ppermute | solution.py:54
  25.1 34.4 %collective-permute-start.6 = (bf16[2048,256]{1,0:T(8,128)(2,1)S(1)}, bf16[2048,256]{1,0:T(8,128)(2,1)S(1)}, u32[]{:S(2)}, u32[]{:S(2)}) collective-permute-start(bf16[2048,256]{1,0:T(8,128)(2,1)S(1)} %pad_maximum_fusion.1.refs_0_), channel_id=1, source_target_pairs={{0,32},{1,5},{2,34},{3,7},{4,36},{5,9},{6,38},{7,11},{8,40},{9,13}... | collective-permute-start | bytes 3145736 | tf_op jit(solution)/shard_map/ppermute | solution.py:54
  28.7 32.9 %collective-permute-start.8 = (bf16[2048,256]{1,0:T(8,128)(2,1)S(1)}, bf16[2048,256]{1,0:T(8,128)(2,1)}, u32[]{:S(2)}, u32[]{:S(2)}) collective-permute-start(bf16[2048,256]{1,0:T(8,128)(2,1)S(1)} %pad_maximum_fusion.1.refs_0_), channel_id=1, source_target_pairs={{0,96},{1,13},{2,98},{3,15},{4,100},{5,1},{6,102},{7,3},{8,104},{9... | collective-permute-start | bytes 3145736 | tf_op jit(solution)/shard_map/ppermute | solution.py:54
  45.9 18.8 %collective-permute-start.11 = (bf16[2048,256]{1,0:T(8,128)(2,1)}, bf16[2048,256]{1,0:T(8,128)(2,1)}, u32[]{:S(2)}, u32[]{:S(2)}) collective-permute-start(bf16[2048,256]{1,0:T(8,128)(2,1)} %collective-permute-done.10.refs_4_), channel_id=1, source_target_pairs={{0,32},{1,5},{2,34},{3,7},{4,36},{5,9},{6,38},{7,11},{8,40},{9,13}... | collective-permute-start | bytes 3145736 | tf_op jit(solution)/shard_map/ppermute | solution.py:54
  48.5 19.1 %collective-permute-start.13 = (bf16[2048,256]{1,0:T(8,128)(2,1)}, bf16[2048,256]{1,0:T(8,128)(2,1)}, u32[]{:S(2)}, u32[]{:S(2)}) collective-permute-start(bf16[2048,256]{1,0:T(8,128)(2,1)} %collective-permute-done.10.refs_4_), channel_id=1, source_target_pairs={{0,96},{1,13},{2,98},{3,15},{4,100},{5,1},{6,102},{7,3},{8,104},{9... | collective-permute-start | bytes 3145736 | tf_op jit(solution)/shard_map/ppermute | solution.py:54
  52.5 22.8 %collective-permute-start = (bf16[512,256]{1,0:T(8,128)(2,1)S(1)}, bf16[512,256]{1,0:T(8,128)(2,1)}, u32[]{:S(2)}, u32[]{:S(2)}) collective-permute-start(bf16[512,256]{1,0:T(8,128)(2,1)S(1)} %bitcast.68), channel_id=1, source_target_pairs={{0,4},{1,33},{2,6},{3,35},{4,8},{5,37},{6,10},{7,39},{9,41},{11,43... | collective-permute-start | bytes 786440 | tf_op jit(solution)/shard_map/ppermute | solution.py:54
  59.5 15.9 %copy-start.4 = (bf16[2048,256]{1,0:T(8,128)(2,1)}, bf16[2048,256]{1,0:T(8,128)(2,1)S(1)}, u32[]{:S(2)}) copy-start(bf16[2048,256]{1,0:T(8,128)(2,1)S(1)} %collective-permute-done.6.refs_1_) | copy-start | bytes 3145732
  59.5 17.8 %collective-permute-start.1 = (bf16[512,256]{1,0:T(8,128)(2,1)}, bf16[512,256]{1,0:T(8,128)(2,1)}, u32[]{:S(2)}, u32[]{:S(2)}) collective-permute-start(bf16[512,256]{1,0:T(8,128)(2,1)} %bitcast.70), channel_id=1, source_target_pairs={{0,8},{1,65},{2,10},{3,67},{5,69},{7,71},{8,0},{9,73},{10,2},{11,7... | collective-permute-start | bytes 786440 | tf_op jit(solution)/shard_map/ppermute | solution.py:54
  61.5 21.2 %collective-permute-start.2 = (bf16[512,256]{1,0:T(8,128)(2,1)S(1)}, bf16[512,256]{1,0:T(8,128)(2,1)}, u32[]{:S(2)}, u32[]{:S(2)}) collective-permute-start(bf16[512,256]{1,0:T(8,128)(2,1)S(1)} %bitcast.69), channel_id=1, source_target_pairs={{4,0},{6,2},{8,4},{10,6},{12,8},{14,10},{20,16},{22,18},{24,20},{2... | collective-permute-start | bytes 786440 | tf_op jit(solution)/shard_map/ppermute | solution.py:54
  64.7 20.2 %collective-permute-start.7 = (bf16[1024,256]{1,0:T(8,128)(2,1)S(1)}, bf16[1024,256]{1,0:T(8,128)(2,1)}, u32[]{:S(2)}, u32[]{:S(2)}) collective-permute-start(bf16[1024,256]{1,0:T(8,128)(2,1)S(1)} %slice.118), channel_id=1, source_target_pairs={{0,32},{1,5},{2,34},{3,7},{4,36},{5,9},{6,38},{7,11},{8,40},{9,13}... | collective-permute-start | bytes 1572872 | tf_op jit(solution)/shard_map/ppermute | solution.py:54
  67.6 17.3 %collective-permute-start.9 = (bf16[1024,256]{1,0:T(8,128)(2,1)}, bf16[1024,256]{1,0:T(8,128)(2,1)}, u32[]{:S(2)}, u32[]{:S(2)}) collective-permute-start(bf16[1024,256]{1,0:T(8,128)(2,1)} %slice.119), channel_id=1, source_target_pairs={{0,96},{1,13},{2,98},{3,15},{4,100},{5,1},{6,102},{7,3},{8,104},{9... | collective-permute-start | bytes 1572872 | tf_op jit(solution)/shard_map/ppermute | solution.py:54
  75.3 11.8 %collective-permute-start.12 = (bf16[1024,256]{1,0:T(8,128)(2,1)}, bf16[1024,256]{1,0:T(8,128)(2,1)S(1)}, u32[]{:S(2)}, u32[]{:S(2)}) collective-permute-start(bf16[1024,256]{1,0:T(8,128)(2,1)} %slice.120), channel_id=1, source_target_pairs={{0,32},{1,5},{2,34},{3,7},{4,36},{5,9},{6,38},{7,11},{8,40},{9,13}... | collective-permute-start | bytes 1572872 | tf_op jit(solution)/shard_map/ppermute | solution.py:54
  77.3 11.0 %collective-permute-start.14 = (bf16[1024,256]{1,0:T(8,128)(2,1)}, bf16[1024,256]{1,0:T(8,128)(2,1)S(1)}, u32[]{:S(2)}, u32[]{:S(2)}) collective-permute-start(bf16[1024,256]{1,0:T(8,128)(2,1)} %slice.121), channel_id=1, source_target_pairs={{0,96},{1,13},{2,98},{3,15},{4,100},{5,1},{6,102},{7,3},{8,104},{9... | collective-permute-start | bytes 1572872 | tf_op jit(solution)/shard_map/ppermute | solution.py:54
  115.4 8.4 %copy-start.10 = (bf16[2048,256]{1,0:T(8,128)(2,1)S(1)}, bf16[2048,256]{1,0:T(8,128)(2,1)}, u32[]{:S(2)}) copy-start(bf16[2048,256]{1,0:T(8,128)(2,1)} %get-tuple-element.17) | copy-start | bytes 3145732
  115.4 10.4 %copy-start.9 = (bf16[2048,256]{1,0:T(8,128)(2,1)S(1)}, bf16[2048,256]{1,0:T(8,128)(2,1)}, u32[]{:S(2)}) copy-start(bf16[2048,256]{1,0:T(8,128)(2,1)} %get-tuple-element.20) | copy-start | bytes 3145732
  116.8 9.1 %copy-start.8 = (bf16[2048,256]{1,0:T(8,128)(2,1)S(1)}, bf16[2048,256]{1,0:T(8,128)(2,1)}, u32[]{:S(2)}) copy-start(bf16[2048,256]{1,0:T(8,128)(2,1)} %get-tuple-element.22) | copy-start | bytes 3145732
  116.8 11.6 %collective-permute-start.22 = (bf16[1024,256]{1,0:T(8,128)(2,1)S(1)}, bf16[1024,256]{1,0:T(8,128)(2,1)S(1)}, u32[]{:S(2)}, u32[]{:S(2)}) collective-permute-start(bf16[1024,256]{1,0:T(8,128)(2,1)S(1)} %get-tuple-element.34), channel_id=1, source_target_pairs={{0,32},{1,5},{2,34},{3,7},{4,36},{5,9},{6,38},{7,11},{8,40},{9,13}... | collective-permute-start | bytes 1572872 | tf_op jit(solution)/shard_map/ppermute | solution.py:54
  119.6 11.1 %collective-permute-start.24 = (bf16[1024,256]{1,0:T(8,128)(2,1)S(1)}, bf16[1024,256]{1,0:T(8,128)(2,1)S(1)}, u32[]{:S(2)}, u32[]{:S(2)}) collective-permute-start(bf16[1024,256]{1,0:T(8,128)(2,1)S(1)} %get-tuple-element.35), channel_id=1, source_target_pairs={{0,96},{1,13},{2,98},{3,15},{4,100},{5,1},{6,102},{7,3},{8,104},{9... | collective-permute-start | bytes 1572872 | tf_op jit(solution)/shard_map/ppermute | solution.py:54
  123.9 13.9 %collective-permute-start.18 = (bf16[1024,256]{1,0:T(8,128)(2,1)S(1)}, bf16[1024,256]{1,0:T(8,128)(2,1)S(1)}, u32[]{:S(2)}, u32[]{:S(2)}) collective-permute-start(bf16[1024,256]{1,0:T(8,128)(2,1)S(1)} %get-tuple-element.32), channel_id=1, source_target_pairs={{0,32},{1,5},{2,34},{3,7},{4,36},{5,9},{6,38},{7,11},{8,40},{9,13}... | collective-permute-start | bytes 1572872 | tf_op jit(solution)/shard_map/ppermute | solution.py:54
  128.6 9.1 %copy-start.7 = (bf16[2048,256]{1,0:T(8,128)(2,1)S(1)}, bf16[2048,256]{1,0:T(8,128)(2,1)}, u32[]{:S(2)}) copy-start(bf16[2048,256]{1,0:T(8,128)(2,1)} %get-tuple-element.16) | copy-start | bytes 3145732
  128.7 9.1 %copy-start.6 = (bf16[2048,256]{1,0:T(8,128)(2,1)S(1)}, bf16[2048,256]{1,0:T(8,128)(2,1)}, u32[]{:S(2)}) copy-start(bf16[2048,256]{1,0:T(8,128)(2,1)} %get-tuple-element.18) | copy-start | bytes 3145732
  128.7 30.4 %collective-permute-start.23 = (bf16[2048,256]{1,0:T(8,128)(2,1)S(1)}, bf16[2048,256]{1,0:T(8,128)(2,1)S(1)}, u32[]{:S(2)}, u32[]{:S(2)}) collective-permute-start(bf16[2048,256]{1,0:T(8,128)(2,1)S(1)} %pad_maximum_fusion.6), channel_id=1, source_target_pairs={{0,32},{1,5},{2,34},{3,7},{4,36},{5,9},{6,38},{7,11},{8,40},{9,13}... | collective-permute-start | bytes 3145736 | tf_op jit(solution)/shard_map/ppermute | solution.py:54
  131.0 28.2 %collective-permute-start.25 = (bf16[2048,256]{1,0:T(8,128)(2,1)S(1)}, bf16[2048,256]{1,0:T(8,128)(2,1)S(1)}, u32[]{:S(2)}, u32[]{:S(2)}) collective-permute-start(bf16[2048,256]{1,0:T(8,128)(2,1)S(1)} %pad_maximum_fusion.7), channel_id=1, source_target_pairs={{0,96},{1,13},{2,98},{3,15},{4,100},{5,1},{6,102},{7,3},{8,104},{9... | collective-permute-start | bytes 3145736 | tf_op jit(solution)/shard_map/ppermute | solution.py:54
  135.5 17.3 %collective-permute-start.20 = (bf16[1024,256]{1,0:T(8,128)(2,1)S(1)}, bf16[1024,256]{1,0:T(8,128)(2,1)S(1)}, u32[]{:S(2)}, u32[]{:S(2)}) collective-permute-start(bf16[1024,256]{1,0:T(8,128)(2,1)S(1)} %get-tuple-element.33), channel_id=1, source_target_pairs={{0,96},{1,13},{2,98},{3,15},{4,100},{5,1},{6,102},{7,3},{8,104},{9... | collective-permute-start | bytes 1572872 | tf_op jit(solution)/shard_map/ppermute | solution.py:54
  139.0 20.1 %copy-start.11 = (bf16[2048,256]{1,0:T(8,128)(2,1)S(1)}, bf16[2048,256]{1,0:T(8,128)(2,1)}, u32[]{:S(2)}) copy-start(bf16[2048,256]{1,0:T(8,128)(2,1)} %get-tuple-element.19) | copy-start | bytes 3145732
  139.0 43.6 %collective-permute-start.19 = (bf16[2048,256]{1,0:T(8,128)(2,1)}, bf16[2048,256]{1,0:T(8,128)(2,1)}, u32[]{:S(2)}, u32[]{:S(2)}) collective-permute-start(bf16[2048,256]{1,0:T(8,128)(2,1)} %pad_maximum_fusion.4), channel_id=1, source_target_pairs={{0,32},{1,5},{2,34},{3,7},{4,36},{5,9},{6,38},{7,11},{8,40},{9,13}... | collective-permute-start | bytes 3145736 | tf_op jit(solution)/shard_map/ppermute | solution.py:54
  154.1 29.8 %collective-permute-start.21 = (bf16[2048,256]{1,0:T(8,128)(2,1)}, bf16[2048,256]{1,0:T(8,128)(2,1)S(1)}, u32[]{:S(2)}, u32[]{:S(2)}) collective-permute-start(bf16[2048,256]{1,0:T(8,128)(2,1)} %pad_maximum_fusion.5), channel_id=1, source_target_pairs={{0,96},{1,13},{2,98},{3,15},{4,100},{5,1},{6,102},{7,3},{8,104},{9... | collective-permute-start | bytes 3145736 | tf_op jit(solution)/shard_map/ppermute | solution.py:54
  160.5 23.4 %collective-permute-start.26 = (bf16[2048,256]{1,0:T(8,128)(2,1)}, bf16[2048,256]{1,0:T(8,128)(2,1)}, u32[]{:S(2)}, u32[]{:S(2)}) collective-permute-start(bf16[2048,256]{1,0:T(8,128)(2,1)} %add_convert_fusion.1), channel_id=1, source_target_pairs={{0,16},{1,17},{2,18},{3,19},{4,20},{5,21},{6,22},{7,23},{8,24},{9,... | collective-permute-start | bytes 3145736 | tf_op jit(solution)/shard_map/ppermute | solution.py:54
  163.7 6.3 %copy-start.12 = (bf16[2048,128]{1,0:T(8,128)(2,1)S(1)}, bf16[2048,128]{1,0:T(8,128)(2,1)}, u32[]{:S(2)}) copy-start(bf16[2048,128]{1,0:T(8,128)(2,1)} %get-tuple-element.14) | copy-start | bytes 1572868
  163.7 20.2 %copy-start.5 = (bf16[2048,256]{1,0:T(8,128)(2,1)S(1)}, bf16[2048,256]{1,0:T(8,128)(2,1)}, u32[]{:S(2)}) copy-start(bf16[2048,256]{1,0:T(8,128)(2,1)} %get-tuple-element.15) | copy-start | bytes 3145732
  170.0 27.7 %collective-permute-start.15 = (bf16[512,128]{1,0:T(8,128)(2,1)S(1)}, bf16[512,128]{1,0:T(8,128)(2,1)S(1)}, u32[]{:S(2)}, u32[]{:S(2)}) collective-permute-start(bf16[512,128]{1,0:T(8,128)(2,1)S(1)} %get-tuple-element.52), channel_id=1, source_target_pairs={{4,0},{33,1},{6,2},{35,3},{8,4},{37,5},{10,6},{39,7},{41,9},{43,11... | collective-permute-start | bytes 393224 | tf_op jit(solution)/shard_map/ppermute | solution.py:54
  171.9 27.3 %collective-permute-start.16 = (bf16[512,128]{1,0:T(8,128)(2,1)S(1)}, bf16[512,128]{1,0:T(8,128)(2,1)S(1)}, u32[]{:S(2)}, u32[]{:S(2)}) collective-permute-start(bf16[512,128]{1,0:T(8,128)(2,1)S(1)} %get-tuple-element.51), channel_id=1, source_target_pairs={{8,0},{65,1},{10,2},{67,3},{69,5},{71,7},{0,8},{73,9},{2,10},{75,1... | collective-permute-start | bytes 393224 | tf_op jit(solution)/shard_map/ppermute | solution.py:54
  182.6 16.7 %collective-permute-start.17 = (bf16[512,128]{1,0:T(8,128)(2,1)S(1)}, bf16[512,128]{1,0:T(8,128)(2,1)S(1)}, u32[]{:S(2)}, u32[]{:S(2)}) collective-permute-start(bf16[512,128]{1,0:T(8,128)(2,1)S(1)} %get-tuple-element.50), channel_id=1, source_target_pairs={{0,4},{2,6},{4,8},{6,10},{8,12},{10,14},{16,20},{18,22},{20,24},{2... | collective-permute-start | bytes 393224 | tf_op jit(solution)/shard_map/ppermute | solution.py:54
  186.1 13.4 %collective-permute-start.27 = (bf16[512,256]{1,0:T(8,128)(2,1)S(1)}, bf16[512,256]{1,0:T(8,128)(2,1)S(1)}, u32[]{:S(2)}, u32[]{:S(2)}) collective-permute-start(bf16[512,256]{1,0:T(8,128)(2,1)S(1)} %get-tuple-element.31), channel_id=1, source_target_pairs={{4,0},{33,1},{6,2},{35,3},{8,4},{37,5},{10,6},{39,7},{41,9},{43,11... | collective-permute-start | bytes 786440 | tf_op jit(solution)/shard_map/ppermute | solution.py:54
  188.0 13.5 %collective-permute-start.28 = (bf16[512,256]{1,0:T(8,128)(2,1)S(1)}, bf16[512,256]{1,0:T(8,128)(2,1)S(1)}, u32[]{:S(2)}, u32[]{:S(2)}) collective-permute-start(bf16[512,256]{1,0:T(8,128)(2,1)S(1)} %get-tuple-element.30), channel_id=1, source_target_pairs={{8,0},{65,1},{10,2},{67,3},{69,5},{71,7},{0,8},{73,9},{2,10},{75,1... | collective-permute-start | bytes 786440 | tf_op jit(solution)/shard_map/ppermute | solution.py:54
  197.7 6.1 %collective-permute-start.29 = (bf16[512,256]{1,0:T(8,128)(2,1)S(1)}, bf16[512,256]{1,0:T(8,128)(2,1)S(1)}, u32[]{:S(2)}, u32[]{:S(2)}) collective-permute-start(bf16[512,256]{1,0:T(8,128)(2,1)S(1)} %get-tuple-element.29), channel_id=1, source_target_pairs={{0,4},{2,6},{4,8},{6,10},{8,12},{10,14},{16,20},{18,22},{20,24},{2... | collective-permute-start | bytes 786440 | tf_op jit(solution)/shard_map/ppermute | solution.py:54
  204.0 2.0 copy-start.3
  217.7 7.3 %collective-permute-start.30 = (bf16[2,384,512]{2,1,0:T(8,128)(2,1)}, bf16[2,384,512]{2,1,0:T(8,128)(2,1)}, u32[]{:S(2)}, u32[]{:S(2)}) collective-permute-start(bf16[2,384,512]{2,1,0:T(8,128)(2,1)} %bitcast.32), channel_id=1, source_target_pairs={{0,1},{1,0},{2,3},{3,2},{4,5},{5,4},{6,7},{7,6},{8,9},{9,8},{10,11... | collective-permute-start | bytes 2359304 | tf_op jit(solution)/shard_map/ppermute | solution.py:54
  221.7 18.0 %copy-start.1 = (bf16[512,1536]{1,0:T(8,128)(2,1)S(1)}, bf16[512,1536]{1,0:T(8,128)(2,1)}, u32[]{:S(2)}) copy-start(bf16[512,1536]{1,0:T(8,128)(2,1)} %param.11) | copy-start | bytes 4718596
  226.6 12.3 %collective-permute-start.31 = (bf16[384,512]{1,0:T(8,128)(2,1)S(1)}, bf16[384,512]{1,0:T(8,128)(2,1)S(1)}, u32[]{:S(2)}, u32[]{:S(2)}) collective-permute-start(bf16[384,512]{1,0:T(8,128)(2,1)S(1)} %dynamic-slice_bitcast_fusion), channel_id=1, source_target_pairs={{0,2},{1,3},{2,0},{3,1},{4,6},{5,7},{6,4},{7,5},{8,10},{9,11},{10,... | collective-permute-start | bytes 1179656 | tf_op jit(solution)/shard_map/ppermute | solution.py:54

commit v2 on v1

v2 whole, which is shorter than its diff:
```python
import functools

import jax
import jax.numpy as jnp
from jax import lax
from jax.experimental import pallas as pl
from jax.experimental.pallas import tpu as pltpu
from jax.sharding import PartitionSpec as P

HD = 128
BLK = 128
R = 3
G = 2
BLK_DEV = 4
NKEY = 3 + R + G
AXES = ("seq", "head")
LINE = 4
NQ = LINE * BLK_DEV
ROWS = NQ * BLK
NSHARD = 8
F32 = jnp.float32
BF16 = jnp.bfloat16


def moved(dev, ring, pair, line):
    h, s = dev % 4, dev // 4
    x, y, z = s // 8, (s // 4) % 2, s % 4
    if h % 2 == 0:
        x, z = (x + ring) % 4, (z + line) % 4
    else:
        z, x = (z + ring) % 4, (x + line) % 4
    y = (y + pair) % 2
    return ((x * 2 + y) * 4 + z) * 4 + h


def line_pos(dev):
    h, s = dev % 4, dev // 4
    return s % 4 if h % 2 == 0 else s // 8


DEVS = range(128)


def groups(step):
    seen, out = set(), []
    for d in DEVS:
        if d not in seen:
            out.append([d] + [step(d, k) for k in (1, 2, 3)])
            seen.update(out[-1])
    return out


LINES = groups(lambda d, k: moved(d, 0, 0, k))
RINGS = groups(lambda d, k: moved(d, k, 0, 0))
PAIR = [(d, moved(d, 0, 1, 0)) for d in DEVS if line_pos(d) < 3]
CORE = [(d, d ^ 1) for d in DEVS]
FAR = [(d, d ^ 2) for d in DEVS]


def send(x, perm):
    return lax.ppermute(x, AXES, perm)


def attend_kernel(table, qd_ref, own_ref, other_ref, gq_ref, own_out, other_out, kv, acc, kv_now, qd_now, sems):
    scale = HD ** (-0.5)
    side = NSHARD // 2 * ROWS
    copies = [
        pltpu.make_async_copy(ref, kv.at[pl.ds(n * side, side)], sems.at[n])
        for n, ref in enumerate((own_ref, other_ref))
    ]
    for c in copies:
        c.start()

    def zero(n, carry):
        acc[pl.ds(n * BLK, BLK), :] = jnp.zeros((BLK, 2 * HD), F32)
        return carry

    lax.fori_loop(0, NSHARD * NQ, zero, 0, unroll=4)
    qd_now[...] = jnp.zeros((2 * BLK, 2 * HD), BF16)
    for c in copies:
        c.wait()

    def step(n, carry):
        rows = pl.ds(pl.multiple_of(n * BLK, BLK), BLK)
        qd_now[:BLK, :HD] = qd_ref[rows, :HD]
        qd_now[BLK:, HD:] = qd_ref[rows, HD:]
        qd = qd_now[...]
        for j in range(NKEY):
            at = pl.multiple_of(table[n, j] * BLK, BLK)
            kv_now[j * BLK : (j + 1) * BLK, :] = kv[pl.ds(at, BLK), :]
        both = lax.dot_general(
            kv_now[...], qd, (((1,), (1,)), ((), ())), preferred_element_type=F32
        )
        scores, slope = both[:, :BLK], both[:, BLK:]
        peak = jnp.max(scores, axis=0, keepdims=True)
        e = jnp.exp((scores - peak) * scale)
        inv = 1.0 / jnp.sum(e, axis=0, keepdims=True)
        weighted = jnp.sum(e * slope, axis=0, keepdims=True) * inv
        probs = e * inv
        coeff = (probs * (slope - weighted)).astype(BF16)
        gq = lax.dot_general(
            coeff, kv_now[:, :HD], (((0,), (0,)), ((), ())), preferred_element_type=F32
        )
        gq_ref[rows, :] = (gq * scale).astype(BF16)
        gkv = lax.dot_general(
            jnp.concatenate([coeff, probs.astype(BF16)], axis=1),
            qd,
            (((1,), (0,)), ((), ())),
            preferred_element_type=F32,
        )
        for j in range(NKEY):
            at = pl.multiple_of(table[n, j] * BLK, BLK)
            acc[pl.ds(at, BLK), :] += gkv[j * BLK : (j + 1) * BLK]
        return carry

    lax.fori_loop(0, NQ, step, 0)

    for m, out in enumerate((own_out, other_out)):

        def put(n, carry, m=m, out=out):
            rows = pl.ds(pl.multiple_of(n * BLK, BLK), BLK)
            src = pl.ds(pl.multiple_of(m * side + n * BLK, BLK), BLK)
            out[rows, :HD] = (acc[src, :HD] * scale).astype(BF16)
            out[rows, HD:] = acc[src, HD:].astype(BF16)
            return carry

        lax.fori_loop(0, side // BLK, put, 0, unroll=2)


def attend(table, qd, own_row, other_row):
    side = jax.ShapeDtypeStruct(own_row.shape, BF16)
    vmem = pl.BlockSpec(memory_space=pltpu.VMEM)
    return pl.pallas_call(
        attend_kernel,
        name="attend",
        out_shape=(jax.ShapeDtypeStruct((ROWS, HD), BF16), side, side),
        grid_spec=pltpu.PrefetchScalarGridSpec(
            num_scalar_prefetch=1,
            grid=(),
            in_specs=[vmem] + [pl.BlockSpec(memory_space=pl.ANY)] * 2,
            out_specs=(vmem,) * 3,
            scratch_shapes=[
                pltpu.VMEM((NSHARD * ROWS, 2 * HD), BF16),
                pltpu.VMEM((NSHARD * ROWS, 2 * HD), F32),
                pltpu.VMEM((NKEY * BLK, 2 * HD), BF16),
                pltpu.VMEM((2 * BLK, 2 * HD), BF16),
                pltpu.SemaphoreType.DMA((2,)),
            ],
        ),
        compiler_params=pltpu.CompilerParams(vmem_limit_bytes=56 << 20),
    )(table, qd, own_row, other_row)


def add(*terms):
    return functools.reduce(lambda a, b: a + b, [t.astype(F32) for t in terms]).astype(BF16)


def exchange(x, who):
    return lax.all_to_all(x, AXES, 0, 0, axis_index_groups=who, tiled=True)


def ring_gather(shard):
    return exchange(jnp.concatenate([shard] * 4, axis=0), RINGS)


def ring_reduce(parts):
    return exchange(parts, RINGS).reshape(4, ROWS, -1)


def deal(pair):
    heads = pair.reshape(2, BLK_DEV * BLK, 3, HD).transpose(2, 1, 0, 3)
    heads = heads.reshape(3, BLK_DEV * BLK, 2 * HD)
    return exchange(jnp.concatenate([heads, heads[:1]], axis=0), LINES).reshape(ROWS, 2 * HD)


def give_back(grads, width):
    return exchange(grads.reshape(LINE, BLK_DEV * BLK, width), LINES)[:3]


def body(queries, keys, values, upstream_out, out_weight, qkv_weight, rand_links, global_links):
    s = lax.axis_index("seq")
    h = lax.axis_index("head")
    x, y, z = s // 8, (s // 4) % 2, s % 4
    core = h % 2

    n = jnp.arange(NQ, dtype=jnp.int32)
    line = n // BLK_DEV
    seq = jnp.where(core == 0, (x * 2 + y) * 4 + line, (line * 2 + y) * 4 + z)
    block = seq * BLK_DEV + n % BLK_DEV
    total = rand_links.shape[0]
    mine = block[:, None, None] == jnp.arange(total, dtype=jnp.int32)[None, :, None]
    rand = jnp.sum(jnp.where(mine, rand_links[None], 0), axis=1)
    window = (block[:, None] + jnp.arange(-1, 2, dtype=jnp.int32)[None]) % total
    glob = jnp.broadcast_to(global_links[None], (NQ, G))
    key = jnp.concatenate([window, rand, glob], axis=1)
    ks = key // BLK_DEV
    kx, ky, kz = ks // 8, (ks // 4) % 2, ks % 4
    k_ring = jnp.where(core == 0, kx, kz)
    k_pos = jnp.where(core == 0, kz, kx)
    shard_of = jnp.where(ky == y, 0, 4) + k_ring
    table = (shard_of * LINE + k_pos) * BLK_DEV + key % BLK_DEV

    own = deal(jnp.stack([keys, values], axis=0))
    other = send(own, PAIR)
    own_row = ring_gather(own)
    grad_ctx = lax.dot_general(
        upstream_out, out_weight, (((1,), (1,)), ((), ())), preferred_element_type=F32
    ).astype(BF16)
    qd = deal(jnp.stack([queries, grad_ctx], axis=0))
    grad_q, own_parts, other_parts = attend(table, qd, own_row, ring_gather(other))

    other_sum = add(*ring_reduce(other_parts))
    grad_kv = add(*ring_reduce(own_parts), send(other_sum, PAIR))
    q_back = give_back(grad_q, HD)
    kv_back = give_back(grad_kv, 2 * HD)
    stacked = jnp.stack([q_back, kv_back[:, :, :HD], kv_back[:, :, HD:]], axis=0)
    weight = qkv_weight.reshape(3, qkv_weight.shape[1], 3, HD)
    share = lax.dot_general(
        weight, stacked, (((0, 2, 3), (0, 1, 3)), ((), ())), preferred_element_type=F32
    ).astype(BF16)
    share = share.reshape(2, 2, share.shape[0] // 4, share.shape[1])
    mine_of = lax.dynamic_index_in_dim(share, core, 1, keepdims=False)
    theirs = lax.dynamic_index_in_dim(share, 1 - core, 1, keepdims=False)
    both = add(mine_of, send(theirs, CORE))
    far = h // 2
    keep = lax.dynamic_index_in_dim(both, far, 0, keepdims=False)
    give = lax.dynamic_index_in_dim(both, 1 - far, 0, keepdims=False)
    return add(keep, send(give, FAR))


def solution(mesh):
    in_specs = (
        P("seq", "head"),
        P("seq", "head"),
        P("seq", "head"),
        P("seq", None),
        P("head", None),
        P(None, None, "head"),
        P(),
        P(),
    )
    out_specs = P("head", "seq")
    return jax.shard_map(body, mesh=mesh, in_specs=in_specs, out_specs=out_specs, check_vma=False)
```

time: 242 us -> 258 us (1.066)
  starting transfers between devices: 110 us -> 48.4 us
  waiting for transfers between devices: 47.8 us -> 96.4 us
  blocking collectives: 0 us -> 32.6 us
  local copies, waits for them, and re-layouts: 35 us -> 25.7 us
  Pallas kernels: 26.1 us -> 30.5 us
    ppermute x32 -> x4, starting transfers between devices: 110 us -> 17.9 us  [send(): return lax.ppermute(x, AXES, perm)]
    all_to_all x0 -> x7, waiting for transfers between devices: none -> 67.4 us  [exchange(): return lax.all_to_all(x, AXES, 0, 0, axis_index_groups=who, tiled=True)]
    all_to_all x0 -> x1, blocking collectives: none -> 32.6 us  [exchange(): return lax.all_to_all(x, AXES, 0, 0, axis_index_groups=who, tiled=True)]
    all_to_all x0 -> x7, starting transfers between devices: none -> 30.5 us  [exchange(): return lax.all_to_all(x, AXES, 0, 0, axis_index_groups=who, tiled=True)]
    ppermute x32 -> x4, waiting for transfers between devices: 47.8 us -> 29 us  [send(): return lax.ppermute(x, AXES, perm)]
    slice x12 -> x2, local copies, waits for them, and re-layouts: 7.42 us -> 0.04 us  [deal(): heads[:1]]
    pallas_call x1, Pallas kernels: 26.1 us -> 30.5 us  [attend(): pl.pallas_call(attend_kernel, name='attend', out_shape=(jax.ShapeDtypeStr...]
    dynamic_slice x11 -> x0, local copies, waits for them, and re-layouts: 3.74 us -> none  [the longest x9 3.64 us: head(): lax.dynamic_index_in_dim(heads, jnp.minimum((pos + k) % 4, 2), 0, keepdim...]
  transfers between devices with their start and end apart: 32 -> 11, of which waited for: 10 -> 9; matrix products, arithmetic and copies ran while one was open for 12% -> 11% of each run, Pallas kernels for 0% -> 0%
where the time goes in v2:
time: 258 us; the launch traced here: 257 us
  waiting for transfers between devices  96.4 us (37%)
  starting transfers between devices  48.4 us (19%)
  blocking collectives  32.6 us (13%)
  Pallas kernels  30.5 us (12%)
  local copies, waits for them, and re-layouts  25.7 us (10%)
  other arithmetic  16.6 us (6%)
  matrix products  6.27 us (2%)
    all_to_all x7, waiting for transfers between devices, exchange(): return lax.all_to_all(x, AXES, 0, 0, axis_index_groups=who, tiled=True)  67.4 us
    all_to_all x1, blocking collectives, exchange(): return lax.all_to_all(x, AXES, 0, 0, axis_index_groups=who, tiled=True)  32.6 us
    pallas_call x1, Pallas kernels, attend(): pl.pallas_call(attend_kernel, name='attend', out_shape=(jax.ShapeDtypeStr...  30.5 us
    all_to_all x7, starting transfers between devices, exchange(): return lax.all_to_all(x, AXES, 0, 0, axis_index_groups=who, tiled=True)  30.5 us
    ppermute x4, waiting for transfers between devices, send(): return lax.ppermute(x, AXES, perm)  29 us
    ppermute x4, starting transfers between devices, send(): return lax.ppermute(x, AXES, perm)  17.9 us
    unnamed x17, local copies, waits for them, and re-layouts  12.9 us
    convert_element_type x3, other arithmetic, add(): functools.reduce(lambda a, b: a + b, [t.astype(F32) for t in terms])  6.25 us
  transfers between devices with their start and end apart: 11, of which 9 were waited for; matrix products, arithmetic and copies ran while one was open for 11% of the time, Pallas kernels for 0%

profile of v2, /device:TPU:1, one launch (start us, length us, event | category | flops | bytes accessed | tf_op | source)
XLA Modules:
  0.0 256.6 jit_solution(5617895254571430099)
XLA Ops:
  0.0 1.3 copy.42
  1.3 1.2 copy.43
  2.7 1.1 pad_maximum_fusion.3
  3.7 4.8 %all-to-all-start.1 = ((bf16[4,512,256]{1,2,0:T(8,128)(2,1)}), bf16[4,512,256]{1,2,0:T(8,128)(2,1)S(1)}, u32[]{:S(2)}, u32[]{:S(2)}) async-start(bf16[4,512,256]{1,2,0:T(8,128)(2,1)} %pad_maximum_fusion.3), calls=%async_computation.1 | async-start | bytes 2097152 | tf_op jit(solution)/shard_map/all_to_all | solution.py:159
  8.6 0.2 copy.39
  8.8 2.1 convolution_convert_fusion
  11.0 1.1 pad_maximum_fusion.2
  12.1 6.5 %all-to-all-done.1 = bf16[4,512,256]{1,2,0:T(8,128)(2,1)S(1)} async-done(((bf16[4,512,256]{1,2,0:T(8,128)(2,1)}), bf16[4,512,256]{1,2,0:T(8,128)(2,1)S(1)}, u32[]{:S(2)}, u32[]{:S(2)}) %all-to-all-start.1) | async-done | bytes 1048608 | tf_op jit(solution)/shard_map/all_to_all | solution.py:159
  18.6 1.0 copy-done.2
  19.6 3.5 %all-to-all-start = ((bf16[4,512,256]{1,2,0:T(8,128)(2,1)}), bf16[4,512,256]{1,2,0:T(8,128)(2,1)S(1)}, u32[]{:S(2)}, u32[]{:S(2)}) async-start(bf16[4,512,256]{1,2,0:T(8,128)(2,1)} %pad_maximum_fusion.2), calls=%async_computation | async-start | bytes 2097152 | tf_op jit(solution)/shard_map/all_to_all | solution.py:159
  23.1 1.5 copy.45
  24.6 2.2 pad_maximum_fusion
  26.8 6.0 %all-to-all-done = bf16[4,512,256]{1,2,0:T(8,128)(2,1)S(1)} async-done(((bf16[4,512,256]{1,2,0:T(8,128)(2,1)}), bf16[4,512,256]{1,2,0:T(8,128)(2,1)S(1)}, u32[]{:S(2)}, u32[]{:S(2)}) %all-to-all-start) | async-done | bytes 1048608 | tf_op jit(solution)/shard_map/all_to_all | solution.py:159
  32.8 5.0 %all-to-all-start.2 = ((bf16[4,2048,256]{2,1,0:T(8,128)(2,1)}), bf16[4,2048,256]{2,1,0:T(8,128)(2,1)}, u32[]{:S(2)}, u32[]{:S(2)}) async-start(bf16[4,2048,256]{2,1,0:T(8,128)(2,1)} %bitcast.60), calls=%async_computation.2 | async-start | bytes 8388608 | tf_op jit(solution)/shard_map/all_to_all | solution.py:159
  37.8 3.2 %collective-permute-start = (bf16[2048,256]{1,0:T(8,128)(2,1)S(1)}, bf16[2048,256]{1,0:T(8,128)(2,1)S(1)}, u32[]{:S(2)}, u32[]{:S(2)}) collective-permute-start(bf16[2048,256]{1,0:T(8,128)(2,1)S(1)} %bitcast.62), channel_id=1, source_target_pairs={{0,16},{1,17},{2,18},{3,19},{4,20},{5,21},{6,22},{7,23},{8,24},{9,... | collective-permute-start | bytes 3145736 | tf_op jit(solution)/shard_map/ppermute | solution.py:61
  41.0 19.6 %collective-permute-done = bf16[2048,256]{1,0:T(8,128)(2,1)S(1)} collective-permute-done((bf16[2048,256]{1,0:T(8,128)(2,1)S(1)}, bf16[2048,256]{1,0:T(8,128)(2,1)S(1)}, u32[]{:S(2)}, u32[]{:S(2)}) %collective-permute-start) | collective-permute-done | bytes 1048608 | tf_op jit(solution)/shard_map/ppermute | solution.py:61
  60.6 2.1 pad_maximum_fusion.1
  62.8 2.6 %all-to-all-done.2 = bf16[4,2048,256]{2,1,0:T(8,128)(2,1)} async-done(((bf16[4,2048,256]{2,1,0:T(8,128)(2,1)}), bf16[4,2048,256]{2,1,0:T(8,128)(2,1)}, u32[]{:S(2)}, u32[]{:S(2)}) %all-to-all-start.2) | async-done | bytes 4194336 | tf_op jit(solution)/shard_map/all_to_all | solution.py:159
  65.4 5.0 %all-to-all-start.3 = ((bf16[4,2048,256]{2,1,0:T(8,128)(2,1)}), bf16[4,2048,256]{2,1,0:T(8,128)(2,1)}, u32[]{:S(2)}, u32[]{:S(2)}) async-start(bf16[4,2048,256]{2,1,0:T(8,128)(2,1)} %bitcast.59), calls=%async_computation.3 | async-start | bytes 8388608 | tf_op jit(solution)/shard_map/all_to_all | solution.py:159
  70.6 0.1 select_reduce_fusion
  70.7 0.1 copy.38
  70.9 0.1 add_select_fusion.7
  71.0 0.7 fusion.14.table
  71.7 1.3 copy.41
  73.0 24.7 %all-to-all-done.3 = bf16[4,2048,256]{2,1,0:T(8,128)(2,1)} async-done(((bf16[4,2048,256]{2,1,0:T(8,128)(2,1)}), bf16[4,2048,256]{2,1,0:T(8,128)(2,1)}, u32[]{:S(2)}, u32[]{:S(2)}) %all-to-all-start.3) | async-done | bytes 4194336 | tf_op jit(solution)/shard_map/all_to_all | solution.py:159
  97.8 30.5 %attend.1 = (bf16[2048,128]{1,0:T(8,128)(2,1)}, bf16[8192,256]{1,0:T(8,128)(2,1)}, bf16[8192,256]{1,0:T(8,128)(2,1)}) custom-call(s32[16,8]{1,0:T(8,128)} %fusion.14.table, bf16[2048,256]{1,0:T(8,128)(2,1)} %bitcast.65, bf16[8192,256]{1,0:T(8,128)(2,1)} %bitcast.13.own_ref, bf16[8192,256]{1,0:T(8,128)(2,1)} %bitcast.15.other_ref), custom_call_target="tpu_custom_call" | custom-call | tf_op jit(solution)/shard_map/attend/pallas_call | solution.py:133
  128.2 32.6 %all_to_all.60 = bf16[4,2048,256]{2,1,0:T(8,128)(2,1)} all-to-all(bf16[4,2048,256]{2,1,0:T(8,128)(2,1)} %bitcast.64), channel_id=1, replica_groups={{0,32,64,96},{1,5,9,13},{2,34,66,98},{3,7,11,15},{4,36,68,100},{6,38,70..., dimensions={0} | all-to-all | bytes 8388608 | tf_op jit(solution)/shard_map/all_to_all | solution.py:159
  160.8 4.9 %all-to-all-start.5 = ((bf16[4,2048,256]{2,1,0:T(8,128)(2,1)}), bf16[4,2048,256]{2,1,0:T(8,128)(2,1)}, u32[]{:S(2)}, u32[]{:S(2)}) async-start(bf16[4,2048,256]{2,1,0:T(8,128)(2,1)} %bitcast.63), calls=%async_computation.5 | async-start | bytes 8388608 | tf_op jit(solution)/shard_map/all_to_all | solution.py:159
  165.7 2.7 %fusion.9 = bf16[2048,256]{1,0:T(8,128)(2,1)S(1)} fusion(bf16[4,2048,256]{2,1,0:T(8,128)(2,1)} %all_to_all.60), kind=kLoop, calls=%fused_computation.16 | loop fusion | flops 4194304 | bytes 5242880 | tf_op jit(solution)/shard_map/add | solution.py:155
  168.3 3.2 %collective-permute-start.1 = (bf16[2048,256]{1,0:T(8,128)(2,1)S(1)}, bf16[2048,256]{1,0:T(8,128)(2,1)S(1)}, u32[]{:S(2)}, u32[]{:S(2)}) collective-permute-start(bf16[2048,256]{1,0:T(8,128)(2,1)S(1)} %fusion.9), channel_id=1, source_target_pairs={{0,16},{1,17},{2,18},{3,19},{4,20},{5,21},{6,22},{7,23},{8,24},{9,... | collective-permute-start | bytes 3145736 | tf_op jit(solution)/shard_map/ppermute | solution.py:61
  171.6 21.0 %all-to-all-done.5 = bf16[4,2048,256]{2,1,0:T(8,128)(2,1)} async-done(((bf16[4,2048,256]{2,1,0:T(8,128)(2,1)}), bf16[4,2048,256]{2,1,0:T(8,128)(2,1)}, u32[]{:S(2)}, u32[]{:S(2)}) %all-to-all-start.5) | async-done | bytes 4194336 | tf_op jit(solution)/shard_map/all_to_all | solution.py:159
  192.6 3.5 %all-to-all-start.4 = ((bf16[4,512,128]{2,1,0:T(8,128)(2,1)}), bf16[4,512,128]{2,1,0:T(8,128)(2,1)S(1)}, u32[]{:S(2)}, u32[]{:S(2)}) async-start(bf16[4,512,128]{2,1,0:T(8,128)(2,1)} %bitcast.16), calls=%async_computation.4 | async-start | bytes 1048576 | tf_op jit(solution)/shard_map/all_to_all | solution.py:159
  196.1 3.8 %fusion.2 = bf16[2048,256]{1,0:T(8,128)(2,1)} fusion(bf16[2048,256]{1,0:T(8,128)(2,1)S(1)} %collective-permute-done.1, bf16[4,2048,256]{2,1,0:T(8,128)(2,1)} %all-to-all-done.5), kind=kLoop, calls=%fused_computation.6 | loop fusion | flops 5242880 | bytes 6291456 | tf_op jit(solution)/shard_map/convert_element_type | solution.py:155
  199.9 3.1 %all-to-all-done.4 = bf16[4,512,128]{2,1,0:T(8,128)(2,1)S(1)} async-done(((bf16[4,512,128]{2,1,0:T(8,128)(2,1)}), bf16[4,512,128]{2,1,0:T(8,128)(2,1)S(1)}, u32[]{:S(2)}, u32[]{:S(2)}) %all-to-all-start.4) | async-done | bytes 524320 | tf_op jit(solution)/shard_map/all_to_all | solution.py:159
  203.0 3.7 %all-to-all-start.7 = ((bf16[4,512,256]{2,1,0:T(8,128)(2,1)}), bf16[4,512,256]{2,1,0:T(8,128)(2,1)S(1)}, u32[]{:S(2)}, u32[]{:S(2)}) async-start(bf16[4,512,256]{2,1,0:T(8,128)(2,1)} %bitcast.22), calls=%async_computation.7 | async-start | bytes 2097152 | tf_op jit(solution)/shard_map/all_to_all | solution.py:159
  206.7 6.1 %copy.46 = bf16[3,1536,384]{1,2,0:T(8,128)(2,1)} copy(bf16[3,1536,384]{2,1,0:T(8,128)(2,1)} %param.13) | data formatting | bytes 7077888 | tf_op args[5]
  212.8 3.4 %all-to-all-done.7 = bf16[4,512,256]{2,1,0:T(8,128)(2,1)S(1)} async-done(((bf16[4,512,256]{2,1,0:T(8,128)(2,1)}), bf16[4,512,256]{2,1,0:T(8,128)(2,1)S(1)}, u32[]{:S(2)}, u32[]{:S(2)}) %all-to-all-start.7) | async-done | bytes 1048608 | tf_op jit(solution)/shard_map/all_to_all | solution.py:159
  216.2 0.1 slice_bitcast_fusion.1
  216.4 4.2 %fusion.1 = bf16[1536,512]{0,1:T(8,128)(2,1)S(1)} fusion(bf16[3,1536,3,128]{1,3,2,0:T(8,128)(2,1)} %bitcast.66, bf16[1,3,512,128]{3,2,1,0:T(8,128)(2,1)S(1)} %get-tuple-element.14, bf16[1,3,512,128]{3,2,1,0:T(8,128)(2,1)S(1)} %get-tuple-element.13, bf16[1,3,512,128]{3,2,1,0:T(8,128)(2,1)S(1)} %slice_bitcast_fusion.2), kind=kOutput, calls=%fused_computation.4 | convolution fusion | flops 1813905408 | bytes 6291456 | tf_op jit(solution)/shard_map/dot_general | solution.py:218
  220.6 0.4 reshape.182
  221.0 4.4 %constant_dynamic-slice_fusion.1 = (bf16[2,1,384,512]{2,1,0,3:T(2,128)(2,1)S(1)}, bf16[2,1,384,512]{2,1,0,3:T(2,128)(2,1)}) fusion(bf16[2,2,384,512]{2,1,0,3:T(2,128)(2,1)S(1)} %reshape.182, s32[]{:T(128)S(6)} %select_n.156, s32[]{:T(128)S(6)} %select_n.157), kind=kLoop, calls=%fused_computation.69 | loop fusion | bytes 3145736 | tf_op jit(solution)/shard_map/jit(dynamic_index_in_dim)/dynamic_slice | solution.py:222
  225.4 4.6 %copy.49 = bf16[2,1,384,512]{3,2,0,1:T(8,128)(2,1)} copy(bf16[2,1,384,512]{2,1,0,3:T(2,128)(2,1)} %get-tuple-element.12) | data formatting | bytes 1572864 | tf_op jit(solution)/shard_map/jit(dynamic_index_in_dim)/dynamic_slice | solution.py:223
  230.0 8.6 %collective-permute-start.2 = (bf16[2,384,512]{2,1,0:T(8,128)(2,1)}, bf16[2,384,512]{2,1,0:T(8,128)(2,1)}, u32[]{:S(2)}, u32[]{:S(2)}) collective-permute-start(bf16[2,384,512]{2,1,0:T(8,128)(2,1)} %bitcast.30), channel_id=1, source_target_pairs={{0,1},{1,0},{2,3},{3,2},{4,5},{5,4},{6,7},{7,6},{8,9},{9,8},{10,11... | collective-permute-start | bytes 2359304 | tf_op jit(solution)/shard_map/ppermute | solution.py:61
  238.6 3.3 %copy.52 = bf16[2,1,384,512]{3,2,0,1:T(8,128)(2,1)} copy(bf16[2,1,384,512]{2,1,0,3:T(2,128)(2,1)S(1)} %get-tuple-element.11) | data formatting | bytes 1572864
  241.8 1.6 fusion.3
  243.5 3.0 %collective-permute-start.3 = (bf16[384,512]{1,0:T(8,128)(2,1)S(1)}, bf16[384,512]{1,0:T(8,128)(2,1)S(1)}, u32[]{:S(2)}, u32[]{:S(2)}) collective-permute-start(bf16[384,512]{1,0:T(8,128)(2,1)S(1)} %dynamic-slice_bitcast_fusion), channel_id=1, source_target_pairs={{0,2},{1,3},{2,0},{3,1},{4,6},{5,7},{6,4},{7,5},{8,10},{9,11},{10,... | collective-permute-start | bytes 1179656 | tf_op jit(solution)/shard_map/ppermute | solution.py:61
  246.4 9.3 %collective-permute-done.3 = bf16[384,512]{1,0:T(8,128)(2,1)S(1)} collective-permute-done((bf16[384,512]{1,0:T(8,128)(2,1)S(1)}, bf16[384,512]{1,0:T(8,128)(2,1)S(1)}, u32[]{:S(2)}, u32[]{:S(2)}) %collective-permute-start.3) | collective-permute-done | bytes 393248 | tf_op jit(solution)/shard_map/ppermute | solution.py:61
  255.8 0.8 fusion.10
  (25 shorter events, 0.6 us)
Async XLA Ops:
  0.0 8.8 %copy-start = (bf16[512,1536]{1,0:T(8,128)(2,1)S(1)}, bf16[512,1536]{1,0:T(8,128)(2,1)}, u32[]{:S(2)}) copy-start(bf16[512,1536]{1,0:T(8,128)(2,1)} %param.11) | copy-start | bytes 4718596
  2.6 5.9 %copy-start.3 = (bf16[512,384]{1,0:T(8,128)(2,1)S(1)}, bf16[512,384]{1,0:T(8,128)(2,1)}, u32[]{:S(2)}) copy-start(bf16[512,384]{1,0:T(8,128)(2,1)} %param.8) | copy-start | bytes 1179652
  3.7 14.9 %all-to-all-start.1 = ((bf16[4,512,256]{1,2,0:T(8,128)(2,1)}), bf16[4,512,256]{1,2,0:T(8,128)(2,1)S(1)}, u32[]{:S(2)}, u32[]{:S(2)}) async-start(bf16[4,512,256]{1,2,0:T(8,128)(2,1)} %pad_maximum_fusion.3), calls=%async_computation.1 | async-start | bytes 2097152 | tf_op jit(solution)/shard_map/all_to_all | solution.py:159
  18.6 1.0 copy-start.2
  19.6 13.2 %all-to-all-start = ((bf16[4,512,256]{1,2,0:T(8,128)(2,1)}), bf16[4,512,256]{1,2,0:T(8,128)(2,1)S(1)}, u32[]{:S(2)}, u32[]{:S(2)}) async-start(bf16[4,512,256]{1,2,0:T(8,128)(2,1)} %pad_maximum_fusion.2), calls=%async_computation | async-start | bytes 2097152 | tf_op jit(solution)/shard_map/all_to_all | solution.py:159
  32.8 32.6 %all-to-all-start.2 = ((bf16[4,2048,256]{2,1,0:T(8,128)(2,1)}), bf16[4,2048,256]{2,1,0:T(8,128)(2,1)}, u32[]{:S(2)}, u32[]{:S(2)}) async-start(bf16[4,2048,256]{2,1,0:T(8,128)(2,1)} %bitcast.60), calls=%async_computation.2 | async-start | bytes 8388608 | tf_op jit(solution)/shard_map/all_to_all | solution.py:159
  37.8 22.8 %collective-permute-start = (bf16[2048,256]{1,0:T(8,128)(2,1)S(1)}, bf16[2048,256]{1,0:T(8,128)(2,1)S(1)}, u32[]{:S(2)}, u32[]{:S(2)}) collective-permute-start(bf16[2048,256]{1,0:T(8,128)(2,1)S(1)} %bitcast.62), channel_id=1, source_target_pairs={{0,16},{1,17},{2,18},{3,19},{4,20},{5,21},{6,22},{7,23},{8,24},{9,... | collective-permute-start | bytes 3145736 | tf_op jit(solution)/shard_map/ppermute | solution.py:61
  65.4 5.2 %copy-start.4 = (s32[128,3]{0,1:T(4,128)S(1)}, s32[128,3]{0,1:T(4,128)}, u32[]{:S(2)}) copy-start(s32[128,3]{0,1:T(4,128)} %param.14) | copy-start | bytes 4612
  65.4 5.4 %copy-start.5 = (s32[2]{0:T(128)S(1)}, s32[2]{0:T(128)}, u32[]{:S(2)}) copy-start(s32[2]{0:T(128)} %param.15) | copy-start | bytes 28
  65.4 32.4 %all-to-all-start.3 = ((bf16[4,2048,256]{2,1,0:T(8,128)(2,1)}), bf16[4,2048,256]{2,1,0:T(8,128)(2,1)}, u32[]{:S(2)}, u32[]{:S(2)}) async-start(bf16[4,2048,256]{2,1,0:T(8,128)(2,1)} %bitcast.59), calls=%async_computation.3 | async-start | bytes 8388608 | tf_op jit(solution)/shard_map/all_to_all | solution.py:159
  160.8 31.8 %all-to-all-start.5 = ((bf16[4,2048,256]{2,1,0:T(8,128)(2,1)}), bf16[4,2048,256]{2,1,0:T(8,128)(2,1)}, u32[]{:S(2)}, u32[]{:S(2)}) async-start(bf16[4,2048,256]{2,1,0:T(8,128)(2,1)} %bitcast.63), calls=%async_computation.5 | async-start | bytes 8388608 | tf_op jit(solution)/shard_map/all_to_all | solution.py:159
  168.3 27.7 %collective-permute-start.1 = (bf16[2048,256]{1,0:T(8,128)(2,1)S(1)}, bf16[2048,256]{1,0:T(8,128)(2,1)S(1)}, u32[]{:S(2)}, u32[]{:S(2)}) collective-permute-start(bf16[2048,256]{1,0:T(8,128)(2,1)S(1)} %fusion.9), channel_id=1, source_target_pairs={{0,16},{1,17},{2,18},{3,19},{4,20},{5,21},{6,22},{7,23},{8,24},{9,... | collective-permute-start | bytes 3145736 | tf_op jit(solution)/shard_map/ppermute | solution.py:61
  192.6 10.4 %all-to-all-start.4 = ((bf16[4,512,128]{2,1,0:T(8,128)(2,1)}), bf16[4,512,128]{2,1,0:T(8,128)(2,1)S(1)}, u32[]{:S(2)}, u32[]{:S(2)}) async-start(bf16[4,512,128]{2,1,0:T(8,128)(2,1)} %bitcast.16), calls=%async_computation.4 | async-start | bytes 1048576 | tf_op jit(solution)/shard_map/all_to_all | solution.py:159
  203.0 13.2 %all-to-all-start.7 = ((bf16[4,512,256]{2,1,0:T(8,128)(2,1)}), bf16[4,512,256]{2,1,0:T(8,128)(2,1)S(1)}, u32[]{:S(2)}, u32[]{:S(2)}) async-start(bf16[4,512,256]{2,1,0:T(8,128)(2,1)} %bitcast.22), calls=%async_computation.7 | async-start | bytes 2097152 | tf_op jit(solution)/shard_map/all_to_all | solution.py:159
  230.0 11.8 %collective-permute-start.2 = (bf16[2,384,512]{2,1,0:T(8,128)(2,1)}, bf16[2,384,512]{2,1,0:T(8,128)(2,1)}, u32[]{:S(2)}, u32[]{:S(2)}) collective-permute-start(bf16[2,384,512]{2,1,0:T(8,128)(2,1)} %bitcast.30), channel_id=1, source_target_pairs={{0,1},{1,0},{2,3},{3,2},{4,5},{5,4},{6,7},{7,6},{8,9},{9,8},{10,11... | collective-permute-start | bytes 2359304 | tf_op jit(solution)/shard_map/ppermute | solution.py:61
  238.6 18.1 %copy-start.1 = (bf16[512,1536]{1,0:T(8,128)(2,1)S(1)}, bf16[512,1536]{1,0:T(8,128)(2,1)}, u32[]{:S(2)}) copy-start(bf16[512,1536]{1,0:T(8,128)(2,1)} %param.11) | copy-start | bytes 4718596
  243.5 12.3 %collective-permute-start.3 = (bf16[384,512]{1,0:T(8,128)(2,1)S(1)}, bf16[384,512]{1,0:T(8,128)(2,1)S(1)}, u32[]{:S(2)}, u32[]{:S(2)}) collective-permute-start(bf16[384,512]{1,0:T(8,128)(2,1)S(1)} %dynamic-slice_bitcast_fusion), channel_id=1, source_target_pairs={{0,2},{1,3},{2,0},{3,1},{4,6},{5,7},{6,4},{7,5},{8,10},{9,11},{10,... | collective-permute-start | bytes 1179656 | tf_op jit(solution)/shard_map/ppermute | solution.py:61

commit v3 on v1

v3 whole, which is shorter than its diff:
```python
import functools

import jax
import jax.numpy as jnp
from jax import lax
from jax.experimental import pallas as pl
from jax.experimental.pallas import tpu as pltpu
from jax.sharding import PartitionSpec as P

HD = 128
BLK = 128
R = 3
G = 2
BLK_DEV = 4
NKEY = 3 + R + G
AXES = ("seq", "head")
LINE = 4
NQ = LINE * BLK_DEV
ROWS = NQ * BLK
NSHARD = 8
F32 = jnp.float32
BF16 = jnp.bfloat16


def moved(dev, ring, pair, line):
    h, s = dev % 4, dev // 4
    x, y, z = s // 8, (s // 4) % 2, s % 4
    if h % 2 == 0:
        x, z = (x + ring) % 4, (z + line) % 4
    else:
        z, x = (z + ring) % 4, (x + line) % 4
    y = (y + pair) % 2
    return ((x * 2 + y) * 4 + z) * 4 + h


def line_pos(dev):
    h, s = dev % 4, dev // 4
    return s % 4 if h % 2 == 0 else s // 8


DEVS = range(128)


def groups(step):
    seen, out = set(), []
    for d in DEVS:
        if d not in seen:
            out.append([d] + [step(d, k) for k in (1, 2, 3)])
            seen.update(out[-1])
    return out


LINES = groups(lambda d, k: moved(d, 0, 0, k))
RING = {k: [(d, moved(d, k, 0, 0)) for d in DEVS if line_pos(d) < 3] for k in (1, 2, 3)}
PAIR = [(d, moved(d, 0, 1, 0)) for d in DEVS if line_pos(d) < 3]
CORE = [(d, d ^ 1) for d in DEVS]
FAR = [(d, d ^ 2) for d in DEVS]


def send(x, perm):
    return lax.ppermute(x, AXES, perm)


def attend_kernel(table, qd_ref, *refs):
    kv_refs, gq_ref = refs[:NSHARD], refs[NSHARD]
    out_refs = refs[NSHARD + 1 : 2 * NSHARD + 1]
    kv, acc, kv_now, stage, in_sems, out_sems = refs[2 * NSHARD + 1 :]
    scale = HD ** (-0.5)
    loads = [
        pltpu.make_async_copy(kv_refs[m], kv.at[pl.ds(m * ROWS, ROWS)], in_sems.at[m])
        for m in range(NSHARD)
    ]
    for c in loads:
        c.start()

    def zero(n, carry):
        acc[pl.ds(pl.multiple_of(n * BLK, BLK), BLK), :] = jnp.zeros((BLK, 2 * HD), F32)
        return carry

    lax.fori_loop(0, NSHARD * NQ, zero, 0, unroll=2)
    for c in loads:
        c.wait()

    nt = (((1,), (1,)), ((), ()))
    nn = (((1,), (0,)), ((), ()))
    tn = (((0,), (0,)), ((), ()))

    def step(n, carry):
        rows = pl.ds(pl.multiple_of(n * BLK, BLK), BLK)
        q = qd_ref[rows, :HD]
        d = qd_ref[rows, HD:]
        at = [pl.multiple_of(table[n, j] * BLK, BLK) for j in range(NKEY)]
        for j in range(NKEY):
            kv_now[j * BLK : (j + 1) * BLK, :] = kv[pl.ds(at[j], BLK), :]
        scores = lax.dot_general(kv_now[:, :HD], q, nt, preferred_element_type=F32)
        slope = lax.dot_general(kv_now[:, HD:], d, nt, preferred_element_type=F32)
        peak = jnp.max(scores, axis=0, keepdims=True)
        e = jnp.exp((scores - peak) * scale)
        inv = 1.0 / jnp.sum(e, axis=0, keepdims=True)
        weighted = jnp.sum(e * slope, axis=0, keepdims=True) * inv
        probs = e * inv
        coeff = (probs * (slope - weighted)).astype(BF16)
        low = probs.astype(BF16)
        gq = lax.dot_general(coeff, kv_now[:, :HD], tn, preferred_element_type=F32)
        gq_ref[rows, :] = (gq * scale).astype(BF16)
        gk = lax.dot_general(coeff, q, nn, preferred_element_type=F32)
        gv = lax.dot_general(low, d, nn, preferred_element_type=F32)
        for j in range(NKEY):
            part = slice(j * BLK, (j + 1) * BLK)
            acc[pl.ds(at[j], BLK), :HD] += gk[part]
            acc[pl.ds(at[j], BLK), HD:] += gv[part]
        return carry

    lax.fori_loop(0, NQ, step, 0, unroll=2)

    stores = [pltpu.make_async_copy(stage.at[m], out_refs[m], out_sems.at[m]) for m in range(NSHARD)]
    for m in range(NSHARD):

        def put(n, carry, m=m):
            rows = pl.ds(pl.multiple_of(n * BLK, BLK), BLK)
            src = pl.ds(pl.multiple_of(m * ROWS + n * BLK, BLK), BLK)
            stage[m, rows, :HD] = (acc[src, :HD] * scale).astype(BF16)
            stage[m, rows, HD:] = acc[src, HD:].astype(BF16)
            return carry

        lax.fori_loop(0, NQ, put, 0, unroll=2)
        stores[m].start()
    for c in stores:
        c.wait()


def attend(table, qd, shards):
    shard = jax.ShapeDtypeStruct((ROWS, 2 * HD), BF16)
    vmem = pl.BlockSpec(memory_space=pltpu.VMEM)
    far = pl.BlockSpec(memory_space=pl.ANY)
    out = pl.pallas_call(
        attend_kernel,
        name="attend",
        out_shape=(jax.ShapeDtypeStruct((ROWS, HD), BF16),) + (shard,) * NSHARD,
        grid_spec=pltpu.PrefetchScalarGridSpec(
            num_scalar_prefetch=1,
            grid=(),
            in_specs=[vmem] + [far] * NSHARD,
            out_specs=(vmem,) + (far,) * NSHARD,
            scratch_shapes=[
                pltpu.VMEM((NSHARD * ROWS, 2 * HD), BF16),
                pltpu.VMEM((NSHARD * ROWS, 2 * HD), F32),
                pltpu.VMEM((NKEY * BLK, 2 * HD), BF16),
                pltpu.VMEM((NSHARD, ROWS, 2 * HD), BF16),
                pltpu.SemaphoreType.DMA((NSHARD,)),
                pltpu.SemaphoreType.DMA((NSHARD,)),
            ],
        ),
        compiler_params=pltpu.CompilerParams(vmem_limit_bytes=56 << 20),
    )(table, qd, *shards)
    return out[0], out[1:]


def add(*terms):
    return functools.reduce(lambda a, b: a + b, [t.astype(F32) for t in terms]).astype(BF16)


def exchange(x):
    return lax.all_to_all(x, AXES, 0, 0, axis_index_groups=LINES, tiled=True)


def deal(a, b):
    heads = [
        jnp.concatenate([a[:, p * HD : (p + 1) * HD], b[:, p * HD : (p + 1) * HD]], axis=1)
        for p in (0, 1, 2, 0)
    ]
    return exchange(jnp.concatenate(heads, axis=0))


def ring_gather(shard):
    return [shard] + [send(shard, RING[k]) for k in (3, 2, 1)]


def ring_sends(parts):
    return [parts[0]] + [send(parts[k], RING[k]) for k in (1, 3, 2)]


def body(queries, keys, values, upstream_out, out_weight, qkv_weight, rand_links, global_links):
    s = lax.axis_index("seq")
    h = lax.axis_index("head")
    x, y, z = s // 8, (s // 4) % 2, s % 4
    core, far = h % 2, h // 2
    ring = jnp.where(core == 0, x, z)

    n = jnp.arange(NQ, dtype=jnp.int32)
    line = n // BLK_DEV
    seq = jnp.where(core == 0, (x * 2 + y) * 4 + line, (line * 2 + y) * 4 + z)
    block = seq * BLK_DEV + n % BLK_DEV
    total = rand_links.shape[0]
    mine = block[:, None, None] == jnp.arange(total, dtype=jnp.int32)[None, :, None]
    rand = jnp.sum(jnp.where(mine, rand_links[None], 0), axis=1)
    window = (block[:, None] + jnp.arange(-1, 2, dtype=jnp.int32)[None]) % total
    glob = jnp.broadcast_to(global_links[None], (NQ, G))
    key = jnp.concatenate([window, rand, glob], axis=1)
    ks = key // BLK_DEV
    kx, ky, kz = ks // 8, (ks // 4) % 2, ks % 4
    k_ring = jnp.where(core == 0, kx, kz)
    k_pos = jnp.where(core == 0, kz, kx)
    shard_of = jnp.where(ky == y, 0, 4) + (k_ring - ring) % 4
    table = (shard_of * LINE + k_pos) * BLK_DEV + key % BLK_DEV

    own = deal(keys, values)
    other = send(own, PAIR)
    own_row = ring_gather(own)
    grad_ctx = lax.dot_general(
        upstream_out, out_weight, (((1,), (1,)), ((), ())), preferred_element_type=F32
    ).astype(BF16)
    grad_ctx, other = lax.optimization_barrier((grad_ctx, other))
    qd = deal(queries, grad_ctx)
    grad_q, parts = attend(table, qd, own_row + ring_gather(other))

    other_sum = add(*ring_sends(parts[4:]))
    own_sum = ring_sends(parts[:4])
    q_back = exchange(grad_q)
    other_sum, q_back = lax.optimization_barrier((other_sum, q_back))
    kv_back = exchange(add(*own_sum, send(other_sum, PAIR)))

    def tokens(back, lanes):
        back = back.reshape(LINE, BLK_DEV * BLK, -1)
        return jnp.concatenate([back[p, :, lanes] for p in range(3)], axis=1)

    grads = jnp.stack(
        [
            tokens(q_back, slice(0, HD)),
            tokens(kv_back, slice(0, HD)),
            tokens(kv_back, slice(HD, 2 * HD)),
        ],
        axis=0,
    )
    weight = qkv_weight.reshape(3, 2, 2, qkv_weight.shape[1] // 4, qkv_weight.shape[2])

    def share(to_far, to_core):
        w = lax.dynamic_index_in_dim(weight, to_far, 1, keepdims=False)
        w = lax.dynamic_index_in_dim(w, to_core, 1, keepdims=False)
        return lax.dot_general(
            w, grads, (((0, 2), (0, 2)), ((), ())), preferred_element_type=F32
        ).astype(BF16)

    from_far = send(add(share(1 - far, core), send(share(1 - far, 1 - core), CORE)), FAR)
    here = send(share(far, 1 - core), CORE)
    return add(share(far, core), here, from_far)


def solution(mesh):
    in_specs = (
        P("seq", "head"),
        P("seq", "head"),
        P("seq", "head"),
        P("seq", None),
        P("head", None),
        P(None, None, "head"),
        P(),
        P(),
    )
    out_specs = P("head", "seq")
    return jax.shard_map(body, mesh=mesh, in_specs=in_specs, out_specs=out_specs, check_vma=False)
```

time: 242 us -> 210 us (0.87)
  starting transfers between devices: 110 us -> 71.1 us
  local copies, waits for them, and re-layouts: 35 us -> 5.56 us
  waiting for transfers between devices: 47.8 us -> 73.5 us
  blocking collectives: 0 us -> 14.8 us
  matrix products: 4.26 us -> 8.66 us
  other arithmetic: 15.6 us -> 12.1 us
  Pallas kernels: 26.1 us -> 23.2 us
    ppermute x32 -> x17, starting transfers between devices: 110 us -> 58.4 us  [send(): return lax.ppermute(x, AXES, perm)]
    all_to_all x0 -> x3, waiting for transfers between devices: none -> 24.2 us  [exchange(): return lax.all_to_all(x, AXES, 0, 0, axis_index_groups=LINES, tiled=True)]
    all_to_all x0 -> x1, blocking collectives: none -> 14.8 us  [exchange(): return lax.all_to_all(x, AXES, 0, 0, axis_index_groups=LINES, tiled=True)]
    unnamed x37 -> x18, local copies, waits for them, and re-layouts: 13.9 us -> 0.04 us
    dynamic_slice x13 -> x0, local copies, waits for them, and re-layouts: 12.8 us -> none  [the longest x1 4.65 us: body(): theirs = lax.dynamic_index_in_dim(share, 1 - core, 1, keepdims=False)]
    all_to_all x0 -> x3, starting transfers between devices: none -> 12.6 us  [exchange(): return lax.all_to_all(x, AXES, 0, 0, axis_index_groups=LINES, tiled=True)]
    concatenate x8 -> x2, other arithmetic: 7.77 us -> 1.17 us  [deal(): return exchange(jnp.concatenate(heads, axis=0))]
    slice x12 -> x4, local copies, waits for them, and re-layouts: 7.42 us -> 3.58 us  [the longest x2 2.45 us: deal(): a[:, p * HD:(p + 1) * HD]]
  transfers between devices with their start and end apart: 32 -> 20, of which waited for: 10 -> 11; matrix products, arithmetic and copies ran while one was open for 12% -> 8% of each run, Pallas kernels for 0% -> 0%
where the time goes in v3:
time: 210 us; the launch traced here: 209 us
  waiting for transfers between devices  73.5 us (35%)
  starting transfers between devices  71.1 us (34%)
  Pallas kernels  23.2 us (11%)
  blocking collectives  14.8 us (7%)
  other arithmetic  12.1 us (6%)
  matrix products  8.66 us (4%)
  local copies, waits for them, and re-layouts  5.56 us (3%)
    ppermute x17, starting transfers between devices, send(): return lax.ppermute(x, AXES, perm)  58.4 us
    ppermute x17, waiting for transfers between devices, send(): return lax.ppermute(x, AXES, perm)  49.3 us
    all_to_all x3, waiting for transfers between devices, exchange(): return lax.all_to_all(x, AXES, 0, 0, axis_index_groups=LINES, tiled=True)  24.2 us
    pallas_call x1, Pallas kernels, attend(): pl.pallas_call(attend_kernel, name='attend', out_shape=(jax.ShapeDtypeStr...  23.2 us
    all_to_all x1, blocking collectives, exchange(): return lax.all_to_all(x, AXES, 0, 0, axis_index_groups=LINES, tiled=True)  14.8 us
    all_to_all x3, starting transfers between devices, exchange(): return lax.all_to_all(x, AXES, 0, 0, axis_index_groups=LINES, tiled=True)  12.6 us
    convert_element_type x3, other arithmetic, add(): functools.reduce(lambda a, b: a + b, [t.astype(F32) for t in terms])  8.46 us
    dot_general x4, matrix products, share(): lax.dot_general(w, grads, (((0, 2), (0, 2)), ((), ())), preferred_element...  5.93 us
  transfers between devices with their start and end apart: 20, of which 11 were waited for; matrix products, arithmetic and copies ran while one was open for 8% of the time, Pallas kernels for 0%

profile of v3, /device:TPU:1, one launch (start us, length us, event | category | flops | bytes accessed | tf_op | source)
XLA Modules:
  0.0 209.4 jit_solution(16583003072224704726)
XLA Ops:
  0.0 1.4 fusion.38
  1.5 14.8 %all_to_all.43 = bf16[4,512,256]{2,1,0:T(8,128)(2,1)} all-to-all(bf16[4,512,256]{2,1,0:T(8,128)(2,1)S(1)} %bitcast.77), channel_id=1, replica_groups={{0,4,8,12},{1,33,65,97},{2,6,10,14},{3,35,67,99},{5,37,69,101},{7,39,71..., dimensions={0} | all-to-all | bytes 2097152 | tf_op jit(solution)/shard_map/all_to_all | solution.py:164
  16.3 3.2 %collective-permute-start = (bf16[2048,256]{1,0:T(8,128)(2,1)}, bf16[2048,256]{1,0:T(8,128)(2,1)}, u32[]{:S(2)}, u32[]{:S(2)}) collective-permute-start(bf16[2048,256]{1,0:T(8,128)(2,1)} %bitcast.3.refs_0_), channel_id=1, source_target_pairs={{0,16},{1,17},{2,18},{3,19},{4,20},{5,21},{6,22},{7,23},{8,24},{9,... | collective-permute-start | bytes 3145736 | tf_op jit(solution)/shard_map/ppermute | solution.py:61
  19.5 3.3 %collective-permute-start.3 = (bf16[2048,256]{1,0:T(8,128)(2,1)}, bf16[2048,256]{1,0:T(8,128)(2,1)}, u32[]{:S(2)}, u32[]{:S(2)}) collective-permute-start(bf16[2048,256]{1,0:T(8,128)(2,1)} %bitcast.3.refs_0_), channel_id=1, source_target_pairs={{0,32},{1,5},{2,34},{3,7},{4,36},{5,9},{6,38},{7,11},{8,40},{9,13}... | collective-permute-start | bytes 3145736 | tf_op jit(solution)/shard_map/ppermute | solution.py:61
  22.8 0.6 pad.30.clone
  23.4 1.1 fusion.36
  24.5 2.7 %convolution_convert_fusion = bf16[512,384]{1,0:T(8,128)(2,1)S(1)} fusion(bf16[512,1536]{1,0:T(8,128)(2,1)} %param.11, bf16[384,1536]{1,0:T(8,128)(2,1)} %param.12), kind=kOutput, calls=%fused_computation.12 | convolution fusion | flops 604176384 | bytes 3145728 | tf_op jit(solution)/shard_map/dot_general | solution.py:210
  27.2 5.2 %collective-permute-start.2 = (bf16[2048,256]{1,0:T(8,128)(2,1)}, bf16[2048,256]{1,0:T(8,128)(2,1)}, u32[]{:S(2)}, u32[]{:S(2)}) collective-permute-start(bf16[2048,256]{1,0:T(8,128)(2,1)} %bitcast.3.refs_0_), channel_id=1, source_target_pairs={{0,64},{1,9},{2,66},{3,11},{4,68},{5,13},{6,70},{7,15},{8,72},{9,1... | collective-permute-start | bytes 3145736 | tf_op jit(solution)/shard_map/ppermute | solution.py:61
  32.4 2.6 %collective-permute-start.1 = (bf16[2048,256]{1,0:T(8,128)(2,1)}, bf16[2048,256]{1,0:T(8,128)(2,1)}, u32[]{:S(2)}, u32[]{:S(2)}) collective-permute-start(bf16[2048,256]{1,0:T(8,128)(2,1)} %bitcast.3.refs_0_), channel_id=1, source_target_pairs={{0,96},{1,13},{2,98},{3,15},{4,100},{5,1},{6,102},{7,3},{8,104},{9... | collective-permute-start | bytes 3145736 | tf_op jit(solution)/shard_map/ppermute | solution.py:61
  35.1 5.3 %collective-permute-done.refs_4_ = bf16[2048,256]{1,0:T(8,128)(2,1)} collective-permute-done((bf16[2048,256]{1,0:T(8,128)(2,1)}, bf16[2048,256]{1,0:T(8,128)(2,1)}, u32[]{:S(2)}, u32[]{:S(2)}) %collective-permute-start) | collective-permute-done | bytes 1048608 | tf_op jit(solution)/shard_map/ppermute | solution.py:61
  40.3 4.3 %collective-permute-start.6 = (bf16[2048,256]{1,0:T(8,128)(2,1)}, bf16[2048,256]{1,0:T(8,128)(2,1)}, u32[]{:S(2)}, u32[]{:S(2)}) collective-permute-start(bf16[2048,256]{1,0:T(8,128)(2,1)} %collective-permute-done.refs_4_), channel_id=1, source_target_pairs={{0,32},{1,5},{2,34},{3,7},{4,36},{5,9},{6,38},{7,11},{8,40},{9,13}... | collective-permute-start | bytes 3145736 | tf_op jit(solution)/shard_map/ppermute | solution.py:61
  44.6 5.7 %collective-permute-start.5 = (bf16[2048,256]{1,0:T(8,128)(2,1)}, bf16[2048,256]{1,0:T(8,128)(2,1)}, u32[]{:S(2)}, u32[]{:S(2)}) collective-permute-start(bf16[2048,256]{1,0:T(8,128)(2,1)} %collective-permute-done.refs_4_), channel_id=1, source_target_pairs={{0,64},{1,9},{2,66},{3,11},{4,68},{5,13},{6,70},{7,15},{8,72},{9,1... | collective-permute-start | bytes 3145736 | tf_op jit(solution)/shard_map/ppermute | solution.py:61
  50.5 4.0 %collective-permute-start.4 = (bf16[2048,256]{1,0:T(8,128)(2,1)}, bf16[2048,256]{1,0:T(8,128)(2,1)}, u32[]{:S(2)}, u32[]{:S(2)}) collective-permute-start(bf16[2048,256]{1,0:T(8,128)(2,1)} %collective-permute-done.refs_4_), channel_id=1, source_target_pairs={{0,96},{1,13},{2,98},{3,15},{4,100},{5,1},{6,102},{7,3},{8,104},{9... | collective-permute-start | bytes 3145736 | tf_op jit(solution)/shard_map/ppermute | solution.py:61
  54.4 1.1 maximum_maximum_fusion.1
  55.5 4.2 %all-to-all-start.1 = ((bf16[4,512,256]{2,1,0:T(8,128)(2,1)}), bf16[4,512,256]{2,1,0:T(8,128)(2,1)}, u32[]{:S(2)}, u32[]{:S(2)}) async-start(bf16[4,512,256]{2,1,0:T(8,128)(2,1)} %bitcast.76), calls=%async_computation.1 | async-start | bytes 2097152 | tf_op jit(solution)/shard_map/all_to_all | solution.py:164
  60.2 1.3 fusion.22.table
  61.5 16.3 %all-to-all-done.1 = bf16[4,512,256]{2,1,0:T(8,128)(2,1)} async-done(((bf16[4,512,256]{2,1,0:T(8,128)(2,1)}), bf16[4,512,256]{2,1,0:T(8,128)(2,1)}, u32[]{:S(2)}, u32[]{:S(2)}) %all-to-all-start.1) | async-done | bytes 1048608 | tf_op jit(solution)/shard_map/all_to_all | solution.py:164
  77.7 0.5 collective-permute-done.5.refs_6_
  78.2 5.8 %collective-permute-done.4.refs_5_ = bf16[2048,256]{1,0:T(8,128)(2,1)} collective-permute-done((bf16[2048,256]{1,0:T(8,128)(2,1)}, bf16[2048,256]{1,0:T(8,128)(2,1)}, u32[]{:S(2)}, u32[]{:S(2)}) %collective-permute-start.4) | collective-permute-done | bytes 1048608 | tf_op jit(solution)/shard_map/ppermute | solution.py:61
  84.0 23.2 %attend.1 = (bf16[2048,128]{1,0:T(8,128)(2,1)}, bf16[2048,256]{1,0:T(8,128)(2,1)}, bf16[2048,256]{1,0:T(8,128)(2,1)}, bf16[2048,256]{1,0:T(8,128)(2,1)}, bf16[20...) custom-call(s32[16,8]{1,0:T(8,128)} %fusion.22.table, ...), custom_call_target="tpu_custom_call" | custom-call | tf_op jit(solution)/shard_map/attend/pallas_call | solution.py:136
  107.2 3.7 %collective-permute-start.7 = (bf16[2048,256]{1,0:T(8,128)(2,1)}, bf16[2048,256]{1,0:T(8,128)(2,1)}, u32[]{:S(2)}, u32[]{:S(2)}) collective-permute-start(bf16[2048,256]{1,0:T(8,128)(2,1)} %get-tuple-element.21), channel_id=1, source_target_pairs={{0,32},{1,5},{2,34},{3,7},{4,36},{5,9},{6,38},{7,11},{8,40},{9,13}... | collective-permute-start | bytes 3145736 | tf_op jit(solution)/shard_map/ppermute | solution.py:61
  111.0 2.8 %collective-permute-start.8 = (bf16[2048,256]{1,0:T(8,128)(2,1)}, bf16[2048,256]{1,0:T(8,128)(2,1)}, u32[]{:S(2)}, u32[]{:S(2)}) collective-permute-start(bf16[2048,256]{1,0:T(8,128)(2,1)} %get-tuple-element.22), channel_id=1, source_target_pairs={{0,96},{1,13},{2,98},{3,15},{4,100},{5,1},{6,102},{7,3},{8,104},{9... | collective-permute-start | bytes 3145736 | tf_op jit(solution)/shard_map/ppermute | solution.py:61
  113.7 3.2 %collective-permute-start.9 = (bf16[2048,256]{1,0:T(8,128)(2,1)}, bf16[2048,256]{1,0:T(8,128)(2,1)}, u32[]{:S(2)}, u32[]{:S(2)}) collective-permute-start(bf16[2048,256]{1,0:T(8,128)(2,1)} %get-tuple-element.23), channel_id=1, source_target_pairs={{0,64},{1,9},{2,66},{3,11},{4,68},{5,13},{6,70},{7,15},{8,72},{9,1... | collective-permute-start | bytes 3145736 | tf_op jit(solution)/shard_map/ppermute | solution.py:61
  117.0 4.1 %all-to-all-start.2 = ((bf16[4,512,128]{2,1,0:T(8,128)(2,1)}), bf16[4,512,128]{2,1,0:T(8,128)(2,1)}, u32[]{:S(2)}, u32[]{:S(2)}) async-start(bf16[4,512,128]{2,1,0:T(8,128)(2,1)} %bitcast.79), calls=%async_computation.2 | async-start | bytes 1048576 | tf_op jit(solution)/shard_map/all_to_all | solution.py:164
  121.1 2.0 collective-permute-start.10
  123.2 4.5 %collective-permute-start.11 = (bf16[2048,256]{1,0:T(8,128)(2,1)}, bf16[2048,256]{1,0:T(8,128)(2,1)}, u32[]{:S(2)}, u32[]{:S(2)}) collective-permute-start(bf16[2048,256]{1,0:T(8,128)(2,1)} %get-tuple-element.28), channel_id=1, source_target_pairs={{0,96},{1,13},{2,98},{3,15},{4,100},{5,1},{6,102},{7,3},{8,104},{9... | collective-permute-start | bytes 3145736 | tf_op jit(solution)/shard_map/ppermute | solution.py:61
  127.6 2.4 %collective-permute-start.12 = (bf16[2048,256]{1,0:T(8,128)(2,1)}, bf16[2048,256]{1,0:T(8,128)(2,1)}, u32[]{:S(2)}, u32[]{:S(2)}) collective-permute-start(bf16[2048,256]{1,0:T(8,128)(2,1)} %get-tuple-element.29), channel_id=1, source_target_pairs={{0,64},{1,9},{2,66},{3,11},{4,68},{5,13},{6,70},{7,15},{8,72},{9,1... | collective-permute-start | bytes 3145736 | tf_op jit(solution)/shard_map/ppermute | solution.py:61
  130.0 9.2 %collective-permute-done.9 = bf16[2048,256]{1,0:T(8,128)(2,1)} collective-permute-done((bf16[2048,256]{1,0:T(8,128)(2,1)}, bf16[2048,256]{1,0:T(8,128)(2,1)}, u32[]{:S(2)}, u32[]{:S(2)}) %collective-permute-start.9) | collective-permute-done | bytes 1048608 | tf_op jit(solution)/shard_map/ppermute | solution.py:61
  139.2 3.7 %add_convert_fusion.1 = bf16[2048,256]{1,0:T(8,128)(2,1)} fusion(bf16[2048,256]{1,0:T(8,128)(2,1)} %collective-permute-done.9, bf16[2048,256]{1,0:T(8,128)(2,1)} %collective-permute-done.8, bf16[2048,256]{1,0:T(8,128)(2,1)} %collective-permute-done.7, bf16[2048,256]{1,0:T(8,128)(2,1)} %get-tuple-element.20), kind=kLoop, calls=%fused_computation.1 | loop fusion | flops 4194304 | bytes 5242880 | tf_op jit(solution)/shard_map/convert_element_type | solution.py:160
  142.9 2.1 collective-permute-start.13
  145.0 5.4 %collective-permute-done.10 = bf16[2048,256]{1,0:T(8,128)(2,1)} collective-permute-done((bf16[2048,256]{1,0:T(8,128)(2,1)}, bf16[2048,256]{1,0:T(8,128)(2,1)}, u32[]{:S(2)}, u32[]{:S(2)}) %collective-permute-start.10) | collective-permute-done | bytes 1048608 | tf_op jit(solution)/shard_map/ppermute | solution.py:61
  150.4 2.0 collective-permute-done.11
  152.4 9.3 %collective-permute-done.12 = bf16[2048,256]{1,0:T(8,128)(2,1)} collective-permute-done((bf16[2048,256]{1,0:T(8,128)(2,1)}, bf16[2048,256]{1,0:T(8,128)(2,1)}, u32[]{:S(2)}, u32[]{:S(2)}) %collective-permute-start.12) | collective-permute-done | bytes 1048608 | tf_op jit(solution)/shard_map/ppermute | solution.py:61
  161.7 3.5 %collective-permute-done.13 = bf16[2048,256]{1,0:T(8,128)(2,1)S(1)} collective-permute-done((bf16[2048,256]{1,0:T(8,128)(2,1)}, bf16[2048,256]{1,0:T(8,128)(2,1)S(1)}, u32[]{:S(2)}, u32[]{:S(2)}) %collective-permute-start.13) | collective-permute-done | bytes 1048608 | tf_op jit(solution)/shard_map/ppermute | solution.py:61
  165.2 3.9 %add_convert_fusion = bf16[2048,256]{1,0:T(8,128)(2,1)} fusion(bf16[2048,256]{1,0:T(8,128)(2,1)S(1)} %collective-permute-done.13, bf16[2048,256]{1,0:T(8,128)(2,1)} %collective-permute-done.12, bf16[2048,256]{1,0:T(8,128)(2,1)} %collective-permute-done.11, bf16[2048,256]{1,0:T(8,128)(2,1)} %collective-permute-done.10, bf16[2048,256]{1,0:T(8,128)(2,1)} %get-tuple-element.26), kind=kLoop, calls=%fused_computation | loop fusion | flops 5242880 | bytes 6291456 | tf_op jit(solution)/shard_map/convert_element_type | solution.py:160
  169.0 4.2 %all-to-all-start.3 = ((bf16[4,512,256]{2,1,0:T(8,128)(2,1)}), bf16[4,512,256]{2,1,0:T(8,128)(2,1)}, u32[]{:S(2)}, u32[]{:S(2)}) async-start(bf16[4,512,256]{2,1,0:T(8,128)(2,1)} %bitcast.78), calls=%async_computation.3 | async-start | bytes 2097152 | tf_op jit(solution)/shard_map/all_to_all | solution.py:164
  173.3 1.1 fusion.35
  174.4 0.8 maximum_bitcast_fusion
  175.2 7.9 %all-to-all-done.3 = bf16[4,512,256]{2,1,0:T(8,128)(2,1)} async-done(((bf16[4,512,256]{2,1,0:T(8,128)(2,1)}), bf16[4,512,256]{2,1,0:T(8,128)(2,1)}, u32[]{:S(2)}, u32[]{:S(2)}) %all-to-all-start.3) | async-done | bytes 1048608 | tf_op jit(solution)/shard_map/all_to_all | solution.py:164
  183.1 1.3 slice_bitcast_fusion.5
  184.5 1.5 fusion.5
  186.0 6.7 %collective-permute-start.15 = (bf16[384,512]{1,0:T(8,128)(2,1)}, bf16[384,512]{1,0:T(8,128)(2,1)}, u32[]{:S(2)}, u32[]{:S(2)}) collective-permute-start(bf16[384,512]{1,0:T(8,128)(2,1)} %fusion.5), channel_id=1, source_target_pairs={{0,1},{1,0},{2,3},{3,2},{4,5},{5,4},{6,7},{7,6},{8,9},{9,8},{10,11... | collective-permute-start | bytes 1179656 | tf_op jit(solution)/shard_map/ppermute | solution.py:61
  192.7 2.0 fusion.2
  194.9 1.7 add_convert_fusion.3
  196.6 2.7 %collective-permute-start.16 = (bf16[384,512]{1,0:T(8,128)(2,1)S(1)}, bf16[384,512]{1,0:T(8,128)(2,1)S(1)}, u32[]{:S(2)}, u32[]{:S(2)}) collective-permute-start(bf16[384,512]{1,0:T(8,128)(2,1)S(1)} %add_convert_fusion.3), channel_id=1, source_target_pairs={{0,2},{1,3},{2,0},{3,1},{4,6},{5,7},{6,4},{7,5},{8,10},{9,11},{10,... | collective-permute-start | bytes 1179656 | tf_op jit(solution)/shard_map/ppermute | solution.py:61
  199.3 0.7 fusion.1
  200.0 8.4 %collective-permute-done.16 = bf16[384,512]{1,0:T(8,128)(2,1)S(1)} collective-permute-done((bf16[384,512]{1,0:T(8,128)(2,1)S(1)}, bf16[384,512]{1,0:T(8,128)(2,1)S(1)}, u32[]{:S(2)}, u32[]{:S(2)}) %collective-permute-start.16) | collective-permute-done | bytes 393248 | tf_op jit(solution)/shard_map/ppermute | solution.py:61
  208.4 0.9 add_convert_fusion.2
  (38 shorter events, 0.9 us)
Async XLA Ops:
  0.0 184.5 %copy-start = (bf16[3,1536,384]{2,1,0:T(8,128)(2,1)S(1)}, bf16[3,1536,384]{2,1,0:T(8,128)(2,1)}, u32[]{:S(2)}) copy-start(bf16[3,1536,384]{2,1,0:T(8,128)(2,1)} %param.13) | copy-start | bytes 10616836
  1.4 21.4 %copy-start.8 = (s32[2]{0:T(128)S(1)}, s32[2]{0:T(128)}, u32[]{:S(2)}) copy-start(s32[2]{0:T(128)} %param.15) | copy-start | bytes 28
  16.3 24.0 %collective-permute-start = (bf16[2048,256]{1,0:T(8,128)(2,1)}, bf16[2048,256]{1,0:T(8,128)(2,1)}, u32[]{:S(2)}, u32[]{:S(2)}) collective-permute-start(bf16[2048,256]{1,0:T(8,128)(2,1)} %bitcast.3.refs_0_), channel_id=1, source_target_pairs={{0,16},{1,17},{2,18},{3,19},{4,20},{5,21},{6,22},{7,23},{8,24},{9,... | collective-permute-start | bytes 3145736 | tf_op jit(solution)/shard_map/ppermute | solution.py:61
  19.5 31.0 %collective-permute-start.3 = (bf16[2048,256]{1,0:T(8,128)(2,1)}, bf16[2048,256]{1,0:T(8,128)(2,1)}, u32[]{:S(2)}, u32[]{:S(2)}) collective-permute-start(bf16[2048,256]{1,0:T(8,128)(2,1)} %bitcast.3.refs_0_), channel_id=1, source_target_pairs={{0,32},{1,5},{2,34},{3,7},{4,36},{5,9},{6,38},{7,11},{8,40},{9,13}... | collective-permute-start | bytes 3145736 | tf_op jit(solution)/shard_map/ppermute | solution.py:61
  27.2 34.3 %collective-permute-start.2 = (bf16[2048,256]{1,0:T(8,128)(2,1)}, bf16[2048,256]{1,0:T(8,128)(2,1)}, u32[]{:S(2)}, u32[]{:S(2)}) collective-permute-start(bf16[2048,256]{1,0:T(8,128)(2,1)} %bitcast.3.refs_0_), channel_id=1, source_target_pairs={{0,64},{1,9},{2,66},{3,11},{4,68},{5,13},{6,70},{7,15},{8,72},{9,1... | collective-permute-start | bytes 3145736 | tf_op jit(solution)/shard_map/ppermute | solution.py:61
  32.4 29.0 %collective-permute-start.1 = (bf16[2048,256]{1,0:T(8,128)(2,1)}, bf16[2048,256]{1,0:T(8,128)(2,1)}, u32[]{:S(2)}, u32[]{:S(2)}) collective-permute-start(bf16[2048,256]{1,0:T(8,128)(2,1)} %bitcast.3.refs_0_), channel_id=1, source_target_pairs={{0,96},{1,13},{2,98},{3,15},{4,100},{5,1},{6,102},{7,3},{8,104},{9... | collective-permute-start | bytes 3145736 | tf_op jit(solution)/shard_map/ppermute | solution.py:61
  40.3 37.4 %collective-permute-start.6 = (bf16[2048,256]{1,0:T(8,128)(2,1)}, bf16[2048,256]{1,0:T(8,128)(2,1)}, u32[]{:S(2)}, u32[]{:S(2)}) collective-permute-start(bf16[2048,256]{1,0:T(8,128)(2,1)} %collective-permute-done.refs_4_), channel_id=1, source_target_pairs={{0,32},{1,5},{2,34},{3,7},{4,36},{5,9},{6,38},{7,11},{8,40},{9,13}... | collective-permute-start | bytes 3145736 | tf_op jit(solution)/shard_map/ppermute | solution.py:61
  44.6 33.6 %collective-permute-start.5 = (bf16[2048,256]{1,0:T(8,128)(2,1)}, bf16[2048,256]{1,0:T(8,128)(2,1)}, u32[]{:S(2)}, u32[]{:S(2)}) collective-permute-start(bf16[2048,256]{1,0:T(8,128)(2,1)} %collective-permute-done.refs_4_), channel_id=1, source_target_pairs={{0,64},{1,9},{2,66},{3,11},{4,68},{5,13},{6,70},{7,15},{8,72},{9,1... | collective-permute-start | bytes 3145736 | tf_op jit(solution)/shard_map/ppermute | solution.py:61
  50.4 9.4 %copy-start.7 = (s32[128,3]{0,1:T(4,128)S(1)}, s32[128,3]{0,1:T(4,128)}, u32[]{:S(2)}) copy-start(s32[128,3]{0,1:T(4,128)} %param.14) | copy-start | bytes 4612
  50.5 33.5 %collective-permute-start.4 = (bf16[2048,256]{1,0:T(8,128)(2,1)}, bf16[2048,256]{1,0:T(8,128)(2,1)}, u32[]{:S(2)}, u32[]{:S(2)}) collective-permute-start(bf16[2048,256]{1,0:T(8,128)(2,1)} %collective-permute-done.refs_4_), channel_id=1, source_target_pairs={{0,96},{1,13},{2,98},{3,15},{4,100},{5,1},{6,102},{7,3},{8,104},{9... | collective-permute-start | bytes 3145736 | tf_op jit(solution)/shard_map/ppermute | solution.py:61
  55.5 22.2 %all-to-all-start.1 = ((bf16[4,512,256]{2,1,0:T(8,128)(2,1)}), bf16[4,512,256]{2,1,0:T(8,128)(2,1)}, u32[]{:S(2)}, u32[]{:S(2)}) async-start(bf16[4,512,256]{2,1,0:T(8,128)(2,1)} %bitcast.76), calls=%async_computation.1 | async-start | bytes 2097152 | tf_op jit(solution)/shard_map/all_to_all | solution.py:164
  107.2 20.4 %collective-permute-start.7 = (bf16[2048,256]{1,0:T(8,128)(2,1)}, bf16[2048,256]{1,0:T(8,128)(2,1)}, u32[]{:S(2)}, u32[]{:S(2)}) collective-permute-start(bf16[2048,256]{1,0:T(8,128)(2,1)} %get-tuple-element.21), channel_id=1, source_target_pairs={{0,32},{1,5},{2,34},{3,7},{4,36},{5,9},{6,38},{7,11},{8,40},{9,13}... | collective-permute-start | bytes 3145736 | tf_op jit(solution)/shard_map/ppermute | solution.py:61
  111.0 19.1 %collective-permute-start.8 = (bf16[2048,256]{1,0:T(8,128)(2,1)}, bf16[2048,256]{1,0:T(8,128)(2,1)}, u32[]{:S(2)}, u32[]{:S(2)}) collective-permute-start(bf16[2048,256]{1,0:T(8,128)(2,1)} %get-tuple-element.22), channel_id=1, source_target_pairs={{0,96},{1,13},{2,98},{3,15},{4,100},{5,1},{6,102},{7,3},{8,104},{9... | collective-permute-start | bytes 3145736 | tf_op jit(solution)/shard_map/ppermute | solution.py:61
  113.7 25.5 %collective-permute-start.9 = (bf16[2048,256]{1,0:T(8,128)(2,1)}, bf16[2048,256]{1,0:T(8,128)(2,1)}, u32[]{:S(2)}, u32[]{:S(2)}) collective-permute-start(bf16[2048,256]{1,0:T(8,128)(2,1)} %get-tuple-element.23), channel_id=1, source_target_pairs={{0,64},{1,9},{2,66},{3,11},{4,68},{5,13},{6,70},{7,15},{8,72},{9,1... | collective-permute-start | bytes 3145736 | tf_op jit(solution)/shard_map/ppermute | solution.py:61
  117.0 26.0 %all-to-all-start.2 = ((bf16[4,512,128]{2,1,0:T(8,128)(2,1)}), bf16[4,512,128]{2,1,0:T(8,128)(2,1)}, u32[]{:S(2)}, u32[]{:S(2)}) async-start(bf16[4,512,128]{2,1,0:T(8,128)(2,1)} %bitcast.79), calls=%async_computation.2 | async-start | bytes 1048576 | tf_op jit(solution)/shard_map/all_to_all | solution.py:164
  121.1 29.3 %collective-permute-start.10 = (bf16[2048,256]{1,0:T(8,128)(2,1)}, bf16[2048,256]{1,0:T(8,128)(2,1)}, u32[]{:S(2)}, u32[]{:S(2)}) collective-permute-start(bf16[2048,256]{1,0:T(8,128)(2,1)} %get-tuple-element.27), channel_id=1, source_target_pairs={{0,32},{1,5},{2,34},{3,7},{4,36},{5,9},{6,38},{7,11},{8,40},{9,13}... | collective-permute-start | bytes 3145736 | tf_op jit(solution)/shard_map/ppermute | solution.py:61
  123.2 29.2 %collective-permute-start.11 = (bf16[2048,256]{1,0:T(8,128)(2,1)}, bf16[2048,256]{1,0:T(8,128)(2,1)}, u32[]{:S(2)}, u32[]{:S(2)}) collective-permute-start(bf16[2048,256]{1,0:T(8,128)(2,1)} %get-tuple-element.28), channel_id=1, source_target_pairs={{0,96},{1,13},{2,98},{3,15},{4,100},{5,1},{6,102},{7,3},{8,104},{9... | collective-permute-start | bytes 3145736 | tf_op jit(solution)/shard_map/ppermute | solution.py:61
  127.6 34.1 %collective-permute-start.12 = (bf16[2048,256]{1,0:T(8,128)(2,1)}, bf16[2048,256]{1,0:T(8,128)(2,1)}, u32[]{:S(2)}, u32[]{:S(2)}) collective-permute-start(bf16[2048,256]{1,0:T(8,128)(2,1)} %get-tuple-element.29), channel_id=1, source_target_pairs={{0,64},{1,9},{2,66},{3,11},{4,68},{5,13},{6,70},{7,15},{8,72},{9,1... | collective-permute-start | bytes 3145736 | tf_op jit(solution)/shard_map/ppermute | solution.py:61
  142.9 22.2 %collective-permute-start.13 = (bf16[2048,256]{1,0:T(8,128)(2,1)}, bf16[2048,256]{1,0:T(8,128)(2,1)S(1)}, u32[]{:S(2)}, u32[]{:S(2)}) collective-permute-start(bf16[2048,256]{1,0:T(8,128)(2,1)} %add_convert_fusion.1), channel_id=1, source_target_pairs={{0,16},{1,17},{2,18},{3,19},{4,20},{5,21},{6,22},{7,23},{8,24},{9,... | collective-permute-start | bytes 3145736 | tf_op jit(solution)/shard_map/ppermute | solution.py:61
  169.0 14.0 %all-to-all-start.3 = ((bf16[4,512,256]{2,1,0:T(8,128)(2,1)}), bf16[4,512,256]{2,1,0:T(8,128)(2,1)}, u32[]{:S(2)}, u32[]{:S(2)}) async-start(bf16[4,512,256]{2,1,0:T(8,128)(2,1)} %bitcast.78), calls=%async_computation.3 | async-start | bytes 2097152 | tf_op jit(solution)/shard_map/all_to_all | solution.py:164
  183.1 1.5 copy-start.1
  184.4 1.6 copy-start.3
  184.5 1.5 copy-start.5
  186.0 8.9 %collective-permute-start.15 = (bf16[384,512]{1,0:T(8,128)(2,1)}, bf16[384,512]{1,0:T(8,128)(2,1)}, u32[]{:S(2)}, u32[]{:S(2)}) collective-permute-start(bf16[384,512]{1,0:T(8,128)(2,1)} %fusion.5), channel_id=1, source_target_pairs={{0,1},{1,0},{2,3},{3,2},{4,5},{5,4},{6,7},{7,6},{8,9},{9,8},{10,11... | collective-permute-start | bytes 1179656 | tf_op jit(solution)/shard_map/ppermute | solution.py:61
  192.7 2.2 %copy-start.2 = (bf16[1,512,384]{2,1,0:T(8,128)(2,1)S(1)}, bf16[1,512,384]{2,1,0:T(8,128)(2,1)}, u32[]{:S(2)}) copy-start(bf16[1,512,384]{2,1,0:T(8,128)(2,1)} %maximum_bitcast_fusion) | copy-start | bytes 1179652
  192.7 2.2 %copy-start.4 = (bf16[1,512,384]{2,1,0:T(8,128)(2,1)S(1)}, bf16[1,512,384]{2,1,0:T(8,128)(2,1)}, u32[]{:S(2)}) copy-start(bf16[1,512,384]{2,1,0:T(8,128)(2,1)} %copy-done.3) | copy-start | bytes 1179652
  192.7 2.2 %copy-start.6 = (bf16[1,512,384]{2,1,0:T(8,128)(2,1)S(1)}, bf16[1,512,384]{2,1,0:T(8,128)(2,1)}, u32[]{:S(2)}) copy-start(bf16[1,512,384]{2,1,0:T(8,128)(2,1)} %copy-done.5) | copy-start | bytes 1179652
  194.7 5.3 %collective-permute-start.14 = (bf16[384,512]{1,0:T(8,128)(2,1)S(1)}, bf16[384,512]{1,0:T(8,128)(2,1)S(1)}, u32[]{:S(2)}, u32[]{:S(2)}) collective-permute-start(bf16[384,512]{1,0:T(8,128)(2,1)S(1)} %fusion.2), channel_id=1, source_target_pairs={{0,1},{1,0},{2,3},{3,2},{4,5},{5,4},{6,7},{7,6},{8,9},{9,8},{10,11... | collective-permute-start | bytes 1179656 | tf_op jit(solution)/shard_map/ppermute | solution.py:61
  196.6 11.8 %collective-permute-start.16 = (bf16[384,512]{1,0:T(8,128)(2,1)S(1)}, bf16[384,512]{1,0:T(8,128)(2,1)S(1)}, u32[]{:S(2)}, u32[]{:S(2)}) collective-permute-start(bf16[384,512]{1,0:T(8,128)(2,1)S(1)} %add_convert_fusion.3), channel_id=1, source_target_pairs={{0,2},{1,3},{2,0},{3,1},{4,6},{5,7},{6,4},{7,5},{8,10},{9,11},{10,... | collective-permute-start | bytes 1179656 | tf_op jit(solution)/shard_map/ppermute | solution.py:61

commit v4 on v3

--- a/solution.py
+++ b/solution.py
@@ -172,14 +172,6 @@
     return exchange(jnp.concatenate(heads, axis=0))
 
 
-def ring_gather(shard):
-    return [shard] + [send(shard, RING[k]) for k in (3, 2, 1)]
-
-
-def ring_sends(parts):
-    return [parts[0]] + [send(parts[k], RING[k]) for k in (1, 3, 2)]
-
-
 def body(queries, keys, values, upstream_out, out_weight, qkv_weight, rand_links, global_links):
     s = lax.axis_index("seq")
     h = lax.axis_index("head")
@@ -206,39 +198,41 @@
 
     own = deal(keys, values)
     other = send(own, PAIR)
-    own_row = ring_gather(own)
+    next_, last = send(own, RING[3]), send(own, RING[1])
+    across = send(own, RING[2])
     grad_ctx = lax.dot_general(
         upstream_out, out_weight, (((1,), (1,)), ((), ())), preferred_element_type=F32
     ).astype(BF16)
     grad_ctx, other = lax.optimization_barrier((grad_ctx, other))
     qd = deal(queries, grad_ctx)
-    grad_q, parts = attend(table, qd, own_row + ring_gather(other))
-
-    other_sum = add(*ring_sends(parts[4:]))
-    own_sum = ring_sends(parts[:4])
+    other_row = [other, send(other, RING[3]), send(across, PAIR), send(other, RING[1])]
+    grad_q, parts = attend(table, qd, [own, next_, across, last] + other_row)
+
+    corner = send(parts[6], PAIR)
+    other_sum = add(parts[4], send(parts[5], RING[1]), send(parts[7], RING[3]))
     q_back = exchange(grad_q)
-    other_sum, q_back = lax.optimization_barrier((other_sum, q_back))
-    kv_back = exchange(add(*own_sum, send(other_sum, PAIR)))
+    sides = [send(parts[1], RING[1]), send(parts[3], RING[3])]
+    other_sum = send(other_sum, PAIR)
+    across = send(add(parts[2], corner), RING[2])
+    kv_back = exchange(add(parts[0], *sides, across, other_sum))
 
     def tokens(back, lanes):
         back = back.reshape(LINE, BLK_DEV * BLK, -1)
         return jnp.concatenate([back[p, :, lanes] for p in range(3)], axis=1)
 
-    grads = jnp.stack(
-        [
-            tokens(q_back, slice(0, HD)),
-            tokens(kv_back, slice(0, HD)),
-            tokens(kv_back, slice(HD, 2 * HD)),
-        ],
-        axis=0,
-    )
+    grads = [
+        tokens(q_back, slice(0, HD)),
+        tokens(kv_back, slice(0, HD)),
+        tokens(kv_back, slice(HD, 2 * HD)),
+    ]
     weight = qkv_weight.reshape(3, 2, 2, qkv_weight.shape[1] // 4, qkv_weight.shape[2])
 
     def share(to_far, to_core):
         w = lax.dynamic_index_in_dim(weight, to_far, 1, keepdims=False)
         w = lax.dynamic_index_in_dim(w, to_core, 1, keepdims=False)
-        return lax.dot_general(
-            w, grads, (((0, 2), (0, 2)), ((), ())), preferred_element_type=F32
+        return sum(
+            lax.dot_general(w[j], g, (((1,), (1,)), ((), ())), preferred_element_type=F32)
+            for j, g in enumerate(grads)
         ).astype(BF16)
 
     from_far = send(add(share(1 - far, core), send(share(1 - far, 1 - core), CORE)), FAR)

time: 210 us -> 193 us (0.919)
  waiting for transfers between devices: 73.5 us -> 56.5 us
  starting transfers between devices: 71.1 us -> 68.6 us
  matrix products: 8.66 us -> 11.1 us
    all_to_all x3, waiting for transfers between devices: 24.2 us -> 15.5 us  [exchange(): return lax.all_to_all(x, AXES, 0, 0, axis_index_groups=LINES, tiled=True)]
    ppermute x17, waiting for transfers between devices: 49.3 us -> 40.9 us  [send(): return lax.ppermute(x, AXES, perm)]
    dot_general x4 -> x12, matrix products: 5.93 us -> 8.38 us  [share(): lax.dot_general(w[j], g, (((1,), (1,)), ((), ())), preferred_element_type...]
    ppermute x17, starting transfers between devices: 58.4 us -> 56 us  [send(): return lax.ppermute(x, AXES, perm)]
    convert_element_type x3 -> x4, other arithmetic: 8.46 us -> 9.22 us  [add(): functools.reduce(lambda a, b: a + b, [t.astype(F32) for t in terms])]
  transfers between devices with their start and end apart: 20 -> 20, of which waited for: 11 -> 9; matrix products, arithmetic and copies ran while one was open for 8% -> 12% of each run, Pallas kernels for 0% -> 0%
where the time goes in v4:
time: 193 us; the launch traced here: 192 us
  starting transfers between devices  68.6 us (36%)
  waiting for transfers between devices  56.5 us (29%)
  Pallas kernels  23.3 us (12%)
  blocking collectives  14.8 us (8%)
  other arithmetic  11.4 us (6%)
  matrix products  11.1 us (6%)
  local copies, waits for them, and re-layouts  5.89 us (3%)
    ppermute x17, starting transfers between devices, send(): return lax.ppermute(x, AXES, perm)  56 us
    ppermute x17, waiting for transfers between devices, send(): return lax.ppermute(x, AXES, perm)  40.9 us
    pallas_call x1, Pallas kernels, attend(): pl.pallas_call(attend_kernel, name='attend', out_shape=(jax.ShapeDtypeStr...  23.3 us
    all_to_all x3, waiting for transfers between devices, exchange(): return lax.all_to_all(x, AXES, 0, 0, axis_index_groups=LINES, tiled=True)  15.5 us
    all_to_all x1, blocking collectives, exchange(): return lax.all_to_all(x, AXES, 0, 0, axis_index_groups=LINES, tiled=True)  14.8 us
    all_to_all x3, starting transfers between devices, exchange(): return lax.all_to_all(x, AXES, 0, 0, axis_index_groups=LINES, tiled=True)  12.6 us
    convert_element_type x4, other arithmetic, add(): functools.reduce(lambda a, b: a + b, [t.astype(F32) for t in terms])  9.22 us
    dot_general x12, matrix products, share(): lax.dot_general(w[j], g, (((1,), (1,)), ((), ())), preferred_element_type...  8.38 us
  transfers between devices with their start and end apart: 20, of which 9 were waited for; matrix products, arithmetic and copies ran while one was open for 12% of the time, Pallas kernels for 0%

profile of v4, /device:TPU:1, one launch (start us, length us, event | category | flops | bytes accessed | tf_op | source)
XLA Modules:
  0.0 192.0 jit_solution(558248771030493495)
XLA Ops:
  0.0 1.4 fusion.39
  1.5 14.8 %all_to_all.40 = bf16[4,512,256]{2,1,0:T(8,128)(2,1)} all-to-all(bf16[4,512,256]{2,1,0:T(8,128)(2,1)S(1)} %bitcast.78), channel_id=1, replica_groups={{0,4,8,12},{1,33,65,97},{2,6,10,14},{3,35,67,99},{5,37,69,101},{7,39,71..., dimensions={0} | all-to-all | bytes 2097152 | tf_op jit(solution)/shard_map/all_to_all | solution.py:164
  16.3 3.2 %collective-permute-start = (bf16[2048,256]{1,0:T(8,128)(2,1)}, bf16[2048,256]{1,0:T(8,128)(2,1)}, u32[]{:S(2)}, u32[]{:S(2)}) collective-permute-start(bf16[2048,256]{1,0:T(8,128)(2,1)} %bitcast.3.refs_0_), channel_id=1, source_target_pairs={{0,16},{1,17},{2,18},{3,19},{4,20},{5,21},{6,22},{7,23},{8,24},{9,... | collective-permute-start | bytes 3145736 | tf_op jit(solution)/shard_map/ppermute | solution.py:61
  19.5 5.2 %collective-permute-start.2 = (bf16[2048,256]{1,0:T(8,128)(2,1)}, bf16[2048,256]{1,0:T(8,128)(2,1)}, u32[]{:S(2)}, u32[]{:S(2)}) collective-permute-start(bf16[2048,256]{1,0:T(8,128)(2,1)} %bitcast.3.refs_0_), channel_id=1, source_target_pairs={{0,64},{1,9},{2,66},{3,11},{4,68},{5,13},{6,70},{7,15},{8,72},{9,1... | collective-permute-start | bytes 3145736 | tf_op jit(solution)/shard_map/ppermute | solution.py:61
  24.8 1.1 fusion.37
  25.9 2.7 %convolution_convert_fusion = bf16[512,384]{1,0:T(8,128)(2,1)S(1)} fusion(bf16[512,1536]{1,0:T(8,128)(2,1)} %param.11, bf16[384,1536]{1,0:T(8,128)(2,1)} %param.12), kind=kOutput, calls=%fused_computation.17 | convolution fusion | flops 604176384 | bytes 3145728 | tf_op jit(solution)/shard_map/dot_general | solution.py:203
  28.6 2.3 %collective-permute-start.1 = (bf16[2048,256]{1,0:T(8,128)(2,1)}, bf16[2048,256]{1,0:T(8,128)(2,1)}, u32[]{:S(2)}, u32[]{:S(2)}) collective-permute-start(bf16[2048,256]{1,0:T(8,128)(2,1)} %bitcast.3.refs_0_), channel_id=1, source_target_pairs={{0,96},{1,13},{2,98},{3,15},{4,100},{5,1},{6,102},{7,3},{8,104},{9... | collective-permute-start | bytes 3145736 | tf_op jit(solution)/shard_map/ppermute | solution.py:61
  31.0 2.9 %collective-permute-start.3 = (bf16[2048,256]{1,0:T(8,128)(2,1)}, bf16[2048,256]{1,0:T(8,128)(2,1)}, u32[]{:S(2)}, u32[]{:S(2)}) collective-permute-start(bf16[2048,256]{1,0:T(8,128)(2,1)} %bitcast.3.refs_0_), channel_id=1, source_target_pairs={{0,32},{1,5},{2,34},{3,7},{4,36},{5,9},{6,38},{7,11},{8,40},{9,13}... | collective-permute-start | bytes 3145736 | tf_op jit(solution)/shard_map/ppermute | solution.py:61
  33.9 6.4 %collective-permute-done.refs_4_ = bf16[2048,256]{1,0:T(8,128)(2,1)} collective-permute-done((bf16[2048,256]{1,0:T(8,128)(2,1)}, bf16[2048,256]{1,0:T(8,128)(2,1)}, u32[]{:S(2)}, u32[]{:S(2)}) %collective-permute-start) | collective-permute-done | bytes 1048608 | tf_op jit(solution)/shard_map/ppermute | solution.py:61
  40.3 1.9 collective-permute-start.4
  42.2 4.3 %collective-permute-start.6 = (bf16[2048,256]{1,0:T(8,128)(2,1)}, bf16[2048,256]{1,0:T(8,128)(2,1)}, u32[]{:S(2)}, u32[]{:S(2)}) collective-permute-start(bf16[2048,256]{1,0:T(8,128)(2,1)} %collective-permute-done.refs_4_), channel_id=1, source_target_pairs={{0,32},{1,5},{2,34},{3,7},{4,36},{5,9},{6,38},{7,11},{8,40},{9,13}... | collective-permute-start | bytes 3145736 | tf_op jit(solution)/shard_map/ppermute | solution.py:61
  46.7 3.2 %collective-permute-start.5 = (bf16[2048,256]{1,0:T(8,128)(2,1)}, bf16[2048,256]{1,0:T(8,128)(2,1)}, u32[]{:S(2)}, u32[]{:S(2)}) collective-permute-start(bf16[2048,256]{1,0:T(8,128)(2,1)} %collective-permute-done.2.refs_2_), channel_id=1, source_target_pairs={{0,16},{1,17},{2,18},{3,19},{4,20},{5,21},{6,22},{7,23},{8,24},{9,... | collective-permute-start | bytes 3145736 | tf_op jit(solution)/shard_map/ppermute | solution.py:61
  49.9 1.1 maximum_maximum_fusion.1
  51.0 4.2 %all-to-all-start.1 = ((bf16[4,512,256]{2,1,0:T(8,128)(2,1)}), bf16[4,512,256]{2,1,0:T(8,128)(2,1)}, u32[]{:S(2)}, u32[]{:S(2)}) async-start(bf16[4,512,256]{2,1,0:T(8,128)(2,1)} %bitcast.77), calls=%async_computation.1 | async-start | bytes 2097152 | tf_op jit(solution)/shard_map/all_to_all | solution.py:164
  55.5 0.7 pad.27.clone
  56.3 0.7 fusion.18.table
  57.1 12.0 %all-to-all-done.1 = bf16[4,512,256]{2,1,0:T(8,128)(2,1)} async-done(((bf16[4,512,256]{2,1,0:T(8,128)(2,1)}), bf16[4,512,256]{2,1,0:T(8,128)(2,1)}, u32[]{:S(2)}, u32[]{:S(2)}) %all-to-all-start.1) | async-done | bytes 1048608 | tf_op jit(solution)/shard_map/all_to_all | solution.py:164
  69.1 1.1 collective-permute-done.5.refs_6_
  70.2 23.3 %attend.1 = (bf16[2048,128]{1,0:T(8,128)(2,1)}, bf16[2048,256]{1,0:T(8,128)(2,1)}, bf16[2048,256]{1,0:T(8,128)(2,1)}, bf16[2048,256]{1,0:T(8,128)(2,1)}, bf16[20...) custom-call(s32[16,8]{1,0:T(8,128)} %fusion.18.table, ...), custom_call_target="tpu_custom_call" | custom-call | tf_op jit(solution)/shard_map/attend/pallas_call | solution.py:136
  93.4 1.9 collective-permute-start.12
  95.4 7.5 %collective-permute-start.11 = (bf16[2048,256]{1,0:T(8,128)(2,1)}, bf16[2048,256]{1,0:T(8,128)(2,1)S(1)}, u32[]{:S(2)}, u32[]{:S(2)}) collective-permute-start(bf16[2048,256]{1,0:T(8,128)(2,1)} %get-tuple-element.25), channel_id=1, source_target_pairs={{0,32},{1,5},{2,34},{3,7},{4,36},{5,9},{6,38},{7,11},{8,40},{9,13}... | collective-permute-start | bytes 3145736 | tf_op jit(solution)/shard_map/ppermute | solution.py:61
  102.9 3.2 %collective-permute-start.9 = (bf16[2048,256]{1,0:T(8,128)(2,1)}, bf16[2048,256]{1,0:T(8,128)(2,1)S(1)}, u32[]{:S(2)}, u32[]{:S(2)}) collective-permute-start(bf16[2048,256]{1,0:T(8,128)(2,1)} %get-tuple-element.23), channel_id=1, source_target_pairs={{0,16},{1,17},{2,18},{3,19},{4,20},{5,21},{6,22},{7,23},{8,24},{9,... | collective-permute-start | bytes 3145736 | tf_op jit(solution)/shard_map/ppermute | solution.py:61
  106.1 3.8 %collective-permute-start.8 = (bf16[2048,256]{1,0:T(8,128)(2,1)}, bf16[2048,256]{1,0:T(8,128)(2,1)}, u32[]{:S(2)}, u32[]{:S(2)}) collective-permute-start(bf16[2048,256]{1,0:T(8,128)(2,1)} %get-tuple-element.21), channel_id=1, source_target_pairs={{0,96},{1,13},{2,98},{3,15},{4,100},{5,1},{6,102},{7,3},{8,104},{9... | collective-permute-start | bytes 3145736 | tf_op jit(solution)/shard_map/ppermute | solution.py:61
  109.9 1.9 %collective-permute-start.7 = (bf16[2048,256]{1,0:T(8,128)(2,1)}, bf16[2048,256]{1,0:T(8,128)(2,1)}, u32[]{:S(2)}, u32[]{:S(2)}) collective-permute-start(bf16[2048,256]{1,0:T(8,128)(2,1)} %get-tuple-element.20), channel_id=1, source_target_pairs={{0,32},{1,5},{2,34},{3,7},{4,36},{5,9},{6,38},{7,11},{8,40},{9,13}... | collective-permute-start | bytes 3145736 | tf_op jit(solution)/shard_map/ppermute | solution.py:61
  111.8 1.8 collective-permute-done.12
  113.6 3.9 %collective-permute-done.11 = bf16[2048,256]{1,0:T(8,128)(2,1)S(1)} collective-permute-done((bf16[2048,256]{1,0:T(8,128)(2,1)}, bf16[2048,256]{1,0:T(8,128)(2,1)S(1)}, u32[]{:S(2)}, u32[]{:S(2)}) %collective-permute-start.11) | collective-permute-done | bytes 1048608 | tf_op jit(solution)/shard_map/ppermute | solution.py:61
  117.5 2.9 %add_convert_fusion.1 = bf16[2048,256]{1,0:T(8,128)(2,1)} fusion(bf16[2048,256]{1,0:T(8,128)(2,1)S(1)} %collective-permute-done.12, bf16[2048,256]{1,0:T(8,128)(2,1)S(1)} %collective-permute-done.11, bf16[2048,256]{1,0:T(8,128)(2,1)} %get-tuple-element.24), kind=kLoop, calls=%fused_computation.1 | loop fusion | flops 3145728 | bytes 4194304 | tf_op jit(solution)/shard_map/convert_element_type | solution.py:160
  120.4 3.2 %collective-permute-start.13 = (bf16[2048,256]{1,0:T(8,128)(2,1)}, bf16[2048,256]{1,0:T(8,128)(2,1)}, u32[]{:S(2)}, u32[]{:S(2)}) collective-permute-start(bf16[2048,256]{1,0:T(8,128)(2,1)} %add_convert_fusion.1), channel_id=1, source_target_pairs={{0,16},{1,17},{2,18},{3,19},{4,20},{5,21},{6,22},{7,23},{8,24},{9,... | collective-permute-start | bytes 3145736 | tf_op jit(solution)/shard_map/ppermute | solution.py:61
  123.6 5.4 %collective-permute-done.9 = bf16[2048,256]{1,0:T(8,128)(2,1)S(1)} collective-permute-done((bf16[2048,256]{1,0:T(8,128)(2,1)}, bf16[2048,256]{1,0:T(8,128)(2,1)S(1)}, u32[]{:S(2)}, u32[]{:S(2)}) %collective-permute-start.9) | collective-permute-done | bytes 1048608 | tf_op jit(solution)/shard_map/ppermute | solution.py:61
  129.0 1.4 add_convert_fusion.2
  130.4 2.8 %collective-permute-start.10 = (bf16[2048,256]{1,0:T(8,128)(2,1)}, bf16[2048,256]{1,0:T(8,128)(2,1)}, u32[]{:S(2)}, u32[]{:S(2)}) collective-permute-start(bf16[2048,256]{1,0:T(8,128)(2,1)} %add_convert_fusion.2), channel_id=1, source_target_pairs={{0,64},{1,9},{2,66},{3,11},{4,68},{5,13},{6,70},{7,15},{8,72},{9,1... | collective-permute-start | bytes 3145736 | tf_op jit(solution)/shard_map/ppermute | solution.py:61
  133.2 4.1 %all-to-all-start.2 = ((bf16[4,512,128]{2,1,0:T(8,128)(2,1)}), bf16[4,512,128]{2,1,0:T(8,128)(2,1)}, u32[]{:S(2)}, u32[]{:S(2)}) async-start(bf16[4,512,128]{2,1,0:T(8,128)(2,1)} %bitcast.80), calls=%async_computation.2 | async-start | bytes 1048576 | tf_op jit(solution)/shard_map/all_to_all | solution.py:164
  137.4 14.2 %collective-permute-done.13 = bf16[2048,256]{1,0:T(8,128)(2,1)} collective-permute-done((bf16[2048,256]{1,0:T(8,128)(2,1)}, bf16[2048,256]{1,0:T(8,128)(2,1)}, u32[]{:S(2)}, u32[]{:S(2)}) %collective-permute-start.13) | collective-permute-done | bytes 1048608 | tf_op jit(solution)/shard_map/ppermute | solution.py:61
  151.6 4.1 %add_convert_fusion = bf16[2048,256]{1,0:T(8,128)(2,1)} fusion(bf16[2048,256]{1,0:T(8,128)(2,1)} %collective-permute-done.13, bf16[2048,256]{1,0:T(8,128)(2,1)} %collective-permute-done.10, bf16[2048,256]{1,0:T(8,128)(2,1)} %collective-permute-done.8, bf16[2048,256]{1,0:T(8,128)(2,1)} %collective-permute-done.7, bf16[2048,256]{1,0:T(8,128)(2,1)} %get-tuple-element.19), kind=kLoop, calls=%fused_computation | loop fusion | flops 5242880 | bytes 6291456 | tf_op jit(solution)/shard_map/convert_element_type | solution.py:160
  155.7 4.2 %all-to-all-start.3 = ((bf16[4,512,256]{2,1,0:T(8,128)(2,1)}), bf16[4,512,256]{2,1,0:T(8,128)(2,1)}, u32[]{:S(2)}, u32[]{:S(2)}) async-start(bf16[4,512,256]{2,1,0:T(8,128)(2,1)} %bitcast.79), calls=%async_computation.3 | async-start | bytes 2097152 | tf_op jit(solution)/shard_map/all_to_all | solution.py:164
  160.0 1.1 slice_bitcast_fusion.8
  161.1 1.3 fusion.6
  162.4 1.3 fusion.7
  163.6 1.3 fusion.9
  164.9 1.3 fusion.8
  166.2 3.5 %all-to-all-done.3 = bf16[4,512,256]{2,1,0:T(8,128)(2,1)} async-done(((bf16[4,512,256]{2,1,0:T(8,128)(2,1)}), bf16[4,512,256]{2,1,0:T(8,128)(2,1)}, u32[]{:S(2)}, u32[]{:S(2)}) %all-to-all-start.3) | async-done | bytes 1048608 | tf_op jit(solution)/shard_map/all_to_all | solution.py:164
  169.7 1.3 slice_bitcast_fusion.2
  171.6 0.4 fusion.5
  172.0 5.3 %collective-permute-start.15 = (bf16[384,512]{1,0:T(8,128)(2,1)S(1)}, bf16[384,512]{1,0:T(8,128)(2,1)S(1)}, u32[]{:S(2)}, u32[]{:S(2)}) collective-permute-start(bf16[384,512]{1,0:T(8,128)(2,1)S(1)} %fusion.5), channel_id=1, source_target_pairs={{0,1},{1,0},{2,3},{3,2},{4,5},{5,4},{6,7},{7,6},{8,9},{9,8},{10,11... | collective-permute-start | bytes 1179656 | tf_op jit(solution)/shard_map/ppermute | solution.py:61
  178.8 0.4 add_convert_fusion.4
  179.2 3.0 %collective-permute-start.16 = (bf16[384,512]{1,0:T(8,128)(2,1)S(1)}, bf16[384,512]{1,0:T(8,128)(2,1)S(1)}, u32[]{:S(2)}, u32[]{:S(2)}) collective-permute-start(bf16[384,512]{1,0:T(8,128)(2,1)S(1)} %add_convert_fusion.4), channel_id=1, source_target_pairs={{0,2},{1,3},{2,0},{3,1},{4,6},{5,7},{6,4},{7,5},{8,10},{9,11},{10,... | collective-permute-start | bytes 1179656 | tf_op jit(solution)/shard_map/ppermute | solution.py:61
  183.0 8.1 %collective-permute-done.16 = bf16[384,512]{1,0:T(8,128)(2,1)S(1)} collective-permute-done((bf16[384,512]{1,0:T(8,128)(2,1)S(1)}, bf16[384,512]{1,0:T(8,128)(2,1)S(1)}, u32[]{:S(2)}, u32[]{:S(2)}) %collective-permute-start.16) | collective-permute-done | bytes 393248 | tf_op jit(solution)/shard_map/ppermute | solution.py:61
  191.1 0.9 add_convert_fusion.3
  (40 shorter events, 3.3 us)
Async XLA Ops:
  0.0 161.1 %copy-start = (bf16[3,1536,384]{2,1,0:T(8,128)(2,1)S(1)}, bf16[3,1536,384]{2,1,0:T(8,128)(2,1)}, u32[]{:S(2)}) copy-start(bf16[3,1536,384]{2,1,0:T(8,128)(2,1)} %param.13) | copy-start | bytes 10616836
  16.3 24.0 %collective-permute-start = (bf16[2048,256]{1,0:T(8,128)(2,1)}, bf16[2048,256]{1,0:T(8,128)(2,1)}, u32[]{:S(2)}, u32[]{:S(2)}) collective-permute-start(bf16[2048,256]{1,0:T(8,128)(2,1)} %bitcast.3.refs_0_), channel_id=1, source_target_pairs={{0,16},{1,17},{2,18},{3,19},{4,20},{5,21},{6,22},{7,23},{8,24},{9,... | collective-permute-start | bytes 3145736 | tf_op jit(solution)/shard_map/ppermute | solution.py:61
  19.5 27.2 %collective-permute-start.2 = (bf16[2048,256]{1,0:T(8,128)(2,1)}, bf16[2048,256]{1,0:T(8,128)(2,1)}, u32[]{:S(2)}, u32[]{:S(2)}) collective-permute-start(bf16[2048,256]{1,0:T(8,128)(2,1)} %bitcast.3.refs_0_), channel_id=1, source_target_pairs={{0,64},{1,9},{2,66},{3,11},{4,68},{5,13},{6,70},{7,15},{8,72},{9,1... | collective-permute-start | bytes 3145736 | tf_op jit(solution)/shard_map/ppermute | solution.py:61
  28.6 28.5 %collective-permute-start.1 = (bf16[2048,256]{1,0:T(8,128)(2,1)}, bf16[2048,256]{1,0:T(8,128)(2,1)}, u32[]{:S(2)}, u32[]{:S(2)}) collective-permute-start(bf16[2048,256]{1,0:T(8,128)(2,1)} %bitcast.3.refs_0_), channel_id=1, source_target_pairs={{0,96},{1,13},{2,98},{3,15},{4,100},{5,1},{6,102},{7,3},{8,104},{9... | collective-permute-start | bytes 3145736 | tf_op jit(solution)/shard_map/ppermute | solution.py:61
  31.0 26.1 %collective-permute-start.3 = (bf16[2048,256]{1,0:T(8,128)(2,1)}, bf16[2048,256]{1,0:T(8,128)(2,1)}, u32[]{:S(2)}, u32[]{:S(2)}) collective-permute-start(bf16[2048,256]{1,0:T(8,128)(2,1)} %bitcast.3.refs_0_), channel_id=1, source_target_pairs={{0,32},{1,5},{2,34},{3,7},{4,36},{5,9},{6,38},{7,11},{8,40},{9,13}... | collective-permute-start | bytes 3145736 | tf_op jit(solution)/shard_map/ppermute | solution.py:61
  40.3 28.8 %collective-permute-start.4 = (bf16[2048,256]{1,0:T(8,128)(2,1)}, bf16[2048,256]{1,0:T(8,128)(2,1)}, u32[]{:S(2)}, u32[]{:S(2)}) collective-permute-start(bf16[2048,256]{1,0:T(8,128)(2,1)} %collective-permute-done.refs_4_), channel_id=1, source_target_pairs={{0,96},{1,13},{2,98},{3,15},{4,100},{5,1},{6,102},{7,3},{8,104},{9... | collective-permute-start | bytes 3145736 | tf_op jit(solution)/shard_map/ppermute | solution.py:61
  42.2 27.9 %collective-permute-start.6 = (bf16[2048,256]{1,0:T(8,128)(2,1)}, bf16[2048,256]{1,0:T(8,128)(2,1)}, u32[]{:S(2)}, u32[]{:S(2)}) collective-permute-start(bf16[2048,256]{1,0:T(8,128)(2,1)} %collective-permute-done.refs_4_), channel_id=1, source_target_pairs={{0,32},{1,5},{2,34},{3,7},{4,36},{5,9},{6,38},{7,11},{8,40},{9,13}... | collective-permute-start | bytes 3145736 | tf_op jit(solution)/shard_map/ppermute | solution.py:61
  46.6 8.6 %copy-start.6 = (s32[128,3]{0,1:T(4,128)S(1)}, s32[128,3]{0,1:T(4,128)}, u32[]{:S(2)}) copy-start(s32[128,3]{0,1:T(4,128)} %param.14) | copy-start | bytes 4612
  46.7 23.5 %collective-permute-start.5 = (bf16[2048,256]{1,0:T(8,128)(2,1)}, bf16[2048,256]{1,0:T(8,128)(2,1)}, u32[]{:S(2)}, u32[]{:S(2)}) collective-permute-start(bf16[2048,256]{1,0:T(8,128)(2,1)} %collective-permute-done.2.refs_2_), channel_id=1, source_target_pairs={{0,16},{1,17},{2,18},{3,19},{4,20},{5,21},{6,22},{7,23},{8,24},{9,... | collective-permute-start | bytes 3145736 | tf_op jit(solution)/shard_map/ppermute | solution.py:61
  51.0 18.1 %all-to-all-start.1 = ((bf16[4,512,256]{2,1,0:T(8,128)(2,1)}), bf16[4,512,256]{2,1,0:T(8,128)(2,1)}, u32[]{:S(2)}, u32[]{:S(2)}) async-start(bf16[4,512,256]{2,1,0:T(8,128)(2,1)} %bitcast.77), calls=%async_computation.1 | async-start | bytes 2097152 | tf_op jit(solution)/shard_map/all_to_all | solution.py:164
  93.4 20.2 %collective-permute-start.12 = (bf16[2048,256]{1,0:T(8,128)(2,1)}, bf16[2048,256]{1,0:T(8,128)(2,1)S(1)}, u32[]{:S(2)}, u32[]{:S(2)}) collective-permute-start(bf16[2048,256]{1,0:T(8,128)(2,1)} %get-tuple-element.26), channel_id=1, source_target_pairs={{0,96},{1,13},{2,98},{3,15},{4,100},{5,1},{6,102},{7,3},{8,104},{9... | collective-permute-start | bytes 3145736 | tf_op jit(solution)/shard_map/ppermute | solution.py:61
  95.4 22.2 %collective-permute-start.11 = (bf16[2048,256]{1,0:T(8,128)(2,1)}, bf16[2048,256]{1,0:T(8,128)(2,1)S(1)}, u32[]{:S(2)}, u32[]{:S(2)}) collective-permute-start(bf16[2048,256]{1,0:T(8,128)(2,1)} %get-tuple-element.25), channel_id=1, source_target_pairs={{0,32},{1,5},{2,34},{3,7},{4,36},{5,9},{6,38},{7,11},{8,40},{9,13}... | collective-permute-start | bytes 3145736 | tf_op jit(solution)/shard_map/ppermute | solution.py:61
  102.9 26.1 %collective-permute-start.9 = (bf16[2048,256]{1,0:T(8,128)(2,1)}, bf16[2048,256]{1,0:T(8,128)(2,1)S(1)}, u32[]{:S(2)}, u32[]{:S(2)}) collective-permute-start(bf16[2048,256]{1,0:T(8,128)(2,1)} %get-tuple-element.23), channel_id=1, source_target_pairs={{0,16},{1,17},{2,18},{3,19},{4,20},{5,21},{6,22},{7,23},{8,24},{9,... | collective-permute-start | bytes 3145736 | tf_op jit(solution)/shard_map/ppermute | solution.py:61
  106.1 31.2 %collective-permute-start.8 = (bf16[2048,256]{1,0:T(8,128)(2,1)}, bf16[2048,256]{1,0:T(8,128)(2,1)}, u32[]{:S(2)}, u32[]{:S(2)}) collective-permute-start(bf16[2048,256]{1,0:T(8,128)(2,1)} %get-tuple-element.21), channel_id=1, source_target_pairs={{0,96},{1,13},{2,98},{3,15},{4,100},{5,1},{6,102},{7,3},{8,104},{9... | collective-permute-start | bytes 3145736 | tf_op jit(solution)/shard_map/ppermute | solution.py:61
  109.9 27.5 %collective-permute-start.7 = (bf16[2048,256]{1,0:T(8,128)(2,1)}, bf16[2048,256]{1,0:T(8,128)(2,1)}, u32[]{:S(2)}, u32[]{:S(2)}) collective-permute-start(bf16[2048,256]{1,0:T(8,128)(2,1)} %get-tuple-element.20), channel_id=1, source_target_pairs={{0,32},{1,5},{2,34},{3,7},{4,36},{5,9},{6,38},{7,11},{8,40},{9,13}... | collective-permute-start | bytes 3145736 | tf_op jit(solution)/shard_map/ppermute | solution.py:61
  117.5 11.5 %copy-start.1 = (bf16[2048,256]{1,0:T(8,128)(2,1)S(1)}, bf16[2048,256]{1,0:T(8,128)(2,1)}, u32[]{:S(2)}) copy-start(bf16[2048,256]{1,0:T(8,128)(2,1)} %get-tuple-element.22) | copy-start | bytes 3145732
  120.4 31.2 %collective-permute-start.13 = (bf16[2048,256]{1,0:T(8,128)(2,1)}, bf16[2048,256]{1,0:T(8,128)(2,1)}, u32[]{:S(2)}, u32[]{:S(2)}) collective-permute-start(bf16[2048,256]{1,0:T(8,128)(2,1)} %add_convert_fusion.1), channel_id=1, source_target_pairs={{0,16},{1,17},{2,18},{3,19},{4,20},{5,21},{6,22},{7,23},{8,24},{9,... | collective-permute-start | bytes 3145736 | tf_op jit(solution)/shard_map/ppermute | solution.py:61
  130.4 21.2 %collective-permute-start.10 = (bf16[2048,256]{1,0:T(8,128)(2,1)}, bf16[2048,256]{1,0:T(8,128)(2,1)}, u32[]{:S(2)}, u32[]{:S(2)}) collective-permute-start(bf16[2048,256]{1,0:T(8,128)(2,1)} %add_convert_fusion.2), channel_id=1, source_target_pairs={{0,64},{1,9},{2,66},{3,11},{4,68},{5,13},{6,70},{7,15},{8,72},{9,1... | collective-permute-start | bytes 3145736 | tf_op jit(solution)/shard_map/ppermute | solution.py:61
  133.2 22.5 %all-to-all-start.2 = ((bf16[4,512,128]{2,1,0:T(8,128)(2,1)}), bf16[4,512,128]{2,1,0:T(8,128)(2,1)}, u32[]{:S(2)}, u32[]{:S(2)}) async-start(bf16[4,512,128]{2,1,0:T(8,128)(2,1)} %bitcast.80), calls=%async_computation.2 | async-start | bytes 1048576 | tf_op jit(solution)/shard_map/all_to_all | solution.py:164
  155.7 14.0 %all-to-all-start.3 = ((bf16[4,512,256]{2,1,0:T(8,128)(2,1)}), bf16[4,512,256]{2,1,0:T(8,128)(2,1)}, u32[]{:S(2)}, u32[]{:S(2)}) async-start(bf16[4,512,256]{2,1,0:T(8,128)(2,1)} %bitcast.79), calls=%async_computation.3 | async-start | bytes 2097152 | tf_op jit(solution)/shard_map/all_to_all | solution.py:164
  169.7 1.5 copy-start.5
  171.1 6.3 %copy-start.4 = (f32[384,512]{1,0:T(8,128)S(1)}, f32[384,512]{1,0:T(8,128)}, u32[]{:S(2)}) copy-start(f32[384,512]{1,0:T(8,128)} %fusion.8) | copy-start | bytes 2359300
  172.0 6.4 %copy-start.3 = (f32[384,512]{1,0:T(8,128)S(1)}, f32[384,512]{1,0:T(8,128)}, u32[]{:S(2)}) copy-start(f32[384,512]{1,0:T(8,128)} %fusion.7) | copy-start | bytes 2359300
  172.0 6.8 %collective-permute-start.15 = (bf16[384,512]{1,0:T(8,128)(2,1)S(1)}, bf16[384,512]{1,0:T(8,128)(2,1)S(1)}, u32[]{:S(2)}, u32[]{:S(2)}) collective-permute-start(bf16[384,512]{1,0:T(8,128)(2,1)S(1)} %fusion.5), channel_id=1, source_target_pairs={{0,1},{1,0},{2,3},{3,2},{4,5},{5,4},{6,7},{7,6},{8,9},{9,8},{10,11... | collective-permute-start | bytes 1179656 | tf_op jit(solution)/shard_map/ppermute | solution.py:61
  178.2 4.0 %copy-start.2 = (f32[384,512]{1,0:T(8,128)S(1)}, f32[384,512]{1,0:T(8,128)}, u32[]{:S(2)}) copy-start(f32[384,512]{1,0:T(8,128)} %fusion.9) | copy-start | bytes 2359300
  178.2 4.8 %collective-permute-start.14 = (bf16[384,512]{1,0:T(8,128)(2,1)S(1)}, bf16[384,512]{1,0:T(8,128)(2,1)S(1)}, u32[]{:S(2)}, u32[]{:S(2)}) collective-permute-start(bf16[384,512]{1,0:T(8,128)(2,1)S(1)} %fusion.2), channel_id=1, source_target_pairs={{0,1},{1,0},{2,3},{3,2},{4,5},{5,4},{6,7},{7,6},{8,9},{9,8},{10,11... | collective-permute-start | bytes 1179656 | tf_op jit(solution)/shard_map/ppermute | solution.py:61
  179.2 11.9 %collective-permute-start.16 = (bf16[384,512]{1,0:T(8,128)(2,1)S(1)}, bf16[384,512]{1,0:T(8,128)(2,1)S(1)}, u32[]{:S(2)}, u32[]{:S(2)}) collective-permute-start(bf16[384,512]{1,0:T(8,128)(2,1)S(1)} %add_convert_fusion.4), channel_id=1, source_target_pairs={{0,2},{1,3},{2,0},{3,1},{4,6},{5,7},{6,4},{7,5},{8,10},{9,11},{10,... | collective-permute-start | bytes 1179656 | tf_op jit(solution)/shard_map/ppermute | solution.py:61

commit v5 on v4

--- a/solution.py
+++ b/solution.py
@@ -53,6 +53,7 @@
 LINES = groups(lambda d, k: moved(d, 0, 0, k))
 RING = {k: [(d, moved(d, k, 0, 0)) for d in DEVS if line_pos(d) < 3] for k in (1, 2, 3)}
 PAIR = [(d, moved(d, 0, 1, 0)) for d in DEVS if line_pos(d) < 3]
+SWAP = [(d, moved(d, 0, 1, 0)) for d in DEVS]
 CORE = [(d, d ^ 1) for d in DEVS]
 FAR = [(d, d ^ 2) for d in DEVS]
 
@@ -156,6 +157,10 @@
     return out[0], out[1:]
 
 
+def after(x, other):
+    return lax.optimization_barrier((x, other))[0]
+
+
 def add(*terms):
     return functools.reduce(lambda a, b: a + b, [t.astype(F32) for t in terms]).astype(BF16)
 
@@ -164,12 +169,16 @@
     return lax.all_to_all(x, AXES, 0, 0, axis_index_groups=LINES, tiled=True)
 
 
-def deal(a, b):
+def by_head(a, b):
     heads = [
         jnp.concatenate([a[:, p * HD : (p + 1) * HD], b[:, p * HD : (p + 1) * HD]], axis=1)
-        for p in (0, 1, 2, 0)
+        for p in range(3)
     ]
-    return exchange(jnp.concatenate(heads, axis=0))
+    return jnp.concatenate(heads, axis=0)
+
+
+def deal(heads):
+    return exchange(jnp.concatenate([heads, heads[: BLK_DEV * BLK]], axis=0))
 
 
 def body(queries, keys, values, upstream_out, out_weight, qkv_weight, rand_links, global_links):
@@ -196,32 +205,41 @@
     shard_of = jnp.where(ky == y, 0, 4) + (k_ring - ring) % 4
     table = (shard_of * LINE + k_pos) * BLK_DEV + key % BLK_DEV
 
-    own = deal(keys, values)
-    other = send(own, PAIR)
+    heads = by_head(keys, values)
+    swapped = send(heads, SWAP)
+    own = deal(heads)
+    across = send(own, RING[2])
+    other = deal(swapped)
     next_, last = send(own, RING[3]), send(own, RING[1])
-    across = send(own, RING[2])
+    corner = send(across, PAIR)
     grad_ctx = lax.dot_general(
         upstream_out, out_weight, (((1,), (1,)), ((), ())), preferred_element_type=F32
     ).astype(BF16)
-    grad_ctx, other = lax.optimization_barrier((grad_ctx, other))
-    qd = deal(queries, grad_ctx)
-    other_row = [other, send(other, RING[3]), send(across, PAIR), send(other, RING[1])]
-    grad_q, parts = attend(table, qd, [own, next_, across, last] + other_row)
+    grad_ctx = after(grad_ctx, other)
+    other_next, other_last = send(other, RING[3]), send(other, RING[1])
+    qd = deal(by_head(queries, grad_ctx))
+    grad_q, parts = attend(
+        table, qd, [own, next_, across, last, other, other_next, corner, other_last]
+    )
 
     corner = send(parts[6], PAIR)
     other_sum = add(parts[4], send(parts[5], RING[1]), send(parts[7], RING[3]))
-    q_back = exchange(grad_q)
     sides = [send(parts[1], RING[1]), send(parts[3], RING[3])]
-    other_sum = send(other_sum, PAIR)
+    first = jnp.concatenate([other_sum, grad_q], axis=1)
+    corner = after(corner, first)
+    first = exchange(first).reshape(LINE, -1, 3 * HD)
     across = send(add(parts[2], corner), RING[2])
-    kv_back = exchange(add(parts[0], *sides, across, other_sum))
+    for_pair = first[:3, :, : 2 * HD]
+    across = after(across, for_pair)
+    from_pair = send(for_pair, SWAP)
+    second = exchange(add(parts[0], *sides, across)).reshape(LINE, -1, 2 * HD)
+    kv_back = add(second[:3], from_pair)
 
     def tokens(back, lanes):
-        back = back.reshape(LINE, BLK_DEV * BLK, -1)
         return jnp.concatenate([back[p, :, lanes] for p in range(3)], axis=1)
 
     grads = [
-        tokens(q_back, slice(0, HD)),
+        tokens(first, slice(2 * HD, 3 * HD)),
         tokens(kv_back, slice(0, HD)),
         tokens(kv_back, slice(HD, 2 * HD)),
     ]

time: 193 us -> 210 us (1.088)
  waiting for transfers between devices: 56.5 us -> 73.2 us
  blocking collectives: 14.8 us -> 0 us
  other arithmetic: 11.4 us -> 20.5 us
  local copies, waits for them, and re-layouts: 5.89 us -> 10.1 us
    all_to_all x1 -> x0, blocking collectives: 14.8 us -> none  [exchange(): return lax.all_to_all(x, AXES, 0, 0, axis_index_groups=LINES, tiled=True)]
    all_to_all x3 -> x5, starting transfers between devices: 12.6 us -> 22.8 us  [exchange(): return lax.all_to_all(x, AXES, 0, 0, axis_index_groups=LINES, tiled=True)]
    ppermute x17, starting transfers between devices: 56 us -> 45.8 us  [send(): return lax.ppermute(x, AXES, perm)]
    all_to_all x3 -> x5, waiting for transfers between devices: 15.5 us -> 24.8 us  [exchange(): return lax.all_to_all(x, AXES, 0, 0, axis_index_groups=LINES, tiled=True)]
    concatenate x2 -> x5, other arithmetic: 1.19 us -> 8.99 us  [the longest x3 5.49 us: deal(): return exchange(jnp.concatenate([heads, heads[:BLK_DEV * BLK]], axis=0))]
    ppermute x17, waiting for transfers between devices: 40.9 us -> 48.4 us  [send(): return lax.ppermute(x, AXES, perm)]
    slice x4 -> x5, local copies, waits for them, and re-layouts: 3.59 us -> 7.41 us  [the longest x2 3.21 us: by_head(): a[:, p * HD:(p + 1) * HD]]
    convert_element_type x4 -> x5, other arithmetic: 9.22 us -> 10.5 us  [add(): functools.reduce(lambda a, b: a + b, [t.astype(F32) for t in terms])]
  transfers between devices with their start and end apart: 20 -> 22, of which waited for: 9 -> 12; matrix products, arithmetic and copies ran while one was open for 12% -> 17% of each run, Pallas kernels for 0% -> 0%
where the time goes in v5:
time: 210 us; the launch traced here: 208 us
  waiting for transfers between devices  73.2 us (35%)
  starting transfers between devices  68.6 us (33%)
  Pallas kernels  23.2 us (11%)
  other arithmetic  20.5 us (10%)
  matrix products  11.9 us (6%)
  local copies, waits for them, and re-layouts  10.1 us (5%)
    ppermute x17, waiting for transfers between devices, send(): return lax.ppermute(x, AXES, perm)  48.4 us
    ppermute x17, starting transfers between devices, send(): return lax.ppermute(x, AXES, perm)  45.8 us
    all_to_all x5, waiting for transfers between devices, exchange(): return lax.all_to_all(x, AXES, 0, 0, axis_index_groups=LINES, tiled=True)  24.8 us
    pallas_call x1, Pallas kernels, attend(): pl.pallas_call(attend_kernel, name='attend', out_shape=(jax.ShapeDtypeStr...  23.2 us
    all_to_all x5, starting transfers between devices, exchange(): return lax.all_to_all(x, AXES, 0, 0, axis_index_groups=LINES, tiled=True)  22.8 us
    convert_element_type x5, other arithmetic, add(): functools.reduce(lambda a, b: a + b, [t.astype(F32) for t in terms])  10.5 us
    dot_general x12, matrix products, share(): lax.dot_general(w[j], g, (((1,), (1,)), ((), ())), preferred_element_type...  8.41 us
    concatenate x3, other arithmetic, deal(): return exchange(jnp.concatenate([heads, heads[:BLK_DEV * BLK]], axis=0))  5.49 us
  transfers between devices with their start and end apart: 22, of which 12 were waited for; matrix products, arithmetic and copies ran while one was open for 17% of the time, Pallas kernels for 0%

profile of v5, /device:TPU:1, one launch (start us, length us, event | category | flops | bytes accessed | tf_op | source)
XLA Modules:
  0.0 208.0 jit_solution(10386600771102495625)
XLA Ops:
  0.0 1.4 fusion.39
  3.2 4.9 %all-to-all-start.2 = ((bf16[4,512,256]{2,1,0:T(8,128)(2,1)}), bf16[4,512,256]{2,1,0:T(8,128)(2,1)}, u32[]{:S(2)}, u32[]{:S(2)}) async-start(bf16[4,512,256]{2,1,0:T(8,128)(2,1)} %bitcast.82), calls=%async_computation.2 | async-start | bytes 2097152 | tf_op jit(solution)/shard_map/all_to_all | solution.py:169
  8.0 2.2 %maximum_maximum_fusion.2 = bf16[1536,256]{1,0:T(8,128)(2,1)} fusion(bf16[512,128]{1,0:T(8,128)(2,1)} %copy-done.5, bf16[512,128]{1,0:T(8,128)(2,1)} %copy-done.2, bf16[512,128]{1,0:T(8,128)(2,1)} %copy-done.4, bf16[512,128]{1,0:T(8,128)(2,1)} %copy-done.3, bf16[512,128]{1,0:T(8,128)(2,1)} %copy-done.6, bf16[512,128]{1,0:T(8,128)(2,1)} %copy-done.1), kind=kLoop, calls=%fused_computation.23 | loop fusion | flops 4718592 | bytes 1572864 | tf_op jit(solution)/shard_map/concatenate | solution.py:177
  10.2 1.5 collective-permute-start
  11.7 6.4 %all-to-all-done.2 = bf16[4,512,256]{2,1,0:T(8,128)(2,1)} async-done(((bf16[4,512,256]{2,1,0:T(8,128)(2,1)}), bf16[4,512,256]{2,1,0:T(8,128)(2,1)}, u32[]{:S(2)}, u32[]{:S(2)}) %all-to-all-start.2) | async-done | bytes 1048608 | tf_op jit(solution)/shard_map/all_to_all | solution.py:169
  18.2 5.4 %collective-permute-start.2 = (bf16[2048,256]{1,0:T(8,128)(2,1)}, bf16[2048,256]{1,0:T(8,128)(2,1)}, u32[]{:S(2)}, u32[]{:S(2)}) collective-permute-start(bf16[2048,256]{1,0:T(8,128)(2,1)} %bitcast.7.refs_0_), channel_id=1, source_target_pairs={{0,64},{1,9},{2,66},{3,11},{4,68},{5,13},{6,70},{7,15},{8,72},{9,1... | collective-permute-start | bytes 3145736 | tf_op jit(solution)/shard_map/ppermute | solution.py:62
  23.5 4.2 %collective-permute-done = bf16[1536,256]{1,0:T(8,128)(2,1)} collective-permute-done((bf16[1536,256]{1,0:T(8,128)(2,1)}, bf16[1536,256]{1,0:T(8,128)(2,1)}, u32[]{:S(2)}, u32[]{:S(2)}) %collective-permute-start) | collective-permute-done | bytes 786464 | tf_op jit(solution)/shard_map/ppermute | solution.py:62
  28.7 2.2 %pad_maximum_fusion.1 = bf16[2048,256]{1,0:T(8,128)(2,1)} fusion(bf16[512,256]{1,0:T(8,128)(2,1)S(1)} %slice.158, bf16[1536,256]{1,0:T(8,128)(2,1)} %collective-permute-done), kind=kLoop, calls=%fused_computation.20 | loop fusion | flops 2097152 | bytes 2097152 | tf_op jit(solution)/shard_map/concatenate | solution.py:181
  30.9 4.4 %all-to-all-start = ((bf16[4,512,256]{2,1,0:T(8,128)(2,1)}), bf16[4,512,256]{2,1,0:T(8,128)(2,1)}, u32[]{:S(2)}, u32[]{:S(2)}) async-start(bf16[4,512,256]{2,1,0:T(8,128)(2,1)} %bitcast.83), calls=%async_computation | async-start | bytes 2097152 | tf_op jit(solution)/shard_map/all_to_all | solution.py:169
  35.2 1.8 fusion.37
  37.1 3.5 %convolution_convert_fusion = bf16[512,384]{1,0:T(8,128)(2,1)} fusion(bf16[512,1536]{1,0:T(8,128)(2,1)} %param.11, bf16[384,1536]{1,0:T(8,128)(2,1)} %param.12), kind=kOutput, calls=%fused_computation.19 | convolution fusion | flops 604176384 | bytes 3145728 | tf_op jit(solution)/shard_map/dot_general | solution.py:215
  40.5 6.8 %collective-permute-start.1 = (bf16[2048,256]{1,0:T(8,128)(2,1)}, bf16[2048,256]{1,0:T(8,128)(2,1)}, u32[]{:S(2)}, u32[]{:S(2)}) collective-permute-start(bf16[2048,256]{1,0:T(8,128)(2,1)} %bitcast.7.refs_0_), channel_id=1, source_target_pairs={{0,96},{1,13},{2,98},{3,15},{4,100},{5,1},{6,102},{7,3},{8,104},{9... | collective-permute-start | bytes 3145736 | tf_op jit(solution)/shard_map/ppermute | solution.py:62
  47.4 1.9 collective-permute-start.3
  49.3 4.6 %collective-permute-start.4 = (bf16[2048,256]{1,0:T(8,128)(2,1)}, bf16[2048,256]{1,0:T(8,128)(2,1)}, u32[]{:S(2)}, u32[]{:S(2)}) collective-permute-start(bf16[2048,256]{1,0:T(8,128)(2,1)} %bitcast.3.refs_4_), channel_id=1, source_target_pairs={{0,96},{1,13},{2,98},{3,15},{4,100},{5,1},{6,102},{7,3},{8,104},{9... | collective-permute-start | bytes 3145736 | tf_op jit(solution)/shard_map/ppermute | solution.py:62
  53.9 1.9 collective-permute-start.6
  56.9 3.2 %collective-permute-start.5 = (bf16[2048,256]{1,0:T(8,128)(2,1)}, bf16[2048,256]{1,0:T(8,128)(2,1)}, u32[]{:S(2)}, u32[]{:S(2)}) collective-permute-start(bf16[2048,256]{1,0:T(8,128)(2,1)} %collective-permute-done.2.refs_2_), channel_id=1, source_target_pairs={{0,16},{1,17},{2,18},{3,19},{4,20},{5,21},{6,22},{7,23},{8,24},{9,... | collective-permute-start | bytes 3145736 | tf_op jit(solution)/shard_map/ppermute | solution.py:62
  60.1 2.2 %maximum_maximum_fusion = bf16[2048,256]{1,0:T(8,128)(2,1)} fusion(bf16[512,128]{1,0:T(8,128)(2,1)S(1)} %get-tuple-element.43, bf16[512,128]{1,0:T(8,128)(2,1)} %get-tuple-element.39, bf16[512,128]{1,0:T(8,128)(2,1)S(1)} %get-tuple-element.42, bf16[512,128]{1,0:T(8,128)(2,1)} %get-tuple-element.40, bf16[512,128]{1,0:T(8,128)(2,1)S(1)} %get-tuple-element.41, ...), kind=kLoop, calls=%fused_computation.21 | loop fusion | flops 8388608 | bytes 1835008 | tf_op jit(solution)/shard_map/concatenate | solution.py:181
  62.3 4.3 %all-to-all-start.1 = ((bf16[4,512,256]{2,1,0:T(8,128)(2,1)}), bf16[4,512,256]{2,1,0:T(8,128)(2,1)}, u32[]{:S(2)}, u32[]{:S(2)}) async-start(bf16[4,512,256]{2,1,0:T(8,128)(2,1)} %bitcast.81), calls=%async_computation.1 | async-start | bytes 2097152 | tf_op jit(solution)/shard_map/all_to_all | solution.py:169
  68.5 13.7 %all-to-all-done.1 = bf16[4,512,256]{2,1,0:T(8,128)(2,1)} async-done(((bf16[4,512,256]{2,1,0:T(8,128)(2,1)}), bf16[4,512,256]{2,1,0:T(8,128)(2,1)}, u32[]{:S(2)}, u32[]{:S(2)}) %all-to-all-start.1) | async-done | bytes 1048608 | tf_op jit(solution)/shard_map/all_to_all | solution.py:169
  82.2 23.2 %attend.1 = (bf16[2048,128]{1,0:T(8,128)(2,1)}, bf16[2048,256]{1,0:T(8,128)(2,1)}, bf16[2048,256]{1,0:T(8,128)(2,1)}, bf16[2048,256]{1,0:T(8,128)(2,1)}, bf16[20...) custom-call(s32[16,8]{1,0:T(8,128)} %fusion.18.table, ...), custom_call_target="tpu_custom_call" | custom-call | tf_op jit(solution)/shard_map/attend/pallas_call | solution.py:137
  105.4 1.9 collective-permute-start.8
  107.4 3.4 %collective-permute-start.7 = (bf16[2048,256]{1,0:T(8,128)(2,1)}, bf16[2048,256]{1,0:T(8,128)(2,1)S(1)}, u32[]{:S(2)}, u32[]{:S(2)}) collective-permute-start(bf16[2048,256]{1,0:T(8,128)(2,1)} %get-tuple-element.19), channel_id=1, source_target_pairs={{0,32},{1,5},{2,34},{3,7},{4,36},{5,9},{6,38},{7,11},{8,40},{9,13}... | collective-permute-start | bytes 3145736 | tf_op jit(solution)/shard_map/ppermute | solution.py:62
  110.7 2.3 %collective-permute-start.11 = (bf16[2048,256]{1,0:T(8,128)(2,1)}, bf16[2048,256]{1,0:T(8,128)(2,1)}, u32[]{:S(2)}, u32[]{:S(2)}) collective-permute-start(bf16[2048,256]{1,0:T(8,128)(2,1)} %get-tuple-element.26), channel_id=1, source_target_pairs={{0,16},{1,17},{2,18},{3,19},{4,20},{5,21},{6,22},{7,23},{8,24},{9,... | collective-permute-start | bytes 3145736 | tf_op jit(solution)/shard_map/ppermute | solution.py:62
  113.0 8.6 %collective-permute-done.8 = bf16[2048,256]{1,0:T(8,128)(2,1)S(1)} collective-permute-done((bf16[2048,256]{1,0:T(8,128)(2,1)}, bf16[2048,256]{1,0:T(8,128)(2,1)S(1)}, u32[]{:S(2)}, u32[]{:S(2)}) %collective-permute-start.8) | collective-permute-done | bytes 1048608 | tf_op jit(solution)/shard_map/ppermute | solution.py:62
  121.6 3.0 %collective-permute-done.7 = bf16[2048,256]{1,0:T(8,128)(2,1)S(1)} collective-permute-done((bf16[2048,256]{1,0:T(8,128)(2,1)}, bf16[2048,256]{1,0:T(8,128)(2,1)S(1)}, u32[]{:S(2)}, u32[]{:S(2)}) %collective-permute-start.7) | collective-permute-done | bytes 1048608 | tf_op jit(solution)/shard_map/ppermute | solution.py:62
  124.6 1.8 add_convert_fusion.2
  126.4 1.3 pad_maximum_fusion
  127.8 5.0 %all-to-all-start.3 = ((bf16[4,512,384]{2,1,0:T(8,128)(2,1)}), bf16[4,512,384]{2,1,0:T(8,128)(2,1)}, u32[]{:S(2)}, u32[]{:S(2)}) async-start(bf16[4,512,384]{2,1,0:T(8,128)(2,1)} %bitcast.79), calls=%async_computation.3 | async-start | bytes 3145728 | tf_op jit(solution)/shard_map/all_to_all | solution.py:169
  132.8 1.8 collective-permute-done.11
  134.6 2.8 %add_convert_fusion.1 = bf16[2048,256]{1,0:T(8,128)(2,1)} fusion(bf16[2048,256]{1,0:T(8,128)(2,1)} %collective-permute-done.11, bf16[2048,256]{1,0:T(8,128)(2,1)} %get-tuple-element.25), kind=kLoop, calls=%fused_computation.1 | loop fusion | flops 2097152 | bytes 3145728 | tf_op jit(solution)/shard_map/convert_element_type | solution.py:165
  137.3 1.9 collective-permute-start.12
  139.3 3.1 %collective-permute-start.10 = (bf16[2048,256]{1,0:T(8,128)(2,1)}, bf16[2048,256]{1,0:T(8,128)(2,1)}, u32[]{:S(2)}, u32[]{:S(2)}) collective-permute-start(bf16[2048,256]{1,0:T(8,128)(2,1)} %get-tuple-element.24), channel_id=1, source_target_pairs={{0,96},{1,13},{2,98},{3,15},{4,100},{5,1},{6,102},{7,3},{8,104},{9... | collective-permute-start | bytes 3145736 | tf_op jit(solution)/shard_map/ppermute | solution.py:62
  142.4 2.1 %collective-permute-start.9 = (bf16[2048,256]{1,0:T(8,128)(2,1)}, bf16[2048,256]{1,0:T(8,128)(2,1)}, u32[]{:S(2)}, u32[]{:S(2)}) collective-permute-start(bf16[2048,256]{1,0:T(8,128)(2,1)} %get-tuple-element.23), channel_id=1, source_target_pairs={{0,32},{1,5},{2,34},{3,7},{4,36},{5,9},{6,38},{7,11},{8,40},{9,13}... | collective-permute-start | bytes 3145736 | tf_op jit(solution)/shard_map/ppermute | solution.py:62
  145.5 2.2 %slice.162 = bf16[3,512,256]{2,1,0:T(8,128)(2,1)} slice(bf16[4,512,384]{2,1,0:T(8,128)(2,1)} %all-to-all-done.3), slice={[0:3], [0:512], [0:256]} | slice | bytes 1572864 | tf_op jit(solution)/shard_map/slice | solution.py:232
  147.7 1.3 collective-permute-start.13
  149.0 11.5 %collective-permute-done.12 = bf16[2048,256]{1,0:T(8,128)(2,1)} collective-permute-done((bf16[2048,256]{1,0:T(8,128)(2,1)}, bf16[2048,256]{1,0:T(8,128)(2,1)}, u32[]{:S(2)}, u32[]{:S(2)}) %collective-permute-start.12) | collective-permute-done | bytes 1048608 | tf_op jit(solution)/shard_map/ppermute | solution.py:62
  160.5 10.0 %collective-permute-done.10 = bf16[2048,256]{1,0:T(8,128)(2,1)} collective-permute-done((bf16[2048,256]{1,0:T(8,128)(2,1)}, bf16[2048,256]{1,0:T(8,128)(2,1)}, u32[]{:S(2)}, u32[]{:S(2)}) %collective-permute-start.10) | collective-permute-done | bytes 1048608 | tf_op jit(solution)/shard_map/ppermute | solution.py:62
  170.5 1.2 collective-permute-done.9
  171.6 3.4 %add_convert_fusion = bf16[2048,256]{1,0:T(8,128)(2,1)} fusion(bf16[2048,256]{1,0:T(8,128)(2,1)} %collective-permute-done.12, bf16[2048,256]{1,0:T(8,128)(2,1)} %collective-permute-done.10, bf16[2048,256]{1,0:T(8,128)(2,1)} %collective-permute-done.9, bf16[2048,256]{1,0:T(8,128)(2,1)S(1)} %copy-done.7), kind=kLoop, calls=%fused_computation | loop fusion | flops 4194304 | bytes 5242880 | tf_op jit(solution)/shard_map/convert_element_type | solution.py:165
  175.0 4.3 %all-to-all-start.4 = ((bf16[4,512,256]{2,1,0:T(8,128)(2,1)}), bf16[4,512,256]{2,1,0:T(8,128)(2,1)}, u32[]{:S(2)}, u32[]{:S(2)}) async-start(bf16[4,512,256]{2,1,0:T(8,128)(2,1)} %bitcast.80), calls=%async_computation.4 | async-start | bytes 2097152 | tf_op jit(solution)/shard_map/all_to_all | solution.py:169
  180.4 1.3 fusion.6
  181.7 1.3 fusion.7
  183.0 1.3 fusion.9
  184.3 1.3 fusion.8
  185.6 3.8 %all-to-all-done.4 = bf16[4,512,256]{2,1,0:T(8,128)(2,1)} async-done(((bf16[4,512,256]{2,1,0:T(8,128)(2,1)}), bf16[4,512,256]{2,1,0:T(8,128)(2,1)}, u32[]{:S(2)}, u32[]{:S(2)}) %all-to-all-start.4) | async-done | bytes 1048608 | tf_op jit(solution)/shard_map/all_to_all | solution.py:169
  189.4 1.6 add_convert_fusion.3
  195.1 3.0 %collective-permute-start.16 = (bf16[384,512]{1,0:T(8,128)(2,1)S(1)}, bf16[384,512]{1,0:T(8,128)(2,1)S(1)}, u32[]{:S(2)}, u32[]{:S(2)}) collective-permute-start(bf16[384,512]{1,0:T(8,128)(2,1)S(1)} %add_convert_fusion.5), channel_id=1, source_target_pairs={{0,2},{1,3},{2,0},{3,1},{4,6},{5,7},{6,4},{7,5},{8,10},{9,11},{10,... | collective-permute-start | bytes 1179656 | tf_op jit(solution)/shard_map/ppermute | solution.py:62
  198.9 8.2 %collective-permute-done.16 = bf16[384,512]{1,0:T(8,128)(2,1)S(1)} collective-permute-done((bf16[384,512]{1,0:T(8,128)(2,1)S(1)}, bf16[384,512]{1,0:T(8,128)(2,1)S(1)}, u32[]{:S(2)}, u32[]{:S(2)}) %collective-permute-start.16) | collective-permute-done | bytes 393248 | tf_op jit(solution)/shard_map/ppermute | solution.py:62
  (63 shorter events, 13.3 us)
Async XLA Ops:
  0.0 180.4 %copy-start = (bf16[3,1536,384]{2,1,0:T(8,128)(2,1)S(1)}, bf16[3,1536,384]{2,1,0:T(8,128)(2,1)}, u32[]{:S(2)}) copy-start(bf16[3,1536,384]{2,1,0:T(8,128)(2,1)} %param.13) | copy-start | bytes 10616836
  1.4 0.6 copy-start.1
  1.4 1.7 copy-start.2
  1.4 1.7 copy-start.3
  1.4 1.7 copy-start.4
  1.4 1.7 copy-start.5
  1.5 1.7 copy-start.6
  3.2 15.0 %all-to-all-start.2 = ((bf16[4,512,256]{2,1,0:T(8,128)(2,1)}), bf16[4,512,256]{2,1,0:T(8,128)(2,1)}, u32[]{:S(2)}, u32[]{:S(2)}) async-start(bf16[4,512,256]{2,1,0:T(8,128)(2,1)} %bitcast.82), calls=%async_computation.2 | async-start | bytes 2097152 | tf_op jit(solution)/shard_map/all_to_all | solution.py:169
  10.2 17.5 %collective-permute-start = (bf16[1536,256]{1,0:T(8,128)(2,1)}, bf16[1536,256]{1,0:T(8,128)(2,1)}, u32[]{:S(2)}, u32[]{:S(2)}) collective-permute-start(bf16[1536,256]{1,0:T(8,128)(2,1)} %maximum_maximum_fusion.2), channel_id=1, source_target_pairs={{0,16},{1,17},{2,18},{3,19},{4,20},{5,21},{6,22},{7,23},{8,24},{9,... | collective-permute-start | bytes 2359304 | tf_op jit(solution)/shard_map/ppermute | solution.py:62
  18.2 38.7 %collective-permute-start.2 = (bf16[2048,256]{1,0:T(8,128)(2,1)}, bf16[2048,256]{1,0:T(8,128)(2,1)}, u32[]{:S(2)}, u32[]{:S(2)}) collective-permute-start(bf16[2048,256]{1,0:T(8,128)(2,1)} %bitcast.7.refs_0_), channel_id=1, source_target_pairs={{0,64},{1,9},{2,66},{3,11},{4,68},{5,13},{6,70},{7,15},{8,72},{9,1... | collective-permute-start | bytes 3145736 | tf_op jit(solution)/shard_map/ppermute | solution.py:62
  30.9 18.4 %all-to-all-start = ((bf16[4,512,256]{2,1,0:T(8,128)(2,1)}), bf16[4,512,256]{2,1,0:T(8,128)(2,1)}, u32[]{:S(2)}, u32[]{:S(2)}) async-start(bf16[4,512,256]{2,1,0:T(8,128)(2,1)} %bitcast.83), calls=%async_computation | async-start | bytes 2097152 | tf_op jit(solution)/shard_map/all_to_all | solution.py:169
  40.5 28.0 %collective-permute-start.1 = (bf16[2048,256]{1,0:T(8,128)(2,1)}, bf16[2048,256]{1,0:T(8,128)(2,1)}, u32[]{:S(2)}, u32[]{:S(2)}) collective-permute-start(bf16[2048,256]{1,0:T(8,128)(2,1)} %bitcast.7.refs_0_), channel_id=1, source_target_pairs={{0,96},{1,13},{2,98},{3,15},{4,100},{5,1},{6,102},{7,3},{8,104},{9... | collective-permute-start | bytes 3145736 | tf_op jit(solution)/shard_map/ppermute | solution.py:62
  47.4 21.1 %collective-permute-start.3 = (bf16[2048,256]{1,0:T(8,128)(2,1)}, bf16[2048,256]{1,0:T(8,128)(2,1)}, u32[]{:S(2)}, u32[]{:S(2)}) collective-permute-start(bf16[2048,256]{1,0:T(8,128)(2,1)} %bitcast.7.refs_0_), channel_id=1, source_target_pairs={{0,32},{1,5},{2,34},{3,7},{4,36},{5,9},{6,38},{7,11},{8,40},{9,13}... | collective-permute-start | bytes 3145736 | tf_op jit(solution)/shard_map/ppermute | solution.py:62
  49.3 32.9 %collective-permute-start.4 = (bf16[2048,256]{1,0:T(8,128)(2,1)}, bf16[2048,256]{1,0:T(8,128)(2,1)}, u32[]{:S(2)}, u32[]{:S(2)}) collective-permute-start(bf16[2048,256]{1,0:T(8,128)(2,1)} %bitcast.3.refs_4_), channel_id=1, source_target_pairs={{0,96},{1,13},{2,98},{3,15},{4,100},{5,1},{6,102},{7,3},{8,104},{9... | collective-permute-start | bytes 3145736 | tf_op jit(solution)/shard_map/ppermute | solution.py:62
  53.9 28.3 %collective-permute-start.6 = (bf16[2048,256]{1,0:T(8,128)(2,1)}, bf16[2048,256]{1,0:T(8,128)(2,1)}, u32[]{:S(2)}, u32[]{:S(2)}) collective-permute-start(bf16[2048,256]{1,0:T(8,128)(2,1)} %bitcast.3.refs_4_), channel_id=1, source_target_pairs={{0,32},{1,5},{2,34},{3,7},{4,36},{5,9},{6,38},{7,11},{8,40},{9,13}... | collective-permute-start | bytes 3145736 | tf_op jit(solution)/shard_map/ppermute | solution.py:62
  56.9 9.9 %copy-start.13 = (s32[128,3]{0,1:T(4,128)S(1)}, s32[128,3]{0,1:T(4,128)}, u32[]{:S(2)}) copy-start(s32[128,3]{0,1:T(4,128)} %param.14) | copy-start | bytes 4612
  56.9 25.3 %collective-permute-start.5 = (bf16[2048,256]{1,0:T(8,128)(2,1)}, bf16[2048,256]{1,0:T(8,128)(2,1)}, u32[]{:S(2)}, u32[]{:S(2)}) collective-permute-start(bf16[2048,256]{1,0:T(8,128)(2,1)} %collective-permute-done.2.refs_2_), channel_id=1, source_target_pairs={{0,16},{1,17},{2,18},{3,19},{4,20},{5,21},{6,22},{7,23},{8,24},{9,... | collective-permute-start | bytes 3145736 | tf_op jit(solution)/shard_map/ppermute | solution.py:62
  62.3 19.8 %all-to-all-start.1 = ((bf16[4,512,256]{2,1,0:T(8,128)(2,1)}), bf16[4,512,256]{2,1,0:T(8,128)(2,1)}, u32[]{:S(2)}, u32[]{:S(2)}) async-start(bf16[4,512,256]{2,1,0:T(8,128)(2,1)} %bitcast.81), calls=%async_computation.1 | async-start | bytes 2097152 | tf_op jit(solution)/shard_map/all_to_all | solution.py:169
  105.4 16.2 %collective-permute-start.8 = (bf16[2048,256]{1,0:T(8,128)(2,1)}, bf16[2048,256]{1,0:T(8,128)(2,1)S(1)}, u32[]{:S(2)}, u32[]{:S(2)}) collective-permute-start(bf16[2048,256]{1,0:T(8,128)(2,1)} %get-tuple-element.20), channel_id=1, source_target_pairs={{0,96},{1,13},{2,98},{3,15},{4,100},{5,1},{6,102},{7,3},{8,104},{9... | collective-permute-start | bytes 3145736 | tf_op jit(solution)/shard_map/ppermute | solution.py:62
  107.4 17.3 %collective-permute-start.7 = (bf16[2048,256]{1,0:T(8,128)(2,1)}, bf16[2048,256]{1,0:T(8,128)(2,1)S(1)}, u32[]{:S(2)}, u32[]{:S(2)}) collective-permute-start(bf16[2048,256]{1,0:T(8,128)(2,1)} %get-tuple-element.19), channel_id=1, source_target_pairs={{0,32},{1,5},{2,34},{3,7},{4,36},{5,9},{6,38},{7,11},{8,40},{9,13}... | collective-permute-start | bytes 3145736 | tf_op jit(solution)/shard_map/ppermute | solution.py:62
  110.7 23.8 %collective-permute-start.11 = (bf16[2048,256]{1,0:T(8,128)(2,1)}, bf16[2048,256]{1,0:T(8,128)(2,1)}, u32[]{:S(2)}, u32[]{:S(2)}) collective-permute-start(bf16[2048,256]{1,0:T(8,128)(2,1)} %get-tuple-element.26), channel_id=1, source_target_pairs={{0,16},{1,17},{2,18},{3,19},{4,20},{5,21},{6,22},{7,23},{8,24},{9,... | collective-permute-start | bytes 3145736 | tf_op jit(solution)/shard_map/ppermute | solution.py:62
  124.6 1.8 copy-start.12
  127.8 17.7 %all-to-all-start.3 = ((bf16[4,512,384]{2,1,0:T(8,128)(2,1)}), bf16[4,512,384]{2,1,0:T(8,128)(2,1)}, u32[]{:S(2)}, u32[]{:S(2)}) async-start(bf16[4,512,384]{2,1,0:T(8,128)(2,1)} %bitcast.79), calls=%async_computation.3 | async-start | bytes 3145728 | tf_op jit(solution)/shard_map/all_to_all | solution.py:169
  137.3 23.1 %collective-permute-start.12 = (bf16[2048,256]{1,0:T(8,128)(2,1)}, bf16[2048,256]{1,0:T(8,128)(2,1)}, u32[]{:S(2)}, u32[]{:S(2)}) collective-permute-start(bf16[2048,256]{1,0:T(8,128)(2,1)} %add_convert_fusion.1), channel_id=1, source_target_pairs={{0,64},{1,9},{2,66},{3,11},{4,68},{5,13},{6,70},{7,15},{8,72},{9,1... | collective-permute-start | bytes 3145736 | tf_op jit(solution)/shard_map/ppermute | solution.py:62
  139.3 31.2 %collective-permute-start.10 = (bf16[2048,256]{1,0:T(8,128)(2,1)}, bf16[2048,256]{1,0:T(8,128)(2,1)}, u32[]{:S(2)}, u32[]{:S(2)}) collective-permute-start(bf16[2048,256]{1,0:T(8,128)(2,1)} %get-tuple-element.24), channel_id=1, source_target_pairs={{0,96},{1,13},{2,98},{3,15},{4,100},{5,1},{6,102},{7,3},{8,104},{9... | collective-permute-start | bytes 3145736 | tf_op jit(solution)/shard_map/ppermute | solution.py:62
  142.4 29.2 %collective-permute-start.9 = (bf16[2048,256]{1,0:T(8,128)(2,1)}, bf16[2048,256]{1,0:T(8,128)(2,1)}, u32[]{:S(2)}, u32[]{:S(2)}) collective-permute-start(bf16[2048,256]{1,0:T(8,128)(2,1)} %get-tuple-element.23), channel_id=1, source_target_pairs={{0,32},{1,5},{2,34},{3,7},{4,36},{5,9},{6,38},{7,11},{8,40},{9,13}... | collective-permute-start | bytes 3145736 | tf_op jit(solution)/shard_map/ppermute | solution.py:62
  145.5 26.1 %copy-start.7 = (bf16[2048,256]{1,0:T(8,128)(2,1)S(1)}, bf16[2048,256]{1,0:T(8,128)(2,1)}, u32[]{:S(2)}) copy-start(bf16[2048,256]{1,0:T(8,128)(2,1)} %get-tuple-element.22) | copy-start | bytes 3145732
  147.7 38.0 %collective-permute-start.13 = (bf16[3,512,256]{2,1,0:T(8,128)(2,1)}, bf16[3,512,256]{2,1,0:T(8,128)(2,1)}, u32[]{:S(2)}, u32[]{:S(2)}) collective-permute-start(bf16[3,512,256]{2,1,0:T(8,128)(2,1)} %slice.162), channel_id=1, source_target_pairs={{0,16},{1,17},{2,18},{3,19},{4,20},{5,21},{6,22},{7,23},{8,24},{9,... | collective-permute-start | bytes 2359304 | tf_op jit(solution)/shard_map/ppermute | solution.py:62
  175.0 14.4 %all-to-all-start.4 = ((bf16[4,512,256]{2,1,0:T(8,128)(2,1)}), bf16[4,512,256]{2,1,0:T(8,128)(2,1)}, u32[]{:S(2)}, u32[]{:S(2)}) async-start(bf16[4,512,256]{2,1,0:T(8,128)(2,1)} %bitcast.80), calls=%async_computation.4 | async-start | bytes 2097152 | tf_op jit(solution)/shard_map/all_to_all | solution.py:169
  189.4 1.8 copy-start.11
  191.2 2.0 copy-start.10
  192.0 2.3 %copy-start.9 = (f32[384,512]{1,0:T(8,128)S(1)}, f32[384,512]{1,0:T(8,128)}, u32[]{:S(2)}) copy-start(f32[384,512]{1,0:T(8,128)} %fusion.7) | copy-start | bytes 2359300
  192.0 2.7 %collective-permute-start.15 = (bf16[384,512]{1,0:T(8,128)(2,1)S(1)}, bf16[384,512]{1,0:T(8,128)(2,1)S(1)}, u32[]{:S(2)}, u32[]{:S(2)}) collective-permute-start(bf16[384,512]{1,0:T(8,128)(2,1)S(1)} %fusion.5), channel_id=1, source_target_pairs={{0,1},{1,0},{2,3},{3,2},{4,5},{5,4},{6,7},{7,6},{8,9},{9,8},{10,11... | collective-permute-start | bytes 1179656 | tf_op jit(solution)/shard_map/ppermute | solution.py:62
  194.0 4.1 %copy-start.8 = (f32[384,512]{1,0:T(8,128)S(1)}, f32[384,512]{1,0:T(8,128)}, u32[]{:S(2)}) copy-start(f32[384,512]{1,0:T(8,128)} %fusion.9) | copy-start | bytes 2359300
  194.0 4.9 %collective-permute-start.14 = (bf16[384,512]{1,0:T(8,128)(2,1)S(1)}, bf16[384,512]{1,0:T(8,128)(2,1)S(1)}, u32[]{:S(2)}, u32[]{:S(2)}) collective-permute-start(bf16[384,512]{1,0:T(8,128)(2,1)S(1)} %fusion.2), channel_id=1, source_target_pairs={{0,1},{1,0},{2,3},{3,2},{4,5},{5,4},{6,7},{7,6},{8,9},{9,8},{10,11... | collective-permute-start | bytes 1179656 | tf_op jit(solution)/shard_map/ppermute | solution.py:62
  195.1 12.0 %collective-permute-start.16 = (bf16[384,512]{1,0:T(8,128)(2,1)S(1)}, bf16[384,512]{1,0:T(8,128)(2,1)S(1)}, u32[]{:S(2)}, u32[]{:S(2)}) collective-permute-start(bf16[384,512]{1,0:T(8,128)(2,1)S(1)} %add_convert_fusion.5), channel_id=1, source_target_pairs={{0,2},{1,3},{2,0},{3,1},{4,6},{5,7},{6,4},{7,5},{8,10},{9,11},{10,... | collective-permute-start | bytes 1179656 | tf_op jit(solution)/shard_map/ppermute | solution.py:62

commit v6 on v4

--- a/solution.py
+++ b/solution.py
@@ -18,6 +18,10 @@
 NQ = LINE * BLK_DEV
 ROWS = NQ * BLK
 NSHARD = 8
+HALF = ROWS // 2
+PIECES = [ROWS] * 6 + [HALF] * 2 + [ROWS]
+STARTS = [sum(PIECES[:m]) for m in range(len(PIECES))]
+NPIECE = len(PIECES)
 F32 = jnp.float32
 BF16 = jnp.bfloat16
 
@@ -61,14 +65,21 @@
     return lax.ppermute(x, AXES, perm)
 
 
-def attend_kernel(table, qd_ref, *refs):
-    kv_refs, gq_ref = refs[:NSHARD], refs[NSHARD]
-    out_refs = refs[NSHARD + 1 : 2 * NSHARD + 1]
-    kv, acc, kv_now, stage, in_sems, out_sems = refs[2 * NSHARD + 1 :]
+def attend_kernel(table, dealt_ref, *refs):
+    kv_refs, gq_ref = refs[:NPIECE], refs[NPIECE]
+    out_refs = refs[NPIECE + 1 : 2 * NPIECE + 1]
+    qd_ref, kv, acc, kv_now, stage, in_sems, out_sems = refs[2 * NPIECE + 1 :]
     scale = HD ** (-0.5)
     loads = [
-        pltpu.make_async_copy(kv_refs[m], kv.at[pl.ds(m * ROWS, ROWS)], in_sems.at[m])
-        for m in range(NSHARD)
+        pltpu.make_async_copy(kv_refs[m], kv.at[pl.ds(STARTS[m], PIECES[m])], in_sems.at[m])
+        for m in range(NPIECE)
+    ]
+    side = BLK_DEV * BLK
+    loads += [
+        pltpu.make_async_copy(
+            dealt_ref.at[m, 1], qd_ref.at[pl.ds(m * side, side)], in_sems.at[NPIECE + m]
+        )
+        for m in range(LINE)
     ]
     for c in loads:
         c.start()
@@ -113,47 +124,54 @@
 
     lax.fori_loop(0, NQ, step, 0, unroll=2)
 
-    stores = [pltpu.make_async_copy(stage.at[m], out_refs[m], out_sems.at[m]) for m in range(NSHARD)]
-    for m in range(NSHARD):
+    stores = [
+        pltpu.make_async_copy(stage.at[pl.ds(STARTS[m], PIECES[m])], out_refs[m], out_sems.at[m])
+        for m in range(NPIECE)
+    ]
+    for m in range(NPIECE):
 
         def put(n, carry, m=m):
-            rows = pl.ds(pl.multiple_of(n * BLK, BLK), BLK)
-            src = pl.ds(pl.multiple_of(m * ROWS + n * BLK, BLK), BLK)
-            stage[m, rows, :HD] = (acc[src, :HD] * scale).astype(BF16)
-            stage[m, rows, HD:] = acc[src, HD:].astype(BF16)
+            rows = pl.ds(pl.multiple_of(STARTS[m] + n * BLK, BLK), BLK)
+            stage[rows, :HD] = (acc[rows, :HD] * scale).astype(BF16)
+            stage[rows, HD:] = acc[rows, HD:].astype(BF16)
             return carry
 
-        lax.fori_loop(0, NQ, put, 0, unroll=2)
+        lax.fori_loop(0, PIECES[m] // BLK, put, 0, unroll=2)
         stores[m].start()
     for c in stores:
         c.wait()
 
 
-def attend(table, qd, shards):
-    shard = jax.ShapeDtypeStruct((ROWS, 2 * HD), BF16)
+def attend(table, dealt, shards):
+    pieces = tuple(jax.ShapeDtypeStruct((rows, 2 * HD), BF16) for rows in PIECES)
     vmem = pl.BlockSpec(memory_space=pltpu.VMEM)
-    far = pl.BlockSpec(memory_space=pl.ANY)
+    far = pl.BlockSpec(memory_space=pltpu.HBM)
     out = pl.pallas_call(
         attend_kernel,
         name="attend",
-        out_shape=(jax.ShapeDtypeStruct((ROWS, HD), BF16),) + (shard,) * NSHARD,
+        out_shape=(jax.ShapeDtypeStruct((ROWS, HD), BF16),) + pieces,
         grid_spec=pltpu.PrefetchScalarGridSpec(
             num_scalar_prefetch=1,
             grid=(),
-            in_specs=[vmem] + [far] * NSHARD,
-            out_specs=(vmem,) + (far,) * NSHARD,
+            in_specs=[far] * (NPIECE + 1),
+            out_specs=(vmem,) + (far,) * NPIECE,
             scratch_shapes=[
+                pltpu.VMEM((ROWS, 2 * HD), BF16),
                 pltpu.VMEM((NSHARD * ROWS, 2 * HD), BF16),
                 pltpu.VMEM((NSHARD * ROWS, 2 * HD), F32),
                 pltpu.VMEM((NKEY * BLK, 2 * HD), BF16),
-                pltpu.VMEM((NSHARD, ROWS, 2 * HD), BF16),
-                pltpu.SemaphoreType.DMA((NSHARD,)),
-                pltpu.SemaphoreType.DMA((NSHARD,)),
+                pltpu.VMEM((NSHARD * ROWS, 2 * HD), BF16),
+                pltpu.SemaphoreType.DMA((NPIECE + LINE,)),
+                pltpu.SemaphoreType.DMA((NPIECE,)),
             ],
         ),
         compiler_params=pltpu.CompilerParams(vmem_limit_bytes=56 << 20),
-    )(table, qd, *shards)
+    )(table, dealt, *shards)
     return out[0], out[1:]
+
+
+def after(x, other):
+    return lax.optimization_barrier((x, other))[0]
 
 
 def add(*terms):
@@ -164,12 +182,47 @@
     return lax.all_to_all(x, AXES, 0, 0, axis_index_groups=LINES, tiled=True)
 
 
-def deal(a, b):
-    heads = [
-        jnp.concatenate([a[:, p * HD : (p + 1) * HD], b[:, p * HD : (p + 1) * HD]], axis=1)
-        for p in (0, 1, 2, 0)
-    ]
-    return exchange(jnp.concatenate(heads, axis=0))
+def prepare_kernel(up_hbm, out_w_hbm, k_hbm, v_hbm, q_hbm, o_hbm, up, out_w, k, v, q, o, sems, out_sem):
+    loads = [
+        pltpu.make_async_copy(src, dst, sems.at[m])
+        for m, (src, dst) in enumerate(
+            ((out_w_hbm, out_w), (up_hbm, up), (k_hbm, k), (v_hbm, v), (q_hbm, q))
+        )
+    ]
+    for c in loads:
+        c.start()
+    loads[0].wait()
+    loads[1].wait()
+    ctx = lax.dot_general(
+        up[...], out_w[...], (((1,), (1,)), ((), ())), preferred_element_type=F32
+    ).astype(BF16)
+    for c in loads[2:]:
+        c.wait()
+    for slot, p in enumerate((0, 1, 2, 0)):
+        lanes = slice(p * HD, (p + 1) * HD)
+        o[slot, 0, :, :HD] = k[:, lanes]
+        o[slot, 0, :, HD:] = v[:, lanes]
+        o[slot, 1, :, :HD] = q[:, lanes]
+        o[slot, 1, :, HD:] = ctx[:, lanes]
+    store = pltpu.make_async_copy(o, o_hbm, out_sem)
+    store.start()
+    store.wait()
+
+
+def prepare(upstream_out, out_weight, keys, values, queries):
+    args = (upstream_out, out_weight, keys, values, queries)
+    out = jax.ShapeDtypeStruct((LINE, 2, BLK_DEV * BLK, 2 * HD), BF16)
+    far = pl.BlockSpec(memory_space=pltpu.HBM)
+    return pl.pallas_call(
+        prepare_kernel,
+        name="prepare",
+        out_shape=out,
+        in_specs=[far] * len(args),
+        out_specs=far,
+        scratch_shapes=[pltpu.VMEM(a.shape, BF16) for a in args + (out,)]
+        + [pltpu.SemaphoreType.DMA((len(args),)), pltpu.SemaphoreType.DMA],
+        compiler_params=pltpu.CompilerParams(vmem_limit_bytes=58 << 20),
+    )(*args)
 
 
 def body(queries, keys, values, upstream_out, out_weight, qkv_weight, rand_links, global_links):
@@ -196,24 +249,28 @@
     shard_of = jnp.where(ky == y, 0, 4) + (k_ring - ring) % 4
     table = (shard_of * LINE + k_pos) * BLK_DEV + key % BLK_DEV
 
-    own = deal(keys, values)
+    dealt = exchange(prepare(upstream_out, out_weight, keys, values, queries))
+    own = dealt[:, 0].reshape(ROWS, 2 * HD)
     other = send(own, PAIR)
     next_, last = send(own, RING[3]), send(own, RING[1])
     across = send(own, RING[2])
-    grad_ctx = lax.dot_general(
-        upstream_out, out_weight, (((1,), (1,)), ((), ())), preferred_element_type=F32
-    ).astype(BF16)
-    grad_ctx, other = lax.optimization_barrier((grad_ctx, other))
-    qd = deal(queries, grad_ctx)
-    other_row = [other, send(other, RING[3]), send(across, PAIR), send(other, RING[1])]
-    grad_q, parts = attend(table, qd, [own, next_, across, last] + other_row)
+    pieces = [own, next_, across, last, other, send(other, RING[3])]
+    pieces += [send(across[:HALF], PAIR), send(other[HALF:], RING[2]), send(other, RING[1])]
+    grad_q, parts = attend(table, dealt, pieces)
 
     corner = send(parts[6], PAIR)
-    other_sum = add(parts[4], send(parts[5], RING[1]), send(parts[7], RING[3]))
+    other_sum = [parts[4], send(parts[5], RING[1]), send(parts[8], RING[3])]
+    corner_far = send(parts[7], RING[2])
+    other_sum = jnp.concatenate(
+        [add(*[t[:HALF] for t in other_sum]), add(*[t[HALF:] for t in other_sum], corner_far)]
+    )
+    corner = after(corner, other_sum)
     q_back = exchange(grad_q)
     sides = [send(parts[1], RING[1]), send(parts[3], RING[3])]
     other_sum = send(other_sum, PAIR)
-    across = send(add(parts[2], corner), RING[2])
+    across = send(
+        jnp.concatenate([add(parts[2][:HALF], corner), parts[2][HALF:]], axis=0), RING[2]
+    )
     kv_back = exchange(add(parts[0], *sides, across, other_sum))
 
     def tokens(back, lanes):

time: 193 us -> 202 us (1.047)
  blocking collectives: 14.8 us -> 20.5 us
  waiting for transfers between devices: 56.5 us -> 52 us
  local copies, waits for them, and re-layouts: 5.89 us -> 9.7 us
  Pallas kernels: 23.3 us -> 27 us
  starting transfers between devices: 68.6 us -> 71.6 us
    all_to_all x3 -> x2, waiting for transfers between devices: 15.5 us -> 3.47 us  [exchange(): return lax.all_to_all(x, AXES, 0, 0, axis_index_groups=LINES, tiled=True)]
    ppermute x17 -> x19, waiting for transfers between devices: 40.9 us -> 48.5 us  [send(): return lax.ppermute(x, AXES, perm)]
    ppermute x17 -> x19, starting transfers between devices: 56 us -> 63.2 us  [send(): return lax.ppermute(x, AXES, perm)]
    all_to_all x1, blocking collectives: 14.8 us -> 20.5 us  [exchange(): return lax.all_to_all(x, AXES, 0, 0, axis_index_groups=LINES, tiled=True)]
    pallas_call x0 -> x1, Pallas kernels: none -> 4.65 us  [prepare(): pl.pallas_call(prepare_kernel, name='prepare', out_shape=out, in_specs=[f...]
    all_to_all x3 -> x2, starting transfers between devices: 12.6 us -> 8.38 us  [exchange(): return lax.all_to_all(x, AXES, 0, 0, axis_index_groups=LINES, tiled=True)]
    dot_general x1 -> x0, matrix products: 2.74 us -> none  [body(): lax.dot_general(upstream_out, out_weight, (((1,), (1,)), ((), ())), prefe...]
    convert_element_type x4, other arithmetic: 9.22 us -> 6.87 us  [add(): functools.reduce(lambda a, b: a + b, [t.astype(F32) for t in terms])]
  transfers between devices with their start and end apart: 20 -> 21, of which waited for: 9 -> 7; matrix products, arithmetic and copies ran while one was open for 12% -> 11% of each run, Pallas kernels for 0% -> 0%
where the time goes in v6:
time: 202 us; the launch traced here: 201 us
  starting transfers between devices  71.6 us (35%)
  waiting for transfers between devices  52 us (26%)
  Pallas kernels  27 us (13%)
  blocking collectives  20.5 us (10%)
  other arithmetic  10.1 us (5%)
  local copies, waits for them, and re-layouts  9.7 us (5%)
  matrix products  9.55 us (5%)
    ppermute x19, starting transfers between devices, send(): return lax.ppermute(x, AXES, perm)  63.2 us
    ppermute x19, waiting for transfers between devices, send(): return lax.ppermute(x, AXES, perm)  48.5 us
    pallas_call x1, Pallas kernels, attend(): pl.pallas_call(attend_kernel, name='attend', out_shape=(jax.ShapeDtypeStr...  22.3 us
    all_to_all x1, blocking collectives, exchange(): return lax.all_to_all(x, AXES, 0, 0, axis_index_groups=LINES, tiled=True)  20.5 us
    dot_general x12, matrix products, share(): lax.dot_general(w[j], g, (((1,), (1,)), ((), ())), preferred_element_type...  9.55 us
    all_to_all x2, starting transfers between devices, exchange(): return lax.all_to_all(x, AXES, 0, 0, axis_index_groups=LINES, tiled=True)  8.38 us
    convert_element_type x4, other arithmetic, add(): functools.reduce(lambda a, b: a + b, [t.astype(F32) for t in terms])  6.87 us
    pallas_call x1, Pallas kernels, prepare(): pl.pallas_call(prepare_kernel, name='prepare', out_shape=out, in_specs=[f...  4.65 us
  transfers between devices with their start and end apart: 21, of which 7 were waited for; matrix products, arithmetic and copies ran while one was open for 11% of the time, Pallas kernels for 0%

profile of v6, /device:TPU:1, one launch (start us, length us, event | category | flops | bytes accessed | tf_op | source)
XLA Modules:
  0.0 201.0 jit_solution(13304019639823670417)
XLA Ops:
  0.0 4.6 %prepare.1 = bf16[4,2,512,256]{3,2,1,0:T(8,128)(2,1)} custom-call(bf16[512,1536]{1,0:T(8,128)(2,1)} %up_hbm.1, bf16[384,1536]{1,0:T(8,128)(2,1)} %out_w_hbm.1, bf16[512,384]{1,0:T(8,128)(2,1)} %k_hbm.1, bf16[512,384]{1,0:T(8,128)(2,1)} %v_hbm.1, bf16[512,384]{1,0:T(8,128)(2,1)} %q_hbm.1), custom_call_target="tpu_custom_call" | custom-call | tf_op jit(solution)/shard_map/prepare/pallas_call | solution.py:216
  4.7 20.5 %all_to_all.23.dealt_ref = bf16[4,2,512,256]{3,2,1,0:T(8,128)(2,1)S(1)} all-to-all(bf16[4,2,512,256]{3,2,1,0:T(8,128)(2,1)} %prepare.1), channel_id=1, replica_groups={{0,4,8,12},{1,33,65,97},{2,6,10,14},{3,35,67,99},{5,37,69,101},{7,39,71..., dimensions={0} | all-to-all | bytes 4194304 | tf_op jit(solution)/shard_map/all_to_all | solution.py:182
  25.2 1.4 copy-done.1
  26.5 1.1 slice.155
  27.6 3.2 %collective-permute-start.3 = (bf16[2048,256]{1,0:T(8,128)(2,1)}, bf16[2048,256]{1,0:T(8,128)(2,1)}, u32[]{:S(2)}, u32[]{:S(2)}) collective-permute-start(bf16[2048,256]{1,0:T(8,128)(2,1)} %bitcast.2.refs_0_), channel_id=1, source_target_pairs={{0,16},{1,17},{2,18},{3,19},{4,20},{5,21},{6,22},{7,23},{8,24},{9,... | collective-permute-start | bytes 3145736 | tf_op jit(solution)/shard_map/ppermute | solution.py:65
  30.8 5.2 %collective-permute-start.1 = (bf16[2048,256]{1,0:T(8,128)(2,1)}, bf16[2048,256]{1,0:T(8,128)(2,1)}, u32[]{:S(2)}, u32[]{:S(2)}) collective-permute-start(bf16[2048,256]{1,0:T(8,128)(2,1)} %bitcast.2.refs_0_), channel_id=1, source_target_pairs={{0,64},{1,9},{2,66},{3,11},{4,68},{5,13},{6,70},{7,15},{8,72},{9,1... | collective-permute-start | bytes 3145736 | tf_op jit(solution)/shard_map/ppermute | solution.py:65
  36.0 2.3 %collective-permute-start = (bf16[2048,256]{1,0:T(8,128)(2,1)}, bf16[2048,256]{1,0:T(8,128)(2,1)}, u32[]{:S(2)}, u32[]{:S(2)}) collective-permute-start(bf16[2048,256]{1,0:T(8,128)(2,1)} %bitcast.2.refs_0_), channel_id=1, source_target_pairs={{0,96},{1,13},{2,98},{3,15},{4,100},{5,1},{6,102},{7,3},{8,104},{9... | collective-permute-start | bytes 3145736 | tf_op jit(solution)/shard_map/ppermute | solution.py:65
  38.4 2.9 %collective-permute-start.2 = (bf16[2048,256]{1,0:T(8,128)(2,1)}, bf16[2048,256]{1,0:T(8,128)(2,1)}, u32[]{:S(2)}, u32[]{:S(2)}) collective-permute-start(bf16[2048,256]{1,0:T(8,128)(2,1)} %bitcast.2.refs_0_), channel_id=1, source_target_pairs={{0,32},{1,5},{2,34},{3,7},{4,36},{5,9},{6,38},{7,11},{8,40},{9,13}... | collective-permute-start | bytes 3145736 | tf_op jit(solution)/shard_map/ppermute | solution.py:65
  41.3 10.3 %collective-permute-done.3.refs_4_ = bf16[2048,256]{1,0:T(8,128)(2,1)} collective-permute-done((bf16[2048,256]{1,0:T(8,128)(2,1)}, bf16[2048,256]{1,0:T(8,128)(2,1)}, u32[]{:S(2)}, u32[]{:S(2)}) %collective-permute-start.3) | collective-permute-done | bytes 1048608 | tf_op jit(solution)/shard_map/ppermute | solution.py:65
  51.6 1.9 collective-permute-start.4
  53.6 4.3 %collective-permute-start.7 = (bf16[2048,256]{1,0:T(8,128)(2,1)}, bf16[2048,256]{1,0:T(8,128)(2,1)}, u32[]{:S(2)}, u32[]{:S(2)}) collective-permute-start(bf16[2048,256]{1,0:T(8,128)(2,1)} %collective-permute-done.3.refs_4_), channel_id=1, source_target_pairs={{0,32},{1,5},{2,34},{3,7},{4,36},{5,9},{6,38},{7,11},{8,40},{9,13}... | collective-permute-start | bytes 3145736 | tf_op jit(solution)/shard_map/ppermute | solution.py:65
  59.0 1.1 slice.156
  60.1 3.2 %collective-permute-start.5 = (bf16[1024,256]{1,0:T(8,128)(2,1)S(1)}, bf16[1024,256]{1,0:T(8,128)(2,1)S(1)}, u32[]{:S(2)}, u32[]{:S(2)}) collective-permute-start(bf16[1024,256]{1,0:T(8,128)(2,1)S(1)} %slice.156), channel_id=1, source_target_pairs={{0,16},{1,17},{2,18},{3,19},{4,20},{5,21},{6,22},{7,23},{8,24},{9,... | collective-permute-start | bytes 1572872 | tf_op jit(solution)/shard_map/ppermute | solution.py:65
  63.3 1.1 slice.157
  64.4 7.2 %collective-permute-start.6 = (bf16[1024,256]{1,0:T(8,128)(2,1)S(1)}, bf16[1024,256]{1,0:T(8,128)(2,1)S(1)}, u32[]{:S(2)}, u32[]{:S(2)}) collective-permute-start(bf16[1024,256]{1,0:T(8,128)(2,1)S(1)} %slice.157), channel_id=1, source_target_pairs={{0,64},{1,9},{2,66},{3,11},{4,68},{5,13},{6,70},{7,15},{8,72},{9,1... | collective-permute-start | bytes 1572872 | tf_op jit(solution)/shard_map/ppermute | solution.py:65
  72.4 8.8 %collective-permute-done.6.refs_7_ = bf16[1024,256]{1,0:T(8,128)(2,1)S(1)} collective-permute-done((bf16[1024,256]{1,0:T(8,128)(2,1)S(1)}, bf16[1024,256]{1,0:T(8,128)(2,1)S(1)}, u32[]{:S(2)}, u32[]{:S(2)}) %collective-permute-start.6) | collective-permute-done | bytes 524320 | tf_op jit(solution)/shard_map/ppermute | solution.py:65
  81.2 0.8 copy-done.7
  81.9 22.3 %attend.1 = (bf16[2048,128]{1,0:T(8,128)(2,1)}, bf16[2048,256]{1,0:T(8,128)(2,1)}, bf16[2048,256]{1,0:T(8,128)(2,1)}, bf16[2048,256]{1,0:T(8,128)(2,1)}, bf16[20...) custom-call(s32[16,8]{1,0:T(8,128)} %fusion.18.table, ...), custom_call_target="tpu_custom_call" | custom-call | tf_op jit(solution)/shard_map/attend/pallas_call | solution.py:149
  104.3 1.9 collective-permute-start.12
  106.2 3.4 %collective-permute-start.11 = (bf16[2048,256]{1,0:T(8,128)(2,1)}, bf16[2048,256]{1,0:T(8,128)(2,1)S(1)}, u32[]{:S(2)}, u32[]{:S(2)}) collective-permute-start(bf16[2048,256]{1,0:T(8,128)(2,1)} %get-tuple-element.23), channel_id=1, source_target_pairs={{0,32},{1,5},{2,34},{3,7},{4,36},{5,9},{6,38},{7,11},{8,40},{9,13}... | collective-permute-start | bytes 3145736 | tf_op jit(solution)/shard_map/ppermute | solution.py:65
  109.6 2.3 %collective-permute-start.13 = (bf16[1024,256]{1,0:T(8,128)(2,1)}, bf16[1024,256]{1,0:T(8,128)(2,1)S(1)}, u32[]{:S(2)}, u32[]{:S(2)}) collective-permute-start(bf16[1024,256]{1,0:T(8,128)(2,1)} %get-tuple-element.25), channel_id=1, source_target_pairs={{0,64},{1,9},{2,66},{3,11},{4,68},{5,13},{6,70},{7,15},{8,72},{9,1... | collective-permute-start | bytes 1572872 | tf_op jit(solution)/shard_map/ppermute | solution.py:65
  111.9 1.1 slice.138
  113.0 3.0 %collective-permute-start.10 = (bf16[1024,256]{1,0:T(8,128)(2,1)}, bf16[1024,256]{1,0:T(8,128)(2,1)S(1)}, u32[]{:S(2)}, u32[]{:S(2)}) collective-permute-start(bf16[1024,256]{1,0:T(8,128)(2,1)} %get-tuple-element.21), channel_id=1, source_target_pairs={{0,16},{1,17},{2,18},{3,19},{4,20},{5,21},{6,22},{7,23},{8,24},{9,... | collective-permute-start | bytes 1572872 | tf_op jit(solution)/shard_map/ppermute | solution.py:65
  115.9 4.3 %collective-permute-start.9 = (bf16[2048,256]{1,0:T(8,128)(2,1)}, bf16[2048,256]{1,0:T(8,128)(2,1)}, u32[]{:S(2)}, u32[]{:S(2)}) collective-permute-start(bf16[2048,256]{1,0:T(8,128)(2,1)} %get-tuple-element.19), channel_id=1, source_target_pairs={{0,96},{1,13},{2,98},{3,15},{4,100},{5,1},{6,102},{7,3},{8,104},{9... | collective-permute-start | bytes 3145736 | tf_op jit(solution)/shard_map/ppermute | solution.py:65
  120.2 8.0 %collective-permute-done.13 = bf16[1024,256]{1,0:T(8,128)(2,1)S(1)} collective-permute-done((bf16[1024,256]{1,0:T(8,128)(2,1)}, bf16[1024,256]{1,0:T(8,128)(2,1)S(1)}, u32[]{:S(2)}, u32[]{:S(2)}) %collective-permute-start.13) | collective-permute-done | bytes 524320 | tf_op jit(solution)/shard_map/ppermute | solution.py:65
  128.3 1.9 collective-permute-start.8
  130.2 1.7 add_convert_fusion.3
  131.9 1.2 pad_maximum_fusion
  133.1 2.4 %collective-permute-start.15 = (bf16[2048,256]{1,0:T(8,128)(2,1)}, bf16[2048,256]{1,0:T(8,128)(2,1)}, u32[]{:S(2)}, u32[]{:S(2)}) collective-permute-start(bf16[2048,256]{1,0:T(8,128)(2,1)} %pad_maximum_fusion), channel_id=1, source_target_pairs={{0,16},{1,17},{2,18},{3,19},{4,20},{5,21},{6,22},{7,23},{8,24},{9,... | collective-permute-start | bytes 3145736 | tf_op jit(solution)/shard_map/ppermute | solution.py:65
  135.7 1.1 pad_maximum_fusion.1
  136.8 5.2 %collective-permute-start.14 = (bf16[2048,256]{1,0:T(8,128)(2,1)}, bf16[2048,256]{1,0:T(8,128)(2,1)}, u32[]{:S(2)}, u32[]{:S(2)}) collective-permute-start(bf16[2048,256]{1,0:T(8,128)(2,1)} %pad_maximum_fusion.1), channel_id=1, source_target_pairs={{0,64},{1,9},{2,66},{3,11},{4,68},{5,13},{6,70},{7,15},{8,72},{9,1... | collective-permute-start | bytes 3145736 | tf_op jit(solution)/shard_map/ppermute | solution.py:65
  142.0 4.1 %all-to-all-start.1 = ((bf16[4,512,128]{2,1,0:T(8,128)(2,1)}), bf16[4,512,128]{2,1,0:T(8,128)(2,1)}, u32[]{:S(2)}, u32[]{:S(2)}) async-start(bf16[4,512,128]{2,1,0:T(8,128)(2,1)} %bitcast.73), calls=%async_computation.1 | async-start | bytes 1048576 | tf_op jit(solution)/shard_map/all_to_all | solution.py:182
  146.2 10.8 %collective-permute-done.15 = bf16[2048,256]{1,0:T(8,128)(2,1)} collective-permute-done((bf16[2048,256]{1,0:T(8,128)(2,1)}, bf16[2048,256]{1,0:T(8,128)(2,1)}, u32[]{:S(2)}, u32[]{:S(2)}) %collective-permute-start.15) | collective-permute-done | bytes 1048608 | tf_op jit(solution)/shard_map/ppermute | solution.py:65
  157.0 2.6 %collective-permute-done.14 = bf16[2048,256]{1,0:T(8,128)(2,1)} collective-permute-done((bf16[2048,256]{1,0:T(8,128)(2,1)}, bf16[2048,256]{1,0:T(8,128)(2,1)}, u32[]{:S(2)}, u32[]{:S(2)}) %collective-permute-start.14) | collective-permute-done | bytes 1048608 | tf_op jit(solution)/shard_map/ppermute | solution.py:65
  159.6 4.1 %add_convert_fusion = bf16[2048,256]{1,0:T(8,128)(2,1)} fusion(bf16[2048,256]{1,0:T(8,128)(2,1)} %collective-permute-done.15, bf16[2048,256]{1,0:T(8,128)(2,1)} %collective-permute-done.14, bf16[2048,256]{1,0:T(8,128)(2,1)} %collective-permute-done.9, bf16[2048,256]{1,0:T(8,128)(2,1)} %collective-permute-done.8, bf16[2048,256]{1,0:T(8,128)(2,1)} %get-tuple-element.17), kind=kLoop, calls=%fused_computation | loop fusion | flops 5242880 | bytes 6291456 | tf_op jit(solution)/shard_map/convert_element_type | solution.py:178
  163.7 4.2 %all-to-all-start.2 = ((bf16[4,512,256]{2,1,0:T(8,128)(2,1)}), bf16[4,512,256]{2,1,0:T(8,128)(2,1)}, u32[]{:S(2)}, u32[]{:S(2)}) async-start(bf16[4,512,256]{2,1,0:T(8,128)(2,1)} %bitcast.72), calls=%async_computation.2 | async-start | bytes 2097152 | tf_op jit(solution)/shard_map/all_to_all | solution.py:182
  168.0 1.1 slice_bitcast_fusion.8
  169.1 1.3 fusion.6
  170.4 1.3 fusion.7
  171.7 1.3 fusion.9
  173.0 1.3 fusion.8
  174.3 3.5 %all-to-all-done.2 = bf16[4,512,256]{2,1,0:T(8,128)(2,1)} async-done(((bf16[4,512,256]{2,1,0:T(8,128)(2,1)}), bf16[4,512,256]{2,1,0:T(8,128)(2,1)}, u32[]{:S(2)}, u32[]{:S(2)}) %all-to-all-start.2) | async-done | bytes 1048608 | tf_op jit(solution)/shard_map/all_to_all | solution.py:182
  177.8 1.3 slice_bitcast_fusion.2
  179.1 1.5 convolution_add_fusion.1
  181.1 5.5 %collective-permute-start.17 = (bf16[384,512]{1,0:T(8,128)(2,1)S(1)}, bf16[384,512]{1,0:T(8,128)(2,1)S(1)}, u32[]{:S(2)}, u32[]{:S(2)}) collective-permute-start(bf16[384,512]{1,0:T(8,128)(2,1)S(1)} %fusion.5), channel_id=1, source_target_pairs={{0,1},{1,0},{2,3},{3,2},{4,5},{5,4},{6,7},{7,6},{8,9},{9,8},{10,11... | collective-permute-start | bytes 1179656 | tf_op jit(solution)/shard_map/ppermute | solution.py:65
  188.3 3.0 %collective-permute-start.18 = (bf16[384,512]{1,0:T(8,128)(2,1)S(1)}, bf16[384,512]{1,0:T(8,128)(2,1)S(1)}, u32[]{:S(2)}, u32[]{:S(2)}) collective-permute-start(bf16[384,512]{1,0:T(8,128)(2,1)S(1)} %add_convert_fusion.5), channel_id=1, source_target_pairs={{0,2},{1,3},{2,0},{3,1},{4,6},{5,7},{6,4},{7,5},{8,10},{9,11},{10,... | collective-permute-start | bytes 1179656 | tf_op jit(solution)/shard_map/ppermute | solution.py:65
  192.1 8.0 %collective-permute-done.18 = bf16[384,512]{1,0:T(8,128)(2,1)S(1)} collective-permute-done((bf16[384,512]{1,0:T(8,128)(2,1)S(1)}, bf16[384,512]{1,0:T(8,128)(2,1)S(1)}, u32[]{:S(2)}, u32[]{:S(2)}) %collective-permute-start.18) | collective-permute-done | bytes 393248 | tf_op jit(solution)/shard_map/ppermute | solution.py:65
  200.1 0.9 add_convert_fusion.4
  (47 shorter events, 5.0 us)
Async XLA Ops:
  0.0 169.1 %copy-start = (bf16[3,1536,384]{2,1,0:T(8,128)(2,1)S(1)}, bf16[3,1536,384]{2,1,0:T(8,128)(2,1)}, u32[]{:S(2)}) copy-start(bf16[3,1536,384]{2,1,0:T(8,128)(2,1)} %param.13) | copy-start | bytes 10616836
  4.7 53.4 %copy-start.8 = (s32[128,3]{0,1:T(4,128)S(1)}, s32[128,3]{0,1:T(4,128)}, u32[]{:S(2)}) copy-start(s32[128,3]{0,1:T(4,128)} %param.14) | copy-start | bytes 4612
  25.2 1.4 copy-start.1
  27.6 24.0 %collective-permute-start.3 = (bf16[2048,256]{1,0:T(8,128)(2,1)}, bf16[2048,256]{1,0:T(8,128)(2,1)}, u32[]{:S(2)}, u32[]{:S(2)}) collective-permute-start(bf16[2048,256]{1,0:T(8,128)(2,1)} %bitcast.2.refs_0_), channel_id=1, source_target_pairs={{0,16},{1,17},{2,18},{3,19},{4,20},{5,21},{6,22},{7,23},{8,24},{9,... | collective-permute-start | bytes 3145736 | tf_op jit(solution)/shard_map/ppermute | solution.py:65
  30.8 28.2 %collective-permute-start.1 = (bf16[2048,256]{1,0:T(8,128)(2,1)}, bf16[2048,256]{1,0:T(8,128)(2,1)}, u32[]{:S(2)}, u32[]{:S(2)}) collective-permute-start(bf16[2048,256]{1,0:T(8,128)(2,1)} %bitcast.2.refs_0_), channel_id=1, source_target_pairs={{0,64},{1,9},{2,66},{3,11},{4,68},{5,13},{6,70},{7,15},{8,72},{9,1... | collective-permute-start | bytes 3145736 | tf_op jit(solution)/shard_map/ppermute | solution.py:65
  36.0 28.3 %collective-permute-start = (bf16[2048,256]{1,0:T(8,128)(2,1)}, bf16[2048,256]{1,0:T(8,128)(2,1)}, u32[]{:S(2)}, u32[]{:S(2)}) collective-permute-start(bf16[2048,256]{1,0:T(8,128)(2,1)} %bitcast.2.refs_0_), channel_id=1, source_target_pairs={{0,96},{1,13},{2,98},{3,15},{4,100},{5,1},{6,102},{7,3},{8,104},{9... | collective-permute-start | bytes 3145736 | tf_op jit(solution)/shard_map/ppermute | solution.py:65
  38.4 34.0 %collective-permute-start.2 = (bf16[2048,256]{1,0:T(8,128)(2,1)}, bf16[2048,256]{1,0:T(8,128)(2,1)}, u32[]{:S(2)}, u32[]{:S(2)}) collective-permute-start(bf16[2048,256]{1,0:T(8,128)(2,1)} %bitcast.2.refs_0_), channel_id=1, source_target_pairs={{0,32},{1,5},{2,34},{3,7},{4,36},{5,9},{6,38},{7,11},{8,40},{9,13}... | collective-permute-start | bytes 3145736 | tf_op jit(solution)/shard_map/ppermute | solution.py:65
  51.6 29.5 %collective-permute-start.4 = (bf16[2048,256]{1,0:T(8,128)(2,1)}, bf16[2048,256]{1,0:T(8,128)(2,1)}, u32[]{:S(2)}, u32[]{:S(2)}) collective-permute-start(bf16[2048,256]{1,0:T(8,128)(2,1)} %collective-permute-done.3.refs_4_), channel_id=1, source_target_pairs={{0,96},{1,13},{2,98},{3,15},{4,100},{5,1},{6,102},{7,3},{8,104},{9... | collective-permute-start | bytes 3145736 | tf_op jit(solution)/shard_map/ppermute | solution.py:65
  53.6 27.6 %collective-permute-start.7 = (bf16[2048,256]{1,0:T(8,128)(2,1)}, bf16[2048,256]{1,0:T(8,128)(2,1)}, u32[]{:S(2)}, u32[]{:S(2)}) collective-permute-start(bf16[2048,256]{1,0:T(8,128)(2,1)} %collective-permute-done.3.refs_4_), channel_id=1, source_target_pairs={{0,32},{1,5},{2,34},{3,7},{4,36},{5,9},{6,38},{7,11},{8,40},{9,13}... | collective-permute-start | bytes 3145736 | tf_op jit(solution)/shard_map/ppermute | solution.py:65
  60.1 12.3 %collective-permute-start.5 = (bf16[1024,256]{1,0:T(8,128)(2,1)S(1)}, bf16[1024,256]{1,0:T(8,128)(2,1)S(1)}, u32[]{:S(2)}, u32[]{:S(2)}) collective-permute-start(bf16[1024,256]{1,0:T(8,128)(2,1)S(1)} %slice.156), channel_id=1, source_target_pairs={{0,16},{1,17},{2,18},{3,19},{4,20},{5,21},{6,22},{7,23},{8,24},{9,... | collective-permute-start | bytes 1572872 | tf_op jit(solution)/shard_map/ppermute | solution.py:65
  64.4 16.7 %collective-permute-start.6 = (bf16[1024,256]{1,0:T(8,128)(2,1)S(1)}, bf16[1024,256]{1,0:T(8,128)(2,1)S(1)}, u32[]{:S(2)}, u32[]{:S(2)}) collective-permute-start(bf16[1024,256]{1,0:T(8,128)(2,1)S(1)} %slice.157), channel_id=1, source_target_pairs={{0,64},{1,9},{2,66},{3,11},{4,68},{5,13},{6,70},{7,15},{8,72},{9,1... | collective-permute-start | bytes 1572872 | tf_op jit(solution)/shard_map/ppermute | solution.py:65
  72.4 8.8 %copy-start.6 = (bf16[1024,256]{1,0:T(8,128)(2,1)}, bf16[1024,256]{1,0:T(8,128)(2,1)S(1)}, u32[]{:S(2)}) copy-start(bf16[1024,256]{1,0:T(8,128)(2,1)S(1)} %collective-permute-done.5.refs_6_) | copy-start | bytes 1572868
  81.1 0.8 copy-start.7
  104.3 25.9 %collective-permute-start.12 = (bf16[2048,256]{1,0:T(8,128)(2,1)}, bf16[2048,256]{1,0:T(8,128)(2,1)S(1)}, u32[]{:S(2)}, u32[]{:S(2)}) collective-permute-start(bf16[2048,256]{1,0:T(8,128)(2,1)} %get-tuple-element.24), channel_id=1, source_target_pairs={{0,96},{1,13},{2,98},{3,15},{4,100},{5,1},{6,102},{7,3},{8,104},{9... | collective-permute-start | bytes 3145736 | tf_op jit(solution)/shard_map/ppermute | solution.py:65
  106.2 24.0 %collective-permute-start.11 = (bf16[2048,256]{1,0:T(8,128)(2,1)}, bf16[2048,256]{1,0:T(8,128)(2,1)S(1)}, u32[]{:S(2)}, u32[]{:S(2)}) collective-permute-start(bf16[2048,256]{1,0:T(8,128)(2,1)} %get-tuple-element.23), channel_id=1, source_target_pairs={{0,32},{1,5},{2,34},{3,7},{4,36},{5,9},{6,38},{7,11},{8,40},{9,13}... | collective-permute-start | bytes 3145736 | tf_op jit(solution)/shard_map/ppermute | solution.py:65
  109.6 18.7 %collective-permute-start.13 = (bf16[1024,256]{1,0:T(8,128)(2,1)}, bf16[1024,256]{1,0:T(8,128)(2,1)S(1)}, u32[]{:S(2)}, u32[]{:S(2)}) collective-permute-start(bf16[1024,256]{1,0:T(8,128)(2,1)} %get-tuple-element.25), channel_id=1, source_target_pairs={{0,64},{1,9},{2,66},{3,11},{4,68},{5,13},{6,70},{7,15},{8,72},{9,1... | collective-permute-start | bytes 1572872 | tf_op jit(solution)/shard_map/ppermute | solution.py:65
  112.9 22.6 %copy-start.2 = (bf16[2048,256]{1,0:T(8,128)(2,1)S(1)}, bf16[2048,256]{1,0:T(8,128)(2,1)}, u32[]{:S(2)}) copy-start(bf16[2048,256]{1,0:T(8,128)(2,1)} %get-tuple-element.20) | copy-start | bytes 3145732
  113.0 22.6 %collective-permute-start.10 = (bf16[1024,256]{1,0:T(8,128)(2,1)}, bf16[1024,256]{1,0:T(8,128)(2,1)S(1)}, u32[]{:S(2)}, u32[]{:S(2)}) collective-permute-start(bf16[1024,256]{1,0:T(8,128)(2,1)} %get-tuple-element.21), channel_id=1, source_target_pairs={{0,16},{1,17},{2,18},{3,19},{4,20},{5,21},{6,22},{7,23},{8,24},{9,... | collective-permute-start | bytes 1572872 | tf_op jit(solution)/shard_map/ppermute | solution.py:65
  115.9 30.2 %collective-permute-start.9 = (bf16[2048,256]{1,0:T(8,128)(2,1)}, bf16[2048,256]{1,0:T(8,128)(2,1)}, u32[]{:S(2)}, u32[]{:S(2)}) collective-permute-start(bf16[2048,256]{1,0:T(8,128)(2,1)} %get-tuple-element.19), channel_id=1, source_target_pairs={{0,96},{1,13},{2,98},{3,15},{4,100},{5,1},{6,102},{7,3},{8,104},{9... | collective-permute-start | bytes 3145736 | tf_op jit(solution)/shard_map/ppermute | solution.py:65
  128.3 17.9 %collective-permute-start.8 = (bf16[2048,256]{1,0:T(8,128)(2,1)}, bf16[2048,256]{1,0:T(8,128)(2,1)}, u32[]{:S(2)}, u32[]{:S(2)}) collective-permute-start(bf16[2048,256]{1,0:T(8,128)(2,1)} %get-tuple-element.18), channel_id=1, source_target_pairs={{0,32},{1,5},{2,34},{3,7},{4,36},{5,9},{6,38},{7,11},{8,40},{9,13}... | collective-permute-start | bytes 3145736 | tf_op jit(solution)/shard_map/ppermute | solution.py:65
  133.1 23.9 %collective-permute-start.15 = (bf16[2048,256]{1,0:T(8,128)(2,1)}, bf16[2048,256]{1,0:T(8,128)(2,1)}, u32[]{:S(2)}, u32[]{:S(2)}) collective-permute-start(bf16[2048,256]{1,0:T(8,128)(2,1)} %pad_maximum_fusion), channel_id=1, source_target_pairs={{0,16},{1,17},{2,18},{3,19},{4,20},{5,21},{6,22},{7,23},{8,24},{9,... | collective-permute-start | bytes 3145736 | tf_op jit(solution)/shard_map/ppermute | solution.py:65
  136.8 22.8 %collective-permute-start.14 = (bf16[2048,256]{1,0:T(8,128)(2,1)}, bf16[2048,256]{1,0:T(8,128)(2,1)}, u32[]{:S(2)}, u32[]{:S(2)}) collective-permute-start(bf16[2048,256]{1,0:T(8,128)(2,1)} %pad_maximum_fusion.1), channel_id=1, source_target_pairs={{0,64},{1,9},{2,66},{3,11},{4,68},{5,13},{6,70},{7,15},{8,72},{9,1... | collective-permute-start | bytes 3145736 | tf_op jit(solution)/shard_map/ppermute | solution.py:65
  142.0 21.7 %all-to-all-start.1 = ((bf16[4,512,128]{2,1,0:T(8,128)(2,1)}), bf16[4,512,128]{2,1,0:T(8,128)(2,1)}, u32[]{:S(2)}, u32[]{:S(2)}) async-start(bf16[4,512,128]{2,1,0:T(8,128)(2,1)} %bitcast.73), calls=%async_computation.1 | async-start | bytes 1048576 | tf_op jit(solution)/shard_map/all_to_all | solution.py:182
  163.7 14.0 %all-to-all-start.2 = ((bf16[4,512,256]{2,1,0:T(8,128)(2,1)}), bf16[4,512,256]{2,1,0:T(8,128)(2,1)}, u32[]{:S(2)}, u32[]{:S(2)}) async-start(bf16[4,512,256]{2,1,0:T(8,128)(2,1)} %bitcast.72), calls=%async_computation.2 | async-start | bytes 2097152 | tf_op jit(solution)/shard_map/all_to_all | solution.py:182
  177.8 8.8 %copy-start.5 = (f32[384,512]{1,0:T(8,128)S(1)}, f32[384,512]{1,0:T(8,128)}, u32[]{:S(2)}) copy-start(f32[384,512]{1,0:T(8,128)} %fusion.8) | copy-start | bytes 2359300
  180.6 6.8 %copy-start.4 = (f32[384,512]{1,0:T(8,128)S(1)}, f32[384,512]{1,0:T(8,128)}, u32[]{:S(2)}) copy-start(f32[384,512]{1,0:T(8,128)} %fusion.7) | copy-start | bytes 2359300
  181.1 6.8 %collective-permute-start.17 = (bf16[384,512]{1,0:T(8,128)(2,1)S(1)}, bf16[384,512]{1,0:T(8,128)(2,1)S(1)}, u32[]{:S(2)}, u32[]{:S(2)}) collective-permute-start(bf16[384,512]{1,0:T(8,128)(2,1)S(1)} %fusion.5), channel_id=1, source_target_pairs={{0,1},{1,0},{2,3},{3,2},{4,5},{5,4},{6,7},{7,6},{8,9},{9,8},{10,11... | collective-permute-start | bytes 1179656 | tf_op jit(solution)/shard_map/ppermute | solution.py:65
  186.9 4.3 %copy-start.3 = (f32[384,512]{1,0:T(8,128)S(1)}, f32[384,512]{1,0:T(8,128)}, u32[]{:S(2)}) copy-start(f32[384,512]{1,0:T(8,128)} %fusion.9) | copy-start | bytes 2359300
  187.4 4.7 %collective-permute-start.16 = (bf16[384,512]{1,0:T(8,128)(2,1)S(1)}, bf16[384,512]{1,0:T(8,128)(2,1)S(1)}, u32[]{:S(2)}, u32[]{:S(2)}) collective-permute-start(bf16[384,512]{1,0:T(8,128)(2,1)S(1)} %fusion.2), channel_id=1, source_target_pairs={{0,1},{1,0},{2,3},{3,2},{4,5},{5,4},{6,7},{7,6},{8,9},{9,8},{10,11... | collective-permute-start | bytes 1179656 | tf_op jit(solution)/shard_map/ppermute | solution.py:65
  188.3 11.8 %collective-permute-start.18 = (bf16[384,512]{1,0:T(8,128)(2,1)S(1)}, bf16[384,512]{1,0:T(8,128)(2,1)S(1)}, u32[]{:S(2)}, u32[]{:S(2)}) collective-permute-start(bf16[384,512]{1,0:T(8,128)(2,1)S(1)} %add_convert_fusion.5), channel_id=1, source_target_pairs={{0,2},{1,3},{2,0},{3,1},{4,6},{5,7},{6,4},{7,5},{8,10},{9,11},{10,... | collective-permute-start | bytes 1179656 | tf_op jit(solution)/shard_map/ppermute | solution.py:65

commit v7 on v4

--- a/solution.py
+++ b/solution.py
@@ -64,7 +64,7 @@
 def attend_kernel(table, qd_ref, *refs):
     kv_refs, gq_ref = refs[:NSHARD], refs[NSHARD]
     out_refs = refs[NSHARD + 1 : 2 * NSHARD + 1]
-    kv, acc, kv_now, stage, in_sems, out_sems = refs[2 * NSHARD + 1 :]
+    kv, acc, kv_now, in_sems, out_sems = refs[2 * NSHARD + 1 :]
     scale = HD ** (-0.5)
     loads = [
         pltpu.make_async_copy(kv_refs[m], kv.at[pl.ds(m * ROWS, ROWS)], in_sems.at[m])
@@ -111,16 +111,18 @@
             acc[pl.ds(at[j], BLK), HD:] += gv[part]
         return carry
 
-    lax.fori_loop(0, NQ, step, 0, unroll=2)
-
-    stores = [pltpu.make_async_copy(stage.at[m], out_refs[m], out_sems.at[m]) for m in range(NSHARD)]
+    lax.fori_loop(0, NQ, step, 0, unroll=4)
+
+    stores = [
+        pltpu.make_async_copy(kv.at[pl.ds(m * ROWS, ROWS)], out_refs[m], out_sems.at[m])
+        for m in range(NSHARD)
+    ]
     for m in range(NSHARD):
 
         def put(n, carry, m=m):
-            rows = pl.ds(pl.multiple_of(n * BLK, BLK), BLK)
-            src = pl.ds(pl.multiple_of(m * ROWS + n * BLK, BLK), BLK)
-            stage[m, rows, :HD] = (acc[src, :HD] * scale).astype(BF16)
-            stage[m, rows, HD:] = acc[src, HD:].astype(BF16)
+            rows = pl.ds(pl.multiple_of(m * ROWS + n * BLK, BLK), BLK)
+            kv[rows, :HD] = (acc[rows, :HD] * scale).astype(BF16)
+            kv[rows, HD:] = acc[rows, HD:].astype(BF16)
             return carry
 
         lax.fori_loop(0, NQ, put, 0, unroll=2)
@@ -146,12 +148,11 @@
                 pltpu.VMEM((NSHARD * ROWS, 2 * HD), BF16),
                 pltpu.VMEM((NSHARD * ROWS, 2 * HD), F32),
                 pltpu.VMEM((NKEY * BLK, 2 * HD), BF16),
-                pltpu.VMEM((NSHARD, ROWS, 2 * HD), BF16),
                 pltpu.SemaphoreType.DMA((NSHARD,)),
                 pltpu.SemaphoreType.DMA((NSHARD,)),
             ],
         ),
-        compiler_params=pltpu.CompilerParams(vmem_limit_bytes=56 << 20),
+        compiler_params=pltpu.CompilerParams(vmem_limit_bytes=32 << 20),
     )(table, qd, *shards)
     return out[0], out[1:]
 

time: 193 us -> 190 us (0.984)
  Pallas kernels: 23.3 us -> 20.4 us
    pallas_call x1, Pallas kernels: 23.3 us -> 20.4 us  [attend(): pl.pallas_call(attend_kernel, name='attend', out_shape=(jax.ShapeDtypeStr...]
where the time goes in v7:
time: 190 us; the launch traced here: 189 us
  starting transfers between devices  68.7 us (36%)
  waiting for transfers between devices  58.1 us (31%)
  Pallas kernels  20.4 us (11%)
  blocking collectives  14.8 us (8%)
  matrix products  11.1 us (6%)
  other arithmetic  9.57 us (5%)
  local copies, waits for them, and re-layouts  5.89 us (3%)
    ppermute x17, starting transfers between devices, send(): return lax.ppermute(x, AXES, perm)  56 us
    ppermute x17, waiting for transfers between devices, send(): return lax.ppermute(x, AXES, perm)  42 us
    pallas_call x1, Pallas kernels, attend(): pl.pallas_call(attend_kernel, name='attend', out_shape=(jax.ShapeDtypeStr...  20.4 us
    all_to_all x3, waiting for transfers between devices, exchange(): return lax.all_to_all(x, AXES, 0, 0, axis_index_groups=LINES, tiled=True)  16.1 us
    all_to_all x1, blocking collectives, exchange(): return lax.all_to_all(x, AXES, 0, 0, axis_index_groups=LINES, tiled=True)  14.8 us
    all_to_all x3, starting transfers between devices, exchange(): return lax.all_to_all(x, AXES, 0, 0, axis_index_groups=LINES, tiled=True)  12.7 us
    dot_general x12, matrix products, share(): lax.dot_general(w[j], g, (((1,), (1,)), ((), ())), preferred_element_type...  8.38 us
    convert_element_type x4, other arithmetic, add(): functools.reduce(lambda a, b: a + b, [t.astype(F32) for t in terms])  7.97 us
  transfers between devices with their start and end apart: 20, of which 9 were waited for; matrix products, arithmetic and copies ran while one was open for 12% of the time, Pallas kernels for 0%

profile of v7, /device:TPU:1, one launch (start us, length us, event | category | flops | bytes accessed | tf_op | source)
XLA Modules:
  0.0 189.0 jit_solution(2572491408707301685)
XLA Ops:
  0.0 1.4 fusion.39
  1.5 14.8 %all_to_all.40 = bf16[4,512,256]{2,1,0:T(8,128)(2,1)} all-to-all(bf16[4,512,256]{2,1,0:T(8,128)(2,1)S(1)} %bitcast.79), channel_id=1, replica_groups={{0,4,8,12},{1,33,65,97},{2,6,10,14},{3,35,67,99},{5,37,69,101},{7,39,71..., dimensions={0} | all-to-all | bytes 2097152 | tf_op jit(solution)/shard_map/all_to_all | solution.py:165
  16.3 3.2 %collective-permute-start = (bf16[2048,256]{1,0:T(8,128)(2,1)}, bf16[2048,256]{1,0:T(8,128)(2,1)}, u32[]{:S(2)}, u32[]{:S(2)}) collective-permute-start(bf16[2048,256]{1,0:T(8,128)(2,1)} %bitcast.3.refs_0_), channel_id=1, source_target_pairs={{0,16},{1,17},{2,18},{3,19},{4,20},{5,21},{6,22},{7,23},{8,24},{9,... | collective-permute-start | bytes 3145736 | tf_op jit(solution)/shard_map/ppermute | solution.py:61
  19.5 5.2 %collective-permute-start.2 = (bf16[2048,256]{1,0:T(8,128)(2,1)}, bf16[2048,256]{1,0:T(8,128)(2,1)}, u32[]{:S(2)}, u32[]{:S(2)}) collective-permute-start(bf16[2048,256]{1,0:T(8,128)(2,1)} %bitcast.3.refs_0_), channel_id=1, source_target_pairs={{0,64},{1,9},{2,66},{3,11},{4,68},{5,13},{6,70},{7,15},{8,72},{9,1... | collective-permute-start | bytes 3145736 | tf_op jit(solution)/shard_map/ppermute | solution.py:61
  24.8 1.1 fusion.37
  25.9 2.7 %convolution_convert_fusion = bf16[512,384]{1,0:T(8,128)(2,1)S(1)} fusion(bf16[512,1536]{1,0:T(8,128)(2,1)} %param.11, bf16[384,1536]{1,0:T(8,128)(2,1)} %param.12), kind=kOutput, calls=%fused_computation.17 | convolution fusion | flops 604176384 | bytes 3145728 | tf_op jit(solution)/shard_map/dot_general | solution.py:204
  28.6 2.3 %collective-permute-start.1 = (bf16[2048,256]{1,0:T(8,128)(2,1)}, bf16[2048,256]{1,0:T(8,128)(2,1)}, u32[]{:S(2)}, u32[]{:S(2)}) collective-permute-start(bf16[2048,256]{1,0:T(8,128)(2,1)} %bitcast.3.refs_0_), channel_id=1, source_target_pairs={{0,96},{1,13},{2,98},{3,15},{4,100},{5,1},{6,102},{7,3},{8,104},{9... | collective-permute-start | bytes 3145736 | tf_op jit(solution)/shard_map/ppermute | solution.py:61
  31.0 2.9 %collective-permute-start.3 = (bf16[2048,256]{1,0:T(8,128)(2,1)}, bf16[2048,256]{1,0:T(8,128)(2,1)}, u32[]{:S(2)}, u32[]{:S(2)}) collective-permute-start(bf16[2048,256]{1,0:T(8,128)(2,1)} %bitcast.3.refs_0_), channel_id=1, source_target_pairs={{0,32},{1,5},{2,34},{3,7},{4,36},{5,9},{6,38},{7,11},{8,40},{9,13}... | collective-permute-start | bytes 3145736 | tf_op jit(solution)/shard_map/ppermute | solution.py:61
  33.9 6.4 %collective-permute-done.refs_4_ = bf16[2048,256]{1,0:T(8,128)(2,1)} collective-permute-done((bf16[2048,256]{1,0:T(8,128)(2,1)}, bf16[2048,256]{1,0:T(8,128)(2,1)}, u32[]{:S(2)}, u32[]{:S(2)}) %collective-permute-start) | collective-permute-done | bytes 1048608 | tf_op jit(solution)/shard_map/ppermute | solution.py:61
  40.3 1.9 %collective-permute-start.4 = (bf16[2048,256]{1,0:T(8,128)(2,1)}, bf16[2048,256]{1,0:T(8,128)(2,1)}, u32[]{:S(2)}, u32[]{:S(2)}) collective-permute-start(bf16[2048,256]{1,0:T(8,128)(2,1)} %collective-permute-done.refs_4_), channel_id=1, source_target_pairs={{0,96},{1,13},{2,98},{3,15},{4,100},{5,1},{6,102},{7,3},{8,104},{9... | collective-permute-start | bytes 3145736 | tf_op jit(solution)/shard_map/ppermute | solution.py:61
  42.2 4.3 %collective-permute-start.6 = (bf16[2048,256]{1,0:T(8,128)(2,1)}, bf16[2048,256]{1,0:T(8,128)(2,1)}, u32[]{:S(2)}, u32[]{:S(2)}) collective-permute-start(bf16[2048,256]{1,0:T(8,128)(2,1)} %collective-permute-done.refs_4_), channel_id=1, source_target_pairs={{0,32},{1,5},{2,34},{3,7},{4,36},{5,9},{6,38},{7,11},{8,40},{9,13}... | collective-permute-start | bytes 3145736 | tf_op jit(solution)/shard_map/ppermute | solution.py:61
  46.7 3.2 %collective-permute-start.5 = (bf16[2048,256]{1,0:T(8,128)(2,1)}, bf16[2048,256]{1,0:T(8,128)(2,1)}, u32[]{:S(2)}, u32[]{:S(2)}) collective-permute-start(bf16[2048,256]{1,0:T(8,128)(2,1)} %collective-permute-done.2.refs_2_), channel_id=1, source_target_pairs={{0,16},{1,17},{2,18},{3,19},{4,20},{5,21},{6,22},{7,23},{8,24},{9,... | collective-permute-start | bytes 3145736 | tf_op jit(solution)/shard_map/ppermute | solution.py:61
  49.9 1.1 maximum_maximum_fusion.1
  50.9 4.3 %all-to-all-start.1 = ((bf16[4,512,256]{2,1,0:T(8,128)(2,1)}), bf16[4,512,256]{2,1,0:T(8,128)(2,1)}, u32[]{:S(2)}, u32[]{:S(2)}) async-start(bf16[4,512,256]{2,1,0:T(8,128)(2,1)} %bitcast.78), calls=%async_computation.1 | async-start | bytes 2097152 | tf_op jit(solution)/shard_map/all_to_all | solution.py:165
  55.5 0.7 pad.27.clone
  56.5 12.6 %all-to-all-done.1 = bf16[4,512,256]{2,1,0:T(8,128)(2,1)} async-done(((bf16[4,512,256]{2,1,0:T(8,128)(2,1)}), bf16[4,512,256]{2,1,0:T(8,128)(2,1)}, u32[]{:S(2)}, u32[]{:S(2)}) %all-to-all-start.1) | async-done | bytes 1048608 | tf_op jit(solution)/shard_map/all_to_all | solution.py:165
  69.1 1.1 collective-permute-done.5.refs_6_
  70.2 20.4 %attend.1 = (bf16[2048,128]{1,0:T(8,128)(2,1)S(1)}, bf16[2048,256]{1,0:T(8,128)(2,1)S(1)}, bf16[2048,256]{1,0:T(8,128)(2,1)}, bf16[2048,256]{1,0:T(8,128)(2,1)S(...) custom-call(s32[16,8]{1,0:T(8,128)S(1)} %fusion.18.table, ...), custom_call_target="tpu_custom_call" | custom-call | tf_op jit(solution)/shard_map/attend/pallas_call | solution.py:138
  90.6 1.9 %collective-permute-start.12 = (bf16[2048,256]{1,0:T(8,128)(2,1)S(1)}, bf16[2048,256]{1,0:T(8,128)(2,1)S(1)}, u32[]{:S(2)}, u32[]{:S(2)}) collective-permute-start(bf16[2048,256]{1,0:T(8,128)(2,1)S(1)} %get-tuple-element.26), channel_id=1, source_target_pairs={{0,96},{1,13},{2,98},{3,15},{4,100},{5,1},{6,102},{7,3},{8,104},{9... | collective-permute-start | bytes 3145736 | tf_op jit(solution)/shard_map/ppermute | solution.py:61
  92.5 7.5 %collective-permute-start.11 = (bf16[2048,256]{1,0:T(8,128)(2,1)S(1)}, bf16[2048,256]{1,0:T(8,128)(2,1)S(1)}, u32[]{:S(2)}, u32[]{:S(2)}) collective-permute-start(bf16[2048,256]{1,0:T(8,128)(2,1)S(1)} %get-tuple-element.25), channel_id=1, source_target_pairs={{0,32},{1,5},{2,34},{3,7},{4,36},{5,9},{6,38},{7,11},{8,40},{9,13}... | collective-permute-start | bytes 3145736 | tf_op jit(solution)/shard_map/ppermute | solution.py:61
  100.1 3.2 %collective-permute-start.9 = (bf16[2048,256]{1,0:T(8,128)(2,1)S(1)}, bf16[2048,256]{1,0:T(8,128)(2,1)S(1)}, u32[]{:S(2)}, u32[]{:S(2)}) collective-permute-start(bf16[2048,256]{1,0:T(8,128)(2,1)S(1)} %get-tuple-element.23), channel_id=1, source_target_pairs={{0,16},{1,17},{2,18},{3,19},{4,20},{5,21},{6,22},{7,23},{8,24},{9,... | collective-permute-start | bytes 3145736 | tf_op jit(solution)/shard_map/ppermute | solution.py:61
  103.3 3.8 %collective-permute-start.8 = (bf16[2048,256]{1,0:T(8,128)(2,1)}, bf16[2048,256]{1,0:T(8,128)(2,1)}, u32[]{:S(2)}, u32[]{:S(2)}) collective-permute-start(bf16[2048,256]{1,0:T(8,128)(2,1)} %get-tuple-element.21), channel_id=1, source_target_pairs={{0,96},{1,13},{2,98},{3,15},{4,100},{5,1},{6,102},{7,3},{8,104},{9... | collective-permute-start | bytes 3145736 | tf_op jit(solution)/shard_map/ppermute | solution.py:61
  107.1 1.9 %collective-permute-start.7 = (bf16[2048,256]{1,0:T(8,128)(2,1)}, bf16[2048,256]{1,0:T(8,128)(2,1)}, u32[]{:S(2)}, u32[]{:S(2)}) collective-permute-start(bf16[2048,256]{1,0:T(8,128)(2,1)} %get-tuple-element.20), channel_id=1, source_target_pairs={{0,32},{1,5},{2,34},{3,7},{4,36},{5,9},{6,38},{7,11},{8,40},{9,13}... | collective-permute-start | bytes 3145736 | tf_op jit(solution)/shard_map/ppermute | solution.py:61
  109.0 1.6 collective-permute-done.12
  110.6 3.9 %collective-permute-done.11 = bf16[2048,256]{1,0:T(8,128)(2,1)S(1)} collective-permute-done((bf16[2048,256]{1,0:T(8,128)(2,1)S(1)}, bf16[2048,256]{1,0:T(8,128)(2,1)S(1)}, u32[]{:S(2)}, u32[]{:S(2)}) %collective-permute-start.11) | collective-permute-done | bytes 1048608 | tf_op jit(solution)/shard_map/ppermute | solution.py:61
  114.5 1.6 add_convert_fusion.1
  116.1 3.2 %collective-permute-start.13 = (bf16[2048,256]{1,0:T(8,128)(2,1)}, bf16[2048,256]{1,0:T(8,128)(2,1)}, u32[]{:S(2)}, u32[]{:S(2)}) collective-permute-start(bf16[2048,256]{1,0:T(8,128)(2,1)} %add_convert_fusion.1), channel_id=1, source_target_pairs={{0,16},{1,17},{2,18},{3,19},{4,20},{5,21},{6,22},{7,23},{8,24},{9,... | collective-permute-start | bytes 3145736 | tf_op jit(solution)/shard_map/ppermute | solution.py:61
  119.3 6.7 %collective-permute-done.9 = bf16[2048,256]{1,0:T(8,128)(2,1)S(1)} collective-permute-done((bf16[2048,256]{1,0:T(8,128)(2,1)S(1)}, bf16[2048,256]{1,0:T(8,128)(2,1)S(1)}, u32[]{:S(2)}, u32[]{:S(2)}) %collective-permute-start.9) | collective-permute-done | bytes 1048608 | tf_op jit(solution)/shard_map/ppermute | solution.py:61
  126.0 1.4 add_convert_fusion.2
  127.3 2.8 %collective-permute-start.10 = (bf16[2048,256]{1,0:T(8,128)(2,1)}, bf16[2048,256]{1,0:T(8,128)(2,1)}, u32[]{:S(2)}, u32[]{:S(2)}) collective-permute-start(bf16[2048,256]{1,0:T(8,128)(2,1)} %add_convert_fusion.2), channel_id=1, source_target_pairs={{0,64},{1,9},{2,66},{3,11},{4,68},{5,13},{6,70},{7,15},{8,72},{9,1... | collective-permute-start | bytes 3145736 | tf_op jit(solution)/shard_map/ppermute | solution.py:61
  130.1 4.2 %all-to-all-start.2 = ((bf16[4,512,128]{2,1,0:T(8,128)(2,1)}), bf16[4,512,128]{2,1,0:T(8,128)(2,1)}, u32[]{:S(2)}, u32[]{:S(2)}) async-start(bf16[4,512,128]{2,1,0:T(8,128)(2,1)} %bitcast.77), calls=%async_computation.2 | async-start | bytes 1048576 | tf_op jit(solution)/shard_map/all_to_all | solution.py:165
  134.3 14.2 %collective-permute-done.13 = bf16[2048,256]{1,0:T(8,128)(2,1)} collective-permute-done((bf16[2048,256]{1,0:T(8,128)(2,1)}, bf16[2048,256]{1,0:T(8,128)(2,1)}, u32[]{:S(2)}, u32[]{:S(2)}) %collective-permute-start.13) | collective-permute-done | bytes 1048608 | tf_op jit(solution)/shard_map/ppermute | solution.py:61
  148.5 4.1 %add_convert_fusion = bf16[2048,256]{1,0:T(8,128)(2,1)} fusion(bf16[2048,256]{1,0:T(8,128)(2,1)} %collective-permute-done.13, bf16[2048,256]{1,0:T(8,128)(2,1)} %collective-permute-done.10, bf16[2048,256]{1,0:T(8,128)(2,1)} %collective-permute-done.8, bf16[2048,256]{1,0:T(8,128)(2,1)} %collective-permute-done.7, bf16[2048,256]{1,0:T(8,128)(2,1)} %copy-done.1), kind=kLoop, calls=%fused_computation | loop fusion | flops 5242880 | bytes 6291456 | tf_op jit(solution)/shard_map/convert_element_type | solution.py:161
  152.7 4.2 %all-to-all-start.3 = ((bf16[4,512,256]{2,1,0:T(8,128)(2,1)}), bf16[4,512,256]{2,1,0:T(8,128)(2,1)}, u32[]{:S(2)}, u32[]{:S(2)}) async-start(bf16[4,512,256]{2,1,0:T(8,128)(2,1)} %bitcast.80), calls=%async_computation.3 | async-start | bytes 2097152 | tf_op jit(solution)/shard_map/all_to_all | solution.py:165
  157.0 1.1 slice_bitcast_fusion.8
  158.0 1.3 fusion.6
  159.3 1.3 fusion.7
  160.6 1.3 fusion.9
  161.9 1.3 fusion.8
  163.2 3.5 %all-to-all-done.3 = bf16[4,512,256]{2,1,0:T(8,128)(2,1)} async-done(((bf16[4,512,256]{2,1,0:T(8,128)(2,1)}), bf16[4,512,256]{2,1,0:T(8,128)(2,1)}, u32[]{:S(2)}, u32[]{:S(2)}) %all-to-all-start.3) | async-done | bytes 1048608 | tf_op jit(solution)/shard_map/all_to_all | solution.py:165
  166.7 1.3 slice_bitcast_fusion.2
  168.6 0.4 fusion.5
  169.0 5.3 %collective-permute-start.15 = (bf16[384,512]{1,0:T(8,128)(2,1)S(1)}, bf16[384,512]{1,0:T(8,128)(2,1)S(1)}, u32[]{:S(2)}, u32[]{:S(2)}) collective-permute-start(bf16[384,512]{1,0:T(8,128)(2,1)S(1)} %fusion.5), channel_id=1, source_target_pairs={{0,1},{1,0},{2,3},{3,2},{4,5},{5,4},{6,7},{7,6},{8,9},{9,8},{10,11... | collective-permute-start | bytes 1179656 | tf_op jit(solution)/shard_map/ppermute | solution.py:61
  175.8 0.4 add_convert_fusion.4
  176.2 3.0 %collective-permute-start.16 = (bf16[384,512]{1,0:T(8,128)(2,1)S(1)}, bf16[384,512]{1,0:T(8,128)(2,1)S(1)}, u32[]{:S(2)}, u32[]{:S(2)}) collective-permute-start(bf16[384,512]{1,0:T(8,128)(2,1)S(1)} %add_convert_fusion.4), channel_id=1, source_target_pairs={{0,2},{1,3},{2,0},{3,1},{4,6},{5,7},{6,4},{7,5},{8,10},{9,11},{10,... | collective-permute-start | bytes 1179656 | tf_op jit(solution)/shard_map/ppermute | solution.py:61
  179.6 0.4 fusion.1
  180.0 8.1 %collective-permute-done.16 = bf16[384,512]{1,0:T(8,128)(2,1)S(1)} collective-permute-done((bf16[384,512]{1,0:T(8,128)(2,1)S(1)}, bf16[384,512]{1,0:T(8,128)(2,1)S(1)}, u32[]{:S(2)}, u32[]{:S(2)}) %collective-permute-start.16) | collective-permute-done | bytes 393248 | tf_op jit(solution)/shard_map/ppermute | solution.py:61
  188.1 0.9 add_convert_fusion.3
  (42 shorter events, 3.1 us)
Async XLA Ops:
  0.0 158.0 %copy-start = (bf16[3,1536,384]{2,1,0:T(8,128)(2,1)S(1)}, bf16[3,1536,384]{2,1,0:T(8,128)(2,1)}, u32[]{:S(2)}) copy-start(bf16[3,1536,384]{2,1,0:T(8,128)(2,1)} %param.13) | copy-start | bytes 10616836
  16.3 24.0 %collective-permute-start = (bf16[2048,256]{1,0:T(8,128)(2,1)}, bf16[2048,256]{1,0:T(8,128)(2,1)}, u32[]{:S(2)}, u32[]{:S(2)}) collective-permute-start(bf16[2048,256]{1,0:T(8,128)(2,1)} %bitcast.3.refs_0_), channel_id=1, source_target_pairs={{0,16},{1,17},{2,18},{3,19},{4,20},{5,21},{6,22},{7,23},{8,24},{9,... | collective-permute-start | bytes 3145736 | tf_op jit(solution)/shard_map/ppermute | solution.py:61
  19.5 27.2 %collective-permute-start.2 = (bf16[2048,256]{1,0:T(8,128)(2,1)}, bf16[2048,256]{1,0:T(8,128)(2,1)}, u32[]{:S(2)}, u32[]{:S(2)}) collective-permute-start(bf16[2048,256]{1,0:T(8,128)(2,1)} %bitcast.3.refs_0_), channel_id=1, source_target_pairs={{0,64},{1,9},{2,66},{3,11},{4,68},{5,13},{6,70},{7,15},{8,72},{9,1... | collective-permute-start | bytes 3145736 | tf_op jit(solution)/shard_map/ppermute | solution.py:61
  28.6 27.9 %collective-permute-start.1 = (bf16[2048,256]{1,0:T(8,128)(2,1)}, bf16[2048,256]{1,0:T(8,128)(2,1)}, u32[]{:S(2)}, u32[]{:S(2)}) collective-permute-start(bf16[2048,256]{1,0:T(8,128)(2,1)} %bitcast.3.refs_0_), channel_id=1, source_target_pairs={{0,96},{1,13},{2,98},{3,15},{4,100},{5,1},{6,102},{7,3},{8,104},{9... | collective-permute-start | bytes 3145736 | tf_op jit(solution)/shard_map/ppermute | solution.py:61
  31.0 25.5 %collective-permute-start.3 = (bf16[2048,256]{1,0:T(8,128)(2,1)}, bf16[2048,256]{1,0:T(8,128)(2,1)}, u32[]{:S(2)}, u32[]{:S(2)}) collective-permute-start(bf16[2048,256]{1,0:T(8,128)(2,1)} %bitcast.3.refs_0_), channel_id=1, source_target_pairs={{0,32},{1,5},{2,34},{3,7},{4,36},{5,9},{6,38},{7,11},{8,40},{9,13}... | collective-permute-start | bytes 3145736 | tf_op jit(solution)/shard_map/ppermute | solution.py:61
  40.3 28.8 %collective-permute-start.4 = (bf16[2048,256]{1,0:T(8,128)(2,1)}, bf16[2048,256]{1,0:T(8,128)(2,1)}, u32[]{:S(2)}, u32[]{:S(2)}) collective-permute-start(bf16[2048,256]{1,0:T(8,128)(2,1)} %collective-permute-done.refs_4_), channel_id=1, source_target_pairs={{0,96},{1,13},{2,98},{3,15},{4,100},{5,1},{6,102},{7,3},{8,104},{9... | collective-permute-start | bytes 3145736 | tf_op jit(solution)/shard_map/ppermute | solution.py:61
  42.2 27.9 %collective-permute-start.6 = (bf16[2048,256]{1,0:T(8,128)(2,1)}, bf16[2048,256]{1,0:T(8,128)(2,1)}, u32[]{:S(2)}, u32[]{:S(2)}) collective-permute-start(bf16[2048,256]{1,0:T(8,128)(2,1)} %collective-permute-done.refs_4_), channel_id=1, source_target_pairs={{0,32},{1,5},{2,34},{3,7},{4,36},{5,9},{6,38},{7,11},{8,40},{9,13}... | collective-permute-start | bytes 3145736 | tf_op jit(solution)/shard_map/ppermute | solution.py:61
  46.6 8.7 %copy-start.7 = (s32[128,3]{0,1:T(4,128)S(1)}, s32[128,3]{0,1:T(4,128)}, u32[]{:S(2)}) copy-start(s32[128,3]{0,1:T(4,128)} %param.14) | copy-start | bytes 4612
  46.7 23.5 %collective-permute-start.5 = (bf16[2048,256]{1,0:T(8,128)(2,1)}, bf16[2048,256]{1,0:T(8,128)(2,1)}, u32[]{:S(2)}, u32[]{:S(2)}) collective-permute-start(bf16[2048,256]{1,0:T(8,128)(2,1)} %collective-permute-done.2.refs_2_), channel_id=1, source_target_pairs={{0,16},{1,17},{2,18},{3,19},{4,20},{5,21},{6,22},{7,23},{8,24},{9,... | collective-permute-start | bytes 3145736 | tf_op jit(solution)/shard_map/ppermute | solution.py:61
  50.9 18.1 %all-to-all-start.1 = ((bf16[4,512,256]{2,1,0:T(8,128)(2,1)}), bf16[4,512,256]{2,1,0:T(8,128)(2,1)}, u32[]{:S(2)}, u32[]{:S(2)}) async-start(bf16[4,512,256]{2,1,0:T(8,128)(2,1)} %bitcast.78), calls=%async_computation.1 | async-start | bytes 2097152 | tf_op jit(solution)/shard_map/all_to_all | solution.py:165
  90.6 25.5 %copy-start.1 = (bf16[2048,256]{1,0:T(8,128)(2,1)}, bf16[2048,256]{1,0:T(8,128)(2,1)S(1)}, u32[]{:S(2)}) copy-start(bf16[2048,256]{1,0:T(8,128)(2,1)S(1)} %get-tuple-element.19) | copy-start | bytes 3145732
  90.6 25.5 %copy-start.2 = (bf16[2048,128]{1,0:T(8,128)(2,1)}, bf16[2048,128]{1,0:T(8,128)(2,1)S(1)}, u32[]{:S(2)}) copy-start(bf16[2048,128]{1,0:T(8,128)(2,1)S(1)} %get-tuple-element.18) | copy-start | bytes 1572868
  90.6 20.0 %collective-permute-start.12 = (bf16[2048,256]{1,0:T(8,128)(2,1)S(1)}, bf16[2048,256]{1,0:T(8,128)(2,1)S(1)}, u32[]{:S(2)}, u32[]{:S(2)}) collective-permute-start(bf16[2048,256]{1,0:T(8,128)(2,1)S(1)} %get-tuple-element.26), channel_id=1, source_target_pairs={{0,96},{1,13},{2,98},{3,15},{4,100},{5,1},{6,102},{7,3},{8,104},{9... | collective-permute-start | bytes 3145736 | tf_op jit(solution)/shard_map/ppermute | solution.py:61
  92.5 22.0 %collective-permute-start.11 = (bf16[2048,256]{1,0:T(8,128)(2,1)S(1)}, bf16[2048,256]{1,0:T(8,128)(2,1)S(1)}, u32[]{:S(2)}, u32[]{:S(2)}) collective-permute-start(bf16[2048,256]{1,0:T(8,128)(2,1)S(1)} %get-tuple-element.25), channel_id=1, source_target_pairs={{0,32},{1,5},{2,34},{3,7},{4,36},{5,9},{6,38},{7,11},{8,40},{9,13}... | collective-permute-start | bytes 3145736 | tf_op jit(solution)/shard_map/ppermute | solution.py:61
  100.1 25.9 %collective-permute-start.9 = (bf16[2048,256]{1,0:T(8,128)(2,1)S(1)}, bf16[2048,256]{1,0:T(8,128)(2,1)S(1)}, u32[]{:S(2)}, u32[]{:S(2)}) collective-permute-start(bf16[2048,256]{1,0:T(8,128)(2,1)S(1)} %get-tuple-element.23), channel_id=1, source_target_pairs={{0,16},{1,17},{2,18},{3,19},{4,20},{5,21},{6,22},{7,23},{8,24},{9,... | collective-permute-start | bytes 3145736 | tf_op jit(solution)/shard_map/ppermute | solution.py:61
  103.3 31.0 %collective-permute-start.8 = (bf16[2048,256]{1,0:T(8,128)(2,1)}, bf16[2048,256]{1,0:T(8,128)(2,1)}, u32[]{:S(2)}, u32[]{:S(2)}) collective-permute-start(bf16[2048,256]{1,0:T(8,128)(2,1)} %get-tuple-element.21), channel_id=1, source_target_pairs={{0,96},{1,13},{2,98},{3,15},{4,100},{5,1},{6,102},{7,3},{8,104},{9... | collective-permute-start | bytes 3145736 | tf_op jit(solution)/shard_map/ppermute | solution.py:61
  107.1 27.3 %collective-permute-start.7 = (bf16[2048,256]{1,0:T(8,128)(2,1)}, bf16[2048,256]{1,0:T(8,128)(2,1)}, u32[]{:S(2)}, u32[]{:S(2)}) collective-permute-start(bf16[2048,256]{1,0:T(8,128)(2,1)} %get-tuple-element.20), channel_id=1, source_target_pairs={{0,32},{1,5},{2,34},{3,7},{4,36},{5,9},{6,38},{7,11},{8,40},{9,13}... | collective-permute-start | bytes 3145736 | tf_op jit(solution)/shard_map/ppermute | solution.py:61
  116.1 32.4 %collective-permute-start.13 = (bf16[2048,256]{1,0:T(8,128)(2,1)}, bf16[2048,256]{1,0:T(8,128)(2,1)}, u32[]{:S(2)}, u32[]{:S(2)}) collective-permute-start(bf16[2048,256]{1,0:T(8,128)(2,1)} %add_convert_fusion.1), channel_id=1, source_target_pairs={{0,16},{1,17},{2,18},{3,19},{4,20},{5,21},{6,22},{7,23},{8,24},{9,... | collective-permute-start | bytes 3145736 | tf_op jit(solution)/shard_map/ppermute | solution.py:61
  127.3 21.2 %collective-permute-start.10 = (bf16[2048,256]{1,0:T(8,128)(2,1)}, bf16[2048,256]{1,0:T(8,128)(2,1)}, u32[]{:S(2)}, u32[]{:S(2)}) collective-permute-start(bf16[2048,256]{1,0:T(8,128)(2,1)} %add_convert_fusion.2), channel_id=1, source_target_pairs={{0,64},{1,9},{2,66},{3,11},{4,68},{5,13},{6,70},{7,15},{8,72},{9,1... | collective-permute-start | bytes 3145736 | tf_op jit(solution)/shard_map/ppermute | solution.py:61
  130.1 22.5 %all-to-all-start.2 = ((bf16[4,512,128]{2,1,0:T(8,128)(2,1)}), bf16[4,512,128]{2,1,0:T(8,128)(2,1)}, u32[]{:S(2)}, u32[]{:S(2)}) async-start(bf16[4,512,128]{2,1,0:T(8,128)(2,1)} %bitcast.77), calls=%async_computation.2 | async-start | bytes 1048576 | tf_op jit(solution)/shard_map/all_to_all | solution.py:165
  152.7 14.1 %all-to-all-start.3 = ((bf16[4,512,256]{2,1,0:T(8,128)(2,1)}), bf16[4,512,256]{2,1,0:T(8,128)(2,1)}, u32[]{:S(2)}, u32[]{:S(2)}) async-start(bf16[4,512,256]{2,1,0:T(8,128)(2,1)} %bitcast.80), calls=%async_computation.3 | async-start | bytes 2097152 | tf_op jit(solution)/shard_map/all_to_all | solution.py:165
  166.7 1.5 copy-start.6
  168.0 6.3 %copy-start.5 = (f32[384,512]{1,0:T(8,128)S(1)}, f32[384,512]{1,0:T(8,128)}, u32[]{:S(2)}) copy-start(f32[384,512]{1,0:T(8,128)} %fusion.8) | copy-start | bytes 2359300
  169.0 6.4 %copy-start.4 = (f32[384,512]{1,0:T(8,128)S(1)}, f32[384,512]{1,0:T(8,128)}, u32[]{:S(2)}) copy-start(f32[384,512]{1,0:T(8,128)} %fusion.7) | copy-start | bytes 2359300
  169.0 6.8 %collective-permute-start.15 = (bf16[384,512]{1,0:T(8,128)(2,1)S(1)}, bf16[384,512]{1,0:T(8,128)(2,1)S(1)}, u32[]{:S(2)}, u32[]{:S(2)}) collective-permute-start(bf16[384,512]{1,0:T(8,128)(2,1)S(1)} %fusion.5), channel_id=1, source_target_pairs={{0,1},{1,0},{2,3},{3,2},{4,5},{5,4},{6,7},{7,6},{8,9},{9,8},{10,11... | collective-permute-start | bytes 1179656 | tf_op jit(solution)/shard_map/ppermute | solution.py:61
  175.1 4.0 %copy-start.3 = (f32[384,512]{1,0:T(8,128)S(1)}, f32[384,512]{1,0:T(8,128)}, u32[]{:S(2)}) copy-start(f32[384,512]{1,0:T(8,128)} %fusion.9) | copy-start | bytes 2359300
  175.2 4.8 %collective-permute-start.14 = (bf16[384,512]{1,0:T(8,128)(2,1)S(1)}, bf16[384,512]{1,0:T(8,128)(2,1)S(1)}, u32[]{:S(2)}, u32[]{:S(2)}) collective-permute-start(bf16[384,512]{1,0:T(8,128)(2,1)S(1)} %fusion.2), channel_id=1, source_target_pairs={{0,1},{1,0},{2,3},{3,2},{4,5},{5,4},{6,7},{7,6},{8,9},{9,8},{10,11... | collective-permute-start | bytes 1179656 | tf_op jit(solution)/shard_map/ppermute | solution.py:61
  176.2 11.9 %collective-permute-start.16 = (bf16[384,512]{1,0:T(8,128)(2,1)S(1)}, bf16[384,512]{1,0:T(8,128)(2,1)S(1)}, u32[]{:S(2)}, u32[]{:S(2)}) collective-permute-start(bf16[384,512]{1,0:T(8,128)(2,1)S(1)} %add_convert_fusion.4), channel_id=1, source_target_pairs={{0,2},{1,3},{2,0},{3,1},{4,6},{5,7},{6,4},{7,5},{8,10},{9,11},{10,... | collective-permute-start | bytes 1179656 | tf_op jit(solution)/shard_map/ppermute | solution.py:61

commit v8 on v7

--- a/solution.py
+++ b/solution.py
@@ -165,12 +165,51 @@
     return lax.all_to_all(x, AXES, 0, 0, axis_index_groups=LINES, tiled=True)
 
 
-def deal(a, b):
+def pack(a, b):
     heads = [
         jnp.concatenate([a[:, p * HD : (p + 1) * HD], b[:, p * HD : (p + 1) * HD]], axis=1)
         for p in (0, 1, 2, 0)
     ]
-    return exchange(jnp.concatenate(heads, axis=0))
+    return jnp.concatenate(heads, axis=0)
+
+
+def prepare_kernel(up_hbm, out_w_hbm, q_hbm, o_hbm, up, out_w, q, o, sems, out_sem):
+    loads = [
+        pltpu.make_async_copy(src, dst, sems.at[m])
+        for m, (src, dst) in enumerate(((out_w_hbm, out_w), (up_hbm, up), (q_hbm, q)))
+    ]
+    for c in loads:
+        c.start()
+    for c in loads:
+        c.wait()
+    ctx = lax.dot_general(
+        up[...], out_w[...], (((1,), (1,)), ((), ())), preferred_element_type=F32
+    ).astype(BF16)
+    side = BLK_DEV * BLK
+    for slot, p in enumerate((0, 1, 2, 0)):
+        rows = slice(slot * side, (slot + 1) * side)
+        lanes = slice(p * HD, (p + 1) * HD)
+        o[rows, :HD] = q[:, lanes]
+        o[rows, HD:] = ctx[:, lanes]
+    store = pltpu.make_async_copy(o, o_hbm, out_sem)
+    store.start()
+    store.wait()
+
+
+def prepare(upstream_out, out_weight, queries):
+    args = (upstream_out, out_weight, queries)
+    out = jax.ShapeDtypeStruct((ROWS, 2 * HD), BF16)
+    far = pl.BlockSpec(memory_space=pl.ANY)
+    return pl.pallas_call(
+        prepare_kernel,
+        name="prepare",
+        out_shape=out,
+        in_specs=[far] * len(args),
+        out_specs=far,
+        scratch_shapes=[pltpu.VMEM(a.shape, BF16) for a in args + (out,)]
+        + [pltpu.SemaphoreType.DMA((len(args),)), pltpu.SemaphoreType.DMA],
+        compiler_params=pltpu.CompilerParams(vmem_limit_bytes=58 << 20),
+    )(*args)
 
 
 def body(queries, keys, values, upstream_out, out_weight, qkv_weight, rand_links, global_links):
@@ -197,16 +236,15 @@
     shard_of = jnp.where(ky == y, 0, 4) + (k_ring - ring) % 4
     table = (shard_of * LINE + k_pos) * BLK_DEV + key % BLK_DEV
 
-    own = deal(keys, values)
+    own = exchange(pack(keys, values))
     other = send(own, PAIR)
     next_, last = send(own, RING[3]), send(own, RING[1])
     across = send(own, RING[2])
-    grad_ctx = lax.dot_general(
-        upstream_out, out_weight, (((1,), (1,)), ((), ())), preferred_element_type=F32
-    ).astype(BF16)
-    grad_ctx, other = lax.optimization_barrier((grad_ctx, other))
-    qd = deal(queries, grad_ctx)
-    other_row = [other, send(other, RING[3]), send(across, PAIR), send(other, RING[1])]
+    packed = prepare(upstream_out, out_weight, queries)
+    corner = send(across, PAIR)
+    other = lax.optimization_barrier((other, packed))[0]
+    qd = exchange(packed)
+    other_row = [other, send(other, RING[3]), corner, send(other, RING[1])]
     grad_q, parts = attend(table, qd, [own, next_, across, last] + other_row)
 
     corner = send(parts[6], PAIR)

time: 190 us -> 188 us (0.989)
  Pallas kernels: 20.4 us -> 24.3 us
  waiting for transfers between devices: 58.1 us -> 54.9 us
  matrix products: 11.1 us -> 8.39 us
  starting transfers between devices: 68.7 us -> 71.2 us
    ppermute x17, waiting for transfers between devices: 42 us -> 36.8 us  [send(): return lax.ppermute(x, AXES, perm)]
    pallas_call x0 -> x1, Pallas kernels: none -> 3.87 us  [prepare(): pl.pallas_call(prepare_kernel, name='prepare', out_shape=out, in_specs=[f...]
    dot_general x1 -> x0, matrix products: 2.74 us -> none  [body(): lax.dot_general(upstream_out, out_weight, (((1,), (1,)), ((), ())), prefe...]
    ppermute x17, starting transfers between devices: 56 us -> 58.4 us  [send(): return lax.ppermute(x, AXES, perm)]
    all_to_all x3, waiting for transfers between devices: 16.1 us -> 18 us  [exchange(): return lax.all_to_all(x, AXES, 0, 0, axis_index_groups=LINES, tiled=True)]
  transfers between devices with their start and end apart: 20 -> 20, of which waited for: 9 -> 9; matrix products, arithmetic and copies ran while one was open for 12% -> 9% of each run, Pallas kernels for 0% -> 2%
where the time goes in v8:
time: 188 us; the launch traced here: 187 us
  starting transfers between devices  71.2 us (38%)
  waiting for transfers between devices  54.9 us (29%)
  Pallas kernels  24.3 us (13%)
  blocking collectives  14.8 us (8%)
  other arithmetic  8.47 us (5%)
  matrix products  8.39 us (4%)
  local copies, waits for them, and re-layouts  4.76 us (3%)
    ppermute x17, starting transfers between devices, send(): return lax.ppermute(x, AXES, perm)  58.4 us
    ppermute x17, waiting for transfers between devices, send(): return lax.ppermute(x, AXES, perm)  36.8 us
    pallas_call x1, Pallas kernels, attend(): pl.pallas_call(attend_kernel, name='attend', out_shape=(jax.ShapeDtypeStr...  20.4 us
    all_to_all x3, waiting for transfers between devices, exchange(): return lax.all_to_all(x, AXES, 0, 0, axis_index_groups=LINES, tiled=True)  18 us
    all_to_all x1, blocking collectives, exchange(): return lax.all_to_all(x, AXES, 0, 0, axis_index_groups=LINES, tiled=True)  14.8 us
    all_to_all x3, starting transfers between devices, exchange(): return lax.all_to_all(x, AXES, 0, 0, axis_index_groups=LINES, tiled=True)  12.8 us
    dot_general x12, matrix products, share(): lax.dot_general(w[j], g, (((1,), (1,)), ((), ())), preferred_element_type...  8.39 us
    convert_element_type x4, other arithmetic, add(): functools.reduce(lambda a, b: a + b, [t.astype(F32) for t in terms])  7.95 us
  transfers between devices with their start and end apart: 20, of which 9 were waited for; matrix products, arithmetic and copies ran while one was open for 9% of the time, Pallas kernels for 2%

profile of v8, /device:TPU:1, one launch (start us, length us, event | category | flops | bytes accessed | tf_op | source)
XLA Modules:
  0.0 187.2 jit_solution(14966460444098727584)
XLA Ops:
  0.0 1.4 fusion.37
  1.5 14.8 %all_to_all.40 = bf16[4,512,256]{2,1,0:T(8,128)(2,1)} all-to-all(bf16[4,512,256]{2,1,0:T(8,128)(2,1)S(1)} %bitcast.76), channel_id=1, replica_groups={{0,4,8,12},{1,33,65,97},{2,6,10,14},{3,35,67,99},{5,37,69,101},{7,39,71..., dimensions={0} | all-to-all | bytes 2097152 | tf_op jit(solution)/shard_map/all_to_all | solution.py:165
  16.3 3.2 %collective-permute-start.3 = (bf16[2048,256]{1,0:T(8,128)(2,1)}, bf16[2048,256]{1,0:T(8,128)(2,1)}, u32[]{:S(2)}, u32[]{:S(2)}) collective-permute-start(bf16[2048,256]{1,0:T(8,128)(2,1)} %bitcast.5.refs_0_), channel_id=1, source_target_pairs={{0,16},{1,17},{2,18},{3,19},{4,20},{5,21},{6,22},{7,23},{8,24},{9,... | collective-permute-start | bytes 3145736 | tf_op jit(solution)/shard_map/ppermute | solution.py:61
  19.5 5.2 %collective-permute-start.1 = (bf16[2048,256]{1,0:T(8,128)(2,1)}, bf16[2048,256]{1,0:T(8,128)(2,1)}, u32[]{:S(2)}, u32[]{:S(2)}) collective-permute-start(bf16[2048,256]{1,0:T(8,128)(2,1)} %bitcast.5.refs_0_), channel_id=1, source_target_pairs={{0,64},{1,9},{2,66},{3,11},{4,68},{5,13},{6,70},{7,15},{8,72},{9,1... | collective-permute-start | bytes 3145736 | tf_op jit(solution)/shard_map/ppermute | solution.py:61
  24.7 3.9 %prepare.1 = bf16[2048,256]{1,0:T(8,128)(2,1)} custom-call(bf16[512,1536]{1,0:T(8,128)(2,1)} %up_hbm.1, bf16[384,1536]{1,0:T(8,128)(2,1)} %out_w_hbm.1, bf16[512,384]{1,0:T(8,128)(2,1)} %q_hbm.1), custom_call_target="tpu_custom_call" | custom-call | tf_op jit(solution)/shard_map/prepare/pallas_call | solution.py:203
  28.6 2.3 %collective-permute-start = (bf16[2048,256]{1,0:T(8,128)(2,1)}, bf16[2048,256]{1,0:T(8,128)(2,1)}, u32[]{:S(2)}, u32[]{:S(2)}) collective-permute-start(bf16[2048,256]{1,0:T(8,128)(2,1)} %bitcast.5.refs_0_), channel_id=1, source_target_pairs={{0,96},{1,13},{2,98},{3,15},{4,100},{5,1},{6,102},{7,3},{8,104},{9... | collective-permute-start | bytes 3145736 | tf_op jit(solution)/shard_map/ppermute | solution.py:61
  31.0 2.9 %collective-permute-start.2 = (bf16[2048,256]{1,0:T(8,128)(2,1)}, bf16[2048,256]{1,0:T(8,128)(2,1)}, u32[]{:S(2)}, u32[]{:S(2)}) collective-permute-start(bf16[2048,256]{1,0:T(8,128)(2,1)} %bitcast.5.refs_0_), channel_id=1, source_target_pairs={{0,32},{1,5},{2,34},{3,7},{4,36},{5,9},{6,38},{7,11},{8,40},{9,13}... | collective-permute-start | bytes 3145736 | tf_op jit(solution)/shard_map/ppermute | solution.py:61
  33.9 6.4 %collective-permute-done.3.refs_4_ = bf16[2048,256]{1,0:T(8,128)(2,1)} collective-permute-done((bf16[2048,256]{1,0:T(8,128)(2,1)}, bf16[2048,256]{1,0:T(8,128)(2,1)}, u32[]{:S(2)}, u32[]{:S(2)}) %collective-permute-start.3) | collective-permute-done | bytes 1048608 | tf_op jit(solution)/shard_map/ppermute | solution.py:61
  40.3 1.9 %collective-permute-start.4 = (bf16[2048,256]{1,0:T(8,128)(2,1)}, bf16[2048,256]{1,0:T(8,128)(2,1)}, u32[]{:S(2)}, u32[]{:S(2)}) collective-permute-start(bf16[2048,256]{1,0:T(8,128)(2,1)} %collective-permute-done.3.refs_4_), channel_id=1, source_target_pairs={{0,96},{1,13},{2,98},{3,15},{4,100},{5,1},{6,102},{7,3},{8,104},{9... | collective-permute-start | bytes 3145736 | tf_op jit(solution)/shard_map/ppermute | solution.py:61
  42.2 3.2 %collective-permute-start.5 = (bf16[2048,256]{1,0:T(8,128)(2,1)}, bf16[2048,256]{1,0:T(8,128)(2,1)}, u32[]{:S(2)}, u32[]{:S(2)}) collective-permute-start(bf16[2048,256]{1,0:T(8,128)(2,1)} %collective-permute-done.1.refs_2_), channel_id=1, source_target_pairs={{0,16},{1,17},{2,18},{3,19},{4,20},{5,21},{6,22},{7,23},{8,24},{9,... | collective-permute-start | bytes 3145736 | tf_op jit(solution)/shard_map/ppermute | solution.py:61
  45.5 4.3 %collective-permute-start.6 = (bf16[2048,256]{1,0:T(8,128)(2,1)}, bf16[2048,256]{1,0:T(8,128)(2,1)}, u32[]{:S(2)}, u32[]{:S(2)}) collective-permute-start(bf16[2048,256]{1,0:T(8,128)(2,1)} %collective-permute-done.3.refs_4_), channel_id=1, source_target_pairs={{0,32},{1,5},{2,34},{3,7},{4,36},{5,9},{6,38},{7,11},{8,40},{9,13}... | collective-permute-start | bytes 3145736 | tf_op jit(solution)/shard_map/ppermute | solution.py:61
  49.8 4.3 %all-to-all-start = ((bf16[4,512,256]{2,1,0:T(8,128)(2,1)}), bf16[4,512,256]{2,1,0:T(8,128)(2,1)}, u32[]{:S(2)}, u32[]{:S(2)}) async-start(bf16[4,512,256]{2,1,0:T(8,128)(2,1)} %bitcast.77), calls=%async_computation | async-start | bytes 2097152 | tf_op jit(solution)/shard_map/all_to_all | solution.py:165
  54.5 0.7 pad.19.clone
  55.4 14.5 %all-to-all-done = bf16[4,512,256]{2,1,0:T(8,128)(2,1)} async-done(((bf16[4,512,256]{2,1,0:T(8,128)(2,1)}), bf16[4,512,256]{2,1,0:T(8,128)(2,1)}, u32[]{:S(2)}, u32[]{:S(2)}) %all-to-all-start) | async-done | bytes 1048608 | tf_op jit(solution)/shard_map/all_to_all | solution.py:165
  69.9 20.4 %attend.1 = (bf16[2048,128]{1,0:T(8,128)(2,1)S(1)}, bf16[2048,256]{1,0:T(8,128)(2,1)S(1)}, bf16[2048,256]{1,0:T(8,128)(2,1)}, bf16[2048,256]{1,0:T(8,128)(2,1)S(...) custom-call(s32[16,8]{1,0:T(8,128)S(1)} %fusion.18.table, ...), custom_call_target="tpu_custom_call" | custom-call | tf_op jit(solution)/shard_map/attend/pallas_call | solution.py:138
  90.4 4.3 %collective-permute-start.12 = (bf16[2048,256]{1,0:T(8,128)(2,1)S(1)}, bf16[2048,256]{1,0:T(8,128)(2,1)S(1)}, u32[]{:S(2)}, u32[]{:S(2)}) collective-permute-start(bf16[2048,256]{1,0:T(8,128)(2,1)S(1)} %get-tuple-element.24), channel_id=1, source_target_pairs={{0,96},{1,13},{2,98},{3,15},{4,100},{5,1},{6,102},{7,3},{8,104},{9... | collective-permute-start | bytes 3145736 | tf_op jit(solution)/shard_map/ppermute | solution.py:61
  94.6 2.7 %collective-permute-start.11 = (bf16[2048,256]{1,0:T(8,128)(2,1)S(1)}, bf16[2048,256]{1,0:T(8,128)(2,1)S(1)}, u32[]{:S(2)}, u32[]{:S(2)}) collective-permute-start(bf16[2048,256]{1,0:T(8,128)(2,1)S(1)} %get-tuple-element.23), channel_id=1, source_target_pairs={{0,32},{1,5},{2,34},{3,7},{4,36},{5,9},{6,38},{7,11},{8,40},{9,13}... | collective-permute-start | bytes 3145736 | tf_op jit(solution)/shard_map/ppermute | solution.py:61
  97.4 2.1 %collective-permute-start.9 = (bf16[2048,256]{1,0:T(8,128)(2,1)S(1)}, bf16[2048,256]{1,0:T(8,128)(2,1)S(1)}, u32[]{:S(2)}, u32[]{:S(2)}) collective-permute-start(bf16[2048,256]{1,0:T(8,128)(2,1)S(1)} %get-tuple-element.21), channel_id=1, source_target_pairs={{0,16},{1,17},{2,18},{3,19},{4,20},{5,21},{6,22},{7,23},{8,24},{9,... | collective-permute-start | bytes 3145736 | tf_op jit(solution)/shard_map/ppermute | solution.py:61
  99.4 4.8 %collective-permute-start.8 = (bf16[2048,256]{1,0:T(8,128)(2,1)}, bf16[2048,256]{1,0:T(8,128)(2,1)}, u32[]{:S(2)}, u32[]{:S(2)}) collective-permute-start(bf16[2048,256]{1,0:T(8,128)(2,1)} %get-tuple-element.19), channel_id=1, source_target_pairs={{0,96},{1,13},{2,98},{3,15},{4,100},{5,1},{6,102},{7,3},{8,104},{9... | collective-permute-start | bytes 3145736 | tf_op jit(solution)/shard_map/ppermute | solution.py:61
  104.2 1.9 %collective-permute-start.7 = (bf16[2048,256]{1,0:T(8,128)(2,1)}, bf16[2048,256]{1,0:T(8,128)(2,1)}, u32[]{:S(2)}, u32[]{:S(2)}) collective-permute-start(bf16[2048,256]{1,0:T(8,128)(2,1)} %get-tuple-element.18), channel_id=1, source_target_pairs={{0,32},{1,5},{2,34},{3,7},{4,36},{5,9},{6,38},{7,11},{8,40},{9,13}... | collective-permute-start | bytes 3145736 | tf_op jit(solution)/shard_map/ppermute | solution.py:61
  106.1 1.8 collective-permute-done.12
  107.9 4.0 %collective-permute-done.11 = bf16[2048,256]{1,0:T(8,128)(2,1)S(1)} collective-permute-done((bf16[2048,256]{1,0:T(8,128)(2,1)S(1)}, bf16[2048,256]{1,0:T(8,128)(2,1)S(1)}, u32[]{:S(2)}, u32[]{:S(2)}) %collective-permute-start.11) | collective-permute-done | bytes 1048608 | tf_op jit(solution)/shard_map/ppermute | solution.py:61
  111.9 1.6 add_convert_fusion.1
  113.5 2.8 %collective-permute-start.13 = (bf16[2048,256]{1,0:T(8,128)(2,1)}, bf16[2048,256]{1,0:T(8,128)(2,1)}, u32[]{:S(2)}, u32[]{:S(2)}) collective-permute-start(bf16[2048,256]{1,0:T(8,128)(2,1)} %add_convert_fusion.1), channel_id=1, source_target_pairs={{0,16},{1,17},{2,18},{3,19},{4,20},{5,21},{6,22},{7,23},{8,24},{9,... | collective-permute-start | bytes 3145736 | tf_op jit(solution)/shard_map/ppermute | solution.py:61
  116.3 4.9 %collective-permute-done.9 = bf16[2048,256]{1,0:T(8,128)(2,1)S(1)} collective-permute-done((bf16[2048,256]{1,0:T(8,128)(2,1)S(1)}, bf16[2048,256]{1,0:T(8,128)(2,1)S(1)}, u32[]{:S(2)}, u32[]{:S(2)}) %collective-permute-start.9) | collective-permute-done | bytes 1048608 | tf_op jit(solution)/shard_map/ppermute | solution.py:61
  121.2 1.4 add_convert_fusion.2
  122.6 5.6 %collective-permute-start.10 = (bf16[2048,256]{1,0:T(8,128)(2,1)}, bf16[2048,256]{1,0:T(8,128)(2,1)}, u32[]{:S(2)}, u32[]{:S(2)}) collective-permute-start(bf16[2048,256]{1,0:T(8,128)(2,1)} %add_convert_fusion.2), channel_id=1, source_target_pairs={{0,64},{1,9},{2,66},{3,11},{4,68},{5,13},{6,70},{7,15},{8,72},{9,1... | collective-permute-start | bytes 3145736 | tf_op jit(solution)/shard_map/ppermute | solution.py:61
  128.2 4.2 %all-to-all-start.2 = ((bf16[4,512,128]{2,1,0:T(8,128)(2,1)}), bf16[4,512,128]{2,1,0:T(8,128)(2,1)}, u32[]{:S(2)}, u32[]{:S(2)}) async-start(bf16[4,512,128]{2,1,0:T(8,128)(2,1)} %bitcast.75), calls=%async_computation.2 | async-start | bytes 1048576 | tf_op jit(solution)/shard_map/all_to_all | solution.py:165
  132.3 11.3 %collective-permute-done.13 = bf16[2048,256]{1,0:T(8,128)(2,1)} collective-permute-done((bf16[2048,256]{1,0:T(8,128)(2,1)}, bf16[2048,256]{1,0:T(8,128)(2,1)}, u32[]{:S(2)}, u32[]{:S(2)}) %collective-permute-start.13) | collective-permute-done | bytes 1048608 | tf_op jit(solution)/shard_map/ppermute | solution.py:61
  143.7 4.1 %add_convert_fusion = bf16[2048,256]{1,0:T(8,128)(2,1)} fusion(bf16[2048,256]{1,0:T(8,128)(2,1)} %collective-permute-done.13, bf16[2048,256]{1,0:T(8,128)(2,1)} %collective-permute-done.10, bf16[2048,256]{1,0:T(8,128)(2,1)} %collective-permute-done.8, bf16[2048,256]{1,0:T(8,128)(2,1)} %collective-permute-done.7, bf16[2048,256]{1,0:T(8,128)(2,1)} %copy-done.1), kind=kLoop, calls=%fused_computation | loop fusion | flops 5242880 | bytes 6291456 | tf_op jit(solution)/shard_map/convert_element_type | solution.py:161
  147.8 4.4 %all-to-all-start.3 = ((bf16[4,512,256]{2,1,0:T(8,128)(2,1)}), bf16[4,512,256]{2,1,0:T(8,128)(2,1)}, u32[]{:S(2)}, u32[]{:S(2)}) async-start(bf16[4,512,256]{2,1,0:T(8,128)(2,1)} %bitcast.78), calls=%async_computation.3 | async-start | bytes 2097152 | tf_op jit(solution)/shard_map/all_to_all | solution.py:165
  152.2 1.1 slice_bitcast_fusion.8
  153.2 1.3 fusion.6
  154.5 1.3 fusion.7
  155.8 1.3 fusion.9
  157.1 1.3 fusion.8
  158.4 3.6 %all-to-all-done.3 = bf16[4,512,256]{2,1,0:T(8,128)(2,1)} async-done(((bf16[4,512,256]{2,1,0:T(8,128)(2,1)}), bf16[4,512,256]{2,1,0:T(8,128)(2,1)}, u32[]{:S(2)}, u32[]{:S(2)}) %all-to-all-start.3) | async-done | bytes 1048608 | tf_op jit(solution)/shard_map/all_to_all | solution.py:165
  162.0 1.3 slice_bitcast_fusion.2
  163.9 0.4 fusion.5
  164.3 8.2 %collective-permute-start.15 = (bf16[384,512]{1,0:T(8,128)(2,1)S(1)}, bf16[384,512]{1,0:T(8,128)(2,1)S(1)}, u32[]{:S(2)}, u32[]{:S(2)}) collective-permute-start(bf16[384,512]{1,0:T(8,128)(2,1)S(1)} %fusion.5), channel_id=1, source_target_pairs={{0,1},{1,0},{2,3},{3,2},{4,5},{5,4},{6,7},{7,6},{8,9},{9,8},{10,11... | collective-permute-start | bytes 1179656 | tf_op jit(solution)/shard_map/ppermute | solution.py:61
  172.5 0.4 convolution_add_fusion.5
  172.9 0.4 fusion.2
  173.9 0.4 add_convert_fusion.4
  174.4 2.7 %collective-permute-start.16 = (bf16[384,512]{1,0:T(8,128)(2,1)S(1)}, bf16[384,512]{1,0:T(8,128)(2,1)S(1)}, u32[]{:S(2)}, u32[]{:S(2)}) collective-permute-start(bf16[384,512]{1,0:T(8,128)(2,1)S(1)} %add_convert_fusion.4), channel_id=1, source_target_pairs={{0,2},{1,3},{2,0},{3,1},{4,6},{5,7},{6,4},{7,5},{8,10},{9,11},{10,... | collective-permute-start | bytes 1179656 | tf_op jit(solution)/shard_map/ppermute | solution.py:61
  177.1 0.4 convolution_add_fusion.7
  177.5 0.4 fusion.1
  177.9 8.4 %collective-permute-done.16 = bf16[384,512]{1,0:T(8,128)(2,1)S(1)} collective-permute-done((bf16[384,512]{1,0:T(8,128)(2,1)S(1)}, bf16[384,512]{1,0:T(8,128)(2,1)S(1)}, u32[]{:S(2)}, u32[]{:S(2)}) %collective-permute-start.16) | collective-permute-done | bytes 393248 | tf_op jit(solution)/shard_map/ppermute | solution.py:61
  186.3 0.9 add_convert_fusion.3
  (39 shorter events, 1.9 us)
Async XLA Ops:
  0.0 153.2 %copy-start = (bf16[3,1536,384]{2,1,0:T(8,128)(2,1)S(1)}, bf16[3,1536,384]{2,1,0:T(8,128)(2,1)}, u32[]{:S(2)}) copy-start(bf16[3,1536,384]{2,1,0:T(8,128)(2,1)} %param.13) | copy-start | bytes 10616836
  16.3 24.0 %collective-permute-start.3 = (bf16[2048,256]{1,0:T(8,128)(2,1)}, bf16[2048,256]{1,0:T(8,128)(2,1)}, u32[]{:S(2)}, u32[]{:S(2)}) collective-permute-start(bf16[2048,256]{1,0:T(8,128)(2,1)} %bitcast.5.refs_0_), channel_id=1, source_target_pairs={{0,16},{1,17},{2,18},{3,19},{4,20},{5,21},{6,22},{7,23},{8,24},{9,... | collective-permute-start | bytes 3145736 | tf_op jit(solution)/shard_map/ppermute | solution.py:61
  19.5 22.7 %collective-permute-start.1 = (bf16[2048,256]{1,0:T(8,128)(2,1)}, bf16[2048,256]{1,0:T(8,128)(2,1)}, u32[]{:S(2)}, u32[]{:S(2)}) collective-permute-start(bf16[2048,256]{1,0:T(8,128)(2,1)} %bitcast.5.refs_0_), channel_id=1, source_target_pairs={{0,64},{1,9},{2,66},{3,11},{4,68},{5,13},{6,70},{7,15},{8,72},{9,1... | collective-permute-start | bytes 3145736 | tf_op jit(solution)/shard_map/ppermute | solution.py:61
  28.6 25.6 %copy-start.7 = (s32[128,3]{0,1:T(4,128)S(1)}, s32[128,3]{0,1:T(4,128)}, u32[]{:S(2)}) copy-start(s32[128,3]{0,1:T(4,128)} %param.14) | copy-start | bytes 4612
  28.6 41.2 %collective-permute-start = (bf16[2048,256]{1,0:T(8,128)(2,1)}, bf16[2048,256]{1,0:T(8,128)(2,1)}, u32[]{:S(2)}, u32[]{:S(2)}) collective-permute-start(bf16[2048,256]{1,0:T(8,128)(2,1)} %bitcast.5.refs_0_), channel_id=1, source_target_pairs={{0,96},{1,13},{2,98},{3,15},{4,100},{5,1},{6,102},{7,3},{8,104},{9... | collective-permute-start | bytes 3145736 | tf_op jit(solution)/shard_map/ppermute | solution.py:61
  31.0 38.9 %collective-permute-start.2 = (bf16[2048,256]{1,0:T(8,128)(2,1)}, bf16[2048,256]{1,0:T(8,128)(2,1)}, u32[]{:S(2)}, u32[]{:S(2)}) collective-permute-start(bf16[2048,256]{1,0:T(8,128)(2,1)} %bitcast.5.refs_0_), channel_id=1, source_target_pairs={{0,32},{1,5},{2,34},{3,7},{4,36},{5,9},{6,38},{7,11},{8,40},{9,13}... | collective-permute-start | bytes 3145736 | tf_op jit(solution)/shard_map/ppermute | solution.py:61
  40.3 29.5 %collective-permute-start.4 = (bf16[2048,256]{1,0:T(8,128)(2,1)}, bf16[2048,256]{1,0:T(8,128)(2,1)}, u32[]{:S(2)}, u32[]{:S(2)}) collective-permute-start(bf16[2048,256]{1,0:T(8,128)(2,1)} %collective-permute-done.3.refs_4_), channel_id=1, source_target_pairs={{0,96},{1,13},{2,98},{3,15},{4,100},{5,1},{6,102},{7,3},{8,104},{9... | collective-permute-start | bytes 3145736 | tf_op jit(solution)/shard_map/ppermute | solution.py:61
  42.2 27.6 %collective-permute-start.5 = (bf16[2048,256]{1,0:T(8,128)(2,1)}, bf16[2048,256]{1,0:T(8,128)(2,1)}, u32[]{:S(2)}, u32[]{:S(2)}) collective-permute-start(bf16[2048,256]{1,0:T(8,128)(2,1)} %collective-permute-done.1.refs_2_), channel_id=1, source_target_pairs={{0,16},{1,17},{2,18},{3,19},{4,20},{5,21},{6,22},{7,23},{8,24},{9,... | collective-permute-start | bytes 3145736 | tf_op jit(solution)/shard_map/ppermute | solution.py:61
  45.5 24.5 %collective-permute-start.6 = (bf16[2048,256]{1,0:T(8,128)(2,1)}, bf16[2048,256]{1,0:T(8,128)(2,1)}, u32[]{:S(2)}, u32[]{:S(2)}) collective-permute-start(bf16[2048,256]{1,0:T(8,128)(2,1)} %collective-permute-done.3.refs_4_), channel_id=1, source_target_pairs={{0,32},{1,5},{2,34},{3,7},{4,36},{5,9},{6,38},{7,11},{8,40},{9,13}... | collective-permute-start | bytes 3145736 | tf_op jit(solution)/shard_map/ppermute | solution.py:61
  49.8 20.1 %all-to-all-start = ((bf16[4,512,256]{2,1,0:T(8,128)(2,1)}), bf16[4,512,256]{2,1,0:T(8,128)(2,1)}, u32[]{:S(2)}, u32[]{:S(2)}) async-start(bf16[4,512,256]{2,1,0:T(8,128)(2,1)} %bitcast.77), calls=%async_computation | async-start | bytes 2097152 | tf_op jit(solution)/shard_map/all_to_all | solution.py:165
  90.3 23.1 %copy-start.1 = (bf16[2048,256]{1,0:T(8,128)(2,1)}, bf16[2048,256]{1,0:T(8,128)(2,1)S(1)}, u32[]{:S(2)}) copy-start(bf16[2048,256]{1,0:T(8,128)(2,1)S(1)} %get-tuple-element.17) | copy-start | bytes 3145732
  90.4 23.1 %copy-start.2 = (bf16[2048,128]{1,0:T(8,128)(2,1)}, bf16[2048,128]{1,0:T(8,128)(2,1)S(1)}, u32[]{:S(2)}) copy-start(bf16[2048,128]{1,0:T(8,128)(2,1)S(1)} %get-tuple-element.16) | copy-start | bytes 1572868
  90.4 17.5 %collective-permute-start.12 = (bf16[2048,256]{1,0:T(8,128)(2,1)S(1)}, bf16[2048,256]{1,0:T(8,128)(2,1)S(1)}, u32[]{:S(2)}, u32[]{:S(2)}) collective-permute-start(bf16[2048,256]{1,0:T(8,128)(2,1)S(1)} %get-tuple-element.24), channel_id=1, source_target_pairs={{0,96},{1,13},{2,98},{3,15},{4,100},{5,1},{6,102},{7,3},{8,104},{9... | collective-permute-start | bytes 3145736 | tf_op jit(solution)/shard_map/ppermute | solution.py:61
  94.6 17.2 %collective-permute-start.11 = (bf16[2048,256]{1,0:T(8,128)(2,1)S(1)}, bf16[2048,256]{1,0:T(8,128)(2,1)S(1)}, u32[]{:S(2)}, u32[]{:S(2)}) collective-permute-start(bf16[2048,256]{1,0:T(8,128)(2,1)S(1)} %get-tuple-element.23), channel_id=1, source_target_pairs={{0,32},{1,5},{2,34},{3,7},{4,36},{5,9},{6,38},{7,11},{8,40},{9,13}... | collective-permute-start | bytes 3145736 | tf_op jit(solution)/shard_map/ppermute | solution.py:61
  97.4 23.9 %collective-permute-start.9 = (bf16[2048,256]{1,0:T(8,128)(2,1)S(1)}, bf16[2048,256]{1,0:T(8,128)(2,1)S(1)}, u32[]{:S(2)}, u32[]{:S(2)}) collective-permute-start(bf16[2048,256]{1,0:T(8,128)(2,1)S(1)} %get-tuple-element.21), channel_id=1, source_target_pairs={{0,16},{1,17},{2,18},{3,19},{4,20},{5,21},{6,22},{7,23},{8,24},{9,... | collective-permute-start | bytes 3145736 | tf_op jit(solution)/shard_map/ppermute | solution.py:61
  99.4 32.9 %collective-permute-start.8 = (bf16[2048,256]{1,0:T(8,128)(2,1)}, bf16[2048,256]{1,0:T(8,128)(2,1)}, u32[]{:S(2)}, u32[]{:S(2)}) collective-permute-start(bf16[2048,256]{1,0:T(8,128)(2,1)} %get-tuple-element.19), channel_id=1, source_target_pairs={{0,96},{1,13},{2,98},{3,15},{4,100},{5,1},{6,102},{7,3},{8,104},{9... | collective-permute-start | bytes 3145736 | tf_op jit(solution)/shard_map/ppermute | solution.py:61
  104.2 28.1 %collective-permute-start.7 = (bf16[2048,256]{1,0:T(8,128)(2,1)}, bf16[2048,256]{1,0:T(8,128)(2,1)}, u32[]{:S(2)}, u32[]{:S(2)}) collective-permute-start(bf16[2048,256]{1,0:T(8,128)(2,1)} %get-tuple-element.18), channel_id=1, source_target_pairs={{0,32},{1,5},{2,34},{3,7},{4,36},{5,9},{6,38},{7,11},{8,40},{9,13}... | collective-permute-start | bytes 3145736 | tf_op jit(solution)/shard_map/ppermute | solution.py:61
  113.5 30.2 %collective-permute-start.13 = (bf16[2048,256]{1,0:T(8,128)(2,1)}, bf16[2048,256]{1,0:T(8,128)(2,1)}, u32[]{:S(2)}, u32[]{:S(2)}) collective-permute-start(bf16[2048,256]{1,0:T(8,128)(2,1)} %add_convert_fusion.1), channel_id=1, source_target_pairs={{0,16},{1,17},{2,18},{3,19},{4,20},{5,21},{6,22},{7,23},{8,24},{9,... | collective-permute-start | bytes 3145736 | tf_op jit(solution)/shard_map/ppermute | solution.py:61
  122.6 21.1 %collective-permute-start.10 = (bf16[2048,256]{1,0:T(8,128)(2,1)}, bf16[2048,256]{1,0:T(8,128)(2,1)}, u32[]{:S(2)}, u32[]{:S(2)}) collective-permute-start(bf16[2048,256]{1,0:T(8,128)(2,1)} %add_convert_fusion.2), channel_id=1, source_target_pairs={{0,64},{1,9},{2,66},{3,11},{4,68},{5,13},{6,70},{7,15},{8,72},{9,1... | collective-permute-start | bytes 3145736 | tf_op jit(solution)/shard_map/ppermute | solution.py:61
  128.2 19.7 %all-to-all-start.2 = ((bf16[4,512,128]{2,1,0:T(8,128)(2,1)}), bf16[4,512,128]{2,1,0:T(8,128)(2,1)}, u32[]{:S(2)}, u32[]{:S(2)}) async-start(bf16[4,512,128]{2,1,0:T(8,128)(2,1)} %bitcast.75), calls=%async_computation.2 | async-start | bytes 1048576 | tf_op jit(solution)/shard_map/all_to_all | solution.py:165
  147.8 14.2 %all-to-all-start.3 = ((bf16[4,512,256]{2,1,0:T(8,128)(2,1)}), bf16[4,512,256]{2,1,0:T(8,128)(2,1)}, u32[]{:S(2)}, u32[]{:S(2)}) async-start(bf16[4,512,256]{2,1,0:T(8,128)(2,1)} %bitcast.78), calls=%async_computation.3 | async-start | bytes 2097152 | tf_op jit(solution)/shard_map/all_to_all | solution.py:165
  162.0 1.5 copy-start.6
  163.4 9.1 %copy-start.5 = (f32[384,512]{1,0:T(8,128)S(1)}, f32[384,512]{1,0:T(8,128)}, u32[]{:S(2)}) copy-start(f32[384,512]{1,0:T(8,128)} %fusion.8) | copy-start | bytes 2359300
  164.3 9.2 %copy-start.4 = (f32[384,512]{1,0:T(8,128)S(1)}, f32[384,512]{1,0:T(8,128)}, u32[]{:S(2)}) copy-start(f32[384,512]{1,0:T(8,128)} %fusion.7) | copy-start | bytes 2359300
  164.3 9.6 %collective-permute-start.15 = (bf16[384,512]{1,0:T(8,128)(2,1)S(1)}, bf16[384,512]{1,0:T(8,128)(2,1)S(1)}, u32[]{:S(2)}, u32[]{:S(2)}) collective-permute-start(bf16[384,512]{1,0:T(8,128)(2,1)S(1)} %fusion.5), channel_id=1, source_target_pairs={{0,1},{1,0},{2,3},{3,2},{4,5},{5,4},{6,7},{7,6},{8,9},{9,8},{10,11... | collective-permute-start | bytes 1179656 | tf_op jit(solution)/shard_map/ppermute | solution.py:61
  173.3 3.8 %copy-start.3 = (f32[384,512]{1,0:T(8,128)S(1)}, f32[384,512]{1,0:T(8,128)}, u32[]{:S(2)}) copy-start(f32[384,512]{1,0:T(8,128)} %fusion.9) | copy-start | bytes 2359300
  173.3 4.6 %collective-permute-start.14 = (bf16[384,512]{1,0:T(8,128)(2,1)S(1)}, bf16[384,512]{1,0:T(8,128)(2,1)S(1)}, u32[]{:S(2)}, u32[]{:S(2)}) collective-permute-start(bf16[384,512]{1,0:T(8,128)(2,1)S(1)} %fusion.2), channel_id=1, source_target_pairs={{0,1},{1,0},{2,3},{3,2},{4,5},{5,4},{6,7},{7,6},{8,9},{9,8},{10,11... | collective-permute-start | bytes 1179656 | tf_op jit(solution)/shard_map/ppermute | solution.py:61
  174.4 11.9 %collective-permute-start.16 = (bf16[384,512]{1,0:T(8,128)(2,1)S(1)}, bf16[384,512]{1,0:T(8,128)(2,1)S(1)}, u32[]{:S(2)}, u32[]{:S(2)}) collective-permute-start(bf16[384,512]{1,0:T(8,128)(2,1)S(1)} %add_convert_fusion.4), channel_id=1, source_target_pairs={{0,2},{1,3},{2,0},{3,1},{4,6},{5,7},{6,4},{7,5},{8,10},{9,11},{10,... | collective-permute-start | bytes 1179656 | tf_op jit(solution)/shard_map/ppermute | solution.py:61

commit v9 on v8

--- a/solution.py
+++ b/solution.py
@@ -101,7 +101,7 @@
         probs = e * inv
         coeff = (probs * (slope - weighted)).astype(BF16)
         low = probs.astype(BF16)
-        gq = lax.dot_general(coeff, kv_now[:, :HD], tn, preferred_element_type=F32)
+        gq = lax.dot_general(kv_now[:, :HD], coeff, tn, preferred_element_type=F32).T
         gq_ref[rows, :] = (gq * scale).astype(BF16)
         gk = lax.dot_general(coeff, q, nn, preferred_element_type=F32)
         gv = lax.dot_general(low, d, nn, preferred_element_type=F32)
@@ -111,7 +111,7 @@
             acc[pl.ds(at[j], BLK), HD:] += gv[part]
         return carry
 
-    lax.fori_loop(0, NQ, step, 0, unroll=4)
+    lax.fori_loop(0, NQ, step, 0, unroll=8)
 
     stores = [
         pltpu.make_async_copy(kv.at[pl.ds(m * ROWS, ROWS)], out_refs[m], out_sems.at[m])

time: 188 us -> 188 us (level)
  no operation moved by 1% of the time
where the time goes in v9:
time: 188 us; the launch traced here: 187 us
  starting transfers between devices  71 us (38%)
  waiting for transfers between devices  55 us (29%)
  Pallas kernels  24.2 us (13%)
  blocking collectives  14.8 us (8%)
  other arithmetic  8.47 us (5%)
  matrix products  8.39 us (4%)
  local copies, waits for them, and re-layouts  4.76 us (3%)
    ppermute x17, starting transfers between devices, send(): return lax.ppermute(x, AXES, perm)  58.2 us
    ppermute x17, waiting for transfers between devices, send(): return lax.ppermute(x, AXES, perm)  36.8 us
    pallas_call x1, Pallas kernels, attend(): pl.pallas_call(attend_kernel, name='attend', out_shape=(jax.ShapeDtypeStr...  20.4 us
    all_to_all x3, waiting for transfers between devices, exchange(): return lax.all_to_all(x, AXES, 0, 0, axis_index_groups=LINES, tiled=True)  18.1 us
    all_to_all x1, blocking collectives, exchange(): return lax.all_to_all(x, AXES, 0, 0, axis_index_groups=LINES, tiled=True)  14.8 us
    all_to_all x3, starting transfers between devices, exchange(): return lax.all_to_all(x, AXES, 0, 0, axis_index_groups=LINES, tiled=True)  12.9 us
    dot_general x12, matrix products, share(): lax.dot_general(w[j], g, (((1,), (1,)), ((), ())), preferred_element_type...  8.39 us
    convert_element_type x4, other arithmetic, add(): functools.reduce(lambda a, b: a + b, [t.astype(F32) for t in terms])  7.95 us
  transfers between devices with their start and end apart: 20, of which 9 were waited for; matrix products, arithmetic and copies ran while one was open for 9% of the time, Pallas kernels for 2%

profile of v9, /device:TPU:1, one launch (start us, length us, event | category | flops | bytes accessed | tf_op | source)
XLA Modules:
  0.0 187.1 jit_solution(5842009048628345135)
XLA Ops:
  0.0 1.4 fusion.37
  1.5 14.8 %all_to_all.40 = bf16[4,512,256]{2,1,0:T(8,128)(2,1)} all-to-all(bf16[4,512,256]{2,1,0:T(8,128)(2,1)S(1)} %bitcast.76), channel_id=1, replica_groups={{0,4,8,12},{1,33,65,97},{2,6,10,14},{3,35,67,99},{5,37,69,101},{7,39,71..., dimensions={0} | all-to-all | bytes 2097152 | tf_op jit(solution)/shard_map/all_to_all | solution.py:165
  16.3 3.2 %collective-permute-start.3 = (bf16[2048,256]{1,0:T(8,128)(2,1)}, bf16[2048,256]{1,0:T(8,128)(2,1)}, u32[]{:S(2)}, u32[]{:S(2)}) collective-permute-start(bf16[2048,256]{1,0:T(8,128)(2,1)} %bitcast.5.refs_0_), channel_id=1, source_target_pairs={{0,16},{1,17},{2,18},{3,19},{4,20},{5,21},{6,22},{7,23},{8,24},{9,... | collective-permute-start | bytes 3145736 | tf_op jit(solution)/shard_map/ppermute | solution.py:61
  19.5 5.2 %collective-permute-start.1 = (bf16[2048,256]{1,0:T(8,128)(2,1)}, bf16[2048,256]{1,0:T(8,128)(2,1)}, u32[]{:S(2)}, u32[]{:S(2)}) collective-permute-start(bf16[2048,256]{1,0:T(8,128)(2,1)} %bitcast.5.refs_0_), channel_id=1, source_target_pairs={{0,64},{1,9},{2,66},{3,11},{4,68},{5,13},{6,70},{7,15},{8,72},{9,1... | collective-permute-start | bytes 3145736 | tf_op jit(solution)/shard_map/ppermute | solution.py:61
  24.7 3.9 %prepare.1 = bf16[2048,256]{1,0:T(8,128)(2,1)} custom-call(bf16[512,1536]{1,0:T(8,128)(2,1)} %up_hbm.1, bf16[384,1536]{1,0:T(8,128)(2,1)} %out_w_hbm.1, bf16[512,384]{1,0:T(8,128)(2,1)} %q_hbm.1), custom_call_target="tpu_custom_call" | custom-call | tf_op jit(solution)/shard_map/prepare/pallas_call | solution.py:203
  28.6 2.3 %collective-permute-start = (bf16[2048,256]{1,0:T(8,128)(2,1)}, bf16[2048,256]{1,0:T(8,128)(2,1)}, u32[]{:S(2)}, u32[]{:S(2)}) collective-permute-start(bf16[2048,256]{1,0:T(8,128)(2,1)} %bitcast.5.refs_0_), channel_id=1, source_target_pairs={{0,96},{1,13},{2,98},{3,15},{4,100},{5,1},{6,102},{7,3},{8,104},{9... | collective-permute-start | bytes 3145736 | tf_op jit(solution)/shard_map/ppermute | solution.py:61
  31.0 2.9 %collective-permute-start.2 = (bf16[2048,256]{1,0:T(8,128)(2,1)}, bf16[2048,256]{1,0:T(8,128)(2,1)}, u32[]{:S(2)}, u32[]{:S(2)}) collective-permute-start(bf16[2048,256]{1,0:T(8,128)(2,1)} %bitcast.5.refs_0_), channel_id=1, source_target_pairs={{0,32},{1,5},{2,34},{3,7},{4,36},{5,9},{6,38},{7,11},{8,40},{9,13}... | collective-permute-start | bytes 3145736 | tf_op jit(solution)/shard_map/ppermute | solution.py:61
  33.9 6.4 %collective-permute-done.3.refs_4_ = bf16[2048,256]{1,0:T(8,128)(2,1)} collective-permute-done((bf16[2048,256]{1,0:T(8,128)(2,1)}, bf16[2048,256]{1,0:T(8,128)(2,1)}, u32[]{:S(2)}, u32[]{:S(2)}) %collective-permute-start.3) | collective-permute-done | bytes 1048608 | tf_op jit(solution)/shard_map/ppermute | solution.py:61
  40.3 1.9 %collective-permute-start.4 = (bf16[2048,256]{1,0:T(8,128)(2,1)}, bf16[2048,256]{1,0:T(8,128)(2,1)}, u32[]{:S(2)}, u32[]{:S(2)}) collective-permute-start(bf16[2048,256]{1,0:T(8,128)(2,1)} %collective-permute-done.3.refs_4_), channel_id=1, source_target_pairs={{0,96},{1,13},{2,98},{3,15},{4,100},{5,1},{6,102},{7,3},{8,104},{9... | collective-permute-start | bytes 3145736 | tf_op jit(solution)/shard_map/ppermute | solution.py:61
  42.2 3.2 %collective-permute-start.5 = (bf16[2048,256]{1,0:T(8,128)(2,1)}, bf16[2048,256]{1,0:T(8,128)(2,1)}, u32[]{:S(2)}, u32[]{:S(2)}) collective-permute-start(bf16[2048,256]{1,0:T(8,128)(2,1)} %collective-permute-done.1.refs_2_), channel_id=1, source_target_pairs={{0,16},{1,17},{2,18},{3,19},{4,20},{5,21},{6,22},{7,23},{8,24},{9,... | collective-permute-start | bytes 3145736 | tf_op jit(solution)/shard_map/ppermute | solution.py:61
  45.5 4.3 %collective-permute-start.6 = (bf16[2048,256]{1,0:T(8,128)(2,1)}, bf16[2048,256]{1,0:T(8,128)(2,1)}, u32[]{:S(2)}, u32[]{:S(2)}) collective-permute-start(bf16[2048,256]{1,0:T(8,128)(2,1)} %collective-permute-done.3.refs_4_), channel_id=1, source_target_pairs={{0,32},{1,5},{2,34},{3,7},{4,36},{5,9},{6,38},{7,11},{8,40},{9,13}... | collective-permute-start | bytes 3145736 | tf_op jit(solution)/shard_map/ppermute | solution.py:61
  49.8 4.3 %all-to-all-start = ((bf16[4,512,256]{2,1,0:T(8,128)(2,1)}), bf16[4,512,256]{2,1,0:T(8,128)(2,1)}, u32[]{:S(2)}, u32[]{:S(2)}) async-start(bf16[4,512,256]{2,1,0:T(8,128)(2,1)} %bitcast.77), calls=%async_computation | async-start | bytes 2097152 | tf_op jit(solution)/shard_map/all_to_all | solution.py:165
  54.5 0.7 pad.19.clone
  55.4 14.5 %all-to-all-done = bf16[4,512,256]{2,1,0:T(8,128)(2,1)} async-done(((bf16[4,512,256]{2,1,0:T(8,128)(2,1)}), bf16[4,512,256]{2,1,0:T(8,128)(2,1)}, u32[]{:S(2)}, u32[]{:S(2)}) %all-to-all-start) | async-done | bytes 1048608 | tf_op jit(solution)/shard_map/all_to_all | solution.py:165
  69.9 20.4 %attend.1 = (bf16[2048,128]{1,0:T(8,128)(2,1)S(1)}, bf16[2048,256]{1,0:T(8,128)(2,1)S(1)}, bf16[2048,256]{1,0:T(8,128)(2,1)}, bf16[2048,256]{1,0:T(8,128)(2,1)S(...) custom-call(s32[16,8]{1,0:T(8,128)S(1)} %fusion.18.table, ...), custom_call_target="tpu_custom_call" | custom-call | tf_op jit(solution)/shard_map/attend/pallas_call | solution.py:138
  90.3 4.2 %collective-permute-start.12 = (bf16[2048,256]{1,0:T(8,128)(2,1)S(1)}, bf16[2048,256]{1,0:T(8,128)(2,1)S(1)}, u32[]{:S(2)}, u32[]{:S(2)}) collective-permute-start(bf16[2048,256]{1,0:T(8,128)(2,1)S(1)} %get-tuple-element.24), channel_id=1, source_target_pairs={{0,96},{1,13},{2,98},{3,15},{4,100},{5,1},{6,102},{7,3},{8,104},{9... | collective-permute-start | bytes 3145736 | tf_op jit(solution)/shard_map/ppermute | solution.py:61
  94.6 2.7 %collective-permute-start.11 = (bf16[2048,256]{1,0:T(8,128)(2,1)S(1)}, bf16[2048,256]{1,0:T(8,128)(2,1)S(1)}, u32[]{:S(2)}, u32[]{:S(2)}) collective-permute-start(bf16[2048,256]{1,0:T(8,128)(2,1)S(1)} %get-tuple-element.23), channel_id=1, source_target_pairs={{0,32},{1,5},{2,34},{3,7},{4,36},{5,9},{6,38},{7,11},{8,40},{9,13}... | collective-permute-start | bytes 3145736 | tf_op jit(solution)/shard_map/ppermute | solution.py:61
  97.3 2.1 %collective-permute-start.9 = (bf16[2048,256]{1,0:T(8,128)(2,1)S(1)}, bf16[2048,256]{1,0:T(8,128)(2,1)S(1)}, u32[]{:S(2)}, u32[]{:S(2)}) collective-permute-start(bf16[2048,256]{1,0:T(8,128)(2,1)S(1)} %get-tuple-element.21), channel_id=1, source_target_pairs={{0,16},{1,17},{2,18},{3,19},{4,20},{5,21},{6,22},{7,23},{8,24},{9,... | collective-permute-start | bytes 3145736 | tf_op jit(solution)/shard_map/ppermute | solution.py:61
  99.4 4.8 %collective-permute-start.8 = (bf16[2048,256]{1,0:T(8,128)(2,1)}, bf16[2048,256]{1,0:T(8,128)(2,1)}, u32[]{:S(2)}, u32[]{:S(2)}) collective-permute-start(bf16[2048,256]{1,0:T(8,128)(2,1)} %get-tuple-element.19), channel_id=1, source_target_pairs={{0,96},{1,13},{2,98},{3,15},{4,100},{5,1},{6,102},{7,3},{8,104},{9... | collective-permute-start | bytes 3145736 | tf_op jit(solution)/shard_map/ppermute | solution.py:61
  104.2 1.9 %collective-permute-start.7 = (bf16[2048,256]{1,0:T(8,128)(2,1)}, bf16[2048,256]{1,0:T(8,128)(2,1)}, u32[]{:S(2)}, u32[]{:S(2)}) collective-permute-start(bf16[2048,256]{1,0:T(8,128)(2,1)} %get-tuple-element.18), channel_id=1, source_target_pairs={{0,32},{1,5},{2,34},{3,7},{4,36},{5,9},{6,38},{7,11},{8,40},{9,13}... | collective-permute-start | bytes 3145736 | tf_op jit(solution)/shard_map/ppermute | solution.py:61
  106.1 1.8 collective-permute-done.12
  107.9 4.0 %collective-permute-done.11 = bf16[2048,256]{1,0:T(8,128)(2,1)S(1)} collective-permute-done((bf16[2048,256]{1,0:T(8,128)(2,1)S(1)}, bf16[2048,256]{1,0:T(8,128)(2,1)S(1)}, u32[]{:S(2)}, u32[]{:S(2)}) %collective-permute-start.11) | collective-permute-done | bytes 1048608 | tf_op jit(solution)/shard_map/ppermute | solution.py:61
  111.8 1.6 add_convert_fusion.1
  113.4 2.9 %collective-permute-start.13 = (bf16[2048,256]{1,0:T(8,128)(2,1)}, bf16[2048,256]{1,0:T(8,128)(2,1)}, u32[]{:S(2)}, u32[]{:S(2)}) collective-permute-start(bf16[2048,256]{1,0:T(8,128)(2,1)} %add_convert_fusion.1), channel_id=1, source_target_pairs={{0,16},{1,17},{2,18},{3,19},{4,20},{5,21},{6,22},{7,23},{8,24},{9,... | collective-permute-start | bytes 3145736 | tf_op jit(solution)/shard_map/ppermute | solution.py:61
  116.3 4.9 %collective-permute-done.9 = bf16[2048,256]{1,0:T(8,128)(2,1)S(1)} collective-permute-done((bf16[2048,256]{1,0:T(8,128)(2,1)S(1)}, bf16[2048,256]{1,0:T(8,128)(2,1)S(1)}, u32[]{:S(2)}, u32[]{:S(2)}) %collective-permute-start.9) | collective-permute-done | bytes 1048608 | tf_op jit(solution)/shard_map/ppermute | solution.py:61
  121.2 1.4 add_convert_fusion.2
  122.5 5.6 %collective-permute-start.10 = (bf16[2048,256]{1,0:T(8,128)(2,1)}, bf16[2048,256]{1,0:T(8,128)(2,1)}, u32[]{:S(2)}, u32[]{:S(2)}) collective-permute-start(bf16[2048,256]{1,0:T(8,128)(2,1)} %add_convert_fusion.2), channel_id=1, source_target_pairs={{0,64},{1,9},{2,66},{3,11},{4,68},{5,13},{6,70},{7,15},{8,72},{9,1... | collective-permute-start | bytes 3145736 | tf_op jit(solution)/shard_map/ppermute | solution.py:61
  128.1 4.2 %all-to-all-start.2 = ((bf16[4,512,128]{2,1,0:T(8,128)(2,1)}), bf16[4,512,128]{2,1,0:T(8,128)(2,1)}, u32[]{:S(2)}, u32[]{:S(2)}) async-start(bf16[4,512,128]{2,1,0:T(8,128)(2,1)} %bitcast.75), calls=%async_computation.2 | async-start | bytes 1048576 | tf_op jit(solution)/shard_map/all_to_all | solution.py:165
  132.3 11.3 %collective-permute-done.13 = bf16[2048,256]{1,0:T(8,128)(2,1)} collective-permute-done((bf16[2048,256]{1,0:T(8,128)(2,1)}, bf16[2048,256]{1,0:T(8,128)(2,1)}, u32[]{:S(2)}, u32[]{:S(2)}) %collective-permute-start.13) | collective-permute-done | bytes 1048608 | tf_op jit(solution)/shard_map/ppermute | solution.py:61
  143.7 4.1 %add_convert_fusion = bf16[2048,256]{1,0:T(8,128)(2,1)} fusion(bf16[2048,256]{1,0:T(8,128)(2,1)} %collective-permute-done.13, bf16[2048,256]{1,0:T(8,128)(2,1)} %collective-permute-done.10, bf16[2048,256]{1,0:T(8,128)(2,1)} %collective-permute-done.8, bf16[2048,256]{1,0:T(8,128)(2,1)} %collective-permute-done.7, bf16[2048,256]{1,0:T(8,128)(2,1)} %copy-done.1), kind=kLoop, calls=%fused_computation | loop fusion | flops 5242880 | bytes 6291456 | tf_op jit(solution)/shard_map/convert_element_type | solution.py:161
  147.8 4.4 %all-to-all-start.3 = ((bf16[4,512,256]{2,1,0:T(8,128)(2,1)}), bf16[4,512,256]{2,1,0:T(8,128)(2,1)}, u32[]{:S(2)}, u32[]{:S(2)}) async-start(bf16[4,512,256]{2,1,0:T(8,128)(2,1)} %bitcast.78), calls=%async_computation.3 | async-start | bytes 2097152 | tf_op jit(solution)/shard_map/all_to_all | solution.py:165
  152.2 1.1 slice_bitcast_fusion.8
  153.3 1.3 fusion.6
  154.6 1.3 fusion.7
  155.9 1.3 fusion.9
  157.2 1.3 fusion.8
  158.5 3.7 %all-to-all-done.3 = bf16[4,512,256]{2,1,0:T(8,128)(2,1)} async-done(((bf16[4,512,256]{2,1,0:T(8,128)(2,1)}), bf16[4,512,256]{2,1,0:T(8,128)(2,1)}, u32[]{:S(2)}, u32[]{:S(2)}) %all-to-all-start.3) | async-done | bytes 1048608 | tf_op jit(solution)/shard_map/all_to_all | solution.py:165
  162.2 1.3 slice_bitcast_fusion.2
  164.0 0.4 fusion.5
  164.5 8.0 %collective-permute-start.15 = (bf16[384,512]{1,0:T(8,128)(2,1)S(1)}, bf16[384,512]{1,0:T(8,128)(2,1)S(1)}, u32[]{:S(2)}, u32[]{:S(2)}) collective-permute-start(bf16[384,512]{1,0:T(8,128)(2,1)S(1)} %fusion.5), channel_id=1, source_target_pairs={{0,1},{1,0},{2,3},{3,2},{4,5},{5,4},{6,7},{7,6},{8,9},{9,8},{10,11... | collective-permute-start | bytes 1179656 | tf_op jit(solution)/shard_map/ppermute | solution.py:61
  172.5 0.4 convolution_add_fusion.5
  172.9 0.4 fusion.2
  173.9 0.4 add_convert_fusion.4
  174.3 2.7 %collective-permute-start.16 = (bf16[384,512]{1,0:T(8,128)(2,1)S(1)}, bf16[384,512]{1,0:T(8,128)(2,1)S(1)}, u32[]{:S(2)}, u32[]{:S(2)}) collective-permute-start(bf16[384,512]{1,0:T(8,128)(2,1)S(1)} %add_convert_fusion.4), channel_id=1, source_target_pairs={{0,2},{1,3},{2,0},{3,1},{4,6},{5,7},{6,4},{7,5},{8,10},{9,11},{10,... | collective-permute-start | bytes 1179656 | tf_op jit(solution)/shard_map/ppermute | solution.py:61
  177.0 0.4 convolution_add_fusion.7
  177.4 0.4 fusion.1
  177.8 8.4 %collective-permute-done.16 = bf16[384,512]{1,0:T(8,128)(2,1)S(1)} collective-permute-done((bf16[384,512]{1,0:T(8,128)(2,1)S(1)}, bf16[384,512]{1,0:T(8,128)(2,1)S(1)}, u32[]{:S(2)}, u32[]{:S(2)}) %collective-permute-start.16) | collective-permute-done | bytes 393248 | tf_op jit(solution)/shard_map/ppermute | solution.py:61
  186.2 0.9 add_convert_fusion.3
  (39 shorter events, 1.9 us)
Async XLA Ops:
  0.0 153.3 %copy-start = (bf16[3,1536,384]{2,1,0:T(8,128)(2,1)S(1)}, bf16[3,1536,384]{2,1,0:T(8,128)(2,1)}, u32[]{:S(2)}) copy-start(bf16[3,1536,384]{2,1,0:T(8,128)(2,1)} %param.13) | copy-start | bytes 10616836
  16.3 24.0 %collective-permute-start.3 = (bf16[2048,256]{1,0:T(8,128)(2,1)}, bf16[2048,256]{1,0:T(8,128)(2,1)}, u32[]{:S(2)}, u32[]{:S(2)}) collective-permute-start(bf16[2048,256]{1,0:T(8,128)(2,1)} %bitcast.5.refs_0_), channel_id=1, source_target_pairs={{0,16},{1,17},{2,18},{3,19},{4,20},{5,21},{6,22},{7,23},{8,24},{9,... | collective-permute-start | bytes 3145736 | tf_op jit(solution)/shard_map/ppermute | solution.py:61
  19.5 22.7 %collective-permute-start.1 = (bf16[2048,256]{1,0:T(8,128)(2,1)}, bf16[2048,256]{1,0:T(8,128)(2,1)}, u32[]{:S(2)}, u32[]{:S(2)}) collective-permute-start(bf16[2048,256]{1,0:T(8,128)(2,1)} %bitcast.5.refs_0_), channel_id=1, source_target_pairs={{0,64},{1,9},{2,66},{3,11},{4,68},{5,13},{6,70},{7,15},{8,72},{9,1... | collective-permute-start | bytes 3145736 | tf_op jit(solution)/shard_map/ppermute | solution.py:61
  28.6 25.6 %copy-start.7 = (s32[128,3]{0,1:T(4,128)S(1)}, s32[128,3]{0,1:T(4,128)}, u32[]{:S(2)}) copy-start(s32[128,3]{0,1:T(4,128)} %param.14) | copy-start | bytes 4612
  28.6 41.2 %collective-permute-start = (bf16[2048,256]{1,0:T(8,128)(2,1)}, bf16[2048,256]{1,0:T(8,128)(2,1)}, u32[]{:S(2)}, u32[]{:S(2)}) collective-permute-start(bf16[2048,256]{1,0:T(8,128)(2,1)} %bitcast.5.refs_0_), channel_id=1, source_target_pairs={{0,96},{1,13},{2,98},{3,15},{4,100},{5,1},{6,102},{7,3},{8,104},{9... | collective-permute-start | bytes 3145736 | tf_op jit(solution)/shard_map/ppermute | solution.py:61
  31.0 38.9 %collective-permute-start.2 = (bf16[2048,256]{1,0:T(8,128)(2,1)}, bf16[2048,256]{1,0:T(8,128)(2,1)}, u32[]{:S(2)}, u32[]{:S(2)}) collective-permute-start(bf16[2048,256]{1,0:T(8,128)(2,1)} %bitcast.5.refs_0_), channel_id=1, source_target_pairs={{0,32},{1,5},{2,34},{3,7},{4,36},{5,9},{6,38},{7,11},{8,40},{9,13}... | collective-permute-start | bytes 3145736 | tf_op jit(solution)/shard_map/ppermute | solution.py:61
  40.3 29.5 %collective-permute-start.4 = (bf16[2048,256]{1,0:T(8,128)(2,1)}, bf16[2048,256]{1,0:T(8,128)(2,1)}, u32[]{:S(2)}, u32[]{:S(2)}) collective-permute-start(bf16[2048,256]{1,0:T(8,128)(2,1)} %collective-permute-done.3.refs_4_), channel_id=1, source_target_pairs={{0,96},{1,13},{2,98},{3,15},{4,100},{5,1},{6,102},{7,3},{8,104},{9... | collective-permute-start | bytes 3145736 | tf_op jit(solution)/shard_map/ppermute | solution.py:61
  42.2 27.6 %collective-permute-start.5 = (bf16[2048,256]{1,0:T(8,128)(2,1)}, bf16[2048,256]{1,0:T(8,128)(2,1)}, u32[]{:S(2)}, u32[]{:S(2)}) collective-permute-start(bf16[2048,256]{1,0:T(8,128)(2,1)} %collective-permute-done.1.refs_2_), channel_id=1, source_target_pairs={{0,16},{1,17},{2,18},{3,19},{4,20},{5,21},{6,22},{7,23},{8,24},{9,... | collective-permute-start | bytes 3145736 | tf_op jit(solution)/shard_map/ppermute | solution.py:61
  45.5 24.5 %collective-permute-start.6 = (bf16[2048,256]{1,0:T(8,128)(2,1)}, bf16[2048,256]{1,0:T(8,128)(2,1)}, u32[]{:S(2)}, u32[]{:S(2)}) collective-permute-start(bf16[2048,256]{1,0:T(8,128)(2,1)} %collective-permute-done.3.refs_4_), channel_id=1, source_target_pairs={{0,32},{1,5},{2,34},{3,7},{4,36},{5,9},{6,38},{7,11},{8,40},{9,13}... | collective-permute-start | bytes 3145736 | tf_op jit(solution)/shard_map/ppermute | solution.py:61
  49.8 20.1 %all-to-all-start = ((bf16[4,512,256]{2,1,0:T(8,128)(2,1)}), bf16[4,512,256]{2,1,0:T(8,128)(2,1)}, u32[]{:S(2)}, u32[]{:S(2)}) async-start(bf16[4,512,256]{2,1,0:T(8,128)(2,1)} %bitcast.77), calls=%async_computation | async-start | bytes 2097152 | tf_op jit(solution)/shard_map/all_to_all | solution.py:165
  90.3 23.1 %copy-start.1 = (bf16[2048,256]{1,0:T(8,128)(2,1)}, bf16[2048,256]{1,0:T(8,128)(2,1)S(1)}, u32[]{:S(2)}) copy-start(bf16[2048,256]{1,0:T(8,128)(2,1)S(1)} %get-tuple-element.17) | copy-start | bytes 3145732
  90.3 23.1 %copy-start.2 = (bf16[2048,128]{1,0:T(8,128)(2,1)}, bf16[2048,128]{1,0:T(8,128)(2,1)S(1)}, u32[]{:S(2)}) copy-start(bf16[2048,128]{1,0:T(8,128)(2,1)S(1)} %get-tuple-element.16) | copy-start | bytes 1572868
  90.3 17.5 %collective-permute-start.12 = (bf16[2048,256]{1,0:T(8,128)(2,1)S(1)}, bf16[2048,256]{1,0:T(8,128)(2,1)S(1)}, u32[]{:S(2)}, u32[]{:S(2)}) collective-permute-start(bf16[2048,256]{1,0:T(8,128)(2,1)S(1)} %get-tuple-element.24), channel_id=1, source_target_pairs={{0,96},{1,13},{2,98},{3,15},{4,100},{5,1},{6,102},{7,3},{8,104},{9... | collective-permute-start | bytes 3145736 | tf_op jit(solution)/shard_map/ppermute | solution.py:61
  94.6 17.2 %collective-permute-start.11 = (bf16[2048,256]{1,0:T(8,128)(2,1)S(1)}, bf16[2048,256]{1,0:T(8,128)(2,1)S(1)}, u32[]{:S(2)}, u32[]{:S(2)}) collective-permute-start(bf16[2048,256]{1,0:T(8,128)(2,1)S(1)} %get-tuple-element.23), channel_id=1, source_target_pairs={{0,32},{1,5},{2,34},{3,7},{4,36},{5,9},{6,38},{7,11},{8,40},{9,13}... | collective-permute-start | bytes 3145736 | tf_op jit(solution)/shard_map/ppermute | solution.py:61
  97.3 23.9 %collective-permute-start.9 = (bf16[2048,256]{1,0:T(8,128)(2,1)S(1)}, bf16[2048,256]{1,0:T(8,128)(2,1)S(1)}, u32[]{:S(2)}, u32[]{:S(2)}) collective-permute-start(bf16[2048,256]{1,0:T(8,128)(2,1)S(1)} %get-tuple-element.21), channel_id=1, source_target_pairs={{0,16},{1,17},{2,18},{3,19},{4,20},{5,21},{6,22},{7,23},{8,24},{9,... | collective-permute-start | bytes 3145736 | tf_op jit(solution)/shard_map/ppermute | solution.py:61
  99.4 32.9 %collective-permute-start.8 = (bf16[2048,256]{1,0:T(8,128)(2,1)}, bf16[2048,256]{1,0:T(8,128)(2,1)}, u32[]{:S(2)}, u32[]{:S(2)}) collective-permute-start(bf16[2048,256]{1,0:T(8,128)(2,1)} %get-tuple-element.19), channel_id=1, source_target_pairs={{0,96},{1,13},{2,98},{3,15},{4,100},{5,1},{6,102},{7,3},{8,104},{9... | collective-permute-start | bytes 3145736 | tf_op jit(solution)/shard_map/ppermute | solution.py:61
  104.2 28.1 %collective-permute-start.7 = (bf16[2048,256]{1,0:T(8,128)(2,1)}, bf16[2048,256]{1,0:T(8,128)(2,1)}, u32[]{:S(2)}, u32[]{:S(2)}) collective-permute-start(bf16[2048,256]{1,0:T(8,128)(2,1)} %get-tuple-element.18), channel_id=1, source_target_pairs={{0,32},{1,5},{2,34},{3,7},{4,36},{5,9},{6,38},{7,11},{8,40},{9,13}... | collective-permute-start | bytes 3145736 | tf_op jit(solution)/shard_map/ppermute | solution.py:61
  113.4 30.2 %collective-permute-start.13 = (bf16[2048,256]{1,0:T(8,128)(2,1)}, bf16[2048,256]{1,0:T(8,128)(2,1)}, u32[]{:S(2)}, u32[]{:S(2)}) collective-permute-start(bf16[2048,256]{1,0:T(8,128)(2,1)} %add_convert_fusion.1), channel_id=1, source_target_pairs={{0,16},{1,17},{2,18},{3,19},{4,20},{5,21},{6,22},{7,23},{8,24},{9,... | collective-permute-start | bytes 3145736 | tf_op jit(solution)/shard_map/ppermute | solution.py:61
  122.5 21.1 %collective-permute-start.10 = (bf16[2048,256]{1,0:T(8,128)(2,1)}, bf16[2048,256]{1,0:T(8,128)(2,1)}, u32[]{:S(2)}, u32[]{:S(2)}) collective-permute-start(bf16[2048,256]{1,0:T(8,128)(2,1)} %add_convert_fusion.2), channel_id=1, source_target_pairs={{0,64},{1,9},{2,66},{3,11},{4,68},{5,13},{6,70},{7,15},{8,72},{9,1... | collective-permute-start | bytes 3145736 | tf_op jit(solution)/shard_map/ppermute | solution.py:61
  128.1 19.7 %all-to-all-start.2 = ((bf16[4,512,128]{2,1,0:T(8,128)(2,1)}), bf16[4,512,128]{2,1,0:T(8,128)(2,1)}, u32[]{:S(2)}, u32[]{:S(2)}) async-start(bf16[4,512,128]{2,1,0:T(8,128)(2,1)} %bitcast.75), calls=%async_computation.2 | async-start | bytes 1048576 | tf_op jit(solution)/shard_map/all_to_all | solution.py:165
  147.8 14.4 %all-to-all-start.3 = ((bf16[4,512,256]{2,1,0:T(8,128)(2,1)}), bf16[4,512,256]{2,1,0:T(8,128)(2,1)}, u32[]{:S(2)}, u32[]{:S(2)}) async-start(bf16[4,512,256]{2,1,0:T(8,128)(2,1)} %bitcast.78), calls=%async_computation.3 | async-start | bytes 2097152 | tf_op jit(solution)/shard_map/all_to_all | solution.py:165
  162.2 1.5 copy-start.6
  163.5 9.0 %copy-start.5 = (f32[384,512]{1,0:T(8,128)S(1)}, f32[384,512]{1,0:T(8,128)}, u32[]{:S(2)}) copy-start(f32[384,512]{1,0:T(8,128)} %fusion.8) | copy-start | bytes 2359300
  164.5 9.0 %copy-start.4 = (f32[384,512]{1,0:T(8,128)S(1)}, f32[384,512]{1,0:T(8,128)}, u32[]{:S(2)}) copy-start(f32[384,512]{1,0:T(8,128)} %fusion.7) | copy-start | bytes 2359300
  164.5 9.4 %collective-permute-start.15 = (bf16[384,512]{1,0:T(8,128)(2,1)S(1)}, bf16[384,512]{1,0:T(8,128)(2,1)S(1)}, u32[]{:S(2)}, u32[]{:S(2)}) collective-permute-start(bf16[384,512]{1,0:T(8,128)(2,1)S(1)} %fusion.5), channel_id=1, source_target_pairs={{0,1},{1,0},{2,3},{3,2},{4,5},{5,4},{6,7},{7,6},{8,9},{9,8},{10,11... | collective-permute-start | bytes 1179656 | tf_op jit(solution)/shard_map/ppermute | solution.py:61
  173.3 3.7 %copy-start.3 = (f32[384,512]{1,0:T(8,128)S(1)}, f32[384,512]{1,0:T(8,128)}, u32[]{:S(2)}) copy-start(f32[384,512]{1,0:T(8,128)} %fusion.9) | copy-start | bytes 2359300
  173.3 4.5 %collective-permute-start.14 = (bf16[384,512]{1,0:T(8,128)(2,1)S(1)}, bf16[384,512]{1,0:T(8,128)(2,1)S(1)}, u32[]{:S(2)}, u32[]{:S(2)}) collective-permute-start(bf16[384,512]{1,0:T(8,128)(2,1)S(1)} %fusion.2), channel_id=1, source_target_pairs={{0,1},{1,0},{2,3},{3,2},{4,5},{5,4},{6,7},{7,6},{8,9},{9,8},{10,11... | collective-permute-start | bytes 1179656 | tf_op jit(solution)/shard_map/ppermute | solution.py:61
  174.3 11.9 %collective-permute-start.16 = (bf16[384,512]{1,0:T(8,128)(2,1)S(1)}, bf16[384,512]{1,0:T(8,128)(2,1)S(1)}, u32[]{:S(2)}, u32[]{:S(2)}) collective-permute-start(bf16[384,512]{1,0:T(8,128)(2,1)S(1)} %add_convert_fusion.4), channel_id=1, source_target_pairs={{0,2},{1,3},{2,0},{3,1},{4,6},{5,7},{6,4},{7,5},{8,10},{9,11},{10,... | collective-permute-start | bytes 1179656 | tf_op jit(solution)/shard_map/ppermute | solution.py:61
